TPU v7x, 32 devices: a whole 2x2x4 slice. The times are simulated.
32 devices in a mesh: batch: 8 (over z, x), shard: 4 (over y, core).
Axes of the slice: x: 2, y: 2, z: 4, core: 2. Of those that a mesh axis runs over, the one named last changes fastest.
Arguments:
- tokens: float32 [32, 256, 1024], P(('batch', 'shard')), may hold values from -6 to 6
- cotangent: float32 [32, 256, 1024], P(('batch', 'shard')), may hold values from -6 to 6
- lengths: int32 [32], P(('batch', 'shard')), may hold values from 50 to 256, as said below
- ffn_in: bfloat16 [2, 1024, 4096], P(None, None, 'shard'), may hold values from -0.1875 to 0.1875
- ffn_out: bfloat16 [2, 4096, 1024], P(None, None, 'shard'), may hold values from -0.09375 to 0.09375
- ffn_bias: bfloat16 [2, 4096], P(None, 'shard'), may hold values from -2 to 2
- qkv_proj: bfloat16 [3, 1024, 1024], P(None, None, 'shard'), may hold values from -0.1875 to 0.1875
- pos_proj: bfloat16 [1024, 1024], P(None, 'shard'), may hold values from -0.1875 to 0.1875
- out_proj: bfloat16 [1024, 1024], P(None, 'shard'), may hold values from -0.75 to 0.75
- conv_in: bfloat16 [1024, 2048], P(None, 'shard'), may hold values from -0.1875 to 0.1875
- conv_out: bfloat16 [1024, 1024], P(None, 'shard'), may hold values from -0.1875 to 0.1875
- depthwise: bfloat16 [5, 1024], P(None, 'shard'), may hold values from -2.5 to 2.5
- norm_gains: bfloat16 [6, 1024], P(None, 'shard'), may hold values from 0.5 to 1.5
- biases: bfloat16 [16, 1024], P(None, 'shard'), may hold values from -2 to 2
Outputs:
- layer_out: float32 [32, 256, 1024], P(('batch', 'shard'))
- grad_tokens: float32 [32, 256, 1024], P(('batch', 'shard'))
- grad_ffn_in: float32 [2, 1024, 4096], P(None, None, 'shard')
- grad_ffn_out: float32 [2, 4096, 1024], P(None, None, 'shard')
- grad_ffn_bias: float32 [2, 4096], P(None, 'shard')
- grad_qkv_proj: float32 [3, 1024, 1024], P(None, None, 'shard')
- grad_pos_proj: float32 [1024, 1024], P(None, 'shard')
- grad_out_proj: float32 [1024, 1024], P(None, 'shard')
- grad_conv_in: float32 [1024, 2048], P(None, 'shard')
- grad_conv_out: float32 [1024, 1024], P(None, 'shard')
- grad_depthwise: float32 [5, 1024], P(None, 'shard')
- grad_norm_gains: float32 [6, 1024], P(None, 'shard')
- grad_biases: float32 [16, 1024], P(None, 'shard')
Inputs may be any that keep to these rules, and one draw needn't show every extreme that they name: `lengths`: each utterance has between 50 and 256 live frames at the start of its 256 slots, the rest padding; some utterance has exactly 256 and some exactly 50.
All inputs are finite; a program needn't handle non-finite values.
Results may differ from a plain program's by a relative error of at most 0.025.
Values may be sent and summed in bfloat16 or wider, within the bound.
A program may use at most 256 MiB of HBM per device.

v0:
```python
import math

import jax
import jax.numpy as jnp
from jax import lax
from jax.sharding import PartitionSpec as P

HEADS = 8


epsilon = 1e-05


def to_single(array_in):
    return array_in.astype(jnp.float32)


def to_brain(array_in):
    return array_in.astype(jnp.bfloat16)


def norm_rows(values_in, gain_row, bias_row):
    row_mean = jnp.mean(values_in, axis=-1, keepdims=True)
    centered = values_in - row_mean
    spread = jnp.mean(centered * centered, axis=-1, keepdims=True)
    return centered * lax.rsqrt(spread + epsilon) * gain_row + bias_row


def dot_rows(left_side, right_side):
    return jnp.dot(left_side, right_side, preferred_element_type=jnp.float32)


def dot_back(left_side, right_side):
    return lax.dot_general(
        left_side, right_side, (((1,), (1,)), ((), ())), preferred_element_type=jnp.float32
    )


def dot_over(left_side, right_side):
    return lax.dot_general(
        left_side, right_side, (((0,), (0,)), ((), ())), preferred_element_type=jnp.float32
    )


def row_total(array_in):
    return jnp.sum(to_single(array_in), axis=0)


def position_table(length, features):
    columns = jnp.arange(2 * length - 1, dtype=jnp.float32)
    offsets = length - 1.0 - columns
    freq_rates = jnp.exp(
        jnp.arange(features // 2, dtype=jnp.float32) * (-2.0 * math.log(10000.0) / features)
    )
    angles = offsets[:, None] * freq_rates[None, :]
    return jnp.concatenate([jnp.sin(angles), jnp.cos(angles)], axis=1)


def depth_conv(gated_rows, kernel):
    length = gated_rows.shape[-2]
    half_width = (kernel.shape[0] - 1) // 2
    padding = [(0, 0)] * (gated_rows.ndim - 2) + [(half_width, half_width), (0, 0)]
    padded = jnp.pad(gated_rows, padding)
    summed = padded[..., 0:length, :] * kernel[0]
    for tap_index in range(1, kernel.shape[0]):
        summed = summed + padded[..., tap_index : tap_index + length, :] * kernel[tap_index]
    return summed


def skewed(wide_scores):
    length = wide_scores.shape[-2]
    leading = wide_scores.shape[:-2]
    flat_rows = wide_scores.reshape(leading + (length * (2 * length - 1),))
    flat_rows = flat_rows[..., length - 1 : length - 1 + length * (2 * length - 2)]
    return flat_rows.reshape(leading + (length, 2 * length - 2))[..., :length]


def gated_conv(pre_act, mask_rows, kernel, count_items, length):
    features = pre_act.shape[1] // 2
    gated_rows = pre_act[:, :features] * jax.nn.sigmoid(pre_act[:, features:]) * mask_rows[:, None]
    return depth_conv(gated_rows.reshape(count_items, length, features), kernel).reshape(
        count_items * length, features
    )


def fetch_ffn(ffn_in, ffn_out, ffn_bias, which_ffn):
    return (
        lax.all_gather(ffn_in[which_ffn], "shard", axis=1, tiled=True),
        lax.all_gather(ffn_out[which_ffn], "shard", axis=1, tiled=True),
        lax.all_gather(ffn_bias[which_ffn], "shard", axis=0, tiled=True),
    )


def fetch_again(ffn_in, ffn_out, ffn_bias, which_ffn):
    return (
        lax.all_gather(ffn_in[which_ffn], "shard", axis=1, tiled=True),
        lax.all_gather(ffn_out[which_ffn], "shard", axis=1, tiled=True),
        lax.all_gather(ffn_bias[which_ffn], "shard", axis=0, tiled=True),
    )


def reduce_ffn(back_parts):
    shard_parts = (
        lax.psum_scatter(
            back_parts[3].astype(jnp.bfloat16), "shard", scatter_dimension=1, tiled=True
        ).astype(jnp.float32),
        lax.psum_scatter(
            back_parts[4].astype(jnp.bfloat16), "shard", scatter_dimension=1, tiled=True
        ).astype(jnp.float32),
    )
    batch_parts = (
        lax.psum_scatter(shard_parts[0], "batch", scatter_dimension=0, tiled=True),
        lax.psum_scatter(shard_parts[1], "batch", scatter_dimension=0, tiled=True),
    )
    return (
        lax.all_gather(batch_parts[0].astype(jnp.bfloat16), "batch", axis=0, tiled=True).astype(
            jnp.float32
        ),
        lax.all_gather(batch_parts[1].astype(jnp.bfloat16), "batch", axis=0, tiled=True).astype(
            jnp.float32
        ),
    )


def ffn_parts(rows_in, weights, gain_row, norm_bias, out_bias):
    w_in, w_out, b_in = weights
    hidden_b = to_brain(norm_rows(rows_in, gain_row, norm_bias))
    pre_act = dot_rows(hidden_b, w_in) + to_single(b_in)
    active_b = to_brain(jax.nn.silu(pre_act))
    return (dot_rows(active_b, w_out) + out_bias, (hidden_b, pre_act, active_b))


def ffn_back(grad_half, rows_in, saved_parts, weights, gain_row, norm_bias):
    w_in, w_out, b_in = weights
    hidden_b, pre_act, active_b = saved_parts
    grad_out = to_brain(grad_half)
    grad_w_out = dot_over(active_b, grad_out)
    grad_b_out = row_total(grad_out)
    silu_back = jax.vjp(jax.nn.silu, pre_act)[1]
    grad_pre = to_brain(silu_back(dot_back(grad_out, w_out))[0])
    grad_w_in = dot_over(hidden_b, grad_pre)
    grad_b_in = row_total(grad_pre)
    norm_back = jax.vjp(norm_rows, rows_in, gain_row, norm_bias)[1]
    grad_rows, grad_gain, grad_bias = norm_back(dot_back(grad_pre, w_in))
    return (
        grad_rows,
        grad_gain,
        grad_bias,
        grad_w_in,
        grad_w_out,
        grad_b_in,
        grad_b_out,
        hidden_b,
        active_b,
        grad_pre,
        grad_out,
    )


def mixer_parts(rows_in, valid_keys, weights, gain_rows, bias_rows):
    w_qkv, w_pos, w_out = weights
    count_items, length = valid_keys.shape
    features = rows_in.shape[1]
    head_size = features // HEADS
    shape_four = (count_items, length, HEADS, head_size)
    hidden_b = to_brain(norm_rows(rows_in, gain_rows[1], bias_rows[2]))
    query_rows = dot_rows(hidden_b, w_qkv[0]) + bias_rows[3]
    key_b = to_brain(dot_rows(hidden_b, w_qkv[1])).reshape(shape_four)
    value_b = to_brain(dot_rows(hidden_b, w_qkv[2]) + bias_rows[4]).reshape(shape_four)
    with_u = to_brain(query_rows + bias_rows[6]).reshape(shape_four)
    with_v = to_brain(query_rows + bias_rows[7]).reshape(shape_four)
    table_b = to_brain(position_table(length, features))
    proj_b = to_brain(dot_rows(table_b, w_pos)).reshape(2 * length - 1, HEADS, head_size)
    content = jnp.einsum("ilhd,imhd->ihlm", with_u, key_b, preferred_element_type=jnp.float32)
    wide_scores = jnp.einsum("ilhd,chd->ihlc", with_v, proj_b, preferred_element_type=jnp.float32)
    raw_scores = content + skewed(wide_scores)
    score_scale = 1.0 / math.sqrt(head_size)
    scores = jnp.where(valid_keys[:, None, None, :], raw_scores * score_scale, -1e30)
    top_score = jnp.max(scores, axis=-1, keepdims=True)
    exp_scores = jnp.exp(scores - top_score)
    softmax_rows = exp_scores / jnp.sum(exp_scores, axis=-1, keepdims=True)
    softmax_b = to_brain(softmax_rows)
    mixed_b = to_brain(
        jnp.einsum(
            "ihlm,imhd->ilhd", softmax_b, value_b, preferred_element_type=jnp.float32
        ).reshape(count_items * length, features)
    )
    out_rows = dot_rows(mixed_b, w_out) + bias_rows[5]
    return (
        out_rows,
        (
            hidden_b,
            key_b,
            value_b,
            with_u,
            with_v,
            table_b,
            proj_b,
            softmax_rows,
            softmax_b,
            mixed_b,
        ),
    )


def mixer_back(grad_rows, rows_in, valid_keys, weights, saved_parts, gain_rows, bias_rows):
    w_qkv, w_pos, w_out = weights
    hidden_b, key_b, value_b, with_u, with_v, table_b, proj_b, softmax_rows, softmax_b, mixed_b = (
        saved_parts
    )
    count_items, length = valid_keys.shape
    features = rows_in.shape[1]
    head_size = features // HEADS
    shape_four = (count_items, length, HEADS, head_size)
    rows_shape = (count_items * length, features)
    score_scale = 1.0 / math.sqrt(head_size)
    grad_out = to_brain(grad_rows)
    grad_w_out = dot_over(mixed_b, grad_out)
    grad_b_out = row_total(grad_out)
    grad_mixed = to_brain(dot_back(grad_out, w_out)).reshape(shape_four)
    grad_soft = jnp.einsum(
        "ilhd,imhd->ihlm", grad_mixed, value_b, preferred_element_type=jnp.float32
    )
    grad_value = jnp.einsum(
        "ihlm,ilhd->imhd", softmax_b, grad_mixed, preferred_element_type=jnp.float32
    )
    grad_scores = softmax_rows * (
        grad_soft - jnp.sum(grad_soft * softmax_rows, axis=-1, keepdims=True)
    )
    grad_raw = to_brain(jnp.where(valid_keys[:, None, None, :], grad_scores, 0.0) * score_scale)
    grad_with_u = jnp.einsum("ihlm,imhd->ilhd", grad_raw, key_b, preferred_element_type=jnp.float32)
    grad_key = jnp.einsum("ihlm,ilhd->imhd", grad_raw, with_u, preferred_element_type=jnp.float32)
    wide_shape = (count_items, HEADS, length, 2 * length - 1)
    unskew = jax.vjp(skewed, jnp.zeros(wide_shape, jnp.float32))[1]
    grad_wide = to_brain(unskew(to_single(grad_raw))[0])
    grad_with_v = jnp.einsum(
        "ihlc,chd->ilhd", grad_wide, proj_b, preferred_element_type=jnp.float32
    )
    grad_proj = jnp.einsum("ihlc,ilhd->ichd", grad_wide, with_v, preferred_element_type=jnp.float32)
    grad_proj = to_brain(grad_proj.reshape(count_items, 2 * length - 1, features))
    grad_w_pos = jnp.einsum("ce,icf->ef", table_b, grad_proj, preferred_element_type=jnp.float32)
    with_u_grad = grad_with_u.reshape(rows_shape)
    with_v_grad = grad_with_v.reshape(rows_shape)
    grad_query = to_brain(with_u_grad + with_v_grad)
    grad_key_b = to_brain(grad_key.reshape(rows_shape))
    grad_value_b = to_brain(grad_value.reshape(rows_shape))
    grad_qkv = jnp.stack(
        [
            dot_over(hidden_b, grad_query),
            dot_over(hidden_b, grad_key_b),
            dot_over(hidden_b, grad_value_b),
        ]
    )
    grad_hidden = (
        dot_back(grad_query, w_qkv[0])
        + dot_back(grad_key_b, w_qkv[1])
        + dot_back(grad_value_b, w_qkv[2])
    )
    norm_back = jax.vjp(norm_rows, rows_in, gain_rows[1], bias_rows[2])[1]
    grad_in, grad_gain, grad_bias = norm_back(grad_hidden)
    return (
        grad_in,
        grad_gain,
        grad_bias,
        grad_qkv,
        grad_w_pos,
        grad_w_out,
        row_total(grad_query),
        row_total(grad_value_b),
        grad_b_out,
        jnp.sum(with_u_grad, axis=0),
        jnp.sum(with_v_grad, axis=0),
        grad_query,
        grad_key_b,
        grad_value_b,
        grad_out,
        grad_proj,
    )


def conv_front(rows_in, mask_rows, count_items, length, w_in, kernel, gain_rows, bias_rows):
    hidden_b = to_brain(norm_rows(rows_in, gain_rows[2], bias_rows[8]))
    pre_act = dot_rows(hidden_b, w_in) + jnp.concatenate([bias_rows[9], bias_rows[10]])
    return (gated_conv(pre_act, mask_rows, kernel, count_items, length), hidden_b, pre_act)


def conv_rear(conv_rows, row_mean, inverse, w_out, gain_rows, bias_rows):
    normed = (conv_rows - row_mean) * inverse * gain_rows[3] + bias_rows[11]
    active_b = to_brain(jax.nn.silu(normed))
    return (dot_rows(active_b, w_out) + bias_rows[12], normed, active_b)


def body(
    tokens,
    cotangent,
    lengths,
    ffn_in,
    ffn_out,
    ffn_bias,
    qkv_proj,
    pos_proj,
    out_proj,
    conv_in,
    conv_out,
    depthwise,
    norm_gains,
    biases,
):
    count_items, length, features = tokens.shape
    positions = lax.broadcasted_iota(jnp.int32, (count_items, length), 1)
    valid_keys = positions < lengths[:, None]
    mask_rows = to_single(valid_keys).reshape(count_items * length)
    mask_col = mask_rows[:, None]
    vector_parts = (
        lax.all_gather(norm_gains, "shard", axis=1, tiled=True),
        lax.all_gather(biases, "shard", axis=1, tiled=True),
        lax.all_gather(depthwise, "shard", axis=1, tiled=True),
    )
    gain_rows = to_single(vector_parts[0])
    bias_rows = to_single(vector_parts[1])
    kernel = to_single(vector_parts[2])
    rows_in = tokens.reshape(count_items * length, features)
    first_w = fetch_ffn(ffn_in, ffn_out, ffn_bias, 0)
    rows_one = (
        rows_in + 0.5 * ffn_parts(rows_in, first_w, gain_rows[0], bias_rows[0], bias_rows[1])[0]
    )
    mixer_w = (
        lax.all_gather(qkv_proj, "shard", axis=2, tiled=True),
        lax.all_gather(pos_proj, "shard", axis=1, tiled=True),
        lax.all_gather(out_proj, "shard", axis=1, tiled=True),
    )
    rows_two = rows_one + mixer_parts(rows_one, valid_keys, mixer_w, gain_rows, bias_rows)[0]
    conv_w = (
        lax.all_gather(conv_in, "shard", axis=1, tiled=True),
        lax.all_gather(conv_out, "shard", axis=1, tiled=True),
    )
    conv_rows = conv_front(
        rows_two, mask_rows, count_items, length, conv_w[0], kernel, gain_rows, bias_rows
    )[0]
    stat_sums = lax.psum(
        (
            jnp.sum(conv_rows * mask_col, axis=0),
            jnp.sum(conv_rows * conv_rows * mask_col, axis=0),
            jnp.sum(mask_rows),
        ),
        ("batch", "shard"),
    )
    frames = stat_sums[2]
    row_mean = stat_sums[0] / frames
    inverse = lax.rsqrt(stat_sums[1] / frames - row_mean * row_mean + epsilon)
    rows_three = (
        rows_two + conv_rear(conv_rows, row_mean, inverse, conv_w[1], gain_rows, bias_rows)[0]
    )
    second_w = fetch_ffn(ffn_in, ffn_out, ffn_bias, 1)
    rows_four = (
        rows_three
        + 0.5 * ffn_parts(rows_three, second_w, gain_rows[4], bias_rows[13], bias_rows[14])[0]
    )
    result = norm_rows(rows_four, gain_rows[5], bias_rows[15]) * mask_col
    final_back = jax.vjp(norm_rows, rows_four, gain_rows[5], bias_rows[15])[1]
    grad_stream, grad_gain_last, grad_bias_last = final_back(
        cotangent.reshape(count_items * length, features) * mask_col
    )
    back_second = fetch_again(ffn_in, ffn_out, ffn_bias, 1)
    saved_two = ffn_parts(rows_three, back_second, gain_rows[4], bias_rows[13], bias_rows[14])[1]
    two_back = ffn_back(
        0.5 * grad_stream, rows_three, saved_two, back_second, gain_rows[4], bias_rows[13]
    )
    grad_stream = grad_stream + two_back[0]
    reduced_two = reduce_ffn(two_back)
    again = (
        lax.all_gather(qkv_proj, "shard", axis=2, tiled=True),
        lax.all_gather(pos_proj, "shard", axis=1, tiled=True),
        lax.all_gather(out_proj, "shard", axis=1, tiled=True),
        lax.all_gather(conv_in, "shard", axis=1, tiled=True),
        lax.all_gather(conv_out, "shard", axis=1, tiled=True),
    )
    back_mixer = (again[0], again[1], again[2])
    back_conv = (again[3], again[4])
    conv_again, hidden_conv, pre_conv = conv_front(
        rows_two, mask_rows, count_items, length, back_conv[0], kernel, gain_rows, bias_rows
    )
    rear_parts = conv_rear(conv_again, row_mean, inverse, back_conv[1], gain_rows, bias_rows)
    normed, active_conv = (rear_parts[1], rear_parts[2])
    grad_out = to_brain(grad_stream)
    grad_conv_out = dot_over(active_conv, grad_out)
    grad_pw_out = row_total(grad_out)
    silu_back = jax.vjp(jax.nn.silu, normed)[1]
    grad_normed = silu_back(dot_back(grad_out, back_conv[1]))[0]
    scaled = (conv_again - row_mean) * inverse
    local_beta = jnp.sum(grad_normed, axis=0)
    local_gamma = jnp.sum(grad_normed * scaled, axis=0)
    totals = lax.psum((local_beta, local_gamma), ("batch", "shard"))
    gamma_row = gain_rows[3]
    grad_conv = inverse * (
        grad_normed * gamma_row
        - mask_col * (gamma_row * totals[0] + scaled * (gamma_row * totals[1])) / frames
    )

    def conv_tail(pre_in, kernel_in):
        return gated_conv(pre_in, mask_rows, kernel_in, count_items, length)

    tail_back = jax.vjp(conv_tail, pre_conv, kernel)[1]
    grad_pre_single, grad_kernel = tail_back(grad_conv)
    grad_pre = to_brain(grad_pre_single)
    grad_conv_in = dot_over(hidden_conv, grad_pre)
    grad_pw_in = row_total(grad_pre)
    conv_norm_back = jax.vjp(norm_rows, rows_two, gain_rows[2], bias_rows[8])[1]
    grad_conv_rows, grad_gain_conv, grad_bias_conv = conv_norm_back(
        dot_back(grad_pre, back_conv[0])
    )
    grad_stream = grad_stream + grad_conv_rows
    saved_mixer = mixer_parts(rows_one, valid_keys, back_mixer, gain_rows, bias_rows)[1]
    mixer_grads = mixer_back(
        grad_stream, rows_one, valid_keys, back_mixer, saved_mixer, gain_rows, bias_rows
    )
    grad_stream = grad_stream + mixer_grads[0]
    back_first = fetch_again(ffn_in, ffn_out, ffn_bias, 0)
    saved_one = ffn_parts(rows_in, back_first, gain_rows[0], bias_rows[0], bias_rows[1])[1]
    one_back = ffn_back(
        0.5 * grad_stream, rows_in, saved_one, back_first, gain_rows[0], bias_rows[0]
    )
    grad_stream = grad_stream + one_back[0]
    reduced_one = reduce_ffn(one_back)
    grad_gains = jnp.stack(
        [one_back[1], mixer_grads[1], grad_gain_conv, local_gamma, two_back[1], grad_gain_last]
    )
    grad_biases = jnp.stack(
        [
            one_back[2],
            one_back[6],
            mixer_grads[2],
            mixer_grads[6],
            mixer_grads[7],
            mixer_grads[8],
            mixer_grads[9],
            mixer_grads[10],
            grad_bias_conv,
            grad_pw_in[:features],
            grad_pw_in[features:],
            local_beta,
            grad_pw_out,
            two_back[2],
            two_back[6],
            grad_bias_last,
        ]
    )
    grad_hidden_bias = jnp.stack([one_back[5], two_back[5]])
    vector_shard = (
        lax.psum_scatter(
            grad_kernel.astype(jnp.bfloat16), "shard", scatter_dimension=1, tiled=True
        ).astype(jnp.float32),
        lax.psum_scatter(
            grad_gains.astype(jnp.bfloat16), "shard", scatter_dimension=1, tiled=True
        ).astype(jnp.float32),
        lax.psum_scatter(
            grad_biases.astype(jnp.bfloat16), "shard", scatter_dimension=1, tiled=True
        ).astype(jnp.float32),
        lax.psum_scatter(
            grad_hidden_bias.astype(jnp.bfloat16), "shard", scatter_dimension=1, tiled=True
        ).astype(jnp.float32),
    )
    matrix_shard = (
        lax.psum_scatter(
            mixer_grads[3].astype(jnp.bfloat16), "shard", scatter_dimension=2, tiled=True
        ).astype(jnp.float32),
        lax.psum_scatter(
            mixer_grads[4].astype(jnp.bfloat16), "shard", scatter_dimension=1, tiled=True
        ).astype(jnp.float32),
        lax.psum_scatter(
            mixer_grads[5].astype(jnp.bfloat16), "shard", scatter_dimension=1, tiled=True
        ).astype(jnp.float32),
        lax.psum_scatter(
            grad_conv_in.astype(jnp.bfloat16), "shard", scatter_dimension=1, tiled=True
        ).astype(jnp.float32),
        lax.psum_scatter(
            grad_conv_out.astype(jnp.bfloat16), "shard", scatter_dimension=1, tiled=True
        ).astype(jnp.float32),
    )
    rest_all = lax.psum(
        (
            matrix_shard[0],
            matrix_shard[1],
            matrix_shard[2],
            matrix_shard[3],
            matrix_shard[4],
            vector_shard[0],
            vector_shard[1],
            vector_shard[2],
            vector_shard[3],
        ),
        "batch",
    )
    grad_ffn_in = jnp.stack([reduced_one[0], reduced_two[0]])
    grad_ffn_out = jnp.stack([reduced_one[1], reduced_two[1]])
    return (
        result.reshape(tokens.shape),
        grad_stream.reshape(tokens.shape),
        grad_ffn_in,
        grad_ffn_out,
        rest_all[8],
        rest_all[0],
        rest_all[1],
        rest_all[2],
        rest_all[3],
        rest_all[4],
        rest_all[5],
        rest_all[6],
        rest_all[7],
    )


def solution(mesh):
    placed = (
        P(("batch", "shard"), None, None),
        P(("batch", "shard"), None, None),
        P(("batch", "shard")),
        P(None, None, "shard"),
        P(None, None, "shard"),
        P(None, "shard"),
        P(None, None, "shard"),
        P(None, "shard"),
        P(None, "shard"),
        P(None, "shard"),
        P(None, "shard"),
        P(None, "shard"),
        P(None, "shard"),
        P(None, "shard"),
    )
    return jax.shard_map(
        body,
        mesh=mesh,
        in_specs=placed,
        out_specs=(
            P(("batch", "shard"), None, None),
            P(("batch", "shard"), None, None),
            P(None, None, "shard"),
            P(None, None, "shard"),
            P(None, "shard"),
            P(None, None, "shard"),
            P(None, "shard"),
            P(None, "shard"),
            P(None, "shard"),
            P(None, "shard"),
            P(None, "shard"),
            P(None, "shard"),
            P(None, "shard"),
        ),
        check_vma=False,
    )
```

profile of v0, /device:TPU:0, one launch (start us, length us, event | category | flops | bytes accessed | tf_op | source)
XLA Modules:
  0.0 1772.6 jit_solution(14776500868009079503)
XLA Ops:
  8.0 4.7 fusion.137
  12.7 4.5 fusion.138
  21.3 6.2 all-gather.1
  28.8 5.4 all-gather.4
  34.4 5.2 all_gather.74
  39.6 5.2 all_gather.65
  44.7 5.7 all_gather.66
  50.9 4.1 fusion.73
  59.4 36.5 %all-gather.38.cloned.1.call-done = bf16[1,1024,4096]{2,1,0:T(8,128)(2,1)} async-done(((bf16[1,1024,1024]{2,1,0:T(8,128)(2,1)}), bf16[1,1024,4096]{2,1,0:T(8,128)(2,1)}) %all-gather.38.cloned.1.call-update) | async-done | bytes 8388624 | tf_op jit(solution)/shard_map/all_gather | solution.py:88
  95.9 7.8 fusion.16
  103.7 53.8 %all-gather.40.cloned.1.call-done = bf16[1,4096,1024]{2,1,0:T(8,128)(2,1)} async-done(((bf16[1,4096,256]{2,1,0:T(8,128)(2,1)}), bf16[1,4096,1024]{2,1,0:T(8,128)(2,1)}) %all-gather.40.cloned.1.call-update) | async-done | bytes 8388624 | tf_op jit(solution)/shard_map/all_gather | solution.py:89
  157.5 7.1 fusion.145
  165.2 41.0 %all-gather.20.cloned.1.call-done = bf16[3,1024,1024]{2,1,0:T(8,128)(2,1)} async-done(((bf16[3,1024,256]{2,1,0:T(8,128)(2,1)}), bf16[3,1024,1024]{2,1,0:T(8,128)(2,1)}) %all-gather.20.cloned.1.call-update) | async-done | bytes 6291472 | tf_op jit(solution)/shard_map/all_gather | solution.py:328
  206.1 3.1 add_convert_fusion.5
  212.3 5.6 copy.66
  217.9 6.4 reshape.450
  224.3 5.3 slice.260
  229.6 8.2 reshape.451
  243.5 3.4 fusion.70
  259.8 6.6 all-gather.26.cloned.1.call-done
  266.4 3.9 convolution_add_fusion
  272.5 40.2 %all-reduce.16 = (f32[1024]{0:T(1024)S(1)}, f32[]{:T(128)}, f32[1024]{0:T(1024)S(1)}) all-reduce(f32[1024]{0:T(1024)S(1)} %get-tuple-element.29, f32[]{:T(128)} %convert_reduce_fusion, f32[1024]{0:T(1024)S(1)} %get-tuple-element.28), channel_id=1, replica_groups=mesh['batch'=8,'shard'=4] {'batch','shard'}, use_global_device_ids=true, to_apply=%region_13.14 | all-reduce | flops 2049 | bytes 16392 | tf_op jit(solution)/shard_map/psum | solution.py:340
  313.4 3.1 fusion.148
  317.7 34.2 %all-gather.42.cloned.1.call-done = bf16[1,1024,4096]{2,1,0:T(8,128)(2,1)} async-done(((bf16[1,1024,1024]{2,1,0:T(8,128)(2,1)}), bf16[1,1024,4096]{2,1,0:T(8,128)(2,1)}) %all-gather.42.cloned.1.call-update) | async-done | bytes 8388624 | tf_op jit(solution)/shard_map/all_gather | solution.py:88
  351.9 8.2 fusion.19
  360.2 53.3 %all-gather.44.cloned.1.call-done = bf16[1,4096,1024]{2,1,0:T(8,128)(2,1)} async-done(((bf16[1,4096,256]{2,1,0:T(8,128)(2,1)}), bf16[1,4096,1024]{2,1,0:T(8,128)(2,1)}) %all-gather.44.cloned.1.call-update) | async-done | bytes 8388624 | tf_op jit(solution)/shard_map/all_gather | solution.py:89
  413.5 7.4 fusion.149
  425.1 3.9 fusion.150
  430.3 5.9 convolution_convert_fusion.2
  436.7 6.9 multiply_reduce_fusion.1
  449.5 39.8 %all-reduce.15 = (f32[1024]{0:T(1024)S(1)}, f32[1024]{0:T(1024)S(1)}) all-reduce(f32[1024]{0:T(1024)S(1)} %get-tuple-element.35, f32[1024]{0:T(1024)S(1)} %get-tuple-element.34), channel_id=1, replica_groups=mesh['batch'=8,'shard'=4] {'batch','shard'}, use_global_device_ids=true, to_apply=%region_25.26 | all-reduce | flops 2048 | bytes 16384 | tf_op jit(solution)/shard_map/psum | solution.py:393
  511.5 5.3 reshape.483
  516.8 5.1 reshape.460
  524.1 4.4 reshape.485
  528.5 5.2 convert_element_type.335
  549.5 3.9 fusion.151
  554.8 5.9 convolution_convert_fusion.3
  561.8 8.7 convolution_convert_fusion
  570.6 8.9 convolution_convert_fusion.1
  580.1 53.3 %reduce-scatter.20.cloned.1.call-done = bf16[1024,1024]{1,0:T(8,128)(2,1)} async-done(((bf16[1024,4096]{1,0:T(8,128)(2,1)}), bf16[1024,1024]{1,0:T(8,128)(2,1)}) %reduce-scatter.20.cloned.1.call-update) | async-done | bytes 2097168 | tf_op jit(solution)/shard_map/reduce_scatter | solution.py:104
  633.5 74.1 %reduce-scatter.32.cloned.1.call-done = bf16[4096,256]{1,0:T(8,128)(2,1)} async-done(((bf16[4096,1024]{1,0:T(8,128)(2,1)}), bf16[4096,256]{1,0:T(8,128)(2,1)}) %reduce-scatter.32.cloned.1.call-update) | async-done | bytes 2097168 | tf_op jit(solution)/shard_map/reduce_scatter | solution.py:107
  707.6 74.4 %reduce-scatter.28.cloned.1.call-done = bf16[4096,256]{1,0:T(8,128)(2,1)} async-done(((bf16[4096,1024]{1,0:T(8,128)(2,1)}), bf16[4096,256]{1,0:T(8,128)(2,1)}) %reduce-scatter.28.cloned.1.call-update) | async-done | bytes 2097168 | tf_op jit(solution)/shard_map/reduce_scatter | solution.py:107
  783.5 7.7 multiply_reduce_fusion.4
  798.2 3.8 convolution_convert_fusion.7
  802.1 3.3 convolution_convert_fusion.6
  805.7 3.6 convolution_convert_fusion.5
  810.5 4.7 convolution_convert_fusion.4
  818.9 3.1 pad_maximum_fusion
  822.1 31.1 %reduce-scatter.26.cloned.1.call-done = bf16[128,1024]{1,0:T(8,128)(2,1)} async-done(((bf16[1024,1024]{1,0:T(8,128)(2,1)}), bf16[128,1024]{1,0:T(8,128)(2,1)}) %reduce-scatter.26.cloned.1.call-update) | async-done | bytes 262160 | tf_op jit(solution)/shard_map/reduce_scatter | solution.py:112
  853.3 70.1 %reduce-scatter.22.cloned.1.call-done = bf16[128,1024]{1,0:T(8,128)(2,1)} async-done(((bf16[1024,1024]{1,0:T(8,128)(2,1)}), bf16[128,1024]{1,0:T(8,128)(2,1)}) %reduce-scatter.22.cloned.1.call-update) | async-done | bytes 262160 | tf_op jit(solution)/shard_map/reduce_scatter | solution.py:112
  923.4 70.0 %reduce-scatter.34.cloned.1.call-done = bf16[512,256]{1,0:T(8,128)(2,1)} async-done(((bf16[4096,256]{1,0:T(8,128)(2,1)}), bf16[512,256]{1,0:T(8,128)(2,1)}) %reduce-scatter.34.cloned.1.call-update) | async-done | bytes 262160 | tf_op jit(solution)/shard_map/reduce_scatter | solution.py:113
  993.5 70.2 %reduce-scatter.30.cloned.1.call-done = bf16[512,256]{1,0:T(8,128)(2,1)} async-done(((bf16[4096,256]{1,0:T(8,128)(2,1)}), bf16[512,256]{1,0:T(8,128)(2,1)}) %reduce-scatter.30.cloned.1.call-update) | async-done | bytes 262160 | tf_op jit(solution)/shard_map/reduce_scatter | solution.py:113
  1065.4 19.6 %reduce-scatter.46.cloned.1.call-done = bf16[5,256]{1,0:T(8,128)(2,1)} async-done(((bf16[5,1024]{1,0:T(8,128)(2,1)}), bf16[5,256]{1,0:T(8,128)(2,1)}) %reduce-scatter.46.cloned.1.call-update) | async-done | bytes 2576 | tf_op jit(solution)/shard_map/reduce_scatter | solution.py:450
  1085.0 21.9 %reduce-scatter.48.cloned.1.call-done = bf16[6,256]{1,0:T(8,128)(2,1)} async-done(((bf16[6,1024]{1,0:T(8,128)(2,1)}), bf16[6,256]{1,0:T(8,128)(2,1)}) %reduce-scatter.48.cloned.1.call-update) | async-done | bytes 3088 | tf_op jit(solution)/shard_map/reduce_scatter | solution.py:453
  1106.9 27.3 %reduce-scatter.52.cloned.1.call-done = bf16[1024,2]{1,0:T(8,128)(2,1)} async-done(((bf16[4096,2]{1,0:T(8,128)(2,1)}), bf16[1024,2]{1,0:T(8,128)(2,1)}) %reduce-scatter.52.cloned.1.call-update) | async-done | bytes 4112
  1135.3 20.9 %reduce-scatter.50.cloned.1.call-done = bf16[16,256]{1,0:T(8,128)(2,1)} async-done(((bf16[16,1024]{1,0:T(8,128)(2,1)}), bf16[16,256]{1,0:T(8,128)(2,1)}) %reduce-scatter.50.cloned.1.call-update) | async-done | bytes 8208 | tf_op jit(solution)/shard_map/reduce_scatter | solution.py:456
  1156.1 34.6 %reduce-scatter.38.cloned.1.call-done = bf16[1024,256]{1,0:T(8,128)(2,1)} async-done(((bf16[1024,1024]{1,0:T(8,128)(2,1)}), bf16[1024,256]{1,0:T(8,128)(2,1)}) %reduce-scatter.38.cloned.1.call-update) | async-done | bytes 524304 | tf_op jit(solution)/shard_map/reduce_scatter | solution.py:467
  1190.7 34.7 %reduce-scatter.40.cloned.1.call-done = bf16[1024,256]{1,0:T(8,128)(2,1)} async-done(((bf16[1024,1024]{1,0:T(8,128)(2,1)}), bf16[1024,256]{1,0:T(8,128)(2,1)}) %reduce-scatter.40.cloned.1.call-update) | async-done | bytes 524304 | tf_op jit(solution)/shard_map/reduce_scatter | solution.py:470
  1225.4 33.8 %reduce-scatter.44.cloned.1.call-done = bf16[1024,256]{1,0:T(8,128)(2,1)} async-done(((bf16[1024,1024]{1,0:T(8,128)(2,1)}), bf16[1024,256]{1,0:T(8,128)(2,1)}) %reduce-scatter.44.cloned.1.call-update) | async-done | bytes 524304 | tf_op jit(solution)/shard_map/reduce_scatter | solution.py:476
  1259.2 47.8 %reduce-scatter.42.cloned.1.call-done = bf16[1024,512]{1,0:T(8,128)(2,1)} async-done(((bf16[1024,2048]{1,0:T(8,128)(2,1)}), bf16[1024,512]{1,0:T(8,128)(2,1)}) %reduce-scatter.42.cloned.1.call-update) | async-done | bytes 1048592 | tf_op jit(solution)/shard_map/reduce_scatter | solution.py:473
  1307.0 61.4 %reduce-scatter.36.cloned.1.call-done = bf16[3,1024,256]{2,1,0:T(8,128)(2,1)} async-done(((bf16[3,1024,1024]{2,1,0:T(8,128)(2,1)}), bf16[3,1024,256]{2,1,0:T(8,128)(2,1)}) %reduce-scatter.36.cloned.1.call-update) | async-done | bytes 1572880 | tf_op jit(solution)/shard_map/reduce_scatter | solution.py:464
  1368.4 384.9 %all-reduce.19 = (f32[2,1024]{1,0:T(2,128)}, f32[3,1024,256]{2,1,0:T(8,128)}, f32[1024,256]{1,0:T(8,128)}, f32[1024,256]{1,0:T(8,128)}, f32[1024,512]{1,0:T(8,12...) all-reduce(bf16[2,1024]{1,0:T(2,128)(2,1)S(1)} %copy.86, ...), channel_id=1, replica_groups=mesh['batch'=8,'shard'=4] {'batch'}, use_global_device_ids=true, to_apply=%region_44.45 | all-reduce | flops 2106112 | bytes 12636672 | tf_op jit(solution)/shard_map/psum | solution.py:480
  1753.3 6.2 maximum_convert_fusion
  1759.5 6.2 maximum_convert_fusion.1
  (354 shorter events, 107.1 us)
Async XLA Ops:
  7.2 47.9 %all-gather.22.cloned.1.call-start = ((), (), s32[]{:S(2)}) async-start(), calls=%async_computation.18 | async-start | bytes 2621440 | tf_op jit(solution)/shard_map/all_gather | solution.py:329
  7.9 88.0 %all-gather.38.cloned.1.call-start = ((), (), s32[]{:S(2)}) async-start(), calls=%async_computation.42 | async-start | bytes 10485760 | tf_op jit(solution)/shard_map/all_gather | solution.py:88
  12.7 144.8 %all-gather.40.cloned.1.call-start = ((), (), s32[]{:S(2)}) async-start(), calls=%async_computation.43 | async-start | bytes 10485760 | tf_op jit(solution)/shard_map/all_gather | solution.py:89
  17.2 188.9 %all-gather.20.cloned.1.call-start = ((), (), s32[]{:S(2)}) async-start(), calls=%async_computation.17 | async-start | bytes 7864320 | tf_op jit(solution)/shard_map/all_gather | solution.py:328
  17.8 238.1 %all-gather.24.cloned.1.call-start = ((), (), s32[]{:S(2)}) async-start(), calls=%async_computation.19 | async-start | bytes 2621440 | tf_op jit(solution)/shard_map/all_gather | solution.py:330
  18.4 248.0 %all-gather.26.cloned.1.call-start = ((), (), s32[]{:S(2)}) async-start(), calls=%async_computation.20 | async-start | bytes 5242880 | tf_op jit(solution)/shard_map/all_gather | solution.py:334
  19.0 294.4 %all-gather.28.cloned.1.call-start = ((), (), s32[]{:S(2)}) async-start(), calls=%async_computation.21 | async-start | bytes 2621440 | tf_op jit(solution)/shard_map/all_gather | solution.py:335
  19.7 332.2 %all-gather.42.cloned.1.call-start = ((), (), s32[]{:S(2)}) async-start(), calls=%async_computation.44 | async-start | bytes 10485760 | tf_op jit(solution)/shard_map/all_gather | solution.py:88
  19.8 14.4 copy-start.3
  20.5 13.9 copy-start.67
  20.5 19.1 %copy-start.68 = (bf16[6,256]{1,0:T(8,128)(2,1)S(1)}, bf16[6,256]{1,0:T(8,128)(2,1)}, u32[]{:S(2)}) copy-start(bf16[6,256]{1,0:T(8,128)(2,1)} %param.26) | copy-start | bytes 9220
  20.5 24.2 %copy-start.66 = (bf16[16,256]{1,0:T(8,128)(2,1)S(1)}, bf16[16,256]{1,0:T(8,128)(2,1)}, u32[]{:S(2)}) copy-start(bf16[16,256]{1,0:T(8,128)(2,1)} %param.27) | copy-start | bytes 24580
  20.5 393.0 %all-gather.44.cloned.1.call-start = ((), (), s32[]{:S(2)}) async-start(), calls=%async_computation.45 | async-start | bytes 10485760 | tf_op jit(solution)/shard_map/all_gather | solution.py:89
  21.2 558.3 %reduce-scatter.24.cloned.1.call-start = ((), (), s32[]{:S(2)}) async-start(), calls=%async_computation.25 | async-start | bytes 10485760 | tf_op jit(solution)/shard_map/reduce_scatter | solution.py:104
  50.5 215.8 %copy-start.61 = (f32[1,1024]{1,0:T(1,128)}, f32[1,1024]{1,0:T(1,128)S(1)}, u32[]{:S(2)}) copy-start(f32[1,1024]{1,0:T(1,128)S(1)} %get-tuple-element.91) | copy-start | bytes 12292
  50.8 8.0 copy-start.64
  59.4 150.1 %copy-start.28 = (bf16[511,1024]{0,1:T(8,128)(2,1)}, bf16[511,1024]{0,1:T(8,128)(2,1)S(1)}, u32[]{:S(2)}) copy-start(bf16[511,1024]{0,1:T(8,128)(2,1)S(1)} %copy.91) | copy-start | bytes 3139588
  165.2 44.1 %copy-start.32 = (bf16[256,1024]{1,0:T(8,128)(2,1)}, bf16[256,1024]{1,0:T(8,128)(2,1)S(1)}, u32[]{:S(2)}) copy-start(bf16[256,1024]{1,0:T(8,128)(2,1)S(1)} %add_convert_fusion.6) | copy-start | bytes 1572868
  243.5 5.4 copy-start.31
  250.7 3.8 copy-start.7
  413.5 7.7 copy-start.43
  413.5 10.7 copy-start.73
  420.9 4.1 copy-start.69
  424.1 4.8 copy-start.56
  425.1 5.2 copy-start.12
  436.3 197.1 %reduce-scatter.20.cloned.1.call-start = ((), (), s32[]{:S(2)}) async-start(), calls=%async_computation.22 | async-start | bytes 10485760 | tf_op jit(solution)/shard_map/reduce_scatter | solution.py:104
  436.7 7.0 copy-start.13
  445.4 4.1 copy-start.20
  494.1 4.0 copy-start.14
  494.4 3.7 copy-start.16
  537.2 6.9 copy-start.38
  537.8 5.6 slice-start.1
  539.8 3.6 slice-start.2
  540.4 6.8 slice-start.3
  547.3 23.3 %copy-start.41 = (f32[256,1024]{1,0:T(8,128)}, f32[256,1024]{1,0:T(8,128)S(1)}, u32[]{:S(2)}) copy-start(f32[256,1024]{1,0:T(8,128)S(1)} %get-tuple-element.59) | copy-start | bytes 3145732
  549.5 5.3 copy-start.4
  560.8 146.8 %reduce-scatter.32.cloned.1.call-start = ((), (), s32[]{:S(2)}) async-start(), calls=%async_computation.31 | async-start | bytes 10485760 | tf_op jit(solution)/shard_map/reduce_scatter | solution.py:107
  570.5 211.5 %reduce-scatter.28.cloned.1.call-start = ((), (), s32[]{:S(2)}) async-start(), calls=%async_computation.28 | async-start | bytes 10485760 | tf_op jit(solution)/shard_map/reduce_scatter | solution.py:107
  579.5 273.7 %reduce-scatter.26.cloned.1.call-start = ((), (), s32[]{:S(2)}) async-start(), calls=%async_computation.26 | async-start | bytes 2359296 | tf_op jit(solution)/shard_map/reduce_scatter | solution.py:112
  580.1 343.3 %reduce-scatter.22.cloned.1.call-start = ((), (), s32[]{:S(2)}) async-start(), calls=%async_computation.23 | async-start | bytes 2359296 | tf_op jit(solution)/shard_map/reduce_scatter | solution.py:112
  633.4 360.1 %reduce-scatter.34.cloned.1.call-start = ((), (), s32[]{:S(2)}) async-start(), calls=%async_computation.32 | async-start | bytes 2359296 | tf_op jit(solution)/shard_map/reduce_scatter | solution.py:113
  707.6 74.6 %copy-start.25 = (f32[1,256,1024]{2,1,0:T(8,128)S(1)}, f32[1,256,1024]{2,1,0:T(8,128)}, u32[]{:S(2)}) copy-start(f32[1,256,1024]{2,1,0:T(8,128)} %copy-done.24) | copy-start | bytes 3145732
  707.6 74.6 %copy-start.30 = (f32[256,1024]{1,0:T(8,128)S(1)}, f32[256,1024]{1,0:T(8,128)}, u32[]{:S(2)}) copy-start(f32[256,1024]{1,0:T(8,128)} %copy-done.29) | copy-start | bytes 3145732
  707.6 356.1 %reduce-scatter.30.cloned.1.call-start = ((), (), s32[]{:S(2)}) async-start(), calls=%async_computation.29 | async-start | bytes 2359296 | tf_op jit(solution)/shard_map/reduce_scatter | solution.py:113
  782.1 302.9 %reduce-scatter.46.cloned.1.call-start = ((), (), s32[]{:S(2)}) async-start(), calls=%async_computation.39 | async-start | bytes 20480 | tf_op jit(solution)/shard_map/reduce_scatter | solution.py:450
  783.5 323.4 %reduce-scatter.48.cloned.1.call-start = ((), (), s32[]{:S(2)}) async-start(), calls=%async_computation.40 | async-start | bytes 20480 | tf_op jit(solution)/shard_map/reduce_scatter | solution.py:453
  783.5 7.7 copy-start.6
  783.5 7.7 copy-start.36
  793.4 340.8 %reduce-scatter.52.cloned.1.call-start = ((), (), s32[]{:S(2)}) async-start(), calls=%async_computation.46 | async-start | bytes 1310720
  793.6 4.6 copy-start.53
  796.5 359.6 %reduce-scatter.50.cloned.1.call-start = ((), (), s32[]{:S(2)}) async-start(), calls=%async_computation.41 | async-start | bytes 40960 | tf_op jit(solution)/shard_map/reduce_scatter | solution.py:456
  798.1 392.6 %reduce-scatter.38.cloned.1.call-start = ((), (), s32[]{:S(2)}) async-start(), calls=%async_computation.35 | async-start | bytes 2621440 | tf_op jit(solution)/shard_map/reduce_scatter | solution.py:467
  802.0 3.6 copy-start.23
  802.1 423.3 %reduce-scatter.40.cloned.1.call-start = ((), (), s32[]{:S(2)}) async-start(), calls=%async_computation.36 | async-start | bytes 2621440 | tf_op jit(solution)/shard_map/reduce_scatter | solution.py:470
  805.5 453.8 %reduce-scatter.44.cloned.1.call-start = ((), (), s32[]{:S(2)}) async-start(), calls=%async_computation.38 | async-start | bytes 2621440 | tf_op jit(solution)/shard_map/reduce_scatter | solution.py:476
  809.3 497.7 %reduce-scatter.42.cloned.1.call-start = ((), (), s32[]{:S(2)}) async-start(), calls=%async_computation.37 | async-start | bytes 5242880 | tf_op jit(solution)/shard_map/reduce_scatter | solution.py:473
  815.2 553.2 %reduce-scatter.36.cloned.1.call-start = ((), (), s32[]{:S(2)}) async-start(), calls=%async_computation.34 | async-start | bytes 7864320 | tf_op jit(solution)/shard_map/reduce_scatter | solution.py:464
  822.1 241.7 %copy-start.65 = (f32[256]{0:T(256)S(1)}, f32[256]{0:T(256)}, u32[]{:S(2)}) copy-start(f32[256]{0:T(256)} %copy-done.64) | copy-start | bytes 3076
  822.1 241.7 %copy-start.52 = (f32[256,1024]{1,0:T(8,128)S(1)}, f32[256,1024]{1,0:T(8,128)}, u32[]{:S(2)}) copy-start(f32[256,1024]{1,0:T(8,128)} %get-tuple-element.141) | copy-start | bytes 3145732
  822.1 931.2 %all-gather.32.cloned.1.call-start = ((), (), s32[]{:S(2)}) async-start(), calls=%async_computation.27 | async-start | bytes 2359296 | tf_op jit(solution)/shard_map/all_gather | solution.py:116
  853.2 211.0 %copy-start.42 = (f32[256,1024]{1,0:T(8,128)S(1)}, f32[256,1024]{1,0:T(8,128)}, u32[]{:S(2)}) copy-start(f32[256,1024]{1,0:T(8,128)} %copy-done.41) | copy-start | bytes 3145732
  853.2 900.1 %all-gather.30.cloned.1.call-start = ((), (), s32[]{:S(2)}) async-start(), calls=%async_computation.24 | async-start | bytes 2359296 | tf_op jit(solution)/shard_map/all_gather | solution.py:116
  923.4 836.1 %all-gather.36.cloned.1.call-start = ((), (), s32[]{:S(2)}) async-start(), calls=%async_computation.33 | async-start | bytes 2359296 | tf_op jit(solution)/shard_map/all_gather | solution.py:119
  993.5 766.0 %all-gather.34.cloned.1.call-start = ((), (), s32[]{:S(2)}) async-start(), calls=%async_computation.30 | async-start | bytes 2359296 | tf_op jit(solution)/shard_map/all_gather | solution.py:119
  (46 other events, 84.4 us)
Sparse Core Ops, SparseCore 0:
  9.6 25.7 all-gather.21
  37.4 58.4 all-gather.37
  98.0 59.3 all-gather.39
  158.9 47.2 all-gather.19
  207.5 22.8 all-gather.23
  231.8 34.4 all-gather.25
  267.9 23.5 all-gather.27
  293.0 58.8 all-gather.41
  354.1 59.3 all-gather.43
  436.4 72.5 reduce-scatter.23
  560.9 72.4 reduce-scatter.19
  635.8 71.7 reduce-scatter.31
  710.3 71.6 reduce-scatter.27
  785.5 67.6 reduce-scatter.25
  856.6 66.7 reduce-scatter.21
  926.8 66.6 reduce-scatter.33
  996.8 66.8 reduce-scatter.29
  1066.6 18.4 reduce-scatter.45
  1087.6 19.2 reduce-scatter.47
  1109.3 24.8 reduce-scatter.51
  1136.8 19.3 reduce-scatter.49
  1159.2 31.4 reduce-scatter.37
  1194.0 31.3 reduce-scatter.39
  1227.8 31.4 reduce-scatter.43
  1262.5 44.4 reduce-scatter.41
  1310.0 58.3 reduce-scatter.35
  1370.6 87.6 all-gather.31
  1460.6 90.5 all-gather.29
  1553.6 90.6 all-gather.35
  1646.5 92.6 all-gather.33
where the time goes:
time: 1780 us; the launch traced here: 1770 us
  waiting for transfers between devices  976 us (55%)
  blocking collectives  493 us (28%)
  matrix products  145 us (8%)
  local copies, waits for them, and re-layouts  100 us (6%)
  other arithmetic  39.9 us (2%)
    psum x1, blocking collectives, body(): lax.psum((matrix_shard[0], matrix_shard[1], matrix_shard[2], matrix_shard...  385 us
    reduce_scatter x2, waiting for transfers between devices, reduce_ffn(): lax.psum_scatter(back_parts[4].astype(jnp.bfloat16), 'shard', scatter_dim...  149 us
    reduce_scatter x2, waiting for transfers between devices, reduce_ffn(): lax.psum_scatter(shard_parts[1], 'batch', scatter_dimension=0, tiled=True)  140 us
    all_gather x2, waiting for transfers between devices, fetch_ffn(): lax.all_gather(ffn_out[which_ffn], 'shard', axis=1, tiled=True)  107 us
    reduce_scatter x2, waiting for transfers between devices, reduce_ffn(): lax.psum_scatter(shard_parts[0], 'batch', scatter_dimension=0, tiled=True)  101 us
    all_gather x2, waiting for transfers between devices, fetch_ffn(): lax.all_gather(ffn_in[which_ffn], 'shard', axis=1, tiled=True)  70.7 us
    reduce_scatter x1, waiting for transfers between devices, body(): lax.psum_scatter(mixer_grads[3].astype(jnp.bfloat16), 'shard', scatter_di...  61.4 us
    reduce_scatter x2, waiting for transfers between devices, reduce_ffn(): lax.psum_scatter(back_parts[3].astype(jnp.bfloat16), 'shard', scatter_dim...  53.3 us
  transfers between devices with their start and end apart: 30, of which 22 were waited for; matrix products, arithmetic and copies ran while one was open for 13% of the time, Pallas kernels for 0%

commit v1 on v0

v1 whole, which is shorter than its diff:
```python
import functools
import math

import jax
import jax.numpy as jnp
from jax import lax
from jax.experimental import pallas as pl
from jax.experimental.pallas import tpu as pltpu
from jax.sharding import PartitionSpec as P

HEADS = 8
MESH = pl.DeviceIdType.MESH
epsilon = 1e-05


def f32(a):
    return a.astype(jnp.float32)


def b16(a):
    return a.astype(jnp.bfloat16)


def norm_rows(values_in, gain_row, bias_row):
    row_mean = jnp.mean(values_in, axis=-1, keepdims=True)
    centered = values_in - row_mean
    spread = jnp.mean(centered * centered, axis=-1, keepdims=True)
    return centered * lax.rsqrt(spread + epsilon) * gain_row + bias_row


def dot_rows(a, b):
    return jnp.dot(a, b, preferred_element_type=jnp.float32)


def dot_back(a, b):
    return lax.dot_general(a, b, (((1,), (1,)), ((), ())), preferred_element_type=jnp.float32)


def dot_over(a, b):
    return lax.dot_general(a, b, (((0,), (0,)), ((), ())), preferred_element_type=jnp.float32)


def row_total(a):
    return jnp.sum(f32(a), axis=0)


def position_table(length, features):
    columns = jnp.arange(2 * length - 1, dtype=jnp.float32)
    offsets = length - 1.0 - columns
    freq_rates = jnp.exp(
        jnp.arange(features // 2, dtype=jnp.float32) * (-2.0 * math.log(10000.0) / features)
    )
    angles = offsets[:, None] * freq_rates[None, :]
    return jnp.concatenate([jnp.sin(angles), jnp.cos(angles)], axis=1)


def depth_conv(gated_rows, kernel):
    length = gated_rows.shape[0]
    half_width = (kernel.shape[0] - 1) // 2
    padded = jnp.pad(gated_rows, [(half_width, half_width), (0, 0)])
    summed = padded[0:length] * kernel[0]
    for tap_index in range(1, kernel.shape[0]):
        summed = summed + padded[tap_index : tap_index + length] * kernel[tap_index]
    return summed


def gated_conv(pre_act, mask_col, kernel):
    features = pre_act.shape[1] // 2
    gated_rows = pre_act[:, :features] * jax.nn.sigmoid(pre_act[:, features:]) * mask_col
    return depth_conv(gated_rows, kernel)


def swap(x, axis, mask):
    n = lax.axis_size(axis)
    return lax.ppermute(x, axis, [(i, i ^ mask) for i in range(n)])


def gather_slots(own):
    far = swap(own, "shard", 2)
    near = swap(own, "shard", 1)
    diag = swap(far, "shard", 1)
    return (jnp.concatenate([own, near], 0), jnp.concatenate([far, diag], 0))


def scatter_slots(near_half, far_half):
    rows = near_half.shape[0] // 2
    got_far = swap(b16(far_half[rows:]), "shard", 1)
    sent = b16(far_half[:rows] + f32(got_far))
    got_near = swap(b16(near_half[rows:]), "shard", 1)
    crossed = swap(sent, "shard", 2)
    return near_half[:rows] + f32(got_near) + f32(crossed)


def true_order(pieces, me, axis):
    stacked = jnp.stack(pieces, 0)
    return jnp.concatenate(
        [lax.dynamic_index_in_dim(stacked, me ^ t, 0, keepdims=False) for t in range(len(pieces))],
        axis,
    )


def to_rows(cols, me):
    n = lax.axis_size("shard")
    rows = cols.shape[0] // n
    pieces = []
    for j in range(n):
        part = lax.dynamic_slice_in_dim(cols, (me ^ j) * rows, rows, 0)
        pieces.append(part if j == 0 else swap(part, "shard", j))
    return true_order(pieces, me, 1)


def to_cols(rows_block, me):
    n = lax.axis_size("shard")
    cols = rows_block.shape[1] // n
    pieces = []
    for j in range(n):
        part = lax.dynamic_slice_in_dim(rows_block, (me ^ j) * cols, cols, 1)
        pieces.append(part if j == 0 else swap(part, "shard", j))
    stacked = jnp.stack(pieces, 0)
    return jnp.stack(
        [lax.dynamic_index_in_dim(stacked, me ^ t, 0, keepdims=False) for t in range(n)], 0
    )


def halve_batch(total, order, place):
    for bit in order:
        half = total.shape[0] // 2
        mine = (place >> bit) & 1
        kept = lax.dynamic_slice_in_dim(total, mine * half, half, 0)
        sent = b16(lax.dynamic_slice_in_dim(total, (1 - mine) * half, half, 0))
        total = kept + f32(swap(sent, "batch", 1 << bit))
    return b16(total)


def double_batch(block, order, place, axis=0):
    for bit in reversed(order):
        other = swap(block, "batch", 1 << bit)
        mine = ((place >> bit) & 1) == 0
        block = jnp.concatenate(
            [jnp.where(mine, block, other), jnp.where(mine, other, block)], axis
        )
    return block


def peers_of(axis, index, count):
    return [{axis: lax.rem(index + j, count)} for j in range(1, count)]


def exchange(axis, index, count, source, landing, send_sem, recv_sem):
    copies = []
    for j in range(1, count):
        peer = lax.rem(index + j, count)
        copies.append(
            pltpu.make_async_remote_copy(
                src_ref=source,
                dst_ref=landing.at[index],
                send_sem=send_sem.at[j],
                recv_sem=recv_sem.at[j],
                device_id={axis: peer},
                device_id_type=MESH,
            )
        )
    return copies


def greet(sizes, places):
    barrier = pltpu.get_barrier_semaphore()
    total = 0
    for axis in ("shard", "batch"):
        for device in peers_of(axis, places[axis], sizes[axis]):
            pl.semaphore_signal(barrier, inc=1, device_id=device, device_id_type=MESH)
            total += 1
    pl.semaphore_wait(barrier, total)


def sum_slots(ref, count):
    total = ref[0]
    for j in range(1, count):
        total = total + ref[j]
    return total


def stats_body(ns, nb, x_ref, o_ref, land_s, mid, land_b, ss, rs, sb, rb):
    s, b = lax.axis_index("shard"), lax.axis_index("batch")
    greet({"shard": ns, "batch": nb}, {"shard": s, "batch": b})
    first = exchange("shard", s, ns, x_ref, land_s, ss, rs)
    for copy in first:
        copy.start()
    land_s[s] = x_ref[...]
    for copy in first:
        copy.wait()
    mid[...] = sum_slots(land_s, ns)
    second = exchange("batch", b, nb, mid, land_b, sb, rb)
    for copy in second:
        copy.start()
    land_b[b] = mid[...]
    for copy in second:
        copy.wait()
    o_ref[...] = sum_slots(land_b, nb)


def stats_sum(x, ident):
    ns, nb = lax.axis_size("shard"), lax.axis_size("batch")
    shape = x.shape
    return pl.pallas_call(
        functools.partial(stats_body, ns, nb),
        out_shape=jax.ShapeDtypeStruct(shape, jnp.float32),
        in_specs=[pl.BlockSpec(memory_space=pltpu.VMEM)],
        out_specs=pl.BlockSpec(memory_space=pltpu.VMEM),
        scratch_shapes=[
            pltpu.VMEM((ns,) + shape, jnp.float32),
            pltpu.VMEM(shape, jnp.float32),
            pltpu.VMEM((nb,) + shape, jnp.float32),
            pltpu.SemaphoreType.DMA((ns,)),
            pltpu.SemaphoreType.DMA((ns,)),
            pltpu.SemaphoreType.DMA((nb,)),
            pltpu.SemaphoreType.DMA((nb,)),
        ],
        compiler_params=pltpu.CompilerParams(collective_id=ident, has_side_effects=True),
        name="stats_sum_%d" % ident,
    )(x)


def vector_body(ns, nb, w_ref, l_ref, o_ref, land_s, mid, land_b, ss, rs, sb, rb):
    s, b = lax.axis_index("shard"), lax.axis_index("batch")
    greet({"shard": ns, "batch": nb}, {"shard": s, "batch": b})
    rows = w_ref.shape[1]
    copies = []
    for j in range(1, ns):
        peer = lax.rem(s + j, ns)
        copies.append(
            pltpu.make_async_remote_copy(
                src_ref=w_ref.at[peer],
                dst_ref=land_s.at[s],
                send_sem=ss.at[j],
                recv_sem=rs.at[j],
                device_id={"shard": peer},
                device_id_type=MESH,
            )
        )
    for copy in copies:
        copy.start()
    land_s[s] = w_ref[s]
    for copy in copies:
        copy.wait()
    mid[0:rows] = sum_slots(land_s, ns)
    mid[rows:] = l_ref[...]
    second = exchange("batch", b, nb, mid, land_b, sb, rb)
    for copy in second:
        copy.start()
    land_b[b] = mid[...]
    for copy in second:
        copy.wait()
    o_ref[...] = sum_slots(land_b, nb)


def vector_sum(wide, local, ident):
    ns, nb = lax.axis_size("shard"), lax.axis_size("batch")
    _, r, c = wide.shape
    rows = r + local.shape[0]
    return pl.pallas_call(
        functools.partial(vector_body, ns, nb),
        out_shape=jax.ShapeDtypeStruct((rows, c), jnp.float32),
        in_specs=[pl.BlockSpec(memory_space=pltpu.VMEM)] * 2,
        out_specs=pl.BlockSpec(memory_space=pltpu.VMEM),
        scratch_shapes=[
            pltpu.VMEM((ns, r, c), jnp.float32),
            pltpu.VMEM((rows, c), jnp.float32),
            pltpu.VMEM((nb, rows, c), jnp.float32),
            pltpu.SemaphoreType.DMA((ns,)),
            pltpu.SemaphoreType.DMA((ns,)),
            pltpu.SemaphoreType.DMA((nb,)),
            pltpu.SemaphoreType.DMA((nb,)),
        ],
        compiler_params=pltpu.CompilerParams(collective_id=ident, has_side_effects=True),
        name="vector_sum",
    )(wide, local)


def attend_body(heads, size, scale, len_ref, u_ref, v_ref, k_ref, x_ref, p_ref, mix_ref, soft_ref):
    live = len_ref[pl.program_id(0)]
    length = u_ref.shape[0]
    for h in range(heads):
        cols = slice(h * size, (h + 1) * size)
        wide = dot_back(v_ref[:, cols], p_ref[:, cols])
        moved = pltpu.roll(wide, length + 1, 1, stride=1, stride_axis=0)[:, :length]
        raw = dot_back(u_ref[:, cols], k_ref[:, cols]) + moved
        keys = lax.broadcasted_iota(jnp.int32, (length, length), 1)
        scores = jnp.where(keys < live, raw * scale, -1e30)
        top = jnp.max(scores, axis=-1, keepdims=True)
        grown = jnp.exp(scores - top)
        soft = grown / jnp.sum(grown, axis=-1, keepdims=True)
        soft_ref[:, h * length : (h + 1) * length] = soft
        mix_ref[:, cols] = b16(dot_rows(b16(soft), x_ref[:, cols]))


def attend(lens, with_u, with_v, key, value, proj, length, heads):
    rows, width = with_u.shape
    size = width // heads
    items = rows // length
    block = pl.BlockSpec((length, width), lambda i, n: (i, 0))
    return pl.pallas_call(
        functools.partial(attend_body, heads, size, 1.0 / math.sqrt(size)),
        grid_spec=pltpu.PrefetchScalarGridSpec(
            num_scalar_prefetch=1,
            grid=(items,),
            in_specs=[block, block, block, block, pl.BlockSpec(proj.shape, lambda i, n: (0, 0))],
            out_specs=[block, pl.BlockSpec((length, heads * length), lambda i, n: (i, 0))],
        ),
        out_shape=[
            jax.ShapeDtypeStruct((rows, width), jnp.bfloat16),
            jax.ShapeDtypeStruct((rows, heads * length), jnp.float32),
        ],
        compiler_params=pltpu.CompilerParams(vmem_limit_bytes=32 << 20),
        name="attend",
        cost_estimate=pl.CostEstimate(
            flops=8 * rows * length * width, transcendentals=rows * length * heads, bytes_accessed=rows * width * 10
        ),
    )(lens, with_u, with_v, key, value, proj)


def attend_back_body(
    heads, size, scale, len_ref, g_ref, soft_ref, u_ref, v_ref, k_ref, x_ref, p_ref,
    dq_ref, dk_ref, dx_ref, dp_ref, sum_ref,
):
    item = pl.program_id(0)
    live = len_ref[item]
    length = u_ref.shape[0]
    at_row = lax.broadcasted_iota(jnp.int32, (length, length), 0)
    at_col = lax.broadcasted_iota(jnp.int32, (length, length), 1)
    flip = b16(f32(at_row + at_col == length - 1))
    for h in range(heads):
        cols = slice(h * size, (h + 1) * size)
        soft = soft_ref[:, h * length : (h + 1) * length]
        grad = g_ref[:, cols]
        grad_soft = dot_back(grad, x_ref[:, cols])
        dx_ref[:, cols] = b16(dot_over(b16(soft), grad))
        grad_scores = soft * (grad_soft - jnp.sum(grad_soft * soft, axis=-1, keepdims=True))
        raw = b16(jnp.where(at_col < live, grad_scores, 0.0) * scale)
        grad_u = dot_rows(raw, k_ref[:, cols])
        dk_ref[:, cols] = b16(dot_over(raw, u_ref[:, cols]))
        turned = dot_rows(flip, raw)
        wide = jnp.concatenate([turned, jnp.zeros_like(turned)], 1)
        wide = b16(pltpu.roll(wide, 0, 1, stride=1, stride_axis=0))
        grad_v_turned = dot_rows(wide, p_ref[:, cols])
        v_turned = b16(dot_rows(flip, v_ref[:, cols]))
        dp_ref[0, :, cols] = b16(dot_over(wide, v_turned))
        high = b16(grad_v_turned)
        low = b16(grad_v_turned - f32(high))
        grad_v = dot_rows(flip, high) + dot_rows(flip, low)
        dq_ref[:, cols] = b16(grad_u + grad_v)
        total = jnp.concatenate(
            [
                jnp.sum(grad_u, axis=0, keepdims=True),
                jnp.sum(grad_v_turned, axis=0, keepdims=True),
                jnp.zeros((6, size), jnp.float32),
            ],
            0,
        )
        sum_ref[0, :, cols] = total


def attend_back(lens, grad, soft, with_u, with_v, key, value, proj, length, heads):
    rows, width = with_u.shape
    size = width // heads
    items = rows // length
    block = pl.BlockSpec((length, width), lambda i, n: (i, 0))
    return pl.pallas_call(
        functools.partial(attend_back_body, heads, size, 1.0 / math.sqrt(size)),
        grid_spec=pltpu.PrefetchScalarGridSpec(
            num_scalar_prefetch=1,
            grid=(items,),
            in_specs=[
                block,
                pl.BlockSpec((length, heads * length), lambda i, n: (i, 0)),
                block, block, block, block,
                pl.BlockSpec(proj.shape, lambda i, n: (0, 0)),
            ],
            out_specs=[
                block, block, block,
                pl.BlockSpec((1,) + proj.shape, lambda i, n: (i, 0, 0)),
                pl.BlockSpec((1, 8, width), lambda i, n: (i, 0, 0)),
            ],
        ),
        out_shape=[
            jax.ShapeDtypeStruct((rows, width), jnp.bfloat16),
            jax.ShapeDtypeStruct((rows, width), jnp.bfloat16),
            jax.ShapeDtypeStruct((rows, width), jnp.bfloat16),
            jax.ShapeDtypeStruct((items,) + proj.shape, jnp.bfloat16),
            jax.ShapeDtypeStruct((items, 8, width), jnp.float32),
        ],
        compiler_params=pltpu.CompilerParams(vmem_limit_bytes=32 << 20),
        name="attend_back",
        cost_estimate=pl.CostEstimate(
            flops=26 * rows * length * width, transcendentals=0, bytes_accessed=rows * width * 30
        ),
    )(lens, grad, soft, with_u, with_v, key, value, proj)


def ffn_forward(rows_in, w_in, w_rows, b_in, gain_row, norm_bias):
    halves = gather_slots(b16(norm_rows(rows_in, gain_row, norm_bias)))
    saved, sums = [], []
    for hidden in halves:
        pre = dot_rows(hidden, w_in) + b_in
        active = b16(jax.nn.silu(pre))
        sums.append(dot_rows(active, w_rows))
        saved.append((hidden, pre, active))
    return scatter_slots(*sums), saved


def ffn_back(grad_own, rows_in, saved, w_in, w_rows, gain_row, norm_bias):
    halves = gather_slots(grad_own)
    grad_in = grad_out = grad_b = 0.0
    sums = []
    for grad, (hidden, pre, active) in zip(halves, saved):
        silu_back = jax.vjp(jax.nn.silu, pre)[1]
        grad_pre = b16(silu_back(dot_back(grad, w_rows))[0])
        sums.append(dot_back(grad_pre, w_in))
        grad_out = grad_out + dot_over(active, grad)
        grad_in = grad_in + dot_over(hidden, grad_pre)
        grad_b = grad_b + row_total(grad_pre)
    norm_back = jax.vjp(norm_rows, rows_in, gain_row, norm_bias)[1]
    grad_rows, grad_gain, grad_bias = norm_back(scatter_slots(*sums))
    return grad_rows, grad_gain, grad_bias, grad_in, grad_out, grad_b, row_total(grad_own)


def body(
    tokens, cotangent, lengths, ffn_in, ffn_out, ffn_bias, qkv_proj, pos_proj, out_proj,
    conv_in, conv_out, depthwise, norm_gains, biases,
):
    _, length, features = tokens.shape
    shard, batch = lax.axis_index("shard"), lax.axis_index("batch")
    ns, nb = lax.axis_size("shard"), lax.axis_size("batch")
    width = features // ns
    bits = nb.bit_length() - 1
    order_a = list(range(bits))
    order_b = [1, 0] + list(range(2, bits)) if bits > 1 else order_a
    heads = HEADS // ns
    rows_in = tokens[0]
    grads_in = cotangent[0]

    own_length = jnp.broadcast_to(b16(f32(lengths))[:, None], (1, width))
    packed = jnp.concatenate([norm_gains, biases, depthwise, own_length], 0)
    packed = f32(lax.all_gather(packed, "shard", axis=1, tiled=True))
    gain_rows, bias_rows = packed[0:6], packed[6:22]
    kernel = packed[22:27]
    group_lengths = packed[27].reshape(ns, width)[:, 0].astype(jnp.int32)
    slot_lengths = jnp.stack(
        [lax.dynamic_index_in_dim(group_lengths, shard ^ j, 0, keepdims=False) for j in range(ns)]
    )
    own_biases = f32(biases)
    mask_col = f32(lax.broadcasted_iota(jnp.int32, (length, 1), 0) < lengths[0])
    w_rows = [to_rows(ffn_out[0], shard), to_rows(ffn_out[1], shard)]
    w_in = [ffn_in[0], ffn_in[1]]
    b_in = f32(ffn_bias)

    branch, saved_one = ffn_forward(rows_in, w_in[0], w_rows[0], b_in[0], gain_rows[0], bias_rows[0])
    rows_one = rows_in + 0.5 * (branch + bias_rows[1])

    table_b = b16(position_table(length, features))
    table_b = jnp.pad(table_b, [(0, 1), (0, 0)])
    proj_b = b16(dot_rows(table_b, pos_proj))
    w_out = lax.all_gather(out_proj, "shard", axis=1, tiled=True)
    wc_in = lax.all_gather(conv_in, "shard", axis=1, tiled=True)
    wc_out = lax.all_gather(conv_out, "shard", axis=1, tiled=True)

    halves = gather_slots(b16(norm_rows(rows_one, gain_rows[1], bias_rows[2])))
    saved_mix = []
    mixed = []
    for half, hidden in enumerate(halves):
        query = dot_rows(hidden, qkv_proj[0]) + own_biases[3]
        key = b16(dot_rows(hidden, qkv_proj[1]))
        value = b16(dot_rows(hidden, qkv_proj[2]) + own_biases[4])
        with_u = b16(query + own_biases[6])
        with_v = b16(query + own_biases[7])
        lens = slot_lengths[2 * half : 2 * half + 2]
        mix, soft = attend(lens, with_u, with_v, key, value, proj_b, length, heads)
        mixed += [mix[:length], mix[length:]]
        saved_mix.append((hidden, lens, soft, with_u, with_v, key, value))
    pieces = [mixed[0]] + [swap(mixed[j], "shard", j) for j in range(1, ns)]
    mixed_own = true_order(pieces, shard, 1)
    rows_two = rows_one + (dot_rows(mixed_own, w_out) + bias_rows[5])

    hidden_conv = b16(norm_rows(rows_two, gain_rows[2], bias_rows[8]))
    pre_conv = dot_rows(hidden_conv, wc_in) + jnp.concatenate([bias_rows[9], bias_rows[10]])
    conv_rows = gated_conv(pre_conv, mask_col, kernel)
    sums = jnp.concatenate(
        [
            jnp.sum(conv_rows * mask_col, axis=0).reshape(-1, 128),
            jnp.sum(conv_rows * conv_rows * mask_col, axis=0).reshape(-1, 128),
            jnp.broadcast_to(f32(lengths)[:, None], (8, 128)),
        ],
        0,
    )
    sums = stats_sum(sums, 1)
    lanes = features // 128
    frames = sums[2 * lanes, 0]
    row_mean = sums[:lanes].reshape(features) / frames
    inverse = lax.rsqrt(
        sums[lanes : 2 * lanes].reshape(features) / frames - row_mean * row_mean + epsilon
    )
    normed = (conv_rows - row_mean) * inverse * gain_rows[3] + bias_rows[11]
    active_conv = b16(jax.nn.silu(normed))
    rows_three = rows_two + (dot_rows(active_conv, wc_out) + bias_rows[12])

    branch, saved_two = ffn_forward(
        rows_three, w_in[1], w_rows[1], b_in[1], gain_rows[4], bias_rows[13]
    )
    rows_four = rows_three + 0.5 * (branch + bias_rows[14])
    result = norm_rows(rows_four, gain_rows[5], bias_rows[15]) * mask_col

    final_back = jax.vjp(norm_rows, rows_four, gain_rows[5], bias_rows[15])[1]
    stream, grad_gain_last, grad_bias_last = final_back(grads_in * mask_col)
    two = ffn_back(
        b16(0.5 * stream), rows_three, saved_two, w_in[1], w_rows[1], gain_rows[4], bias_rows[13]
    )
    stream = stream + two[0]

    def reduced(total, order):
        return double_batch(halve_batch(total, order, batch), order, batch)

    def reduced_rows(total, order):
        block = to_cols(halve_batch(total, order, batch), shard)
        block = double_batch(block, order, batch, axis=1)
        return block.reshape(-1, width)

    ffn_in_two = reduced(two[3], order_a)
    ffn_out_two = reduced_rows(two[4], order_b)

    grad_out = b16(stream)
    grad_conv_out = dot_over(active_conv, grad_out)
    grad_pw_out = row_total(grad_out)
    silu_back = jax.vjp(jax.nn.silu, normed)[1]
    grad_normed = silu_back(dot_back(grad_out, wc_out))[0]
    scaled = (conv_rows - row_mean) * inverse
    totals = stats_sum(
        jnp.concatenate(
            [
                jnp.sum(grad_normed, axis=0).reshape(-1, 128),
                jnp.sum(grad_normed * scaled, axis=0).reshape(-1, 128),
            ],
            0,
        ),
        2,
    )
    beta, gamma = totals[:lanes].reshape(features), totals[lanes:].reshape(features)
    gamma_row = gain_rows[3]
    grad_conv = inverse * (
        grad_normed * gamma_row
        - mask_col * (gamma_row * beta + scaled * (gamma_row * gamma)) / frames
    )
    tail_back = jax.vjp(lambda pre, taps: gated_conv(pre, mask_col, taps), pre_conv, kernel)[1]
    grad_pre_single, grad_kernel = tail_back(grad_conv)
    grad_pre = b16(grad_pre_single)
    grad_conv_in = dot_over(hidden_conv, grad_pre)
    grad_pw_in = row_total(grad_pre)
    conv_norm_back = jax.vjp(norm_rows, rows_two, gain_rows[2], bias_rows[8])[1]
    grad_rows, grad_gain_conv, grad_bias_conv = conv_norm_back(dot_back(grad_pre, wc_in))
    stream = stream + grad_rows

    def scattered(total):
        return f32(lax.psum_scatter(b16(total), "shard", scatter_dimension=1, tiled=True))

    conv_out_red = reduced(scattered(grad_conv_out), order_a)
    conv_in_red = reduced(scattered(grad_conv_in), order_b)

    grad_out = b16(stream)
    grad_w_out = dot_over(mixed_own, grad_out)
    grad_b_out = row_total(grad_out)
    grad_mixed = b16(dot_back(grad_out, w_out))
    slots = []
    for j in range(ns):
        part = lax.dynamic_slice_in_dim(grad_mixed, (shard ^ j) * width, width, 1)
        slots.append(part if j == 0 else swap(part, "shard", j))
    grad_qkv = [0.0, 0.0, 0.0]
    grad_w_pos = 0.0
    grad_uv = 0.0
    grad_q_bias = grad_x_bias = 0.0
    sums = []
    for half, (hidden, lens, soft, with_u, with_v, key, value) in enumerate(saved_mix):
        grad = jnp.concatenate(slots[2 * half : 2 * half + 2], 0)
        dq, dk, dx, dp, duv = attend_back(
            lens, grad, soft, with_u, with_v, key, value, proj_b, length, heads
        )
        for at, part in enumerate((dq, dk, dx)):
            grad_qkv[at] = grad_qkv[at] + dot_over(hidden, part)
        for at in range(dp.shape[0]):
            grad_w_pos = grad_w_pos + dot_over(table_b, dp[at])
        grad_uv = grad_uv + jnp.sum(duv, axis=0)
        grad_q_bias = grad_q_bias + row_total(dq)
        grad_x_bias = grad_x_bias + row_total(dx)
        sums.append(
            dot_back(dq, qkv_proj[0]) + dot_back(dk, qkv_proj[1]) + dot_back(dx, qkv_proj[2])
        )
    norm_back = jax.vjp(norm_rows, rows_one, gain_rows[1], bias_rows[2])[1]
    grad_rows, grad_gain_mix, grad_bias_mix = norm_back(scatter_slots(*sums))
    stream = stream + grad_rows
    pos_red = reduced(grad_w_pos, order_a)
    q_red = reduced(grad_qkv[0], order_b)
    k_red = reduced(grad_qkv[1], order_a)
    x_red = reduced(grad_qkv[2], order_b)
    out_red = reduced(scattered(grad_w_out), order_a)

    one = ffn_back(
        b16(0.5 * stream), rows_in, saved_one, w_in[0], w_rows[0], gain_rows[0], bias_rows[0]
    )
    stream = stream + one[0]
    ffn_in_one = reduced(one[3], order_a)
    ffn_out_one = reduced_rows(one[4], order_b)

    wide = jnp.stack(
        [
            one[1], grad_gain_mix, grad_gain_conv, two[1], grad_gain_last,
            one[2], one[6], grad_bias_mix, grad_b_out, grad_bias_conv,
            grad_pw_in[:features], grad_pw_in[features:], grad_pw_out, two[2], two[6], grad_bias_last,
        ]
        + [grad_kernel[t] for t in range(grad_kernel.shape[0])]
        + [jnp.zeros((features,), jnp.float32)] * 3
    )
    wide = wide.reshape(wide.shape[0], ns, width).transpose(1, 0, 2)
    hidden_bias = jnp.stack([one[5], two[5]]).reshape(-1, width)
    local = jnp.concatenate(
        [grad_q_bias[None], grad_x_bias[None], grad_uv[0:2], hidden_bias], 0
    )
    local = jnp.pad(local, [(0, -local.shape[0] % 8), (0, 0)])
    vec = vector_sum(wide, local, 3)
    mine = lax.dynamic_slice_in_dim(jnp.stack([gamma, beta]), shard * width, width, 1)
    base = wide.shape[1]
    out_gains = jnp.stack([vec[0], vec[1], vec[2], mine[0], vec[3], vec[4]])
    out_biases = jnp.stack(
        [
            vec[5], vec[6], vec[7], vec[base], vec[base + 1], vec[8], vec[base + 2], vec[base + 3],
            vec[9], vec[10], vec[11], mine[1], vec[12], vec[13], vec[14], vec[15],
        ]
    )
    out_kernel = vec[16:21]
    out_hidden = vec[base + 4 : base + 4 + hidden_bias.shape[0]].reshape(2, -1)
    return (
        result[None],
        stream[None],
        f32(jnp.stack([ffn_in_one, ffn_in_two])),
        f32(jnp.stack([ffn_out_one, ffn_out_two])),
        out_hidden,
        f32(jnp.stack([q_red, k_red, x_red])),
        f32(pos_red),
        f32(out_red),
        f32(conv_in_red),
        f32(conv_out_red),
        out_kernel,
        out_gains,
        out_biases,
    )


def solution(mesh):
    rows = P(("batch", "shard"), None, None)
    cube, flat = P(None, None, "shard"), P(None, "shard")
    return jax.shard_map(
        body,
        mesh=mesh,
        in_specs=(rows, rows, P(("batch", "shard")), cube, cube, flat, cube)
        + (flat,) * 7,
        out_specs=(rows, rows, cube, cube, flat, cube) + (flat,) * 7,
        check_vma=False,
    )
```

time: 1780 us -> 835 us (0.47)
  waiting for transfers between devices: 976 us -> 388 us
  blocking collectives: 493 us -> 6.2 us
  starting transfers between devices: 2.18 us -> 105 us
  other arithmetic: 39.9 us -> 105 us
  matrix products: 145 us -> 84.3 us
  Pallas kernels: 0 us -> 53.4 us
  local copies, waits for them, and re-layouts: 100 us -> 63.6 us
    reduce_scatter x16 -> x3, waiting for transfers between devices: 718 us -> 0.01 us  [scattered(): lax.psum_scatter(b16(total), 'shard', scatter_dimension=1, tiled=True)]
    psum x3 -> x0, blocking collectives: 465 us -> none  [the longest x1 385 us: body(): lax.psum((matrix_shard[0], matrix_shard[1], matrix_shard[2], matrix_shard...]
    ppermute x0 -> x114, waiting for transfers between devices: none -> 386 us  [swap(): return lax.ppermute(x, axis, [(i, i ^ mask) for i in range(n)])]
    all_gather x13 -> x3, waiting for transfers between devices: 225 us -> 0.02 us  [the longest x1 0.02 us: body(): wc_in = lax.all_gather(conv_in, 'shard', axis=1, tiled=True)]
    ppermute x0 -> x114, starting transfers between devices: none -> 104 us  [swap(): return lax.ppermute(x, axis, [(i, i ^ mask) for i in range(n)])]
    dot_general x41 -> x56, matrix products: 145 us -> 84.3 us  [the longest x21 34.6 us: dot_over(): lax.dot_general(a, b, (((0,), (0,)), ((), ())), preferred_element_type=jn...]
    pallas_call x0 -> x7, Pallas kernels: none -> 53.4 us  [the longest x2 23.2 us: stats_sum(): pl.pallas_call(functools.partial(stats_body, ns, nb), out_shape=jax.Shape...]
    unnamed x31 -> x6, waiting for transfers between devices: 32.5 us -> 1.44 us
  transfers between devices with their start and end apart: 30 -> 120, of which waited for: 22 -> 63; matrix products, arithmetic and copies ran while one was open for 13% -> 23% of each run, Pallas kernels for 0% -> 5%
where the time goes in v1:
time: 835 us; the launch traced here: 823 us
  waiting for transfers between devices  388 us (46%)
  starting transfers between devices  105 us (13%)
  other arithmetic  105 us (13%)
  matrix products  84.3 us (10%)
  local copies, waits for them, and re-layouts  63.6 us (8%)
  Pallas kernels  53.4 us (6%)
  between operations  18.7 us (2%)
    ppermute x114, waiting for transfers between devices, swap(): return lax.ppermute(x, axis, [(i, i ^ mask) for i in range(n)])  386 us
    ppermute x114, starting transfers between devices, swap(): return lax.ppermute(x, axis, [(i, i ^ mask) for i in range(n)])  104 us
    dot_general x21, matrix products, dot_over(): lax.dot_general(a, b, (((0,), (0,)), ((), ())), preferred_element_type=jn...  34.6 us
    unnamed x403, local copies, waits for them, and re-layouts  32 us
    dot_general x17, matrix products, dot_back(): lax.dot_general(a, b, (((1,), (1,)), ((), ())), preferred_element_type=jn...  25.9 us
    dot_general x18, matrix products, dot_rows(): return jnp.dot(a, b, preferred_element_type=jnp.float32)  23.8 us
    pallas_call x2, Pallas kernels, stats_sum(): pl.pallas_call(functools.partial(stats_body, ns, nb), out_shape=jax.Shape...  23.2 us
    convert_element_type x12, other arithmetic, f32(): return a.astype(jnp.float32)  18.9 us
  transfers between devices with their start and end apart: 120, of which 63 were waited for; matrix products, arithmetic and copies ran while one was open for 23% of the time, Pallas kernels for 5%

profile of v1, /device:TPU:0, one launch (start us, length us, event | category | flops | bytes accessed | tf_op | source)
XLA Modules:
  0.0 823.1 jit_solution(15163795850522631302)
XLA Ops:
  9.7 6.2 all_gather.12
  19.8 4.0 fusion.167
  27.7 2.9 constant_dynamic-slice_fusion.20
  32.4 10.4 %collective-permute-done.5 = bf16[256,1024]{1,0:T(8,128)(2,1)S(1)} collective-permute-done((bf16[256,1024]{1,0:T(8,128)(2,1)S(1)}, bf16[256,1024]{1,0:T(8,128)(2,1)S(1)}, u32[]{:S(2)}, u32[]{:S(2)}) %collective-permute-start.5) | collective-permute-done | bytes 524320 | tf_op jit(solution)/shard_map/ppermute | solution.py:75
  44.7 9.8 %collective-permute-done.3 = bf16[1024,256]{1,0:T(8,128)(2,1)} collective-permute-done((bf16[1024,256]{1,0:T(8,128)(2,1)}, bf16[1024,256]{1,0:T(8,128)(2,1)}, u32[]{:S(2)}, u32[]{:S(2)}) %collective-permute-start.3) | collective-permute-done | bytes 524320 | tf_op jit(solution)/shard_map/ppermute | solution.py:75
  56.2 17.7 %collective-permute-done.2 = bf16[1024,256]{1,0:T(8,128)(2,1)} collective-permute-done((bf16[1024,256]{1,0:T(8,128)(2,1)}, bf16[1024,256]{1,0:T(8,128)(2,1)}, u32[]{:S(2)}, u32[]{:S(2)}) %collective-permute-start.2) | collective-permute-done | bytes 524320 | tf_op jit(solution)/shard_map/ppermute | solution.py:75
  75.8 2.7 copy-done.178
  90.5 37.5 %collective-permute-done.8 = bf16[256,1024]{1,0:T(8,128)(2,1)S(1)} collective-permute-done((bf16[256,1024]{1,0:T(8,128)(2,1)S(1)}, bf16[256,1024]{1,0:T(8,128)(2,1)S(1)}, u32[]{:S(2)}, u32[]{:S(2)}) %collective-permute-start.8) | collective-permute-done | bytes 524320 | tf_op jit(solution)/shard_map/ppermute | solution.py:75
  133.0 4.1 fusion.42
  138.1 6.4 collective-permute-done.11
  147.9 2.8 attend.3
  153.6 3.3 attend.2
  161.4 2.7 fusion.178
  165.9 3.8 convolution_add_fusion
  174.8 12.4 %stats_sum_1.1 = f32[24,128]{1,0:T(8,128)} custom-call(f32[24,128]{1,0:T(8,128)} %maximum_maximum_fusion.1.x_ref), custom_call_target="tpu_custom_call" | custom-call | tf_op jit(solution)/shard_map/stats_sum_1/pallas_call | solution.py:205
  192.1 2.8 fusion.179
  197.8 11.0 %collective-permute-done.20 = bf16[256,1024]{1,0:T(8,128)(2,1)S(1)} collective-permute-done((bf16[256,1024]{1,0:T(8,128)(2,1)S(1)}, bf16[256,1024]{1,0:T(8,128)(2,1)S(1)}, u32[]{:S(2)}, u32[]{:S(2)}) %collective-permute-start.20) | collective-permute-done | bytes 524320 | tf_op jit(solution)/shard_map/ppermute | solution.py:75
  217.1 12.7 %collective-permute-done.23 = bf16[256,1024]{1,0:T(8,128)(2,1)S(1)} collective-permute-done((bf16[256,1024]{1,0:T(8,128)(2,1)S(1)}, bf16[256,1024]{1,0:T(8,128)(2,1)S(1)}, u32[]{:S(2)}, u32[]{:S(2)}) %collective-permute-start.23) | collective-permute-done | bytes 524320 | tf_op jit(solution)/shard_map/ppermute | solution.py:75
  235.1 12.5 %collective-permute-done.26 = bf16[256,1024]{1,0:T(8,128)(2,1)S(1)} collective-permute-done((bf16[256,1024]{1,0:T(8,128)(2,1)S(1)}, bf16[256,1024]{1,0:T(8,128)(2,1)S(1)}, u32[]{:S(2)}, u32[]{:S(2)}) %collective-permute-start.26) | collective-permute-done | bytes 524320 | tf_op jit(solution)/shard_map/ppermute | solution.py:75
  249.5 2.7 convert_reduce_fusion
  259.5 12.6 %collective-permute-done.29 = bf16[256,1024]{1,0:T(8,128)(2,1)S(1)} collective-permute-done((bf16[256,1024]{1,0:T(8,128)(2,1)S(1)}, bf16[256,1024]{1,0:T(8,128)(2,1)S(1)}, u32[]{:S(2)}, u32[]{:S(2)}) %collective-permute-start.29) | collective-permute-done | bytes 524320 | tf_op jit(solution)/shard_map/ppermute | solution.py:75
  278.1 10.8 %stats_sum_2.1 = f32[16,128]{1,0:T(8,128)} custom-call(f32[16,128]{1,0:T(8,128)} %pad_maximum_fusion.56.x_ref), custom_call_target="tpu_custom_call" | custom-call | tf_op jit(solution)/shard_map/stats_sum_2/pallas_call | solution.py:205
  290.2 5.5 multiply_reduce_fusion.4
  307.6 5.0 fusion.73
  312.7 3.4 fusion.71
  318.4 4.3 convolution_add_fusion.3
  333.4 17.3 %collective-permute-done.48 = bf16[512,1024]{1,0:T(8,128)(2,1)} collective-permute-done((bf16[512,1024]{1,0:T(8,128)(2,1)}, bf16[512,1024]{1,0:T(8,128)(2,1)}, u32[]{:S(2)}, u32[]{:S(2)}) %collective-permute-start.48) | collective-permute-done | bytes 1048608 | tf_op jit(solution)/shard_map/ppermute | solution.py:75
  364.7 3.4 convolution_convert_fusion
  370.4 5.4 collective-permute-done.32
  378.0 4.4 attend_back.3
  386.1 4.6 attend_back.2
  412.8 4.4 collective-permute-done.78
  417.2 4.5 collective-permute-done.90
  429.3 2.8 collective-permute-start.50
  437.1 20.0 %collective-permute-done.86 = bf16[128,256]{1,0:T(8,128)(2,1)S(1)} collective-permute-done((bf16[128,256]{1,0:T(8,128)(2,1)S(1)}, bf16[128,256]{1,0:T(8,128)(2,1)S(1)}, u32[]{:S(2)}, u32[]{:S(2)}) %collective-permute-start.86) | collective-permute-done | bytes 65568 | tf_op jit(solution)/shard_map/ppermute | solution.py:75
  457.1 5.1 collective-permute-done.74
  462.4 6.2 collective-permute-done.80
  468.6 7.1 collective-permute-done.92
  475.7 3.0 collective-permute-start.75
  487.0 2.7 collective-permute-start.88
  505.4 10.1 %collective-permute-done.77 = bf16[512,256]{1,0:T(8,128)(2,1)S(1)} collective-permute-done((bf16[512,256]{1,0:T(8,128)(2,1)S(1)}, bf16[512,256]{1,0:T(8,128)(2,1)S(1)}, u32[]{:S(2)}, u32[]{:S(2)}) %collective-permute-start.77) | collective-permute-done | bytes 262176 | tf_op jit(solution)/shard_map/ppermute | solution.py:75
  520.0 3.1 collective-permute-done.95
  527.9 3.2 collective-permute-start.38
  537.0 6.7 collective-permute-done.38
  565.9 3.2 broadcast_select_fusion.5
  569.1 14.2 %collective-permute-done.42 = bf16[512,1024]{1,0:T(8,128)(2,1)} collective-permute-done((bf16[512,1024]{1,0:T(8,128)(2,1)}, bf16[512,1024]{1,0:T(8,128)(2,1)}, u32[]{:S(2)}, u32[]{:S(2)}) %collective-permute-start.42) | collective-permute-done | bytes 1048608 | tf_op jit(solution)/shard_map/ppermute | solution.py:75
  595.5 15.1 %vector_sum.1 = f32[40,256]{1,0:T(8,128)} custom-call(f32[4,24,256]{2,1,0:T(8,128)} %bitcast.286, f32[16,256]{1,0:T(8,128)} %select_maximum_fusion.l_ref), custom_call_target="tpu_custom_call" | custom-call | tf_op jit(solution)/shard_map/vector_sum/pallas_call | solution.py:261
  610.6 2.7 add_bitcast_fusion
  622.3 17.1 %collective-permute-done.56 = bf16[128,1024]{1,0:T(8,128)(2,1)S(1)} collective-permute-done((bf16[128,1024]{1,0:T(8,128)(2,1)S(1)}, bf16[128,1024]{1,0:T(8,128)(2,1)S(1)}, u32[]{:S(2)}, u32[]{:S(2)}) %collective-permute-start.56) | collective-permute-done | bytes 262176 | tf_op jit(solution)/shard_map/ppermute | solution.py:75
  652.3 17.6 %collective-permute-done.45 = bf16[128,1024]{1,0:T(8,128)(2,1)} collective-permute-done((bf16[128,1024]{1,0:T(8,128)(2,1)S(1)}, bf16[128,1024]{1,0:T(8,128)(2,1)}, u32[]{:S(2)}, u32[]{:S(2)}) %collective-permute-start.45) | collective-permute-done | bytes 262176 | tf_op jit(solution)/shard_map/ppermute | solution.py:75
  671.0 4.6 collective-permute-done.69
  685.0 8.0 collective-permute-done.97
  696.1 3.9 collective-permute-done.98
  703.1 3.9 collective-permute-done.99
  709.2 3.4 collective-permute-done.100
  724.5 3.5 collective-permute-done.113
  731.8 14.5 %collective-permute-done.47 = bf16[512,1024]{1,0:T(8,128)(2,1)} collective-permute-done((bf16[512,1024]{1,0:T(8,128)(2,1)}, bf16[512,1024]{1,0:T(8,128)(2,1)}, u32[]{:S(2)}, u32[]{:S(2)}) %collective-permute-start.47) | collective-permute-done | bytes 1048608 | tf_op jit(solution)/shard_map/ppermute | solution.py:75
  748.5 27.3 %collective-permute-done.102 = bf16[512,512]{1,0:T(8,128)(2,1)S(1)} collective-permute-done((bf16[512,512]{1,0:T(8,128)(2,1)S(1)}, bf16[512,512]{1,0:T(8,128)(2,1)S(1)}, u32[]{:S(2)}, u32[]{:S(2)}) %collective-permute-start.102) | collective-permute-done | bytes 524320 | tf_op jit(solution)/shard_map/ppermute | solution.py:75
  777.9 3.9 maximum_convert_fusion
  784.4 8.1 collective-permute-done.104
  794.2 4.2 collective-permute-done.105
  800.4 4.5 collective-permute-done.106
  805.1 3.9 maximum_convert_fusion.1
  809.1 5.2 collective-permute-done.107
  (934 shorter events, 311.8 us)
Async XLA Ops:
  7.2 154.1 %all-gather.4.cloned.1.call-start = ((), (), s32[]{:S(2)}) async-start(), calls=%async_computation.3 | async-start | bytes 2621440 | tf_op jit(solution)/shard_map/all_gather | solution.py:463
  8.0 157.4 %all-gather.6.cloned.1.call-start = ((), (), s32[]{:S(2)}) async-start(), calls=%async_computation.4 | async-start | bytes 5242880 | tf_op jit(solution)/shard_map/all_gather | solution.py:464
  8.7 183.3 %all-gather.8.cloned.1.call-start = ((), (), s32[]{:S(2)}) async-start(), calls=%async_computation.5 | async-start | bytes 2621440 | tf_op jit(solution)/shard_map/all_gather | solution.py:465
  17.7 25.1 %collective-permute-start.5 = (bf16[256,1024]{1,0:T(8,128)(2,1)S(1)}, bf16[256,1024]{1,0:T(8,128)(2,1)S(1)}, u32[]{:S(2)}, u32[]{:S(2)}) collective-permute-start(bf16[256,1024]{1,0:T(8,128)(2,1)S(1)} %add_convert_fusion.4), channel_id=1, source_target_pairs={{0,2},{1,3},{2,0},{3,1},{4,6},{5,7},{6,4},{7,5},{8,10},{9,11},{10,... | collective-permute-start | bytes 1572872 | tf_op jit(solution)/shard_map/ppermute | solution.py:75
  19.7 56.1 %collective-permute-start = (bf16[256,1024]{1,0:T(8,128)(2,1)S(1)}, bf16[256,1024]{1,0:T(8,128)(2,1)}, u32[]{:S(2)}, u32[]{:S(2)}) collective-permute-start(bf16[256,1024]{1,0:T(8,128)(2,1)S(1)} %add_convert_fusion.4), channel_id=1, source_target_pairs={{0,1},{1,0},{2,3},{3,2},{4,5},{5,4},{6,7},{7,6},{8,9},{9,8},{10,11... | collective-permute-start | bytes 1572872 | tf_op jit(solution)/shard_map/ppermute | solution.py:75
  25.0 29.5 %collective-permute-start.3 = (bf16[1024,256]{1,0:T(8,128)(2,1)}, bf16[1024,256]{1,0:T(8,128)(2,1)}, u32[]{:S(2)}, u32[]{:S(2)}) collective-permute-start(bf16[1024,256]{1,0:T(8,128)(2,1)} %get-tuple-element.118), channel_id=1, source_target_pairs={{0,3},{1,2},{2,1},{3,0},{4,7},{5,6},{6,5},{7,4},{8,11},{9,10},{10,... | collective-permute-start | bytes 1572872 | tf_op jit(solution)/shard_map/ppermute | solution.py:75
  25.3 48.6 %collective-permute-start.2 = (bf16[1024,256]{1,0:T(8,128)(2,1)}, bf16[1024,256]{1,0:T(8,128)(2,1)}, u32[]{:S(2)}, u32[]{:S(2)}) collective-permute-start(bf16[1024,256]{1,0:T(8,128)(2,1)} %get-tuple-element.119), channel_id=1, source_target_pairs={{0,2},{1,3},{2,0},{3,1},{4,6},{5,7},{6,4},{7,5},{8,10},{9,11},{10,... | collective-permute-start | bytes 1572872 | tf_op jit(solution)/shard_map/ppermute | solution.py:75
  27.0 46.9 %collective-permute-start.1 = (bf16[1024,256]{1,0:T(8,128)(2,1)}, bf16[1024,256]{1,0:T(8,128)(2,1)}, u32[]{:S(2)}, u32[]{:S(2)}) collective-permute-start(bf16[1024,256]{1,0:T(8,128)(2,1)} %get-tuple-element.120), channel_id=1, source_target_pairs={{0,1},{1,0},{2,3},{3,2},{4,5},{5,4},{6,7},{7,6},{8,9},{9,8},{10,11... | collective-permute-start | bytes 1572872 | tf_op jit(solution)/shard_map/ppermute | solution.py:75
  27.0 620.8 %reduce-scatter.4.cloned.1.call-start = ((), (), s32[]{:S(2)}) async-start(), calls=%async_computation.6 | async-start | bytes 2621440 | tf_op jit(solution)/shard_map/reduce_scatter | solution.py:562
  42.8 153.4 %collective-permute-start.18 = (bf16[1024,256]{1,0:T(8,128)(2,1)}, bf16[1024,256]{1,0:T(8,128)(2,1)}, u32[]{:S(2)}, u32[]{:S(2)}) collective-permute-start(bf16[1024,256]{1,0:T(8,128)(2,1)} %get-tuple-element.110), channel_id=1, source_target_pairs={{0,3},{1,2},{2,1},{3,0},{4,7},{5,6},{6,5},{7,4},{8,11},{9,10},{10,... | collective-permute-start | bytes 1572872 | tf_op jit(solution)/shard_map/ppermute | solution.py:75
  54.4 141.7 %collective-permute-start.17 = (bf16[1024,256]{1,0:T(8,128)(2,1)}, bf16[1024,256]{1,0:T(8,128)(2,1)}, u32[]{:S(2)}, u32[]{:S(2)}) collective-permute-start(bf16[1024,256]{1,0:T(8,128)(2,1)} %get-tuple-element.111), channel_id=1, source_target_pairs={{0,2},{1,3},{2,0},{3,1},{4,6},{5,7},{6,4},{7,5},{8,10},{9,11},{10,... | collective-permute-start | bytes 1572872 | tf_op jit(solution)/shard_map/ppermute | solution.py:75
  86.0 41.9 %collective-permute-start.8 = (bf16[256,1024]{1,0:T(8,128)(2,1)S(1)}, bf16[256,1024]{1,0:T(8,128)(2,1)S(1)}, u32[]{:S(2)}, u32[]{:S(2)}) collective-permute-start(bf16[256,1024]{1,0:T(8,128)(2,1)S(1)} %fusion.63), channel_id=1, source_target_pairs={{0,2},{1,3},{2,0},{3,1},{4,6},{5,7},{6,4},{7,5},{8,10},{9,11},{10,... | collective-permute-start | bytes 1572872 | tf_op jit(solution)/shard_map/ppermute | solution.py:75
  129.0 15.5 %collective-permute-start.9 = (bf16[256,1024]{1,0:T(8,128)(2,1)S(1)}, bf16[256,1024]{1,0:T(8,128)(2,1)S(1)}, u32[]{:S(2)}, u32[]{:S(2)}) collective-permute-start(bf16[256,1024]{1,0:T(8,128)(2,1)S(1)} %add_convert_fusion.3), channel_id=1, source_target_pairs={{0,1},{1,0},{2,3},{3,2},{4,5},{5,4},{6,7},{7,6},{8,9},{9,8},{10,11... | collective-permute-start | bytes 1572872 | tf_op jit(solution)/shard_map/ppermute | solution.py:75
  129.1 15.4 %collective-permute-start.11 = (bf16[256,1024]{1,0:T(8,128)(2,1)S(1)}, bf16[256,1024]{1,0:T(8,128)(2,1)S(1)}, u32[]{:S(2)}, u32[]{:S(2)}) collective-permute-start(bf16[256,1024]{1,0:T(8,128)(2,1)S(1)} %add_convert_fusion.3), channel_id=1, source_target_pairs={{0,2},{1,3},{2,0},{3,1},{4,6},{5,7},{6,4},{7,5},{8,10},{9,11},{10,... | collective-permute-start | bytes 1572872 | tf_op jit(solution)/shard_map/ppermute | solution.py:75
  159.8 36.3 %collective-permute-start.16 = (bf16[1024,256]{1,0:T(8,128)(2,1)}, bf16[1024,256]{1,0:T(8,128)(2,1)}, u32[]{:S(2)}, u32[]{:S(2)}) collective-permute-start(bf16[1024,256]{1,0:T(8,128)(2,1)} %get-tuple-element.112), channel_id=1, source_target_pairs={{0,1},{1,0},{2,3},{3,2},{4,5},{5,4},{6,7},{7,6},{8,9},{9,8},{10,11... | collective-permute-start | bytes 1572872 | tf_op jit(solution)/shard_map/ppermute | solution.py:75
  195.4 13.4 %collective-permute-start.20 = (bf16[256,1024]{1,0:T(8,128)(2,1)S(1)}, bf16[256,1024]{1,0:T(8,128)(2,1)S(1)}, u32[]{:S(2)}, u32[]{:S(2)}) collective-permute-start(bf16[256,1024]{1,0:T(8,128)(2,1)S(1)} %add_convert_fusion.1), channel_id=1, source_target_pairs={{0,2},{1,3},{2,0},{3,1},{4,6},{5,7},{6,4},{7,5},{8,10},{9,11},{10,... | collective-permute-start | bytes 1572872 | tf_op jit(solution)/shard_map/ppermute | solution.py:75
  196.2 12.8 %collective-permute-start.15 = (bf16[256,1024]{1,0:T(8,128)(2,1)S(1)}, bf16[256,1024]{1,0:T(8,128)(2,1)S(1)}, u32[]{:S(2)}, u32[]{:S(2)}) collective-permute-start(bf16[256,1024]{1,0:T(8,128)(2,1)S(1)} %add_convert_fusion.1), channel_id=1, source_target_pairs={{0,1},{1,0},{2,3},{3,2},{4,5},{5,4},{6,7},{7,6},{8,9},{9,8},{10,11... | collective-permute-start | bytes 1572872 | tf_op jit(solution)/shard_map/ppermute | solution.py:75
  215.7 14.1 %collective-permute-start.23 = (bf16[256,1024]{1,0:T(8,128)(2,1)S(1)}, bf16[256,1024]{1,0:T(8,128)(2,1)S(1)}, u32[]{:S(2)}, u32[]{:S(2)}) collective-permute-start(bf16[256,1024]{1,0:T(8,128)(2,1)S(1)} %fusion.55), channel_id=1, source_target_pairs={{0,2},{1,3},{2,0},{3,1},{4,6},{5,7},{6,4},{7,5},{8,10},{9,11},{10,... | collective-permute-start | bytes 1572872 | tf_op jit(solution)/shard_map/ppermute | solution.py:75
  234.4 13.2 %collective-permute-start.26 = (bf16[256,1024]{1,0:T(8,128)(2,1)S(1)}, bf16[256,1024]{1,0:T(8,128)(2,1)S(1)}, u32[]{:S(2)}, u32[]{:S(2)}) collective-permute-start(bf16[256,1024]{1,0:T(8,128)(2,1)S(1)} %get-tuple-element.67), channel_id=1, source_target_pairs={{0,2},{1,3},{2,0},{3,1},{4,6},{5,7},{6,4},{7,5},{8,10},{9,11},{10,... | collective-permute-start | bytes 1572872 | tf_op jit(solution)/shard_map/ppermute | solution.py:75
  258.2 14.0 %collective-permute-start.29 = (bf16[256,1024]{1,0:T(8,128)(2,1)S(1)}, bf16[256,1024]{1,0:T(8,128)(2,1)S(1)}, u32[]{:S(2)}, u32[]{:S(2)}) collective-permute-start(bf16[256,1024]{1,0:T(8,128)(2,1)S(1)} %fusion.53), channel_id=1, source_target_pairs={{0,2},{1,3},{2,0},{3,1},{4,6},{5,7},{6,4},{7,5},{8,10},{9,11},{10,... | collective-permute-start | bytes 1572872 | tf_op jit(solution)/shard_map/ppermute | solution.py:75
  307.5 343.0 %reduce-scatter.8.cloned.1.call-start = ((), (), s32[]{:S(2)}) async-start(), calls=%async_computation.8 | async-start | bytes 2621440 | tf_op jit(solution)/shard_map/reduce_scatter | solution.py:562
  318.3 410.5 %reduce-scatter.6.cloned.1.call-start = ((), (), s32[]{:S(2)}) async-start(), calls=%async_computation.7 | async-start | bytes 5242880 | tf_op jit(solution)/shard_map/reduce_scatter | solution.py:562
  325.9 24.8 %collective-permute-start.48 = (bf16[512,1024]{1,0:T(8,128)(2,1)}, bf16[512,1024]{1,0:T(8,128)(2,1)}, u32[]{:S(2)}, u32[]{:S(2)}) collective-permute-start(bf16[512,1024]{1,0:T(8,128)(2,1)} %dynamic-slice_convert_fusion.2), channel_id=1, source_target_pairs={{0,4},{4,0},{8,12},{12,8},{16,20},{20,16},{24,28},{28,24},{1,5},{5... | collective-permute-start | bytes 3145736 | tf_op jit(solution)/shard_map/ppermute | solution.py:75
  332.0 25.2 %collective-permute-start.63 = (bf16[512,1024]{1,0:T(8,128)(2,1)}, bf16[512,1024]{1,0:T(8,128)(2,1)}, u32[]{:S(2)}, u32[]{:S(2)}) collective-permute-start(bf16[512,1024]{1,0:T(8,128)(2,1)} %dynamic-slice_convert_fusion), channel_id=1, source_target_pairs={{0,8},{4,12},{8,0},{12,4},{16,24},{20,28},{24,16},{28,20},{1,9},{5... | collective-permute-start | bytes 3145736 | tf_op jit(solution)/shard_map/ppermute | solution.py:75
  354.0 69.7 %collective-permute-start.49 = (bf16[256,1024]{1,0:T(8,128)(2,1)}, bf16[256,1024]{1,0:T(8,128)(2,1)}, u32[]{:S(2)}, u32[]{:S(2)}) collective-permute-start(bf16[256,1024]{1,0:T(8,128)(2,1)} %dynamic-slice_convert_fusion.7), channel_id=1, source_target_pairs={{0,8},{4,12},{8,0},{12,4},{16,24},{20,28},{24,16},{28,20},{1,9},{5... | collective-permute-start | bytes 1572872 | tf_op jit(solution)/shard_map/ppermute | solution.py:75
  359.9 65.4 %collective-permute-start.64 = (bf16[256,1024]{1,0:T(8,128)(2,1)}, bf16[256,1024]{1,0:T(8,128)(2,1)}, u32[]{:S(2)}, u32[]{:S(2)}) collective-permute-start(bf16[256,1024]{1,0:T(8,128)(2,1)} %dynamic-slice_convert_fusion.5), channel_id=1, source_target_pairs={{0,4},{4,0},{8,12},{12,8},{16,20},{20,16},{24,28},{28,24},{1,5},{5... | collective-permute-start | bytes 1572872 | tf_op jit(solution)/shard_map/ppermute | solution.py:75
  361.5 14.3 %collective-permute-start.32 = (bf16[256,256]{1,0:T(8,128)(2,1)}, bf16[256,256]{1,0:T(8,128)(2,1)}, u32[]{:S(2)}, u32[]{:S(2)}) collective-permute-start(bf16[256,256]{1,0:T(8,128)(2,1)} %get-tuple-element.161), channel_id=1, source_target_pairs={{0,2},{1,3},{2,0},{3,1},{4,6},{5,7},{6,4},{7,5},{8,10},{9,11},{10,... | collective-permute-start | bytes 393224 | tf_op jit(solution)/shard_map/ppermute | solution.py:75
  362.8 22.3 %collective-permute-start.30 = (bf16[256,256]{1,0:T(8,128)(2,1)}, bf16[256,256]{1,0:T(8,128)(2,1)}, u32[]{:S(2)}, u32[]{:S(2)}) collective-permute-start(bf16[256,256]{1,0:T(8,128)(2,1)} %get-tuple-element.162), channel_id=1, source_target_pairs={{0,1},{1,0},{2,3},{3,2},{4,5},{5,4},{6,7},{7,6},{8,9},{9,8},{10,11... | collective-permute-start | bytes 393224 | tf_op jit(solution)/shard_map/ppermute | solution.py:75
  384.8 90.8 %collective-permute-start.34 = (bf16[256,1024]{1,0:T(8,128)(2,1)}, bf16[256,1024]{1,0:T(8,128)(2,1)}, u32[]{:S(2)}, u32[]{:S(2)}) collective-permute-start(bf16[256,1024]{1,0:T(8,128)(2,1)} %slice.736), channel_id=1, source_target_pairs={{0,1},{1,0},{2,3},{3,2},{4,5},{5,4},{6,7},{7,6},{8,9},{9,8},{10,11... | collective-permute-start | bytes 1572872 | tf_op jit(solution)/shard_map/ppermute | solution.py:75
  396.7 11.2 %collective-permute-start.84 = (bf16[512,256]{1,0:T(8,128)(2,1)S(1)}, bf16[512,256]{1,0:T(8,128)(2,1)S(1)}, u32[]{:S(2)}, u32[]{:S(2)}) collective-permute-start(bf16[512,256]{1,0:T(8,128)(2,1)S(1)} %dynamic-slice_convert_fusion.13), channel_id=1, source_target_pairs={{0,8},{4,12},{8,0},{12,4},{16,24},{20,28},{24,16},{28,20},{1,9},{5... | collective-permute-start | bytes 786440 | tf_op jit(solution)/shard_map/ppermute | solution.py:75
  398.7 12.1 %collective-permute-start.72 = (bf16[512,256]{1,0:T(8,128)(2,1)S(1)}, bf16[512,256]{1,0:T(8,128)(2,1)S(1)}, u32[]{:S(2)}, u32[]{:S(2)}) collective-permute-start(bf16[512,256]{1,0:T(8,128)(2,1)S(1)} %dynamic-slice_convert_fusion.15), channel_id=1, source_target_pairs={{0,8},{4,12},{8,0},{12,4},{16,24},{20,28},{24,16},{28,20},{1,9},{5... | collective-permute-start | bytes 786440 | tf_op jit(solution)/shard_map/ppermute | solution.py:75
  417.2 106.1 %collective-permute-start.31 = (bf16[256,1024]{1,0:T(8,128)(2,1)S(1)}, bf16[256,1024]{1,0:T(8,128)(2,1)S(1)}, u32[]{:S(2)}, u32[]{:S(2)}) collective-permute-start(bf16[256,1024]{1,0:T(8,128)(2,1)S(1)} %slice.737), channel_id=1, source_target_pairs={{0,1},{1,0},{2,3},{3,2},{4,5},{5,4},{6,7},{7,6},{8,9},{9,8},{10,11... | collective-permute-start | bytes 1572872 | tf_op jit(solution)/shard_map/ppermute | solution.py:75
  429.3 62.4 %collective-permute-start.50 = (bf16[128,1024]{1,0:T(8,128)(2,1)S(1)}, bf16[128,1024]{1,0:T(8,128)(2,1)S(1)}, u32[]{:S(2)}, u32[]{:S(2)}) collective-permute-start(bf16[128,1024]{1,0:T(8,128)(2,1)S(1)} %dynamic-slice_convert_fusion.18), channel_id=1, source_target_pairs={{0,16},{4,20},{8,24},{12,28},{16,0},{20,4},{24,8},{28,12},{1,17},{... | collective-permute-start | bytes 786440 | tf_op jit(solution)/shard_map/ppermute | solution.py:75
  432.2 60.1 %collective-permute-start.65 = (bf16[128,1024]{1,0:T(8,128)(2,1)S(1)}, bf16[128,1024]{1,0:T(8,128)(2,1)S(1)}, u32[]{:S(2)}, u32[]{:S(2)}) collective-permute-start(bf16[128,1024]{1,0:T(8,128)(2,1)S(1)} %dynamic-slice_convert_fusion.16), channel_id=1, source_target_pairs={{0,16},{4,20},{8,24},{12,28},{16,0},{20,4},{24,8},{28,12},{1,17},{... | collective-permute-start | bytes 786440 | tf_op jit(solution)/shard_map/ppermute | solution.py:75
  435.7 21.4 %collective-permute-start.86 = (bf16[128,256]{1,0:T(8,128)(2,1)S(1)}, bf16[128,256]{1,0:T(8,128)(2,1)S(1)}, u32[]{:S(2)}, u32[]{:S(2)}) collective-permute-start(bf16[128,256]{1,0:T(8,128)(2,1)S(1)} %dynamic-slice_convert_fusion.30), channel_id=1, source_target_pairs={{0,16},{4,20},{8,24},{12,28},{16,0},{20,4},{24,8},{28,12},{1,17},{... | collective-permute-start | bytes 196616 | tf_op jit(solution)/shard_map/ppermute | solution.py:75
  500.4 22.8 %collective-permute-start.35 = (bf16[256,1024]{1,0:T(8,128)(2,1)S(1)}, bf16[256,1024]{1,0:T(8,128)(2,1)S(1)}, u32[]{:S(2)}, u32[]{:S(2)}) collective-permute-start(bf16[256,1024]{1,0:T(8,128)(2,1)S(1)} %fusion.50), channel_id=1, source_target_pairs={{0,2},{1,3},{2,0},{3,1},{4,6},{5,7},{6,4},{7,5},{8,10},{9,11},{10,... | collective-permute-start | bytes 1572872 | tf_op jit(solution)/shard_map/ppermute | solution.py:75
  501.9 16.0 %collective-permute-start.89 = (bf16[512,256]{1,0:T(8,128)(2,1)S(1)}, bf16[512,256]{1,0:T(8,128)(2,1)S(1)}, u32[]{:S(2)}, u32[]{:S(2)}) collective-permute-start(bf16[512,256]{1,0:T(8,128)(2,1)S(1)} %pad_maximum_fusion.42), channel_id=1, source_target_pairs={{0,8},{4,12},{8,0},{12,4},{16,24},{20,28},{24,16},{28,20},{1,9},{5... | collective-permute-start | bytes 786440 | tf_op jit(solution)/shard_map/ppermute | solution.py:75
  503.4 12.1 %collective-permute-start.77 = (bf16[512,256]{1,0:T(8,128)(2,1)S(1)}, bf16[512,256]{1,0:T(8,128)(2,1)S(1)}, u32[]{:S(2)}, u32[]{:S(2)}) collective-permute-start(bf16[512,256]{1,0:T(8,128)(2,1)S(1)} %pad_maximum_fusion.40), channel_id=1, source_target_pairs={{0,8},{4,12},{8,0},{12,4},{16,24},{20,28},{24,16},{28,20},{1,9},{5... | collective-permute-start | bytes 786440 | tf_op jit(solution)/shard_map/ppermute | solution.py:75
  504.2 13.1 %collective-permute-start.83 = (bf16[512,256]{1,0:T(8,128)(2,1)S(1)}, bf16[512,256]{1,0:T(8,128)(2,1)S(1)}, u32[]{:S(2)}, u32[]{:S(2)}) collective-permute-start(bf16[512,256]{1,0:T(8,128)(2,1)S(1)} %pad_maximum_fusion.41), channel_id=1, source_target_pairs={{0,4},{4,0},{8,12},{12,8},{16,20},{20,16},{24,28},{28,24},{1,5},{5... | collective-permute-start | bytes 786440 | tf_op jit(solution)/shard_map/ppermute | solution.py:75
  517.3 13.7 %collective-permute-start.52 = (bf16[256,1024]{1,0:T(8,128)(2,1)S(1)}, bf16[256,1024]{1,0:T(8,128)(2,1)S(1)}, u32[]{:S(2)}, u32[]{:S(2)}) collective-permute-start(bf16[256,1024]{1,0:T(8,128)(2,1)S(1)} %pad_maximum_fusion.30), channel_id=1, source_target_pairs={{0,8},{4,12},{8,0},{12,4},{16,24},{20,28},{24,16},{28,20},{1,9},{5... | collective-permute-start | bytes 1572872 | tf_op jit(solution)/shard_map/ppermute | solution.py:75
  527.9 15.7 %collective-permute-start.38 = (bf16[256,1024]{1,0:T(8,128)(2,1)S(1)}, bf16[256,1024]{1,0:T(8,128)(2,1)S(1)}, u32[]{:S(2)}, u32[]{:S(2)}) collective-permute-start(bf16[256,1024]{1,0:T(8,128)(2,1)S(1)} %get-tuple-element.73), channel_id=1, source_target_pairs={{0,2},{1,3},{2,0},{3,1},{4,6},{5,7},{6,4},{7,5},{8,10},{9,11},{10,... | collective-permute-start | bytes 1572872 | tf_op jit(solution)/shard_map/ppermute | solution.py:75
  532.4 33.6 %collective-permute-start.53 = (bf16[512,1024]{1,0:T(8,128)(2,1)}, bf16[512,1024]{1,0:T(8,128)(2,1)}, u32[]{:S(2)}, u32[]{:S(2)}) collective-permute-start(bf16[512,1024]{1,0:T(8,128)(2,1)} %pad_maximum_fusion.12), channel_id=1, source_target_pairs={{0,4},{4,0},{8,12},{12,8},{16,20},{20,16},{24,28},{28,24},{1,5},{5... | collective-permute-start | bytes 3145736 | tf_op jit(solution)/shard_map/ppermute | solution.py:75
  536.7 48.3 %collective-permute-start.37 = (bf16[256,1024]{1,0:T(8,128)(2,1)}, bf16[256,1024]{1,0:T(8,128)(2,1)}, u32[]{:S(2)}, u32[]{:S(2)}) collective-permute-start(bf16[256,1024]{1,0:T(8,128)(2,1)} %slice.735), channel_id=1, source_target_pairs={{0,1},{1,0},{2,3},{3,2},{4,5},{5,4},{6,7},{7,6},{8,9},{9,8},{10,11... | collective-permute-start | bytes 1572872 | tf_op jit(solution)/shard_map/ppermute | solution.py:75
  557.4 25.9 %collective-permute-start.42 = (bf16[512,1024]{1,0:T(8,128)(2,1)}, bf16[512,1024]{1,0:T(8,128)(2,1)}, u32[]{:S(2)}, u32[]{:S(2)}) collective-permute-start(bf16[512,1024]{1,0:T(8,128)(2,1)} %dynamic-slice_convert_fusion.3), channel_id=1, source_target_pairs={{0,4},{4,0},{8,12},{12,8},{16,20},{20,16},{24,28},{28,24},{1,5},{5... | collective-permute-start | bytes 3145736 | tf_op jit(solution)/shard_map/ppermute | solution.py:75
  562.3 26.1 %collective-permute-start.54 = (bf16[512,1024]{1,0:T(8,128)(2,1)}, bf16[512,1024]{1,0:T(8,128)(2,1)}, u32[]{:S(2)}, u32[]{:S(2)}) collective-permute-start(bf16[512,1024]{1,0:T(8,128)(2,1)} %dynamic-slice_convert_fusion.1), channel_id=1, source_target_pairs={{0,8},{4,12},{8,0},{12,4},{16,24},{20,28},{24,16},{28,20},{1,9},{5... | collective-permute-start | bytes 3145736 | tf_op jit(solution)/shard_map/ppermute | solution.py:75
  564.5 20.5 %collective-permute-start.41 = (bf16[256,1024]{1,0:T(8,128)(2,1)S(1)}, bf16[256,1024]{1,0:T(8,128)(2,1)S(1)}, u32[]{:S(2)}, u32[]{:S(2)}) collective-permute-start(bf16[256,1024]{1,0:T(8,128)(2,1)S(1)} %fusion.48), channel_id=1, source_target_pairs={{0,2},{1,3},{2,0},{3,1},{4,6},{5,7},{6,4},{7,5},{8,10},{9,11},{10,... | collective-permute-start | bytes 1572872 | tf_op jit(solution)/shard_map/ppermute | solution.py:75
  584.9 34.7 %collective-permute-start.43 = (bf16[256,1024]{1,0:T(8,128)(2,1)S(1)}, bf16[256,1024]{1,0:T(8,128)(2,1)}, u32[]{:S(2)}, u32[]{:S(2)}) collective-permute-start(bf16[256,1024]{1,0:T(8,128)(2,1)S(1)} %dynamic-slice_convert_fusion.8), channel_id=1, source_target_pairs={{0,8},{4,12},{8,0},{12,4},{16,24},{20,28},{24,16},{28,20},{1,9},{5... | collective-permute-start | bytes 1572872 | tf_op jit(solution)/shard_map/ppermute | solution.py:75
  591.5 24.9 %collective-permute-start.55 = (bf16[256,1024]{1,0:T(8,128)(2,1)S(1)}, bf16[256,1024]{1,0:T(8,128)(2,1)}, u32[]{:S(2)}, u32[]{:S(2)}) collective-permute-start(bf16[256,1024]{1,0:T(8,128)(2,1)S(1)} %dynamic-slice_convert_fusion.6), channel_id=1, source_target_pairs={{0,4},{4,0},{8,12},{12,8},{16,20},{20,16},{24,28},{28,24},{1,5},{5... | collective-permute-start | bytes 1572872 | tf_op jit(solution)/shard_map/ppermute | solution.py:75
  617.9 21.4 %collective-permute-start.56 = (bf16[128,1024]{1,0:T(8,128)(2,1)S(1)}, bf16[128,1024]{1,0:T(8,128)(2,1)S(1)}, u32[]{:S(2)}, u32[]{:S(2)}) collective-permute-start(bf16[128,1024]{1,0:T(8,128)(2,1)S(1)} %dynamic-slice_convert_fusion.17), channel_id=1, source_target_pairs={{0,16},{4,20},{8,24},{12,28},{16,0},{20,4},{24,8},{28,12},{1,17},{... | collective-permute-start | bytes 786440 | tf_op jit(solution)/shard_map/ppermute | solution.py:75
  620.8 21.7 %collective-permute-start.44 = (bf16[128,1024]{1,0:T(8,128)(2,1)S(1)}, bf16[128,1024]{1,0:T(8,128)(2,1)S(1)}, u32[]{:S(2)}, u32[]{:S(2)}) collective-permute-start(bf16[128,1024]{1,0:T(8,128)(2,1)S(1)} %dynamic-slice_convert_fusion.19), channel_id=1, source_target_pairs={{0,16},{4,20},{8,24},{12,28},{16,0},{20,4},{24,8},{28,12},{1,17},{... | collective-permute-start | bytes 786440 | tf_op jit(solution)/shard_map/ppermute | solution.py:75
  642.7 27.2 %collective-permute-start.45 = (bf16[128,1024]{1,0:T(8,128)(2,1)S(1)}, bf16[128,1024]{1,0:T(8,128)(2,1)}, u32[]{:S(2)}, u32[]{:S(2)}) collective-permute-start(bf16[128,1024]{1,0:T(8,128)(2,1)S(1)} %add_convert_fusion.8), channel_id=1, source_target_pairs={{0,16},{4,20},{8,24},{12,28},{16,0},{20,4},{24,8},{28,12},{1,17},{... | collective-permute-start | bytes 786440 | tf_op jit(solution)/shard_map/ppermute | solution.py:75
  644.7 30.8 %collective-permute-start.69 = (bf16[4,128,256]{2,1,0:T(8,128)(2,1)S(1)}, bf16[4,128,256]{2,1,0:T(8,128)(2,1)}, u32[]{:S(2)}, u32[]{:S(2)}) collective-permute-start(bf16[4,128,256]{2,1,0:T(8,128)(2,1)S(1)} %pad_maximum_fusion.39), channel_id=1, source_target_pairs={{0,16},{4,20},{8,24},{12,28},{16,0},{20,4},{24,8},{28,12},{1,17},{... | collective-permute-start | bytes 786440 | tf_op jit(solution)/shard_map/ppermute | solution.py:75
  645.9 33.1 %collective-permute-start.60 = (bf16[4,128,256]{2,1,0:T(8,128)(2,1)S(1)}, bf16[4,128,256]{2,1,0:T(8,128)(2,1)}, u32[]{:S(2)}, u32[]{:S(2)}) collective-permute-start(bf16[4,128,256]{2,1,0:T(8,128)(2,1)S(1)} %pad_maximum_fusion.37), channel_id=1, source_target_pairs={{0,16},{4,20},{8,24},{12,28},{16,0},{20,4},{24,8},{28,12},{1,17},{... | collective-permute-start | bytes 786440 | tf_op jit(solution)/shard_map/ppermute | solution.py:75
  649.0 33.6 %collective-permute-start.96 = (bf16[512,256]{1,0:T(8,128)(2,1)S(1)}, bf16[512,256]{1,0:T(8,128)(2,1)S(1)}, u32[]{:S(2)}, u32[]{:S(2)}) collective-permute-start(bf16[512,256]{1,0:T(8,128)(2,1)S(1)} %dynamic-slice_convert_fusion.11), channel_id=1, source_target_pairs={{0,4},{4,0},{8,12},{12,8},{16,20},{20,16},{24,28},{28,24},{1,5},{5... | collective-permute-start | bytes 786440 | tf_op jit(solution)/shard_map/ppermute | solution.py:75
  651.7 31.1 %collective-permute-start.108 = (bf16[512,256]{1,0:T(8,128)(2,1)S(1)}, bf16[512,256]{1,0:T(8,128)(2,1)S(1)}, u32[]{:S(2)}, u32[]{:S(2)}) collective-permute-start(bf16[512,256]{1,0:T(8,128)(2,1)S(1)} %dynamic-slice_convert_fusion.9), channel_id=1, source_target_pairs={{0,4},{4,0},{8,12},{12,8},{16,20},{20,16},{24,28},{28,24},{1,5},{5... | collective-permute-start | bytes 786440 | tf_op jit(solution)/shard_map/ppermute | solution.py:75
  670.9 45.7 %collective-permute-start.46 = (bf16[256,1024]{1,0:T(8,128)(2,1)S(1)}, bf16[256,1024]{1,0:T(8,128)(2,1)S(1)}, u32[]{:S(2)}, u32[]{:S(2)}) collective-permute-start(bf16[256,1024]{1,0:T(8,128)(2,1)S(1)} %pad_maximum_fusion.29), channel_id=1, source_target_pairs={{0,8},{4,12},{8,0},{12,4},{16,24},{20,28},{24,16},{28,20},{1,9},{5... | collective-permute-start | bytes 1572872 | tf_op jit(solution)/shard_map/ppermute | solution.py:75
  676.6 42.1 %collective-permute-start.70 = (bf16[4,256,256]{2,1,0:T(8,128)(2,1)S(1)}, bf16[4,256,256]{2,1,0:T(8,128)(2,1)S(1)}, u32[]{:S(2)}, u32[]{:S(2)}) collective-permute-start(bf16[4,256,256]{2,1,0:T(8,128)(2,1)S(1)} %pad_maximum_fusion.32), channel_id=1, source_target_pairs={{0,4},{4,0},{8,12},{12,8},{16,20},{20,16},{24,28},{28,24},{1,5},{5... | collective-permute-start | bytes 1572872 | tf_op jit(solution)/shard_map/ppermute | solution.py:75
  680.0 40.3 %collective-permute-start.61 = (bf16[4,256,256]{2,1,0:T(8,128)(2,1)S(1)}, bf16[4,256,256]{2,1,0:T(8,128)(2,1)S(1)}, u32[]{:S(2)}, u32[]{:S(2)}) collective-permute-start(bf16[4,256,256]{2,1,0:T(8,128)(2,1)S(1)} %pad_maximum_fusion.31), channel_id=1, source_target_pairs={{0,4},{4,0},{8,12},{12,8},{16,20},{20,16},{24,28},{28,24},{1,5},{5... | collective-permute-start | bytes 1572872 | tf_op jit(solution)/shard_map/ppermute | solution.py:75
  682.9 12.7 %collective-permute-start.109 = (bf16[256,256]{1,0:T(8,128)(2,1)S(1)}, bf16[256,256]{1,0:T(8,128)(2,1)S(1)}, u32[]{:S(2)}, u32[]{:S(2)}) collective-permute-start(bf16[256,256]{1,0:T(8,128)(2,1)S(1)} %dynamic-slice_convert_fusion.20), channel_id=1, source_target_pairs={{0,8},{4,12},{8,0},{12,4},{16,24},{20,28},{24,16},{28,20},{1,9},{5... | collective-permute-start | bytes 393224 | tf_op jit(solution)/shard_map/ppermute | solution.py:75
  715.3 12.7 %collective-permute-start.113 = (bf16[512,256]{1,0:T(8,128)(2,1)S(1)}, bf16[512,256]{1,0:T(8,128)(2,1)S(1)}, u32[]{:S(2)}, u32[]{:S(2)}) collective-permute-start(bf16[512,256]{1,0:T(8,128)(2,1)S(1)} %pad_maximum_fusion.46), channel_id=1, source_target_pairs={{0,4},{4,0},{8,12},{12,8},{16,20},{20,16},{24,28},{28,24},{1,5},{5... | collective-permute-start | bytes 786440 | tf_op jit(solution)/shard_map/ppermute | solution.py:75
  717.9 28.4 %collective-permute-start.47 = (bf16[512,1024]{1,0:T(8,128)(2,1)}, bf16[512,1024]{1,0:T(8,128)(2,1)}, u32[]{:S(2)}, u32[]{:S(2)}) collective-permute-start(bf16[512,1024]{1,0:T(8,128)(2,1)} %pad_maximum_fusion.11), channel_id=1, source_target_pairs={{0,4},{4,0},{8,12},{12,8},{16,20},{20,16},{24,28},{28,24},{1,5},{5... | collective-permute-start | bytes 3145736 | tf_op jit(solution)/shard_map/ppermute | solution.py:75
  719.9 62.8 %collective-permute-start.71 = (bf16[4,512,256]{2,1,0:T(8,128)(2,1)}, bf16[4,512,256]{2,1,0:T(8,128)(2,1)}, u32[]{:S(2)}, u32[]{:S(2)}) collective-permute-start(bf16[4,512,256]{2,1,0:T(8,128)(2,1)} %pad_maximum_fusion.14), channel_id=1, source_target_pairs={{0,8},{4,12},{8,0},{12,4},{16,24},{20,28},{24,16},{28,20},{1,9},{5... | collective-permute-start | bytes 3145736 | tf_op jit(solution)/shard_map/ppermute | solution.py:75
  721.6 71.0 %collective-permute-start.62 = (bf16[4,512,256]{2,1,0:T(8,128)(2,1)}, bf16[4,512,256]{2,1,0:T(8,128)(2,1)}, u32[]{:S(2)}, u32[]{:S(2)}) collective-permute-start(bf16[4,512,256]{2,1,0:T(8,128)(2,1)} %pad_maximum_fusion.13), channel_id=1, source_target_pairs={{0,8},{4,12},{8,0},{12,4},{16,24},{20,28},{24,16},{28,20},{1,9},{5... | collective-permute-start | bytes 3145736 | tf_op jit(solution)/shard_map/ppermute | solution.py:75
  730.5 45.4 %collective-permute-start.102 = (bf16[512,512]{1,0:T(8,128)(2,1)S(1)}, bf16[512,512]{1,0:T(8,128)(2,1)S(1)}, u32[]{:S(2)}, u32[]{:S(2)}) collective-permute-start(bf16[512,512]{1,0:T(8,128)(2,1)S(1)} %dynamic-slice_convert_fusion.4), channel_id=1, source_target_pairs={{0,8},{4,12},{8,0},{12,4},{16,24},{20,28},{24,16},{28,20},{1,9},{5... | collective-permute-start | bytes 1572872 | tf_op jit(solution)/shard_map/ppermute | solution.py:75
  (256 other events, 1651.3 us)
Sparse Core Ops, SparseCore 0:
  9.6 36.7 all-gather.3
  47.9 57.0 all-gather.5
  106.6 28.7 all-gather.7
  307.6 31.7 reduce-scatter.3
  342.0 37.0 reduce-scatter.7
  381.4 44.4 reduce-scatter.5

commit v2 on v1

--- a/solution.py
+++ b/solution.py
@@ -107,39 +107,6 @@
         part = lax.dynamic_slice_in_dim(cols, (me ^ j) * rows, rows, 0)
         pieces.append(part if j == 0 else swap(part, "shard", j))
     return true_order(pieces, me, 1)
-
-
-def to_cols(rows_block, me):
-    n = lax.axis_size("shard")
-    cols = rows_block.shape[1] // n
-    pieces = []
-    for j in range(n):
-        part = lax.dynamic_slice_in_dim(rows_block, (me ^ j) * cols, cols, 1)
-        pieces.append(part if j == 0 else swap(part, "shard", j))
-    stacked = jnp.stack(pieces, 0)
-    return jnp.stack(
-        [lax.dynamic_index_in_dim(stacked, me ^ t, 0, keepdims=False) for t in range(n)], 0
-    )
-
-
-def halve_batch(total, order, place):
-    for bit in order:
-        half = total.shape[0] // 2
-        mine = (place >> bit) & 1
-        kept = lax.dynamic_slice_in_dim(total, mine * half, half, 0)
-        sent = b16(lax.dynamic_slice_in_dim(total, (1 - mine) * half, half, 0))
-        total = kept + f32(swap(sent, "batch", 1 << bit))
-    return b16(total)
-
-
-def double_batch(block, order, place, axis=0):
-    for bit in reversed(order):
-        other = swap(block, "batch", 1 << bit)
-        mine = ((place >> bit) & 1) == 0
-        block = jnp.concatenate(
-            [jnp.where(mine, block, other), jnp.where(mine, other, block)], axis
-        )
-    return block
 
 
 def peers_of(axis, index, count):
@@ -275,6 +242,273 @@
         compiler_params=pltpu.CompilerParams(collective_id=ident, has_side_effects=True),
         name="vector_sum",
     )(wide, local)
+
+
+class Chunk:
+    def __init__(self, at, source, row, rows, columns, first, count):
+        self.at, self.source, self.row, self.rows, self.columns = at, source, row, rows, columns
+        extra = [(1 << k, k) for k in range(3, count.bit_length() - 1)]
+        line = (6, 1)
+        if first == "near":
+            self.pre, self.post = [(1, 0)], [line] + extra
+        else:
+            self.pre, self.post = [], [line, (1, 0)] + extra
+        size, self.landings = rows, []
+        for _ in self.pre:
+            size //= 2
+            self.landings.append((size, columns))
+        self.landings.append((size, columns))
+        for _ in self.post:
+            size //= 2
+            self.landings.append((size, columns))
+        self.steps = len(self.landings)
+
+
+def bit_of(value, k):
+    return lax.rem(lax.div(value, 1 << k), 2)
+
+
+def flip_bits(value, mask):
+    out = value
+    k = 0
+    while (1 << k) <= mask:
+        if mask & (1 << k):
+            out = out + (1 - 2 * bit_of(value, k)) * (1 << k)
+        k += 1
+    return out
+
+
+class Mover:
+    def __init__(self, chunk, batch, source, total, landings, sems, finish):
+        self.c, self.b = chunk, batch
+        self.source, self.total, self.landings, self.sems = source, total, landings, sems
+        lo, hi = bit_of(batch, 1), bit_of(batch, 2)
+        self.inner = lo != hi
+        self.ended = lo == hi
+        self.finish = finish
+        self.stages = []
+        self.build()
+
+    def copy(self, at, src, dst, mask):
+        send, recv = self.sems
+        return pltpu.make_async_remote_copy(
+            src_ref=src,
+            dst_ref=dst,
+            send_sem=send.at[self.c.at, at],
+            recv_sem=recv.at[self.c.at, at],
+            device_id={"batch": flip_bits(self.b, mask)},
+            device_id_type=MESH,
+        )
+
+    def rows(self, ref, start, size):
+        start = start if isinstance(start, int) else pl.multiple_of(start, 16)
+        return ref.at[pl.ds(start, size)]
+
+    def build(self):
+        c = self.c
+        held = lambda off, size: self.rows(self.total, off, size)
+        here, base = self.source, c.row
+        off, size, step = 0, c.rows, 0
+        plan, trail = [], []
+        sequence = [("all",) + p for p in c.pre] + [("fold", 2, None)]
+        sequence += [("inner",) + p for p in c.post]
+        for kind, mask, sel in sequence:
+            landing = self.landings[step]
+            if kind == "fold":
+                own = self.rows(here, base, size)
+                cp = self.copy(step, own, landing, mask)
+            else:
+                size //= 2
+                mine = bit_of(self.b, sel)
+                cp = self.copy(step, self.rows(here, base + (1 - mine) * size, size), landing, mask)
+                own = self.rows(here, base + mine * size, size)
+                off = off + mine * size
+            trail.append((kind, mask, off, size))
+            step += 1
+            out = landing if step < len(sequence) else held(off, size)
+            plan.append((kind, cp, (own, landing, out)))
+            here, base = landing, 0
+        for kind, mask, off, size in reversed(trail):
+            cp = self.copy(step, held(off, size), held(off, size), mask)
+            plan.append(("unfold" if kind == "fold" else kind, cp, None))
+            step += 1
+        self.plan = plan
+
+    def begin(self, k):
+        kind, cp, _ = self.plan[k]
+        if kind == "all":
+            cp.start()
+        elif kind == "fold":
+            pl.when(self.ended)(cp.start)
+        else:
+            pl.when(self.inner)(cp.start)
+
+    def end(self, k):
+        kind, cp, add = self.plan[k]
+
+        def gather():
+            if add is not None:
+                own, landing, out = add
+                out[...] = b16(f32(own[...]) + f32(landing[...]))
+
+        if kind == "all":
+            cp.wait()
+            gather()
+        elif kind in ("fold", "unfold"):
+            sender, taker = (
+                (self.ended, self.inner) if kind == "fold" else (self.inner, self.ended)
+            )
+            pl.when(sender)(cp.wait_send)
+
+            @pl.when(taker)
+            def _():
+                cp.wait_recv()
+                gather()
+        else:
+
+            @pl.when(self.inner)
+            def _():
+                cp.wait()
+                gather()
+
+    def advance(self, k):
+        if k > 0:
+            self.end(k - 1)
+        if k < len(self.plan):
+            self.begin(k)
+        else:
+            self.finish(self.c)
+
+
+def tail_body(specs, chunks, ns, n_in, n_out, *refs):
+    ins, outs = refs[:n_in], refs[n_in : n_in + n_out]
+    scratch = list(refs[n_in + n_out :])
+    send, recv, turn_send, turn_recv, out_sem = scratch[:5]
+    stage, turned = scratch[5], scratch[6]
+    rest = scratch[7:]
+    shard, batch = lax.axis_index("shard"), lax.axis_index("batch")
+    barrier = pltpu.get_barrier_semaphore()
+    greeted = [{"batch": flip_bits(batch, m)} for m in specs["masks"]]
+    greeted += [{"shard": flip_bits(shard, m)} for m in range(1, ns)]
+    for device in greeted:
+        pl.semaphore_signal(barrier, inc=1, device_id=device, device_id_type=MESH)
+    pl.semaphore_wait(barrier, len(greeted))
+    pending = {}
+    used = [0]
+
+    def put(value, target):
+        slot = used[0] % 2
+        used[0] += 1
+        if slot in pending:
+            pending.pop(slot).wait()
+        rows, columns = value.shape
+        place = stage.at[slot, pl.ds(0, rows), pl.ds(0, columns)]
+        place[...] = f32(value)
+        copy = pltpu.make_async_copy(place, target, out_sem.at[slot])
+        copy.start()
+        pending[slot] = copy
+
+    late = []
+
+    def finish(total):
+        def go(c):
+            kind, out, lead = specs["arrays"][c.source]
+            if kind == "plain":
+                target = outs[out] if lead is None else outs[out].at[lead]
+                half = c.rows // specs["parts"]
+                for p in range(specs["parts"]):
+                    put(total[p * half : (p + 1) * half], target.at[pl.ds(c.row + p * half, half)])
+                return
+            columns = c.columns // ns
+            copies = []
+            for j in range(1, ns):
+                peer = flip_bits(shard, j)
+                copies.append(
+                    pltpu.make_async_remote_copy(
+                        src_ref=total.at[:, pl.ds(pl.multiple_of(peer * columns, 128), columns)],
+                        dst_ref=turned.at[lead, shard, pl.ds(c.row, c.rows)],
+                        send_sem=turn_send.at[c.at, j],
+                        recv_sem=turn_recv.at[c.at, j],
+                        device_id={"shard": peer},
+                        device_id_type=MESH,
+                    )
+                )
+                copies[-1].start()
+            turned[lead, shard, c.row : c.row + c.rows] = total[
+                :, pl.ds(pl.multiple_of(shard * columns, 128), columns)
+            ]
+
+            def after():
+                for copy in copies:
+                    copy.wait()
+                height = specs["height"]
+                for t in range(ns):
+                    put(
+                        turned[lead, t, c.row : c.row + c.rows],
+                        outs[out].at[lead, pl.ds(t * height + c.row, c.rows)],
+                    )
+
+            late.append(after)
+
+        return go
+
+    movers, k = [], 0
+    for c in chunks:
+        total = rest[k]
+        landings = rest[k + 1 : k + 1 + c.steps]
+        k += 1 + c.steps
+        movers.append(Mover(c, batch, ins[c.source], total, landings, (send, recv), finish(total)))
+    lag = specs["lag"]
+    depth = max(len(m.plan) for m in movers) + 1
+    rounds = depth + (len(movers) - 1) // lag
+    for r in range(rounds):
+        waiting = late[:]
+        late.clear()
+        for i, m in enumerate(movers):
+            k = r - i // lag
+            if 0 <= k <= len(m.plan):
+                m.advance(k)
+        for after in waiting:
+            after()
+    for after in late:
+        after()
+    for slot in sorted(pending):
+        pending[slot].wait()
+
+
+def tail_sum(arrays, kinds, outputs, firsts, chunk_rows, ident):
+    ns, nb = lax.axis_size("shard"), lax.axis_size("batch")
+    chunks = []
+    for i, a in enumerate(arrays):
+        step = chunk_rows[i]
+        for row in range(0, a.shape[0], step):
+            chunks.append(Chunk(len(chunks), i, row, step, a.shape[1], firsts[len(chunks) % len(firsts)], nb))
+    masks = [1, 2, 6] + [1 << k for k in range(3, nb.bit_length() - 1)]
+    depth = max(2 * c.steps for c in chunks)
+    specs = dict(arrays=kinds, masks=masks, parts=2, height=arrays[0].shape[0], lag=2)
+    scratch = [
+        pltpu.SemaphoreType.DMA((len(chunks), depth)),
+        pltpu.SemaphoreType.DMA((len(chunks), depth)),
+        pltpu.SemaphoreType.DMA((len(chunks), ns)),
+        pltpu.SemaphoreType.DMA((len(chunks), ns)),
+        pltpu.SemaphoreType.DMA((2,)),
+        pltpu.VMEM((2, 512, 1024), jnp.float32),
+        pltpu.VMEM((2, ns, arrays[0].shape[0], arrays[0].shape[1] // ns), jnp.bfloat16),
+    ]
+    for c in chunks:
+        scratch.append(pltpu.VMEM((c.rows, c.columns), jnp.bfloat16))
+        scratch += [pltpu.VMEM(shape, jnp.bfloat16) for shape in c.landings]
+    return pl.pallas_call(
+        functools.partial(tail_body, specs, chunks, ns, len(arrays), len(outputs)),
+        out_shape=[jax.ShapeDtypeStruct(s, jnp.float32) for s in outputs],
+        in_specs=[pl.BlockSpec(memory_space=pltpu.VMEM)] * len(arrays),
+        out_specs=[pl.BlockSpec(memory_space=pl.ANY)] * len(outputs),
+        scratch_shapes=scratch,
+        compiler_params=pltpu.CompilerParams(
+            collective_id=ident, has_side_effects=True, vmem_limit_bytes=60 << 20
+        ),
+        name="tail_sum",
+    )(*arrays)
 
 
 def attend_body(heads, size, scale, len_ref, u_ref, v_ref, k_ref, x_ref, p_ref, mix_ref, soft_ref):
@@ -432,9 +666,6 @@
     shard, batch = lax.axis_index("shard"), lax.axis_index("batch")
     ns, nb = lax.axis_size("shard"), lax.axis_size("batch")
     width = features // ns
-    bits = nb.bit_length() - 1
-    order_a = list(range(bits))
-    order_b = [1, 0] + list(range(2, bits)) if bits > 1 else order_a
     heads = HEADS // ns
     rows_in = tokens[0]
     grads_in = cotangent[0]
@@ -516,17 +747,6 @@
     )
     stream = stream + two[0]
 
-    def reduced(total, order):
-        return double_batch(halve_batch(total, order, batch), order, batch)
-
-    def reduced_rows(total, order):
-        block = to_cols(halve_batch(total, order, batch), shard)
-        block = double_batch(block, order, batch, axis=1)
-        return block.reshape(-1, width)
-
-    ffn_in_two = reduced(two[3], order_a)
-    ffn_out_two = reduced_rows(two[4], order_b)
-
     grad_out = b16(stream)
     grad_conv_out = dot_over(active_conv, grad_out)
     grad_pw_out = row_total(grad_out)
@@ -559,10 +779,10 @@
     stream = stream + grad_rows
 
     def scattered(total):
-        return f32(lax.psum_scatter(b16(total), "shard", scatter_dimension=1, tiled=True))
-
-    conv_out_red = reduced(scattered(grad_conv_out), order_a)
-    conv_in_red = reduced(scattered(grad_conv_in), order_b)
+        return lax.psum_scatter(b16(total), "shard", scatter_dimension=1, tiled=True)
+
+    conv_out_part = scattered(grad_conv_out)
+    conv_in_part = scattered(grad_conv_in)
 
     grad_out = b16(stream)
     grad_w_out = dot_over(mixed_own, grad_out)
@@ -595,18 +815,28 @@
     norm_back = jax.vjp(norm_rows, rows_one, gain_rows[1], bias_rows[2])[1]
     grad_rows, grad_gain_mix, grad_bias_mix = norm_back(scatter_slots(*sums))
     stream = stream + grad_rows
-    pos_red = reduced(grad_w_pos, order_a)
-    q_red = reduced(grad_qkv[0], order_b)
-    k_red = reduced(grad_qkv[1], order_a)
-    x_red = reduced(grad_qkv[2], order_b)
-    out_red = reduced(scattered(grad_w_out), order_a)
+    out_part = scattered(grad_w_out)
 
     one = ffn_back(
         b16(0.5 * stream), rows_in, saved_one, w_in[0], w_rows[0], gain_rows[0], bias_rows[0]
     )
     stream = stream + one[0]
-    ffn_in_one = reduced(one[3], order_a)
-    ffn_out_one = reduced_rows(one[4], order_b)
+    tall, deep = one[3].shape[0], one[3].shape[1]
+    sums = tail_sum(
+        [b16(two[4]), b16(two[3]), conv_in_part, conv_out_part]
+        + [b16(g) for g in grad_qkv]
+        + [b16(grad_w_pos), out_part, b16(one[4]), b16(one[3])],
+        [("turn", 1, 1), ("plain", 0, 1), ("plain", 5, None), ("plain", 6, None)]
+        + [("plain", 2, at) for at in range(3)]
+        + [("plain", 3, None), ("plain", 4, None), ("turn", 1, 0), ("plain", 0, 0)],
+        [
+            (2, tall, deep), (2, ns * deep, width), (3, tall, width), (tall, width), (tall, width),
+            conv_in_part.shape, conv_out_part.shape,
+        ],
+        ["near", "line"],
+        [512, 512, tall, tall, tall, tall, tall, tall, tall, 512, 512],
+        4,
+    )
 
     wide = jnp.stack(
         [
@@ -638,14 +868,14 @@
     return (
         result[None],
         stream[None],
-        f32(jnp.stack([ffn_in_one, ffn_in_two])),
-        f32(jnp.stack([ffn_out_one, ffn_out_two])),
+        sums[0],
+        sums[1],
         out_hidden,
-        f32(jnp.stack([q_red, k_red, x_red])),
-        f32(pos_red),
-        f32(out_red),
-        f32(conv_in_red),
-        f32(conv_out_red),
+        sums[2],
+        sums[3],
+        sums[4],
+        sums[5],
+        sums[6],
         out_kernel,
         out_gains,
         out_biases,

time: 835 us -> 828 us (level)
  Pallas kernels: 53.4 us -> 366 us
  waiting for transfers between devices: 388 us -> 178 us
  starting transfers between devices: 105 us -> 41 us
  other arithmetic: 105 us -> 47.3 us
    pallas_call x0 -> x1, Pallas kernels: none -> 313 us  [tail_sum(): pl.pallas_call(functools.partial(tail_body, specs, chunks, ns, len(arrays...]
    ppermute x114 -> x42, waiting for transfers between devices: 386 us -> 176 us  [swap(): return lax.ppermute(x, axis, [(i, i ^ mask) for i in range(n)])]
    ppermute x114 -> x42, starting transfers between devices: 104 us -> 40.4 us  [swap(): return lax.ppermute(x, axis, [(i, i ^ mask) for i in range(n)])]
    convert_element_type x12 -> x2, other arithmetic: 18.9 us -> 0.58 us  [f32(): return a.astype(jnp.float32)]
    select_n x33 -> x0, other arithmetic: 14 us -> none  [double_batch(): jnp.where(mine, block, other)]
    add x22 -> x0, other arithmetic: 13.1 us -> none  [halve_batch(): total = kept + f32(swap(sent, 'batch', 1 << bit))]
    unnamed x403 -> x382, local copies, waits for them, and re-layouts: 32 us -> 42.4 us
  transfers between devices with their start and end apart: 120 -> 48, of which waited for: 63 -> 17; matrix products, arithmetic and copies ran while one was open for 23% -> 19% of each run, Pallas kernels for 5% -> 7%
where the time goes in v2:
time: 828 us; the launch traced here: 817 us
  Pallas kernels  366 us (44%)
  waiting for transfers between devices  178 us (21%)
  matrix products  92.3 us (11%)
  local copies, waits for them, and re-layouts  68.5 us (8%)
  other arithmetic  47.3 us (6%)
  starting transfers between devices  41 us (5%)
  between operations  17.8 us (2%)
    pallas_call x1, Pallas kernels, tail_sum(): pl.pallas_call(functools.partial(tail_body, specs, chunks, ns, len(arrays...  313 us
    ppermute x42, waiting for transfers between devices, swap(): return lax.ppermute(x, axis, [(i, i ^ mask) for i in range(n)])  176 us
    unnamed x382, local copies, waits for them, and re-layouts  42.4 us
    dot_general x21, matrix products, dot_over(): lax.dot_general(a, b, (((0,), (0,)), ((), ())), preferred_element_type=jn...  41.6 us
    ppermute x42, starting transfers between devices, swap(): return lax.ppermute(x, axis, [(i, i ^ mask) for i in range(n)])  40.4 us
    dot_general x17, matrix products, dot_back(): lax.dot_general(a, b, (((1,), (1,)), ((), ())), preferred_element_type=jn...  27 us
    dot_general x18, matrix products, dot_rows(): return jnp.dot(a, b, preferred_element_type=jnp.float32)  23.7 us
    pallas_call x2, Pallas kernels, stats_sum(): pl.pallas_call(functools.partial(stats_body, ns, nb), out_shape=jax.Shape...  23.2 us
  transfers between devices with their start and end apart: 48, of which 17 were waited for; matrix products, arithmetic and copies ran while one was open for 19% of the time, Pallas kernels for 7%

profile of v2, /device:TPU:0, one launch (start us, length us, event | category | flops | bytes accessed | tf_op | source)
XLA Modules:
  0.0 817.0 jit_solution(7889548805355688423)
XLA Ops:
  9.7 6.2 all_gather.12
  17.7 2.1 collective-permute-start.5
  19.8 4.0 fusion.171
  27.7 2.9 constant_dynamic-slice_fusion.4
  32.4 10.3 %collective-permute-done.5 = bf16[256,1024]{1,0:T(8,128)(2,1)S(1)} collective-permute-done((bf16[256,1024]{1,0:T(8,128)(2,1)S(1)}, bf16[256,1024]{1,0:T(8,128)(2,1)S(1)}, u32[]{:S(2)}, u32[]{:S(2)}) %collective-permute-start.5) | collective-permute-done | bytes 524320 | tf_op jit(solution)/shard_map/ppermute | solution.py:75
  42.7 1.9 collective-permute-start.18
  44.7 9.8 %collective-permute-done.3 = bf16[1024,256]{1,0:T(8,128)(2,1)} collective-permute-done((bf16[1024,256]{1,0:T(8,128)(2,1)}, bf16[1024,256]{1,0:T(8,128)(2,1)}, u32[]{:S(2)}, u32[]{:S(2)}) %collective-permute-start.3) | collective-permute-done | bytes 524320 | tf_op jit(solution)/shard_map/ppermute | solution.py:75
  54.4 1.8 collective-permute-start.17
  56.2 17.7 %collective-permute-done.2 = bf16[1024,256]{1,0:T(8,128)(2,1)} collective-permute-done((bf16[1024,256]{1,0:T(8,128)(2,1)}, bf16[1024,256]{1,0:T(8,128)(2,1)}, u32[]{:S(2)}, u32[]{:S(2)}) %collective-permute-start.2) | collective-permute-done | bytes 524320 | tf_op jit(solution)/shard_map/ppermute | solution.py:75
  75.8 2.7 copy-done.162
  78.6 2.3 fusion.28
  86.0 2.5 collective-permute-start.8
  90.5 37.4 %collective-permute-done.8 = bf16[256,1024]{1,0:T(8,128)(2,1)S(1)} collective-permute-done((bf16[256,1024]{1,0:T(8,128)(2,1)S(1)}, bf16[256,1024]{1,0:T(8,128)(2,1)S(1)}, u32[]{:S(2)}, u32[]{:S(2)}) %collective-permute-start.8) | collective-permute-done | bytes 524320 | tf_op jit(solution)/shard_map/ppermute | solution.py:75
  129.0 2.5 collective-permute-start.11
  132.9 4.1 fusion.46
  137.9 6.6 collective-permute-done.11
  147.9 2.8 attend.3
  153.5 3.1 attend.2
  160.9 2.7 fusion.182
  165.4 3.8 convolution_add_fusion
  174.3 12.4 %stats_sum_1.1 = f32[24,128]{1,0:T(8,128)} custom-call(f32[24,128]{1,0:T(8,128)} %maximum_maximum_fusion.1.x_ref), custom_call_target="tpu_custom_call" | custom-call | tf_op jit(solution)/shard_map/stats_sum_1/pallas_call | solution.py:172
  187.9 1.9 fusion.118
  189.8 1.9 divide_bitcast_fusion
  191.7 2.8 fusion.183
  197.6 10.9 %collective-permute-done.20 = bf16[256,1024]{1,0:T(8,128)(2,1)S(1)} collective-permute-done((bf16[256,1024]{1,0:T(8,128)(2,1)S(1)}, bf16[256,1024]{1,0:T(8,128)(2,1)S(1)}, u32[]{:S(2)}, u32[]{:S(2)}) %collective-permute-start.20) | collective-permute-done | bytes 524320 | tf_op jit(solution)/shard_map/ppermute | solution.py:75
  216.8 12.7 %collective-permute-done.23 = bf16[256,1024]{1,0:T(8,128)(2,1)S(1)} collective-permute-done((bf16[256,1024]{1,0:T(8,128)(2,1)S(1)}, bf16[256,1024]{1,0:T(8,128)(2,1)S(1)}, u32[]{:S(2)}, u32[]{:S(2)}) %collective-permute-start.23) | collective-permute-done | bytes 524320 | tf_op jit(solution)/shard_map/ppermute | solution.py:75
  234.8 12.5 %collective-permute-done.26 = bf16[256,1024]{1,0:T(8,128)(2,1)S(1)} collective-permute-done((bf16[256,1024]{1,0:T(8,128)(2,1)S(1)}, bf16[256,1024]{1,0:T(8,128)(2,1)S(1)}, u32[]{:S(2)}, u32[]{:S(2)}) %collective-permute-start.26) | collective-permute-done | bytes 524320 | tf_op jit(solution)/shard_map/ppermute | solution.py:75
  247.2 10.4 %collective-permute-start.24 = (bf16[256,1024]{1,0:T(8,128)(2,1)S(1)}, bf16[256,1024]{1,0:T(8,128)(2,1)S(1)}, u32[]{:S(2)}, u32[]{:S(2)}) collective-permute-start(bf16[256,1024]{1,0:T(8,128)(2,1)S(1)} %get-tuple-element.81), channel_id=1, source_target_pairs={{0,1},{1,0},{2,3},{3,2},{4,5},{5,4},{6,7},{7,6},{8,9},{9,8},{10,11... | collective-permute-start | bytes 1572872 | tf_op jit(solution)/shard_map/ppermute | solution.py:75
  257.7 2.7 convert_reduce_fusion
  261.9 2.4 convert_reduce_fusion.1
  267.7 12.5 %collective-permute-done.29 = bf16[256,1024]{1,0:T(8,128)(2,1)S(1)} collective-permute-done((bf16[256,1024]{1,0:T(8,128)(2,1)S(1)}, bf16[256,1024]{1,0:T(8,128)(2,1)S(1)}, u32[]{:S(2)}, u32[]{:S(2)}) %collective-permute-start.29) | collective-permute-done | bytes 524320 | tf_op jit(solution)/shard_map/ppermute | solution.py:75
  283.7 2.3 convolution_convert_fusion.2
  286.1 4.3 fusion.156
  291.1 10.8 %stats_sum_2.1 = f32[16,128]{1,0:T(8,128)} custom-call(f32[16,128]{1,0:T(8,128)} %pad_maximum_fusion.28.x_ref), custom_call_target="tpu_custom_call" | custom-call | tf_op jit(solution)/shard_map/stats_sum_2/pallas_call | solution.py:172
  303.2 5.6 multiply_reduce_fusion.4
  312.9 2.1 multiply_reduce_fusion.7
  318.1 2.0 convolution_convert_fusion.1
  320.7 3.0 fusion.77
  325.7 2.8 add_convert_fusion.2.refs_1_
  328.5 2.8 add_convert_fusion.3.refs_0_
  335.6 3.5 convolution_convert_fusion
  340.7 2.4 collective-permute-done.32
  345.3 4.4 attend_back.3
  353.5 4.6 attend_back.2
  369.5 2.0 collective-permute-start.35
  373.3 17.2 %collective-permute-done.35 = bf16[256,1024]{1,0:T(8,128)(2,1)S(1)} collective-permute-done((bf16[256,1024]{1,0:T(8,128)(2,1)S(1)}, bf16[256,1024]{1,0:T(8,128)(2,1)S(1)}, u32[]{:S(2)}, u32[]{:S(2)}) %collective-permute-start.35) | collective-permute-done | bytes 524320 | tf_op jit(solution)/shard_map/ppermute | solution.py:75
  394.0 2.7 fusion.43.refs_7_
  396.7 2.5 collective-permute-start.38
  399.2 1.7 convert_reduce_fusion.3
  402.7 15.1 %collective-permute-done.38 = bf16[256,1024]{1,0:T(8,128)(2,1)S(1)} collective-permute-done((bf16[256,1024]{1,0:T(8,128)(2,1)S(1)}, bf16[256,1024]{1,0:T(8,128)(2,1)S(1)}, u32[]{:S(2)}, u32[]{:S(2)}) %collective-permute-start.38) | collective-permute-done | bytes 524320 | tf_op jit(solution)/shard_map/ppermute | solution.py:75
  417.9 4.7 fusion.78
  422.5 3.3 fusion.73
  426.0 2.1 convert_reduce_fusion.2
  428.1 3.0 fusion.22
  431.9 2.7 add_convert_fusion.1.refs_9_
  434.8 1.8 collective-permute-start.41
  437.2 2.7 add_convert_fusion.refs_10_
  440.1 9.1 %collective-permute-done.41 = bf16[256,1024]{1,0:T(8,128)(2,1)S(1)} collective-permute-done((bf16[256,1024]{1,0:T(8,128)(2,1)S(1)}, bf16[256,1024]{1,0:T(8,128)(2,1)S(1)}, u32[]{:S(2)}, u32[]{:S(2)}) %collective-permute-start.41) | collective-permute-done | bytes 524320 | tf_op jit(solution)/shard_map/ppermute | solution.py:75
  449.8 2.0 stack.150
  451.8 15.0 %vector_sum.1 = f32[40,256]{1,0:T(8,128)} custom-call(f32[4,24,256]{2,1,0:T(8,128)} %bitcast.262, f32[16,256]{1,0:T(8,128)} %select_maximum_fusion.l_ref), custom_call_target="tpu_custom_call" | custom-call | tf_op jit(solution)/shard_map/vector_sum/pallas_call | solution.py:228
  474.6 2.4 add_bitcast_fusion
  477.0 312.9 %tail_sum.1 = (f32[2,1024,1024]{2,1,0:T(8,128)}, f32[2,4096,256]{2,1,0:T(8,128)}, f32[3,1024,256]{2,1,0:T(8,128)}, f32[1024,256]{1,0:T(8,128)}, f32[1024,256]{1,...) custom-call(bf16[1024,1024]{1,0:T(8,128)(2,1)} %add_convert_fusion.3.refs_0_, ...), custom_call_target="tpu_custom_call" | custom-call | tf_op jit(solution)/shard_map/tail_sum/pallas_call | solution.py:501
  789.9 8.6 %copy.40 = f32[2,1024,1024]{2,1,0:T(8,128)} copy(f32[2,1024,1024]{2,1,0:T(8,128)} %get-tuple-element.233) | data formatting | bytes 16777216
  798.5 3.9 copy.41
  (626 shorter events, 122.9 us)
Async XLA Ops:
  7.2 129.8 %copy-start = (bf16[1024,256]{1,0:T(8,128)(2,1)S(1)}, bf16[1024,256]{1,0:T(8,128)(2,1)}, u32[]{:S(2)}) copy-start(bf16[1024,256]{1,0:T(8,128)(2,1)} %param.21) | copy-start | bytes 1572868
  7.2 153.7 %all-gather.4.cloned.1.call-start = ((), (), s32[]{:S(2)}) async-start(), calls=%async_computation.3 | async-start | bytes 2621440 | tf_op jit(solution)/shard_map/all_gather | solution.py:694
  8.0 156.9 %all-gather.6.cloned.1.call-start = ((), (), s32[]{:S(2)}) async-start(), calls=%async_computation.4 | async-start | bytes 5242880 | tf_op jit(solution)/shard_map/all_gather | solution.py:695
  8.7 183.0 %all-gather.8.cloned.1.call-start = ((), (), s32[]{:S(2)}) async-start(), calls=%async_computation.5 | async-start | bytes 2621440 | tf_op jit(solution)/shard_map/all_gather | solution.py:696
  17.7 58.1 %copy-start.50 = (bf16[256,1024]{1,0:T(8,128)(2,1)}, bf16[256,1024]{1,0:T(8,128)(2,1)S(1)}, u32[]{:S(2)}) copy-start(bf16[256,1024]{1,0:T(8,128)(2,1)S(1)} %add_convert_fusion.8) | copy-start | bytes 1572868
  17.7 25.1 %collective-permute-start.5 = (bf16[256,1024]{1,0:T(8,128)(2,1)S(1)}, bf16[256,1024]{1,0:T(8,128)(2,1)S(1)}, u32[]{:S(2)}, u32[]{:S(2)}) collective-permute-start(bf16[256,1024]{1,0:T(8,128)(2,1)S(1)} %add_convert_fusion.8), channel_id=1, source_target_pairs={{0,2},{1,3},{2,0},{3,1},{4,6},{5,7},{6,4},{7,5},{8,10},{9,11},{10,... | collective-permute-start | bytes 1572872 | tf_op jit(solution)/shard_map/ppermute | solution.py:75
  19.7 56.1 %collective-permute-start = (bf16[256,1024]{1,0:T(8,128)(2,1)S(1)}, bf16[256,1024]{1,0:T(8,128)(2,1)}, u32[]{:S(2)}, u32[]{:S(2)}) collective-permute-start(bf16[256,1024]{1,0:T(8,128)(2,1)S(1)} %add_convert_fusion.8), channel_id=1, source_target_pairs={{0,1},{1,0},{2,3},{3,2},{4,5},{5,4},{6,7},{7,6},{8,9},{9,8},{10,11... | collective-permute-start | bytes 1572872 | tf_op jit(solution)/shard_map/ppermute | solution.py:75
  25.0 29.5 %collective-permute-start.3 = (bf16[1024,256]{1,0:T(8,128)(2,1)}, bf16[1024,256]{1,0:T(8,128)(2,1)}, u32[]{:S(2)}, u32[]{:S(2)}) collective-permute-start(bf16[1024,256]{1,0:T(8,128)(2,1)} %get-tuple-element.124), channel_id=1, source_target_pairs={{0,3},{1,2},{2,1},{3,0},{4,7},{5,6},{6,5},{7,4},{8,11},{9,10},{10,... | collective-permute-start | bytes 1572872 | tf_op jit(solution)/shard_map/ppermute | solution.py:75
  25.3 48.6 %collective-permute-start.2 = (bf16[1024,256]{1,0:T(8,128)(2,1)}, bf16[1024,256]{1,0:T(8,128)(2,1)}, u32[]{:S(2)}, u32[]{:S(2)}) collective-permute-start(bf16[1024,256]{1,0:T(8,128)(2,1)} %get-tuple-element.125), channel_id=1, source_target_pairs={{0,2},{1,3},{2,0},{3,1},{4,6},{5,7},{6,4},{7,5},{8,10},{9,11},{10,... | collective-permute-start | bytes 1572872 | tf_op jit(solution)/shard_map/ppermute | solution.py:75
  27.0 46.9 %collective-permute-start.1 = (bf16[1024,256]{1,0:T(8,128)(2,1)}, bf16[1024,256]{1,0:T(8,128)(2,1)}, u32[]{:S(2)}, u32[]{:S(2)}) collective-permute-start(bf16[1024,256]{1,0:T(8,128)(2,1)} %get-tuple-element.126), channel_id=1, source_target_pairs={{0,1},{1,0},{2,3},{3,2},{4,5},{5,4},{6,7},{7,6},{8,9},{9,8},{10,11... | collective-permute-start | bytes 1572872 | tf_op jit(solution)/shard_map/ppermute | solution.py:75
  27.0 449.9 %reduce-scatter.6.cloned.1.call-start = ((), (), s32[]{:S(2)}) async-start(), calls=%async_computation.7 | async-start | bytes 2621440 | tf_op jit(solution)/shard_map/reduce_scatter | solution.py:782
  31.2 53.1 %copy-start.155 = (f32[1,1024]{1,0:T(1,128)}, f32[1,1024]{1,0:T(1,128)S(1)}, u32[]{:S(2)}) copy-start(f32[1,1024]{1,0:T(1,128)S(1)} %get-tuple-element.189) | copy-start | bytes 12292
  42.7 153.2 %collective-permute-start.18 = (bf16[1024,256]{1,0:T(8,128)(2,1)}, bf16[1024,256]{1,0:T(8,128)(2,1)}, u32[]{:S(2)}, u32[]{:S(2)}) collective-permute-start(bf16[1024,256]{1,0:T(8,128)(2,1)} %get-tuple-element.116), channel_id=1, source_target_pairs={{0,3},{1,2},{2,1},{3,0},{4,7},{5,6},{6,5},{7,4},{8,11},{9,10},{10,... | collective-permute-start | bytes 1572872 | tf_op jit(solution)/shard_map/ppermute | solution.py:75
  54.4 141.5 %collective-permute-start.17 = (bf16[1024,256]{1,0:T(8,128)(2,1)}, bf16[1024,256]{1,0:T(8,128)(2,1)}, u32[]{:S(2)}, u32[]{:S(2)}) collective-permute-start(bf16[1024,256]{1,0:T(8,128)(2,1)} %get-tuple-element.117), channel_id=1, source_target_pairs={{0,2},{1,3},{2,0},{3,1},{4,6},{5,7},{6,4},{7,5},{8,10},{9,11},{10,... | collective-permute-start | bytes 1572872 | tf_op jit(solution)/shard_map/ppermute | solution.py:75
  73.9 7.0 collective-permute-start.6
  83.7 2.1 collective-permute-start.7
  85.6 42.3 %copy-start.139 = (f32[1,1024]{1,0:T(1,128)S(1)}, f32[1,1024]{1,0:T(1,128)}, u32[]{:S(2)}) copy-start(f32[1,1024]{1,0:T(1,128)} %get-tuple-element.171) | copy-start | bytes 12292
  85.7 4.8 collective-permute-start.4
  86.0 42.0 %collective-permute-start.8 = (bf16[256,1024]{1,0:T(8,128)(2,1)S(1)}, bf16[256,1024]{1,0:T(8,128)(2,1)S(1)}, u32[]{:S(2)}, u32[]{:S(2)}) collective-permute-start(bf16[256,1024]{1,0:T(8,128)(2,1)S(1)} %fusion.67), channel_id=1, source_target_pairs={{0,2},{1,3},{2,0},{3,1},{4,6},{5,7},{6,4},{7,5},{8,10},{9,11},{10,... | collective-permute-start | bytes 1572872 | tf_op jit(solution)/shard_map/ppermute | solution.py:75
  90.5 38.2 %copy-start.79 = (f32[1,1024]{1,0:T(1,128)}, f32[1,1024]{1,0:T(1,128)S(1)}, u32[]{:S(2)}) copy-start(f32[1,1024]{1,0:T(1,128)S(1)} %get-tuple-element.168) | copy-start | bytes 12292
  128.4 32.5 %copy-start.10 = (f32[256,1024]{1,0:T(8,128)}, f32[256,1024]{1,0:T(8,128)S(1)}, u32[]{:S(2)}) copy-start(f32[256,1024]{1,0:T(8,128)S(1)} %get-tuple-element.108) | copy-start | bytes 3145732
  129.0 15.5 %collective-permute-start.11 = (bf16[256,1024]{1,0:T(8,128)(2,1)S(1)}, bf16[256,1024]{1,0:T(8,128)(2,1)S(1)}, u32[]{:S(2)}, u32[]{:S(2)}) collective-permute-start(bf16[256,1024]{1,0:T(8,128)(2,1)S(1)} %add_convert_fusion.7), channel_id=1, source_target_pairs={{0,2},{1,3},{2,0},{3,1},{4,6},{5,7},{6,4},{7,5},{8,10},{9,11},{10,... | collective-permute-start | bytes 1572872 | tf_op jit(solution)/shard_map/ppermute | solution.py:75
  131.5 13.0 %collective-permute-start.9 = (bf16[256,1024]{1,0:T(8,128)(2,1)S(1)}, bf16[256,1024]{1,0:T(8,128)(2,1)S(1)}, u32[]{:S(2)}, u32[]{:S(2)}) collective-permute-start(bf16[256,1024]{1,0:T(8,128)(2,1)S(1)} %add_convert_fusion.7), channel_id=1, source_target_pairs={{0,1},{1,0},{2,3},{3,2},{4,5},{5,4},{6,7},{7,6},{8,9},{9,8},{10,11... | collective-permute-start | bytes 1572872 | tf_op jit(solution)/shard_map/ppermute | solution.py:75
  144.5 1.9 collective-permute-start.12
  151.8 8.2 collective-permute-start.13
  153.4 6.5 collective-permute-start.14
  157.6 2.4 collective-permute-start.10
  160.0 36.0 %collective-permute-start.16 = (bf16[1024,256]{1,0:T(8,128)(2,1)}, bf16[1024,256]{1,0:T(8,128)(2,1)}, u32[]{:S(2)}, u32[]{:S(2)}) collective-permute-start(bf16[1024,256]{1,0:T(8,128)(2,1)} %get-tuple-element.118), channel_id=1, source_target_pairs={{0,1},{1,0},{2,3},{3,2},{4,5},{5,4},{6,7},{7,6},{8,9},{9,8},{10,11... | collective-permute-start | bytes 1572872 | tf_op jit(solution)/shard_map/ppermute | solution.py:75
  170.6 21.1 %copy-start.17 = (f32[256,1024]{1,0:T(8,128)S(1)}, f32[256,1024]{1,0:T(8,128)}, u32[]{:S(2)}) copy-start(f32[256,1024]{1,0:T(8,128)} %copy-done.16) | copy-start | bytes 3145732
  195.1 13.3 %collective-permute-start.20 = (bf16[256,1024]{1,0:T(8,128)(2,1)S(1)}, bf16[256,1024]{1,0:T(8,128)(2,1)S(1)}, u32[]{:S(2)}, u32[]{:S(2)}) collective-permute-start(bf16[256,1024]{1,0:T(8,128)(2,1)S(1)} %add_convert_fusion.5), channel_id=1, source_target_pairs={{0,2},{1,3},{2,0},{3,1},{4,6},{5,7},{6,4},{7,5},{8,10},{9,11},{10,... | collective-permute-start | bytes 1572872 | tf_op jit(solution)/shard_map/ppermute | solution.py:75
  195.9 12.7 %collective-permute-start.15 = (bf16[256,1024]{1,0:T(8,128)(2,1)S(1)}, bf16[256,1024]{1,0:T(8,128)(2,1)S(1)}, u32[]{:S(2)}, u32[]{:S(2)}) collective-permute-start(bf16[256,1024]{1,0:T(8,128)(2,1)S(1)} %add_convert_fusion.5), channel_id=1, source_target_pairs={{0,1},{1,0},{2,3},{3,2},{4,5},{5,4},{6,7},{7,6},{8,9},{9,8},{10,11... | collective-permute-start | bytes 1572872 | tf_op jit(solution)/shard_map/ppermute | solution.py:75
  208.5 1.9 collective-permute-start.21
  210.0 51.9 %copy-start.183 = (f32[512,1024]{1,0:T(8,128)}, f32[512,1024]{1,0:T(8,128)S(1)}, u32[]{:S(2)}) copy-start(f32[512,1024]{1,0:T(8,128)S(1)} %fusion.20) | copy-start | bytes 6291460
  211.7 46.0 %copy-start.178 = (f32[512,1024]{1,0:T(8,128)}, f32[512,1024]{1,0:T(8,128)S(1)}, u32[]{:S(2)}) copy-start(f32[512,1024]{1,0:T(8,128)S(1)} %fusion.18) | copy-start | bytes 6291460
  213.1 2.0 collective-permute-start.22
  214.8 2.0 collective-permute-start.19
  215.3 14.1 %collective-permute-start.23 = (bf16[256,1024]{1,0:T(8,128)(2,1)S(1)}, bf16[256,1024]{1,0:T(8,128)(2,1)S(1)}, u32[]{:S(2)}, u32[]{:S(2)}) collective-permute-start(bf16[256,1024]{1,0:T(8,128)(2,1)S(1)} %fusion.59), channel_id=1, source_target_pairs={{0,2},{1,3},{2,0},{3,1},{4,6},{5,7},{6,4},{7,5},{8,10},{9,11},{10,... | collective-permute-start | bytes 1572872 | tf_op jit(solution)/shard_map/ppermute | solution.py:75
  234.0 27.9 %copy-start.61 = (bf16[256,1024]{1,0:T(8,128)(2,1)}, bf16[256,1024]{1,0:T(8,128)(2,1)S(1)}, u32[]{:S(2)}) copy-start(bf16[256,1024]{1,0:T(8,128)(2,1)S(1)} %get-tuple-element.81) | copy-start | bytes 1572868
  234.0 13.2 %collective-permute-start.26 = (bf16[256,1024]{1,0:T(8,128)(2,1)S(1)}, bf16[256,1024]{1,0:T(8,128)(2,1)S(1)}, u32[]{:S(2)}, u32[]{:S(2)}) collective-permute-start(bf16[256,1024]{1,0:T(8,128)(2,1)S(1)} %get-tuple-element.81), channel_id=1, source_target_pairs={{0,2},{1,3},{2,0},{3,1},{4,6},{5,7},{6,4},{7,5},{8,10},{9,11},{10,... | collective-permute-start | bytes 1572872 | tf_op jit(solution)/shard_map/ppermute | solution.py:75
  247.2 10.4 %collective-permute-start.27 = (bf16[256,1024]{1,0:T(8,128)(2,1)S(1)}, bf16[256,1024]{1,0:T(8,128)(2,1)S(1)}, u32[]{:S(2)}, u32[]{:S(2)}) collective-permute-start(bf16[256,1024]{1,0:T(8,128)(2,1)S(1)} %collective-permute-done.26), channel_id=1, source_target_pairs={{0,1},{1,0},{2,3},{3,2},{4,5},{5,4},{6,7},{7,6},{8,9},{9,8},{10,11... | collective-permute-start | bytes 1572872 | tf_op jit(solution)/shard_map/ppermute | solution.py:75
  247.2 14.7 %collective-permute-start.24 = (bf16[256,1024]{1,0:T(8,128)(2,1)S(1)}, bf16[256,1024]{1,0:T(8,128)(2,1)S(1)}, u32[]{:S(2)}, u32[]{:S(2)}) collective-permute-start(bf16[256,1024]{1,0:T(8,128)(2,1)S(1)} %get-tuple-element.81), channel_id=1, source_target_pairs={{0,1},{1,0},{2,3},{3,2},{4,5},{5,4},{6,7},{7,6},{8,9},{9,8},{10,11... | collective-permute-start | bytes 1572872 | tf_op jit(solution)/shard_map/ppermute | solution.py:75
  261.8 4.4 collective-permute-start.28
  265.7 2.1 collective-permute-start.25
  266.4 13.9 %collective-permute-start.29 = (bf16[256,1024]{1,0:T(8,128)(2,1)S(1)}, bf16[256,1024]{1,0:T(8,128)(2,1)S(1)}, u32[]{:S(2)}, u32[]{:S(2)}) collective-permute-start(bf16[256,1024]{1,0:T(8,128)(2,1)S(1)} %fusion.57), channel_id=1, source_target_pairs={{0,2},{1,3},{2,0},{3,1},{4,6},{5,7},{6,4},{7,5},{8,10},{9,11},{10,... | collective-permute-start | bytes 1572872 | tf_op jit(solution)/shard_map/ppermute | solution.py:75
  286.1 190.9 %reduce-scatter.8.cloned.1.call-start = ((), (), s32[]{:S(2)}) async-start(), calls=%async_computation.8 | async-start | bytes 2621440 | tf_op jit(solution)/shard_map/reduce_scatter | solution.py:782
  320.2 156.8 %reduce-scatter.4.cloned.1.call-start = ((), (), s32[]{:S(2)}) async-start(), calls=%async_computation.6 | async-start | bytes 5242880 | tf_op jit(solution)/shard_map/reduce_scatter | solution.py:782
  332.9 7.8 collective-permute-start.33
  333.3 9.8 %collective-permute-start.32 = (bf16[256,256]{1,0:T(8,128)(2,1)}, bf16[256,256]{1,0:T(8,128)(2,1)}, u32[]{:S(2)}, u32[]{:S(2)}) collective-permute-start(bf16[256,256]{1,0:T(8,128)(2,1)} %get-tuple-element.135), channel_id=1, source_target_pairs={{0,2},{1,3},{2,0},{3,1},{4,6},{5,7},{6,4},{7,5},{8,10},{9,11},{10,... | collective-permute-start | bytes 393224 | tf_op jit(solution)/shard_map/ppermute | solution.py:75
  339.9 12.4 %collective-permute-start.30 = (bf16[256,256]{1,0:T(8,128)(2,1)}, bf16[256,256]{1,0:T(8,128)(2,1)S(1)}, u32[]{:S(2)}, u32[]{:S(2)}) collective-permute-start(bf16[256,256]{1,0:T(8,128)(2,1)} %get-tuple-element.136), channel_id=1, source_target_pairs={{0,1},{1,0},{2,3},{3,2},{4,5},{5,4},{6,7},{7,6},{8,9},{9,8},{10,11... | collective-permute-start | bytes 393224 | tf_op jit(solution)/shard_map/ppermute | solution.py:75
  364.9 4.5 collective-permute-start.34
  365.8 7.5 collective-permute-start.31
  369.5 21.1 %collective-permute-start.35 = (bf16[256,1024]{1,0:T(8,128)(2,1)S(1)}, bf16[256,1024]{1,0:T(8,128)(2,1)S(1)}, u32[]{:S(2)}, u32[]{:S(2)}) collective-permute-start(bf16[256,1024]{1,0:T(8,128)(2,1)S(1)} %fusion.54), channel_id=1, source_target_pairs={{0,2},{1,3},{2,0},{3,1},{4,6},{5,7},{6,4},{7,5},{8,10},{9,11},{10,... | collective-permute-start | bytes 1572872 | tf_op jit(solution)/shard_map/ppermute | solution.py:75
  371.9 18.6 %copy-start.11 = (f32[256,1024]{1,0:T(8,128)S(1)}, f32[256,1024]{1,0:T(8,128)}, u32[]{:S(2)}) copy-start(f32[256,1024]{1,0:T(8,128)} %copy-done.10) | copy-start | bytes 3145732
  372.0 18.6 %copy-start.80 = (f32[1,1024]{1,0:T(1,128)S(1)}, f32[1,1024]{1,0:T(1,128)}, u32[]{:S(2)}) copy-start(f32[1,1024]{1,0:T(1,128)} %copy-done.79) | copy-start | bytes 12292
  372.0 18.6 %copy-start.105 = (f32[256]{0:T(256)S(1)}, f32[256]{0:T(256)}, u32[]{:S(2)}) copy-start(f32[256]{0:T(256)} %copy-done.104) | copy-start | bytes 3076
  372.0 18.6 %copy-start.113 = (f32[256]{0:T(256)S(1)}, f32[256]{0:T(256)}, u32[]{:S(2)}) copy-start(f32[256]{0:T(256)} %copy-done.112) | copy-start | bytes 3076
  393.9 5.3 collective-permute-start.36
  396.7 21.1 %collective-permute-start.38 = (bf16[256,1024]{1,0:T(8,128)(2,1)S(1)}, bf16[256,1024]{1,0:T(8,128)(2,1)S(1)}, u32[]{:S(2)}, u32[]{:S(2)}) collective-permute-start(bf16[256,1024]{1,0:T(8,128)(2,1)S(1)} %get-tuple-element.87), channel_id=1, source_target_pairs={{0,2},{1,3},{2,0},{3,1},{4,6},{5,7},{6,4},{7,5},{8,10},{9,11},{10,... | collective-permute-start | bytes 1572872 | tf_op jit(solution)/shard_map/ppermute | solution.py:75
  402.3 20.2 %copy-start.41 = (f32[512,1024]{1,0:T(8,128)}, f32[512,1024]{1,0:T(8,128)S(1)}, u32[]{:S(2)}) copy-start(f32[512,1024]{1,0:T(8,128)S(1)} %fusion.24) | copy-start | bytes 6291460
  402.4 37.6 %collective-permute-start.37 = (bf16[256,1024]{1,0:T(8,128)(2,1)S(1)}, bf16[256,1024]{1,0:T(8,128)(2,1)S(1)}, u32[]{:S(2)}, u32[]{:S(2)}) collective-permute-start(bf16[256,1024]{1,0:T(8,128)(2,1)S(1)} %slice.735), channel_id=1, source_target_pairs={{0,1},{1,0},{2,3},{3,2},{4,5},{5,4},{6,7},{7,6},{8,9},{9,8},{10,11... | collective-permute-start | bytes 1572872 | tf_op jit(solution)/shard_map/ppermute | solution.py:75
  417.8 8.1 collective-permute-start.39
  431.2 3.4 collective-permute-start.40
  434.8 14.4 %collective-permute-start.41 = (bf16[256,1024]{1,0:T(8,128)(2,1)S(1)}, bf16[256,1024]{1,0:T(8,128)(2,1)S(1)}, u32[]{:S(2)}, u32[]{:S(2)}) collective-permute-start(bf16[256,1024]{1,0:T(8,128)(2,1)S(1)} %fusion.52), channel_id=1, source_target_pairs={{0,2},{1,3},{2,0},{3,1},{4,6},{5,7},{6,4},{7,5},{8,10},{9,11},{10,... | collective-permute-start | bytes 1572872 | tf_op jit(solution)/shard_map/ppermute | solution.py:75
  440.0 34.1 %copy-start.143 = (f32[256]{0:T(256)S(1)}, f32[256]{0:T(256)}, u32[]{:S(2)}) copy-start(f32[256]{0:T(256)} %copy-done.142) | copy-start | bytes 3076
  (169 other events, 669.6 us)
Sparse Core Ops, SparseCore 0:
  9.6 36.7 all-gather.3
  48.0 57.0 all-gather.5
  106.6 29.1 all-gather.7
  286.2 31.3 reduce-scatter.5
  320.3 33.6 reduce-scatter.7
  356.9 56.9 reduce-scatter.3

commit v3 on v2

--- a/solution.py
+++ b/solution.py
@@ -631,31 +631,249 @@
     )(lens, grad, soft, with_u, with_v, key, value, proj)
 
 
-def ffn_forward(rows_in, w_in, w_rows, b_in, gain_row, norm_bias):
-    halves = gather_slots(b16(norm_rows(rows_in, gain_row, norm_bias)))
-    saved, sums = [], []
-    for hidden in halves:
-        pre = dot_rows(hidden, w_in) + b_in
-        active = b16(jax.nn.silu(pre))
-        sums.append(dot_rows(active, w_rows))
-        saved.append((hidden, pre, active))
-    return scatter_slots(*sums), saved
-
-
-def ffn_back(grad_own, rows_in, saved, w_in, w_rows, gain_row, norm_bias):
-    halves = gather_slots(grad_own)
-    grad_in = grad_out = grad_b = 0.0
-    sums = []
-    for grad, (hidden, pre, active) in zip(halves, saved):
-        silu_back = jax.vjp(jax.nn.silu, pre)[1]
-        grad_pre = b16(silu_back(dot_back(grad, w_rows))[0])
-        sums.append(dot_back(grad_pre, w_in))
-        grad_out = grad_out + dot_over(active, grad)
-        grad_in = grad_in + dot_over(hidden, grad_pre)
-        grad_b = grad_b + row_total(grad_pre)
-    norm_back = jax.vjp(norm_rows, rows_in, gain_row, norm_bias)[1]
-    grad_rows, grad_gain, grad_bias = norm_back(scatter_slots(*sums))
-    return grad_rows, grad_gain, grad_bias, grad_in, grad_out, grad_b, row_total(grad_own)
+class Links:
+    def __init__(self, send, recv):
+        self.send, self.recv, self.count = send, recv, 0
+        s = lax.axis_index("shard")
+        self.shard = s
+        self.near = {"shard": flip_bits(s, 1)}
+        self.far = {"shard": flip_bits(s, 2)}
+        self.across = {"shard": flip_bits(s, 3)}
+
+    def greet(self, devices):
+        barrier = pltpu.get_barrier_semaphore()
+        for device in devices:
+            pl.semaphore_signal(barrier, inc=1, device_id=device, device_id_type=MESH)
+        pl.semaphore_wait(barrier, len(devices))
+
+    def go(self, src, dst, device):
+        at = self.count
+        self.count += 1
+        copy = pltpu.make_async_remote_copy(
+            src_ref=src, dst_ref=dst, send_sem=self.send.at[at], recv_sem=self.recv.at[at],
+            device_id=device, device_id_type=MESH,
+        )
+        copy.start()
+        return copy
+
+
+def gather_work_scatter(links, x, work, part, send, land, cross, land_cross):
+    half = x.shape[1] // 2
+    out = [
+        links.go(x.at[0, pl.ds(h * half, half)], x.at[2 + h, pl.ds(0, half)], links.far)
+        for h in range(2)
+    ]
+    near = links.go(x.at[0], x.at[1], links.near)
+
+    def keep(cols, value):
+        part[0, :, cols] = value
+
+    work(0, keep)
+    near.wait()
+
+    def give(cols, value):
+        send[0, :, cols] = b16(value[:half])
+        send[1, :, cols] = b16(value[half:])
+
+    work(1, give)
+    last = [links.go(send.at[pl.ds(0, 2)], land.at[pl.ds(0, 2)], links.near)]
+    for h in range(2):
+        out[h].wait()
+        on = links.go(x.at[2 + h, pl.ds(0, half)], x.at[2 + h, pl.ds(half, half)], links.near)
+        on.wait()
+
+        def split(cols, value, h=h):
+            part[1, h * half : (h + 1) * half, cols] = value[:half]
+            send[2 + h, :, cols] = b16(value[half:])
+
+        work(2 + h, split)
+        back = links.go(send.at[2 + h], land.at[2 + h], links.near)
+        back.wait()
+        cross[h] = b16(part[1, h * half : (h + 1) * half] + f32(land[2 + h]))
+        last.append(links.go(cross.at[h], land_cross.at[h], links.far))
+
+    def settle():
+        for copy in last:
+            copy.wait()
+
+    def total(h):
+        rows = slice(h * half, (h + 1) * half)
+        return part[0, rows] + f32(land[h]) + f32(land_cross[h])
+
+    return settle, total
+
+
+def gws_scratch(rows, columns):
+    half = rows // 2
+    return [
+        pltpu.VMEM((2, rows, columns), jnp.float32),
+        pltpu.VMEM((4, half, columns), jnp.bfloat16),
+        pltpu.VMEM((4, half, columns), jnp.bfloat16),
+        pltpu.VMEM((2, half, columns), jnp.bfloat16),
+        pltpu.VMEM((2, half, columns), jnp.bfloat16),
+        pltpu.SemaphoreType.DMA((16,)),
+        pltpu.SemaphoreType.DMA((16,)),
+    ]
+
+
+def tiles(total, size):
+    def over(body):
+        pl.loop(0, total // size)(
+            lambda n: body(pl.ds(pl.multiple_of(n * size, size), size))
+        )
+
+    return over
+
+
+def ffn_forward_body(
+    rows_ref, vec_ref, b_ref, w_in, w_rows, out_ref, hid, act, slope,
+    part, send, land, cross, land_cross, send_sem, recv_sem,
+):
+    links = Links(send_sem, recv_sem)
+    links.greet([links.near, links.far])
+    vec = vec_ref[...]
+    hid[0] = b16(norm_rows(rows_ref[...], vec[0:1], vec[1:2]))
+    columns = hid.shape[2]
+
+    def work(block, emit):
+        @tiles(w_in.shape[1], 512)
+        def _(cols):
+            pre = dot_rows(hid[block], w_in[:, cols]) + b_ref[:, cols]
+            gate = jax.nn.sigmoid(pre)
+            act[block, :, cols] = b16(pre * gate)
+            slope[block, :, cols] = b16(gate * (1.0 + pre * (1.0 - gate)))
+
+        @tiles(columns, 512)
+        def _(cols):
+            emit(cols, dot_rows(act[block], w_rows[:, cols]))
+
+    settle, total = gather_work_scatter(links, hid, work, part, send, land, cross, land_cross)
+    settle()
+    half = rows_ref.shape[0] // 2
+    for h in range(2):
+        rows = slice(h * half, (h + 1) * half)
+        out_ref[rows] = rows_ref[rows] + 0.5 * (total(h) + vec[2:3])
+
+
+VMEM_SPEC = pl.BlockSpec(memory_space=pltpu.VMEM)
+
+
+def ffn_forward(rows_in, w_in, w_rows, b_in, gain_row, norm_bias, out_bias, ident):
+    rows, features = rows_in.shape
+    hidden = w_in.shape[1]
+    vec = jnp.concatenate(
+        [gain_row[None], norm_bias[None], out_bias[None], jnp.zeros((5, features), jnp.float32)], 0
+    )
+    shape = lambda c: jax.ShapeDtypeStruct((4, rows, c), jnp.bfloat16)
+    out, hid, act, slope = pl.pallas_call(
+        ffn_forward_body,
+        out_shape=[
+            jax.ShapeDtypeStruct((rows, features), jnp.float32),
+            shape(features), shape(hidden), shape(hidden),
+        ],
+        in_specs=[VMEM_SPEC] * 5,
+        out_specs=[VMEM_SPEC] * 4,
+        scratch_shapes=gws_scratch(rows, features),
+        compiler_params=pltpu.CompilerParams(
+            collective_id=ident, has_side_effects=True, vmem_limit_bytes=40 << 20
+        ),
+        name="ffn_forward_%d" % ident,
+    )(rows_in, vec, b_in[None], w_in, w_rows)
+    return out, (hid, act, slope)
+
+
+def norm_parts(rows):
+    row_mean = jnp.mean(rows, axis=-1, keepdims=True)
+    centered = rows - row_mean
+    inverse = lax.rsqrt(jnp.mean(centered * centered, axis=-1, keepdims=True) + epsilon)
+    return centered * inverse, inverse
+
+
+def norm_slope(grad, scaled, inverse, gain):
+    inner = grad * gain
+    return inverse * (
+        inner
+        - jnp.mean(inner, axis=-1, keepdims=True)
+        - scaled * jnp.mean(inner * scaled, axis=-1, keepdims=True)
+    )
+
+
+def ffn_back_body(
+    stream_ref, rows_ref, vec_ref, hid, act, slope, w_in, w_rows,
+    out_ref, gw_in, gw_out, sums_ref,
+    grad, inner, part, send, land, cross, land_cross, send_sem, recv_sem,
+):
+    links = Links(send_sem, recv_sem)
+    links.greet([links.near, links.far])
+    grad[0] = b16(0.5 * stream_ref[...])
+    columns = grad.shape[2]
+    hidden = w_in.shape[1]
+
+    def work(block, emit):
+        @tiles(hidden, 512)
+        def _(cols):
+            wide = dot_back(grad[block], w_rows[cols, :])
+            inner[block, :, cols] = b16(wide * f32(slope[block, :, cols]))
+
+        @tiles(columns, 512)
+        def _(cols):
+            emit(cols, dot_back(inner[block], w_in[cols, :]))
+
+    settle, total = gather_work_scatter(links, grad, work, part, send, land, cross, land_cross)
+    rows = stream_ref.shape[0]
+    flat = lambda ref: ref[...].reshape(4 * rows, ref.shape[2])
+
+    @tiles(hidden, 256)
+    def _(cols):
+        left = act[:, :, cols].reshape(4 * rows, 256)
+        gw_out[cols, :] = b16(dot_over(left, flat(grad)))
+
+    @tiles(hidden, 256)
+    def _(cols):
+        right = inner[:, :, cols].reshape(4 * rows, 256)
+        gw_in[:, cols] = b16(dot_over(flat(hid), right))
+        sums_ref[3:4, cols] = jnp.sum(f32(right), axis=0, keepdims=True)
+
+    settle()
+    vec = vec_ref[...]
+    sums_ref[0:3, :] = jnp.zeros((3, columns), jnp.float32)
+    sums_ref[4:8, :] = jnp.zeros((4, columns), jnp.float32)
+    sums_ref[2:3, :] = jnp.sum(f32(grad[0]), axis=0, keepdims=True)
+    half = rows // 2
+    for h in range(2):
+        at = slice(h * half, (h + 1) * half)
+        scaled, inverse = norm_parts(rows_ref[at])
+        given = total(h)
+        out_ref[at] = stream_ref[at] + norm_slope(given, scaled, inverse, vec[0:1])
+        sums_ref[0:1, :] += jnp.sum(given * scaled, axis=0, keepdims=True)
+        sums_ref[1:2, :] += jnp.sum(given, axis=0, keepdims=True)
+
+
+def ffn_back(stream, rows_in, saved, w_in, w_rows, gain_row, ident):
+    rows, features = rows_in.shape
+    hidden = w_in.shape[1]
+    hid, act, slope = saved
+    vec = jnp.broadcast_to(gain_row[None], (8, features))
+    return pl.pallas_call(
+        ffn_back_body,
+        out_shape=[
+            jax.ShapeDtypeStruct((rows, features), jnp.float32),
+            jax.ShapeDtypeStruct((features, hidden), jnp.bfloat16),
+            jax.ShapeDtypeStruct((hidden, features), jnp.bfloat16),
+            jax.ShapeDtypeStruct((8, features), jnp.float32),
+        ],
+        in_specs=[VMEM_SPEC] * 8,
+        out_specs=[VMEM_SPEC] * 4,
+        scratch_shapes=[
+            pltpu.VMEM((4, rows, features), jnp.bfloat16),
+            pltpu.VMEM((4, rows, hidden), jnp.bfloat16),
+        ]
+        + gws_scratch(rows, features),
+        compiler_params=pltpu.CompilerParams(
+            collective_id=ident, has_side_effects=True, vmem_limit_bytes=48 << 20
+        ),
+        name="ffn_back_%d" % ident,
+    )(stream, rows_in, vec, hid, act, slope, w_in, w_rows)
 
 
 def body(
@@ -685,8 +903,9 @@
     w_in = [ffn_in[0], ffn_in[1]]
     b_in = f32(ffn_bias)
 
-    branch, saved_one = ffn_forward(rows_in, w_in[0], w_rows[0], b_in[0], gain_rows[0], bias_rows[0])
-    rows_one = rows_in + 0.5 * (branch + bias_rows[1])
+    rows_one, saved_one = ffn_forward(
+        rows_in, w_in[0], w_rows[0], b_in[0], gain_rows[0], bias_rows[0], bias_rows[1], 5
+    )
 
     table_b = b16(position_table(length, features))
     table_b = jnp.pad(table_b, [(0, 1), (0, 0)])
@@ -734,18 +953,16 @@
     active_conv = b16(jax.nn.silu(normed))
     rows_three = rows_two + (dot_rows(active_conv, wc_out) + bias_rows[12])
 
-    branch, saved_two = ffn_forward(
-        rows_three, w_in[1], w_rows[1], b_in[1], gain_rows[4], bias_rows[13]
-    )
-    rows_four = rows_three + 0.5 * (branch + bias_rows[14])
+    rows_four, saved_two = ffn_forward(
+        rows_three, w_in[1], w_rows[1], b_in[1], gain_rows[4], bias_rows[13], bias_rows[14], 6
+    )
     result = norm_rows(rows_four, gain_rows[5], bias_rows[15]) * mask_col
 
     final_back = jax.vjp(norm_rows, rows_four, gain_rows[5], bias_rows[15])[1]
     stream, grad_gain_last, grad_bias_last = final_back(grads_in * mask_col)
-    two = ffn_back(
-        b16(0.5 * stream), rows_three, saved_two, w_in[1], w_rows[1], gain_rows[4], bias_rows[13]
-    )
-    stream = stream + two[0]
+    stream, two_in, two_out, two_sums = ffn_back(
+        stream, rows_three, saved_two, w_in[1], w_rows[1], gain_rows[4], 7
+    )
 
     grad_out = b16(stream)
     grad_conv_out = dot_over(active_conv, grad_out)
@@ -817,15 +1034,14 @@
     stream = stream + grad_rows
     out_part = scattered(grad_w_out)
 
-    one = ffn_back(
-        b16(0.5 * stream), rows_in, saved_one, w_in[0], w_rows[0], gain_rows[0], bias_rows[0]
-    )
-    stream = stream + one[0]
-    tall, deep = one[3].shape[0], one[3].shape[1]
+    stream, one_in, one_out, one_sums = ffn_back(
+        stream, rows_in, saved_one, w_in[0], w_rows[0], gain_rows[0], 8
+    )
+    tall, deep = one_in.shape
     sums = tail_sum(
-        [b16(two[4]), b16(two[3]), conv_in_part, conv_out_part]
+        [two_out, two_in, conv_in_part, conv_out_part]
         + [b16(g) for g in grad_qkv]
-        + [b16(grad_w_pos), out_part, b16(one[4]), b16(one[3])],
+        + [b16(grad_w_pos), out_part, one_out, one_in],
         [("turn", 1, 1), ("plain", 0, 1), ("plain", 5, None), ("plain", 6, None)]
         + [("plain", 2, at) for at in range(3)]
         + [("plain", 3, None), ("plain", 4, None), ("turn", 1, 0), ("plain", 0, 0)],
@@ -840,15 +1056,16 @@
 
     wide = jnp.stack(
         [
-            one[1], grad_gain_mix, grad_gain_conv, two[1], grad_gain_last,
-            one[2], one[6], grad_bias_mix, grad_b_out, grad_bias_conv,
-            grad_pw_in[:features], grad_pw_in[features:], grad_pw_out, two[2], two[6], grad_bias_last,
+            one_sums[0], grad_gain_mix, grad_gain_conv, two_sums[0], grad_gain_last,
+            one_sums[1], one_sums[2], grad_bias_mix, grad_b_out, grad_bias_conv,
+            grad_pw_in[:features], grad_pw_in[features:], grad_pw_out, two_sums[1], two_sums[2],
+            grad_bias_last,
         ]
         + [grad_kernel[t] for t in range(grad_kernel.shape[0])]
         + [jnp.zeros((features,), jnp.float32)] * 3
     )
     wide = wide.reshape(wide.shape[0], ns, width).transpose(1, 0, 2)
-    hidden_bias = jnp.stack([one[5], two[5]]).reshape(-1, width)
+    hidden_bias = jnp.stack([one_sums[3], two_sums[3]]).reshape(-1, width)
     local = jnp.concatenate(
         [grad_q_bias[None], grad_x_bias[None], grad_uv[0:2], hidden_bias], 0
     )

time: 828 us -> 804 us (0.971)
  waiting for transfers between devices: 178 us -> 22.2 us
  Pallas kernels: 366 us -> 512 us
  blocking collectives: 6.2 us -> 69.1 us
  matrix products: 92.3 us -> 43 us
  starting transfers between devices: 41 us -> 11.2 us
    ppermute x42 -> x18, waiting for transfers between devices: 176 us -> 20.7 us  [swap(): return lax.ppermute(x, axis, [(i, i ^ mask) for i in range(n)])]
    pallas_call x0 -> x4, Pallas kernels: none -> 145 us  [the longest x2 76.2 us: ffn_back(): pl.pallas_call(ffn_back_body, out_shape=[jax.ShapeDtypeStruct((rows, feat...]
    all_gather x1, blocking collectives: 6.2 us -> 69.1 us  [body(): packed = f32(lax.all_gather(packed, 'shard', axis=1, tiled=True))]
    ppermute x42 -> x18, starting transfers between devices: 40.4 us -> 10.8 us  [swap(): return lax.ppermute(x, axis, [(i, i ^ mask) for i in range(n)])]
    dot_general x21 -> x13, matrix products: 41.6 us -> 19.1 us  [dot_over(): lax.dot_general(a, b, (((0,), (0,)), ((), ())), preferred_element_type=jn...]
    dot_general x17 -> x9, matrix products: 27 us -> 11.6 us  [dot_back(): lax.dot_general(a, b, (((1,), (1,)), ((), ())), preferred_element_type=jn...]
    dot_general x18 -> x10, matrix products: 23.7 us -> 12.2 us  [dot_rows(): return jnp.dot(a, b, preferred_element_type=jnp.float32)]
    unnamed x382 -> x207, local copies, waits for them, and re-layouts: 42.4 us -> 47.8 us
  transfers between devices with their start and end apart: 48 -> 24, of which waited for: 17 -> 5; matrix products, arithmetic and copies ran while one was open for 19% -> 13% of each run, Pallas kernels for 7% -> 17%
where the time goes in v3:
time: 804 us; the launch traced here: 793 us
  Pallas kernels  512 us (64%)
  local copies, waits for them, and re-layouts  75.2 us (9%)
  blocking collectives  69.1 us (9%)
  other arithmetic  43.8 us (5%)
  matrix products  43 us (5%)
  waiting for transfers between devices  22.2 us (3%)
  between operations  16.7 us (2%)
  starting transfers between devices  11.2 us (1%)
    pallas_call x1, Pallas kernels, tail_sum(): pl.pallas_call(functools.partial(tail_body, specs, chunks, ns, len(arrays...  313 us
    pallas_call x2, Pallas kernels, ffn_back(): pl.pallas_call(ffn_back_body, out_shape=[jax.ShapeDtypeStruct((rows, feat...  76.2 us
    all_gather x1, blocking collectives, body(): packed = f32(lax.all_gather(packed, 'shard', axis=1, tiled=True))  69.1 us
    pallas_call x2, Pallas kernels, ffn_forward(): pl.pallas_call(ffn_forward_body, out_shape=[jax.ShapeDtypeStruct((rows, f...  69 us
    unnamed x207, local copies, waits for them, and re-layouts  47.8 us
    pallas_call x2, Pallas kernels, stats_sum(): pl.pallas_call(functools.partial(stats_body, ns, nb), out_shape=jax.Shape...  23.1 us
    ppermute x18, waiting for transfers between devices, swap(): return lax.ppermute(x, axis, [(i, i ^ mask) for i in range(n)])  20.7 us
    dot_general x13, matrix products, dot_over(): lax.dot_general(a, b, (((0,), (0,)), ((), ())), preferred_element_type=jn...  19.1 us
  transfers between devices with their start and end apart: 24, of which 5 were waited for; matrix products, arithmetic and copies ran while one was open for 13% of the time, Pallas kernels for 17%

profile of v3, /device:TPU:0, one launch (start us, length us, event | category | flops | bytes accessed | tf_op | source)
XLA Modules:
  0.0 792.9 jit_solution(17619737270473309573)
XLA Ops:
  8.8 2.5 fusion.91
  12.4 2.4 collective-permute-start.11
  16.6 1.5 collective-permute-start.2
  19.6 69.1 %all_gather.12 = bf16[28,1024]{1,0:T(8,128)(2,1)S(1)} all-gather(bf16[28,256]{1,0:T(8,128)(2,1)S(1)} %maximum_maximum_fusion.2), channel_id=1, replica_groups=mesh['batch'=8,'shard'=4] {'shard'}, dimensions={1}, use_global_device_ids=true | all-gather | bytes 71680 | tf_op jit(solution)/shard_map/all_gather | solution.py:893
  90.7 1.4 pad_add_fusion.6.len_ref
  92.3 4.0 slice_bitcast_fusion
  96.3 2.2 pad_maximum_fusion.2
  98.6 1.5 pad_maximum_fusion
  100.0 1.4 dynamic-slice_bitcast_fusion.3
  102.7 41.0 %ffn_forward_5.1 = (f32[256,1024]{1,0:T(8,128)S(1)}, bf16[4,256,1024]{2,1,0:T(8,128)(2,1)S(1)}, bf16[4,256,1024]{2,1,0:T(8,128)(2,1)S(1)}, bf16[4,256,1024]{2,1,0:T(8,128)(2,1)S(1)}) custom-call(f32[256,1024]{1,0:T(8,128)S(1)} %bitcast.207, f32[8,1024]{1,0:T(8,128)S(1)} %get-tuple-element.216.vec_ref, f32[1,1024]{1,0:T(1,128)S(1)} %get-tuple-element.204.b_ref, ...), custom_call_target="tpu_custom_call" | custom-call | tf_op jit(solution)/shard_map/ffn_forward_5/pallas_call | solution.py:768
  143.7 1.4 copy-done.10
  145.1 1.3 copy-done.11
  146.4 1.4 copy-done.12
  150.6 4.1 fusion.10
  155.6 7.3 collective-permute-done.5
  166.3 2.8 attend.3
  170.3 1.8 collective-permute-start.7
  172.1 3.0 attend.2
  175.4 1.6 pad_maximum_fusion.3.w_rows
  177.0 1.9 collective-permute-done.7
  179.8 2.7 fusion.104
  182.8 3.6 convolution_add_fusion
  186.4 1.3 copy-done.34
  189.0 4.8 multiply_reduce_fusion.14
  194.5 11.7 %stats_sum_1.1 = f32[24,128]{1,0:T(8,128)} custom-call(f32[24,128]{1,0:T(8,128)} %maximum_maximum_fusion.3.x_ref), custom_call_target="tpu_custom_call" | custom-call | tf_op jit(solution)/shard_map/stats_sum_1/pallas_call | solution.py:172
  207.4 1.3 fusion.62
  208.7 1.3 divide_bitcast_fusion
  210.1 2.9 fusion.2.rows_ref
  213.2 28.1 %ffn_forward_6.1 = (f32[256,1024]{1,0:T(8,128)S(1)}, bf16[4,256,1024]{2,1,0:T(8,128)(2,1)S(1)}, bf16[4,256,1024]{2,1,0:T(8,128)(2,1)S(1)}, bf16[4,256,1024]{2,1,0:T(8,128)(2,1)S(1)}) custom-call(f32[256,1024]{1,0:T(8,128)S(1)} %fusion.2.rows_ref, f32[8,1024]{1,0:T(8,128)S(1)} %get-tuple-element.215.vec_ref, f32[1,1024]{1,0:T(1,128)S(1)} %get-tuple-element.203.b_ref, ...), custom_call_target="tpu_custom_call" | custom-call | tf_op jit(solution)/shard_map/ffn_forward_6/pallas_call | solution.py:768
  241.3 1.3 copy-done.15
  242.6 1.3 copy-done.16
  244.0 1.4 copy-done.17
  245.8 1.7 multiply_reduce_fusion.5
  247.5 1.5 fusion.90
  250.2 32.6 %ffn_back_7.1 = (f32[256,1024]{1,0:T(8,128)S(1)}, bf16[1024,1024]{1,0:T(8,128)(2,1)S(1)}, bf16[1024,1024]{1,0:T(8,128)(2,1)}, f32[8,1024]{1,0:T(8,128)S(1)}) custom-call(f32[256,1024]{1,0:T(8,128)S(1)} %broadcast_add_fusion.stream_ref, f32[256,1024]{1,0:T(8,128)S(1)} %copy-done.9, f32[8,1024]{1,0:T(8,128)S(1)} %broadcast_in_dim.40.vec_ref, ...), custom_call_target="tpu_custom_call" | custom-call | tf_op jit(solution)/shard_map/ffn_back_7/pallas_call | solution.py:857
  282.9 1.3 copy-done.13
  284.2 2.3 convolution_convert_fusion.2
  286.5 4.0 fusion.84
  291.1 11.4 %stats_sum_2.1 = f32[16,128]{1,0:T(8,128)} custom-call(f32[16,128]{1,0:T(8,128)} %pad_maximum_fusion.12.x_ref), custom_call_target="tpu_custom_call" | custom-call | tf_op jit(solution)/shard_map/stats_sum_2/pallas_call | solution.py:172
  304.0 6.0 multiply_reduce_fusion.4
  315.1 2.1 multiply_reduce_fusion.6
  319.6 2.1 convolution_convert_fusion.1
  322.0 2.6 convolution_convert_fusion.3
  327.4 3.4 convolution_convert_fusion
  332.3 1.4 collective-permute-done.14
  337.9 4.4 attend_back.3
  345.1 4.6 attend_back.2
  355.5 1.5 convolution_add_fusion.2
  356.9 1.3 fusion.4.refs_4_
  358.2 1.3 fusion.5.refs_5_
  360.0 1.3 fusion.6.refs_6_
  363.4 3.6 fusion.7.refs_7_
  367.0 9.6 %collective-permute-done.17 = bf16[256,1024]{1,0:T(8,128)(2,1)} collective-permute-done((bf16[256,1024]{1,0:T(8,128)(2,1)}, bf16[256,1024]{1,0:T(8,128)(2,1)}, u32[]{:S(2)}, u32[]{:S(2)}) %collective-permute-start.17) | collective-permute-done | bytes 524320 | tf_op jit(solution)/shard_map/ppermute | solution.py:75
  376.6 1.7 multiply_reduce_fusion.7
  380.8 43.6 %ffn_back_8.1 = (f32[256,1024]{1,0:T(8,128)S(1)}, bf16[1024,1024]{1,0:T(8,128)(2,1)S(1)}, bf16[1024,1024]{1,0:T(8,128)(2,1)}, f32[8,1024]{1,0:T(8,128)S(1)}) custom-call(f32[256,1024]{1,0:T(8,128)S(1)} %get-tuple-element.140.stream_ref, f32[256,1024]{1,0:T(8,128)S(1)} %bitcast.208, f32[8,1024]{1,0:T(8,128)S(1)} %broadcast_in_dim.46.vec_ref, ...), custom_call_target="tpu_custom_call" | custom-call | tf_op jit(solution)/shard_map/ffn_back_8/pallas_call | solution.py:857
  424.5 1.3 copy-done.14
  425.9 2.0 stack.136
  428.5 15.1 %vector_sum.1 = f32[40,256]{1,0:T(8,128)} custom-call(f32[4,24,256]{2,1,0:T(8,128)} %bitcast.214, f32[16,256]{1,0:T(8,128)} %select_maximum_fusion.l_ref), custom_call_target="tpu_custom_call" | custom-call | tf_op jit(solution)/shard_map/vector_sum/pallas_call | solution.py:228
  444.3 1.3 slice.425
  451.0 313.3 %tail_sum.1 = (f32[2,1024,1024]{2,1,0:T(8,128)}, f32[2,4096,256]{2,1,0:T(8,128)}, f32[3,1024,256]{2,1,0:T(8,128)}, f32[1024,256]{1,0:T(8,128)}, f32[1024,256]{1,...) custom-call(bf16[1024,1024]{1,0:T(8,128)(2,1)} %get-tuple-element.70.refs_0_, bf16[1024,1024]{1,0:T(8,128)(2,1)} %copy-done.13, ...), custom_call_target="tpu_custom_call" | custom-call | tf_op jit(solution)/shard_map/tail_sum/pallas_call | solution.py:501
  765.4 9.1 %copy.38 = f32[2,1024,1024]{2,1,0:T(8,128)} copy(f32[2,1024,1024]{2,1,0:T(8,128)} %get-tuple-element.240) | data formatting | bytes 16777216
  774.5 3.9 copy.39
  778.6 1.7 copy.40
  782.7 1.3 copy.43
  (360 shorter events, 66.5 us)
Async XLA Ops:
  7.2 147.5 %copy-start = (bf16[1024,256]{1,0:T(8,128)(2,1)S(1)}, bf16[1024,256]{1,0:T(8,128)(2,1)}, u32[]{:S(2)}) copy-start(bf16[1024,256]{1,0:T(8,128)(2,1)} %param.21) | copy-start | bytes 1572868
  7.2 172.6 %all-gather.4.cloned.1.call-start = ((), (), s32[]{:S(2)}) async-start(), calls=%async_computation.3 | async-start | bytes 2621440 | tf_op jit(solution)/shard_map/all_gather | solution.py:913
  7.9 174.9 %all-gather.6.cloned.1.call-start = ((), (), s32[]{:S(2)}) async-start(), calls=%async_computation.4 | async-start | bytes 5242880 | tf_op jit(solution)/shard_map/all_gather | solution.py:914
  8.7 201.4 %all-gather.8.cloned.1.call-start = ((), (), s32[]{:S(2)}) async-start(), calls=%async_computation.5 | async-start | bytes 2621440 | tf_op jit(solution)/shard_map/all_gather | solution.py:915
  12.4 79.7 %collective-permute-start.11 = (bf16[1024,256]{1,0:T(8,128)(2,1)}, bf16[1024,256]{1,0:T(8,128)(2,1)S(1)}, u32[]{:S(2)}, u32[]{:S(2)}) collective-permute-start(bf16[1024,256]{1,0:T(8,128)(2,1)} %get-tuple-element.127), channel_id=1, source_target_pairs={{0,3},{1,2},{2,1},{3,0},{4,7},{5,6},{6,5},{7,4},{8,11},{9,10},{10,... | collective-permute-start | bytes 1572872 | tf_op jit(solution)/shard_map/ppermute | solution.py:75
  14.8 81.5 %collective-permute-start.10 = (bf16[1024,256]{1,0:T(8,128)(2,1)}, bf16[1024,256]{1,0:T(8,128)(2,1)}, u32[]{:S(2)}, u32[]{:S(2)}) collective-permute-start(bf16[1024,256]{1,0:T(8,128)(2,1)} %get-tuple-element.128), channel_id=1, source_target_pairs={{0,2},{1,3},{2,0},{3,1},{4,6},{5,7},{6,4},{7,5},{8,10},{9,11},{10,... | collective-permute-start | bytes 1572872 | tf_op jit(solution)/shard_map/ppermute | solution.py:75
  15.4 80.9 %collective-permute-start.9 = (bf16[1024,256]{1,0:T(8,128)(2,1)S(1)}, bf16[1024,256]{1,0:T(8,128)(2,1)}, u32[]{:S(2)}, u32[]{:S(2)}) collective-permute-start(bf16[1024,256]{1,0:T(8,128)(2,1)S(1)} %get-tuple-element.129), channel_id=1, source_target_pairs={{0,1},{1,0},{2,3},{3,2},{4,5},{5,4},{6,7},{7,6},{8,9},{9,8},{10,11... | collective-permute-start | bytes 1572872 | tf_op jit(solution)/shard_map/ppermute | solution.py:75
  15.5 4.0 copy-start.73
  15.5 4.0 copy-start.89
  15.5 4.0 copy-start.90
  15.5 74.5 %copy-start.75 = (bf16[2,1024]{1,0:T(2,128)(2,1)S(1)}, bf16[2,1024]{1,0:T(2,128)(2,1)}, u32[]{:S(2)}) copy-start(bf16[2,1024]{1,0:T(2,128)(2,1)} %param.19) | copy-start | bytes 12292
  16.6 81.9 %collective-permute-start.2 = (bf16[1024,256]{1,0:T(8,128)(2,1)}, bf16[1024,256]{1,0:T(8,128)(2,1)}, u32[]{:S(2)}, u32[]{:S(2)}) collective-permute-start(bf16[1024,256]{1,0:T(8,128)(2,1)} %get-tuple-element.135), channel_id=1, source_target_pairs={{0,3},{1,2},{2,1},{3,0},{4,7},{5,6},{6,5},{7,4},{8,11},{9,10},{10,... | collective-permute-start | bytes 1572872 | tf_op jit(solution)/shard_map/ppermute | solution.py:75
  18.1 80.5 %collective-permute-start.1 = (bf16[1024,256]{1,0:T(8,128)(2,1)}, bf16[1024,256]{1,0:T(8,128)(2,1)}, u32[]{:S(2)}, u32[]{:S(2)}) collective-permute-start(bf16[1024,256]{1,0:T(8,128)(2,1)} %get-tuple-element.136), channel_id=1, source_target_pairs={{0,2},{1,3},{2,0},{3,1},{4,6},{5,7},{6,4},{7,5},{8,10},{9,11},{10,... | collective-permute-start | bytes 1572872 | tf_op jit(solution)/shard_map/ppermute | solution.py:75
  18.7 432.3 %reduce-scatter.6.cloned.1.call-start = ((), (), s32[]{:S(2)}) async-start(), calls=%async_computation.7 | async-start | bytes 2621440 | tf_op jit(solution)/shard_map/reduce_scatter | solution.py:999
  89.4 6.9 copy-start.68
  92.1 6.5 collective-permute-start
  96.3 5.5 copy-start.4
  101.8 41.9 %copy-start.2 = (bf16[1024,1024]{1,0:T(8,128)(2,1)}, bf16[1024,1024]{1,0:T(8,128)(2,1)S(1)}, u32[]{:S(2)}) copy-start(bf16[1024,1024]{1,0:T(8,128)(2,1)S(1)} %pad_maximum_fusion.1.w_rows) | copy-start | bytes 6291460
  148.5 15.4 %copy-start.65 = (bf16[256,1024]{1,0:T(8,128)(2,1)}, bf16[256,1024]{1,0:T(8,128)(2,1)S(1)}, u32[]{:S(2)}) copy-start(bf16[256,1024]{1,0:T(8,128)(2,1)S(1)} %add_convert_fusion.2) | copy-start | bytes 1572868
  148.5 14.4 %collective-permute-start.3 = (bf16[256,1024]{1,0:T(8,128)(2,1)S(1)}, bf16[256,1024]{1,0:T(8,128)(2,1)S(1)}, u32[]{:S(2)}, u32[]{:S(2)}) collective-permute-start(bf16[256,1024]{1,0:T(8,128)(2,1)S(1)} %add_convert_fusion.2), channel_id=1, source_target_pairs={{0,1},{1,0},{2,3},{3,2},{4,5},{5,4},{6,7},{7,6},{8,9},{9,8},{10,11... | collective-permute-start | bytes 1572872 | tf_op jit(solution)/shard_map/ppermute | solution.py:75
  148.5 14.3 %collective-permute-start.5 = (bf16[256,1024]{1,0:T(8,128)(2,1)S(1)}, bf16[256,1024]{1,0:T(8,128)(2,1)S(1)}, u32[]{:S(2)}, u32[]{:S(2)}) collective-permute-start(bf16[256,1024]{1,0:T(8,128)(2,1)S(1)} %add_convert_fusion.2), channel_id=1, source_target_pairs={{0,2},{1,3},{2,0},{3,1},{4,6},{5,7},{6,4},{7,5},{8,10},{9,11},{10,... | collective-permute-start | bytes 1572872 | tf_op jit(solution)/shard_map/ppermute | solution.py:75
  154.7 8.2 %copy-start.45 = (bf16[3,1024,256]{2,1,0:T(8,128)(2,1)S(1)}, bf16[3,1024,256]{2,1,0:T(8,128)(2,1)}, u32[]{:S(2)}) copy-start(bf16[3,1024,256]{2,1,0:T(8,128)(2,1)} %param.20) | copy-start | bytes 4718596
  155.6 7.8 copy-start.92
  162.9 1.9 collective-permute-start.6
  163.4 8.7 %copy-start.18 = (bf16[512,256]{1,0:T(8,128)(2,1)}, bf16[512,256]{1,0:T(8,128)(2,1)S(1)}, u32[]{:S(2)}) copy-start(bf16[512,256]{1,0:T(8,128)(2,1)S(1)} %convolution_convert_fusion.6.k_ref) | copy-start | bytes 786436
  163.9 8.2 %copy-start.20 = (bf16[512,256]{1,0:T(8,128)(2,1)}, bf16[512,256]{1,0:T(8,128)(2,1)S(1)}, u32[]{:S(2)}) copy-start(bf16[512,256]{1,0:T(8,128)(2,1)S(1)} %fusion.8.x_ref) | copy-start | bytes 786436
  166.3 9.1 %copy-start.53 = (bf16[1024,256]{1,0:T(8,128)(2,1)S(1)}, bf16[1024,256]{1,0:T(8,128)(2,1)}, u32[]{:S(2)}) copy-start(bf16[1024,256]{1,0:T(8,128)(2,1)} %get-tuple-element.122) | copy-start | bytes 1572868
  166.3 9.1 %copy-start.54 = (bf16[1024,256]{1,0:T(8,128)(2,1)S(1)}, bf16[1024,256]{1,0:T(8,128)(2,1)}, u32[]{:S(2)}) copy-start(bf16[1024,256]{1,0:T(8,128)(2,1)} %get-tuple-element.123) | copy-start | bytes 1572868
  166.3 9.1 %copy-start.55 = (bf16[1024,256]{1,0:T(8,128)(2,1)S(1)}, bf16[1024,256]{1,0:T(8,128)(2,1)}, u32[]{:S(2)}) copy-start(bf16[1024,256]{1,0:T(8,128)(2,1)} %get-tuple-element.124) | copy-start | bytes 1572868
  166.3 9.1 %copy-start.56 = (bf16[1024,256]{1,0:T(8,128)(2,1)S(1)}, bf16[1024,256]{1,0:T(8,128)(2,1)}, u32[]{:S(2)}) copy-start(bf16[1024,256]{1,0:T(8,128)(2,1)} %get-tuple-element.125) | copy-start | bytes 1572868
  170.2 6.8 collective-permute-start.8
  170.3 8.6 %collective-permute-start.7 = (bf16[256,256]{1,0:T(8,128)(2,1)S(1)}, bf16[256,256]{1,0:T(8,128)(2,1)S(1)}, u32[]{:S(2)}, u32[]{:S(2)}) collective-permute-start(bf16[256,256]{1,0:T(8,128)(2,1)S(1)} %get-tuple-element.160), channel_id=1, source_target_pairs={{0,2},{1,3},{2,0},{3,1},{4,6},{5,7},{6,4},{7,5},{8,10},{9,11},{10,... | collective-permute-start | bytes 393224 | tf_op jit(solution)/shard_map/ppermute | solution.py:75
  175.2 3.8 collective-permute-start.4
  182.5 27.6 %copy-start.36 = (f32[256,1024]{1,0:T(8,128)}, f32[256,1024]{1,0:T(8,128)S(1)}, u32[]{:S(2)}) copy-start(f32[256,1024]{1,0:T(8,128)S(1)} %get-tuple-element.218) | copy-start | bytes 3145732
  187.8 6.1 copy-start.93
  187.8 22.3 %copy-start.83 = (f32[1,1024]{1,0:T(1,128)S(1)}, f32[1,1024]{1,0:T(1,128)}, u32[]{:S(2)}) copy-start(f32[1,1024]{1,0:T(1,128)} %get-tuple-element.168) | copy-start | bytes 12292
  187.8 22.3 %copy-start.86 = (f32[1,1024]{1,0:T(1,128)S(1)}, f32[1,1024]{1,0:T(1,128)}, u32[]{:S(2)}) copy-start(f32[1,1024]{1,0:T(1,128)} %get-tuple-element.178) | copy-start | bytes 12292
  213.0 28.3 %copy-start.8 = (f32[256,1024]{1,0:T(8,128)}, f32[256,1024]{1,0:T(8,128)S(1)}, u32[]{:S(2)}) copy-start(f32[256,1024]{1,0:T(8,128)S(1)} %fusion.2.rows_ref) | copy-start | bytes 3145732
  250.2 33.9 %copy-start.49 = (f32[256,1024]{1,0:T(8,128)S(1)}, f32[256,1024]{1,0:T(8,128)}, u32[]{:S(2)}) copy-start(f32[256,1024]{1,0:T(8,128)} %get-tuple-element.117) | copy-start | bytes 3145732
  286.5 164.5 %reduce-scatter.8.cloned.1.call-start = ((), (), s32[]{:S(2)}) async-start(), calls=%async_computation.8 | async-start | bytes 2621440 | tf_op jit(solution)/shard_map/reduce_scatter | solution.py:999
  312.7 4.5 copy-start.41
  313.1 4.1 copy-start.43
  317.7 4.0 copy-start.77
  321.7 129.3 %reduce-scatter.4.cloned.1.call-start = ((), (), s32[]{:S(2)}) async-start(), calls=%async_computation.6 | async-start | bytes 5242880 | tf_op jit(solution)/shard_map/reduce_scatter | solution.py:999
  322.0 4.6 copy-start.42
  322.0 4.6 copy-start.44
  325.5 6.8 collective-permute-start.15
  325.5 8.3 %collective-permute-start.14 = (bf16[256,256]{1,0:T(8,128)(2,1)}, bf16[256,256]{1,0:T(8,128)(2,1)}, u32[]{:S(2)}, u32[]{:S(2)}) collective-permute-start(bf16[256,256]{1,0:T(8,128)(2,1)} %get-tuple-element.148), channel_id=1, source_target_pairs={{0,2},{1,3},{2,0},{3,1},{4,6},{5,7},{6,4},{7,5},{8,10},{9,11},{10,... | collective-permute-start | bytes 393224 | tf_op jit(solution)/shard_map/ppermute | solution.py:75
  331.4 12.6 %collective-permute-start.12 = (bf16[256,256]{1,0:T(8,128)(2,1)}, bf16[256,256]{1,0:T(8,128)(2,1)}, u32[]{:S(2)}, u32[]{:S(2)}) collective-permute-start(bf16[256,256]{1,0:T(8,128)(2,1)} %get-tuple-element.149), channel_id=1, source_target_pairs={{0,1},{1,0},{2,3},{3,2},{4,5},{5,4},{6,7},{7,6},{8,9},{9,8},{10,11... | collective-permute-start | bytes 393224 | tf_op jit(solution)/shard_map/ppermute | solution.py:75
  337.9 4.4 copy-start.46
  342.3 13.2 %copy-start.30 = (bf16[2,512,256]{2,1,0:T(8,128)(2,1)}, bf16[2,512,256]{2,1,0:T(8,128)(2,1)S(1)}, u32[]{:S(2)}) copy-start(bf16[2,512,256]{2,1,0:T(8,128)(2,1)S(1)} %get-tuple-element.73) | copy-start | bytes 1572868
  343.9 17.5 %collective-permute-start.16 = (bf16[256,1024]{1,0:T(8,128)(2,1)S(1)}, bf16[256,1024]{1,0:T(8,128)(2,1)S(1)}, u32[]{:S(2)}, u32[]{:S(2)}) collective-permute-start(bf16[256,1024]{1,0:T(8,128)(2,1)S(1)} %slice.594), channel_id=1, source_target_pairs={{0,1},{1,0},{2,3},{3,2},{4,5},{5,4},{6,7},{7,6},{8,9},{9,8},{10,11... | collective-permute-start | bytes 1572872 | tf_op jit(solution)/shard_map/ppermute | solution.py:75
  352.2 14.8 %collective-permute-start.13 = (bf16[256,1024]{1,0:T(8,128)(2,1)}, bf16[256,1024]{1,0:T(8,128)(2,1)}, u32[]{:S(2)}, u32[]{:S(2)}) collective-permute-start(bf16[256,1024]{1,0:T(8,128)(2,1)} %slice.595), channel_id=1, source_target_pairs={{0,1},{1,0},{2,3},{3,2},{4,5},{5,4},{6,7},{7,6},{8,9},{9,8},{10,11... | collective-permute-start | bytes 1572872 | tf_op jit(solution)/shard_map/ppermute | solution.py:75
  362.3 14.4 %collective-permute-start.17 = (bf16[256,1024]{1,0:T(8,128)(2,1)}, bf16[256,1024]{1,0:T(8,128)(2,1)}, u32[]{:S(2)}, u32[]{:S(2)}) collective-permute-start(bf16[256,1024]{1,0:T(8,128)(2,1)} %fusion.16), channel_id=1, source_target_pairs={{0,2},{1,3},{2,0},{3,1},{4,6},{5,7},{6,4},{7,5},{8,10},{9,11},{10,... | collective-permute-start | bytes 1572872 | tf_op jit(solution)/shard_map/ppermute | solution.py:75
  363.4 13.3 %copy-start.48 = (f32[512,1024]{1,0:T(8,128)S(1)}, f32[512,1024]{1,0:T(8,128)}, u32[]{:S(2)}) copy-start(f32[512,1024]{1,0:T(8,128)} %copy-done.47) | copy-start | bytes 6291460
  367.0 11.4 %copy-start.80 = (f32[256]{0:T(256)S(1)}, f32[256]{0:T(256)}, u32[]{:S(2)}) copy-start(f32[256]{0:T(256)} %copy-done.79) | copy-start | bytes 3076
  380.8 45.0 %copy-start.76 = (f32[1,1024]{1,0:T(1,128)S(1)}, f32[1,1024]{1,0:T(1,128)}, u32[]{:S(2)}) copy-start(f32[1,1024]{1,0:T(1,128)} %get-tuple-element.193) | copy-start | bytes 12292
  380.8 45.1 %copy-start.84 = (f32[1024]{0:T(1024)S(1)}, f32[1024]{0:T(1024)}, u32[]{:S(2)}) copy-start(f32[1024]{0:T(1024)} %get-tuple-element.89) | copy-start | bytes 12292
  380.8 45.1 %copy-start.85 = (f32[1024]{0:T(1024)S(1)}, f32[1024]{0:T(1024)}, u32[]{:S(2)}) copy-start(f32[1024]{0:T(1024)} %get-tuple-element.101) | copy-start | bytes 12292
  380.8 68.3 %copy-start.88 = (f32[1,256]{1,0:T(1,128)S(1)}, f32[1,256]{1,0:T(1,128)}, u32[]{:S(2)}) copy-start(f32[1,256]{1,0:T(1,128)} %get-tuple-element.209) | copy-start | bytes 3076
  380.8 69.6 %copy-start.91 = (f32[1,256]{1,0:T(1,128)S(1)}, f32[1,256]{1,0:T(1,128)}, u32[]{:S(2)}) copy-start(f32[1,256]{1,0:T(1,128)} %get-tuple-element.210) | copy-start | bytes 3076
  764.4 10.1 %slice-start = ((s8[8388608]{0:T(1024)(128)(4,1)}), s8[4194304]{0:T(1024)(128)(4,1)S(1)}, s32[]{:S(2)}) async-start(s8[8388608]{0:T(1024)(128)(4,1)} %bitcast.210), calls=%async_computation.9 | async-start | bytes 8388608
  765.3 9.1 %slice-start.1 = ((s8[8388608]{0:T(1024)(128)(4,1)}), s8[4194304]{0:T(1024)(128)(4,1)S(1)}, s32[]{:S(2)}) async-start(s8[8388608]{0:T(1024)(128)(4,1)} %bitcast.210), calls=%async_computation.10 | async-start | bytes 8388608
  774.5 4.2 copy-start.51
  (59 other events, 100.9 us)
Sparse Core Ops, SparseCore 0:
  9.6 36.8 all-gather.3
  48.1 48.7 all-gather.5
  98.4 36.2 all-gather.7
  286.6 32.2 reduce-scatter.5
  321.9 31.3 reduce-scatter.7
  356.2 56.0 reduce-scatter.3

commit v4 on v3

v4 whole, which is shorter than its diff:
```python
import functools
import math

import jax
import jax.numpy as jnp
from jax import lax
from jax.experimental import pallas as pl
from jax.experimental.pallas import tpu as pltpu
from jax.sharding import PartitionSpec as P

HEADS = 8
MESH = pl.DeviceIdType.MESH
VMEM_SPEC = pl.BlockSpec(memory_space=pltpu.VMEM)
epsilon = 1e-05


def f32(a):
    return a.astype(jnp.float32)


def b16(a):
    return a.astype(jnp.bfloat16)


def norm_rows(values_in, gain_row, bias_row):
    row_mean = jnp.mean(values_in, axis=-1, keepdims=True)
    centered = values_in - row_mean
    spread = jnp.mean(centered * centered, axis=-1, keepdims=True)
    return centered * lax.rsqrt(spread + epsilon) * gain_row + bias_row


def dot_rows(a, b):
    return jnp.dot(a, b, preferred_element_type=jnp.float32)


def dot_back(a, b):
    return lax.dot_general(a, b, (((1,), (1,)), ((), ())), preferred_element_type=jnp.float32)


def dot_over(a, b):
    return lax.dot_general(a, b, (((0,), (0,)), ((), ())), preferred_element_type=jnp.float32)


def exchange(axis, index, count, source, landing, send_sem, recv_sem):
    copies = []
    for j in range(1, count):
        peer = lax.rem(index + j, count)
        copies.append(
            pltpu.make_async_remote_copy(
                src_ref=source,
                dst_ref=landing.at[index],
                send_sem=send_sem.at[j],
                recv_sem=recv_sem.at[j],
                device_id={axis: peer},
                device_id_type=MESH,
            )
        )
    return copies


def sum_slots(ref, count):
    total = ref[0]
    for j in range(1, count):
        total = total + ref[j]
    return total


class Chunk:
    def __init__(self, at, source, row, rows, columns, first, count):
        self.at, self.source, self.row, self.rows, self.columns = at, source, row, rows, columns
        extra = [(1 << k, k) for k in range(3, count.bit_length() - 1)]
        line = (6, 1)
        if first == "near":
            self.pre, self.post = [(1, 0)], [line] + extra
        else:
            self.pre, self.post = [], [line, (1, 0)] + extra
        size, self.landings = rows, []
        for _ in self.pre:
            size //= 2
            self.landings.append((size, columns))
        self.landings.append((size, columns))
        for _ in self.post:
            size //= 2
            self.landings.append((size, columns))
        self.steps = len(self.landings)


def bit_of(value, k):
    return lax.rem(lax.div(value, 1 << k), 2)


def flip_bits(value, mask):
    out = value
    k = 0
    while (1 << k) <= mask:
        if mask & (1 << k):
            out = out + (1 - 2 * bit_of(value, k)) * (1 << k)
        k += 1
    return out


class Mover:
    def __init__(self, chunk, batch, source, base, held, landings, sems, finish, early):
        self.c, self.b = chunk, batch
        self.source, self.base, self.held, self.landings, self.sems = source, base, held, landings, sems
        lo, hi = bit_of(batch, 1), bit_of(batch, 2)
        self.inner = lo != hi
        self.ended = lo == hi
        self.finish, self.early = finish, early
        self.build()

    def copy(self, at, src, dst, mask):
        send, recv = self.sems
        return pltpu.make_async_remote_copy(
            src_ref=src,
            dst_ref=dst,
            send_sem=send.at[self.c.at, at],
            recv_sem=recv.at[self.c.at, at],
            device_id={"batch": flip_bits(self.b, mask)},
            device_id_type=MESH,
        )

    def build(self):
        c = self.c
        held = self.held
        here, base = self.source, self.base
        off, size, step = 0, c.rows, 0
        plan, trail = [], []
        sequence = [("all",) + p for p in c.pre] + [("fold", 2, None)]
        sequence += [("inner",) + p for p in c.post]
        for kind, mask, sel in sequence:
            landing = self.landings[step]
            if kind == "fold":
                own = row_view(here, base, size)
                cp = self.copy(step, own, landing, mask)
            else:
                size //= 2
                mine = bit_of(self.b, sel)
                cp = self.copy(step, row_view(here, base + (1 - mine) * size, size), landing, mask)
                own = row_view(here, base + mine * size, size)
                off = off + mine * size
            trail.append((kind, mask, off, size))
            step += 1
            out = landing if step < len(sequence) else held(off, size)
            plan.append((kind, cp, (own, landing, out)))
            here, base = landing, 0
        for kind, mask, off, size in reversed(trail):
            cp = self.copy(step, held(off, size), held(off, size), mask)
            plan.append(("unfold" if kind == "fold" else kind, cp, None))
            step += 1
        self.plan = plan
        self.depth = len(plan) + len(self.early)

    def begin(self, k):
        kind, cp, _ = self.plan[k]
        if kind == "all":
            cp.start()
        elif kind == "fold":
            pl.when(self.ended)(cp.start)
        else:
            pl.when(self.inner)(cp.start)

    def end(self, k):
        kind, cp, add = self.plan[k]

        def gather():
            if add is not None:
                own, landing, out = add
                out[...] = b16(f32(own[...]) + f32(landing[...]))

        if kind == "all":
            cp.wait()
            gather()
        elif kind in ("fold", "unfold"):
            sender, taker = (
                (self.ended, self.inner) if kind == "fold" else (self.inner, self.ended)
            )
            pl.when(sender)(cp.wait_send)

            @pl.when(taker)
            def _():
                cp.wait_recv()
                gather()
        else:

            @pl.when(self.inner)
            def _():
                cp.wait()
                gather()

    def advance(self, k):
        if k < len(self.early):
            self.early[k]()
            return
        k -= len(self.early)
        if k > 0:
            self.end(k - 1)
        elif self.early:
            self.settle_early()
        if k < len(self.plan):
            self.begin(k)
        else:
            self.finish(self.c)


def row_view(ref, start, size):
    start = start if isinstance(start, int) else pl.multiple_of(start, 16 if size % 16 == 0 else 8)
    return ref.at[pl.ds(start, size)]


def column_block(index, columns):
    return pl.ds(pl.multiple_of(index * columns, 128), columns)


class Rider:
    def __init__(self, batch, send, recv, first):
        self.b, self.send, self.recv, self.at = batch, send, recv, first

    def go(self, src, dst, bit):
        copy = pltpu.make_async_remote_copy(
            src_ref=src, dst_ref=dst, send_sem=self.send.at[self.at], recv_sem=self.recv.at[self.at],
            device_id={"batch": flip_bits(self.b, 1 << bit)}, device_id_type=MESH,
        )
        self.at += 1
        copy.start()
        return copy

    def halve(self, source, landing, bit):
        half = landing.shape[0]
        mine = bit_of(self.b, bit)
        copy = self.go(row_view(source, (1 - mine) * half, half), landing, bit)

        def end():
            copy.wait()
            own = row_view(source, mine * half, half)
            landing[...] = b16(f32(own[...]) + f32(landing[...]))

        return end

    def double(self, source, target, bit):
        half = source.shape[0]
        there = row_view(target, bit_of(self.b, bit) * half, half)
        copy = self.go(source, there, bit)
        there[...] = source[...]
        return copy.wait

    def chain(self, refs, bits, move):
        ends, stages = [], []
        for i, bit in enumerate(bits):

            def stage(i=i, bit=bit):
                if ends:
                    ends.pop()()
                ends.append(move(refs[i], refs[i + 1], bit))

            stages.append(stage)
        stages.append(lambda: ends.pop()())
        return stages


def ride_orders(count):
    bits = list(range(count.bit_length() - 1))
    return bits, [1, 0] + bits[2:]


def tail_body(specs, chunks, ns, nb, n_in, n_out, *refs):
    ins, refs = refs[:n_in], refs[n_in:]
    ridden, refs = refs[:2], refs[2:]
    (one_sums, mix_sums, two_sums, conv_sums, own_sums), refs = refs[:5], refs[5:]
    outs, refs = refs[:n_out], refs[n_out:]
    (o_gains, o_biases, o_taps, o_hidden), refs = refs[:4], refs[4:]
    send, recv, turn_send, turn_recv, pre_send, pre_recv, ride_send, ride_recv = refs[:8]
    ss, rs, sb, rb, wide, land_s, mid, land_b, ride_fin = refs[8:17]
    rest = list(refs[17:])
    shard, batch = lax.axis_index("shard"), lax.axis_index("batch")
    barrier = pltpu.get_barrier_semaphore()
    greeted = [{"batch": lax.rem(batch + j, nb)} for j in range(1, nb)]
    greeted += [{"shard": flip_bits(shard, m)} for m in range(1, ns)]
    for device in greeted:
        pl.semaphore_signal(barrier, inc=1, device_id=device, device_id_type=MESH)
    width = own_sums.shape[1]
    for t in range(ns):
        cols = slice(t * width, (t + 1) * width)
        wide[t, 0:3, :] = one_sums[0:3, cols]
        wide[t, 3:6, :] = mix_sums[0:3, cols]
        wide[t, 6:9, :] = two_sums[0:3, cols]
        wide[t, 9:14, :] = conv_sums[0:5, cols]
        wide[t, 14:19, :] = conv_sums[8:13, cols]
        wide[t, 19:21, :] = two_sums[4:6, cols]
        wide[t, 21:24, :] = jnp.zeros((3, width), jnp.float32)
    pl.semaphore_wait(barrier, len(greeted))

    vector_copies = []
    for j in range(1, ns):
        peer = lax.rem(shard + j, ns)
        copy = pltpu.make_async_remote_copy(
            src_ref=wide.at[peer], dst_ref=land_s.at[shard], send_sem=ss.at[j], recv_sem=rs.at[j],
            device_id={"shard": peer}, device_id_type=MESH,
        )
        copy.start()
        vector_copies.append(copy)
    land_s[shard] = wide[shard]

    def vectors_on():
        for copy in vector_copies:
            copy.wait()
        mid[0:24, :] = sum_slots(land_s, ns)
        mid[24:28, :] = own_sums[0:4, :]
        per = one_sums.shape[1] // width
        for t in range(per):
            cols = slice(t * width, (t + 1) * width)
            mid[28 + t : 29 + t, :] = one_sums[3:4, cols]
            mid[28 + per + t : 29 + per + t, :] = two_sums[3:4, cols]
        mid[28 + 2 * per :, :] = jnp.zeros((mid.shape[0] - 28 - 2 * per, width), jnp.float32)
        vector_copies[:] = exchange("batch", batch, nb, mid, land_b, sb, rb)
        for copy in vector_copies:
            copy.start()
        land_b[batch] = mid[...]

    def vectors_out():
        for copy in vector_copies:
            copy.wait()
        vec = sum_slots(land_b, nb)
        row = lambda k: vec[k : k + 1]
        mine = conv_sums[5:7, column_block(shard, width)]
        gains = [row(0), row(3), row(9), mine[0:1], row(6), row(19)]
        order = [1, 2, 4, 24, 25, 5, 26, 27, 10, 11, 12, None, 13, 7, 8, 20]
        for k, value in enumerate(gains):
            o_gains[k : k + 1, :] = value
        for k, at in enumerate(order):
            o_biases[k : k + 1, :] = mine[1:2] if at is None else row(at)
        o_taps[...] = vec[14:19]
        per = o_hidden.shape[1] // width
        for k in range(2):
            for t in range(per):
                at = 28 + k * per + t
                o_hidden[k : k + 1, t * width : (t + 1) * width] = row(at)

    late = []

    def turn(c_at, total, row, rows, out, lead):
        target = outs[out] if lead is None else outs[out].at[lead]
        columns = target.shape[1]
        height = target.shape[0] // ns
        there = row_view(target, shard * height + row, rows)
        copies = []
        for j in range(1, ns):
            peer = flip_bits(shard, j)
            copy = pltpu.make_async_remote_copy(
                src_ref=total.at[:, column_block(peer, columns)],
                dst_ref=there,
                send_sem=turn_send.at[c_at, j],
                recv_sem=turn_recv.at[c_at, j],
                device_id={"shard": peer},
                device_id_type=MESH,
            )
            copy.start()
            copies.append(copy)
        there[...] = total[:, column_block(shard, columns)]
        late.extend(copies)

    rides = []
    orders = ride_orders(nb)
    plain_target = outs[0].at[1]
    rider_a = Rider(batch, ride_send, ride_recv, 0)
    rider_b = Rider(batch, ride_send, ride_recv, 1)
    end_a = rider_a.double(ridden[0], plain_target, orders[0][0])
    end_b = rider_b.double(ridden[1], ride_fin, orders[1][0])

    movers = []
    for c in chunks:
        kind, out, lead = specs["arrays"][c.source]
        source, base, early, settle = ins[c.source], c.row, [], None
        if kind == "gather":
            near_land, far_land = rest.pop(0), rest.pop(0)
            whole, columns, rows = ins[c.source], c.columns, pl.ds(c.row, c.rows)
            far = flip_bits(shard, 2)
            state = {}

            def pre(at, src, dst, mask, c=c):
                copy = pltpu.make_async_remote_copy(
                    src_ref=src, dst_ref=dst, send_sem=pre_send.at[c.at, at], recv_sem=pre_recv.at[c.at, at],
                    device_id={"shard": flip_bits(shard, mask)}, device_id_type=MESH,
                )
                copy.start()
                return copy

            def first(near_land=near_land, whole=whole, columns=columns, rows=rows, state=state, pre=pre):
                state["n"] = [
                    pre(i, whole.at[rows, column_block(flip_bits(shard, m), columns)], near_land.at[i], 1)
                    for i, m in enumerate((1, 3))
                ]

            def second(
                near_land=near_land, far_land=far_land, whole=whole, columns=columns, rows=rows, state=state,
                pre=pre, far=far,
            ):
                for copy in state["n"]:
                    copy.wait()
                near_land[1] = b16(f32(near_land[1]) + f32(whole[rows, column_block(far, columns)]))
                state["f"] = pre(2, near_land.at[1], far_land, 2)

            def settle(
                near_land=near_land, far_land=far_land, whole=whole, columns=columns, rows=rows, state=state,
            ):
                state["f"].wait()
                far_land[...] = b16(
                    f32(far_land[...]) + f32(near_land[0]) + f32(whole[rows, column_block(shard, columns)])
                )

            early = [first, second]
            source, base = far_land, 0
        if kind == "turn":
            total = rest.pop(0)
            held = lambda off, size, total=total: row_view(total, off, size)

            def finish(c, total=total, out=out, lead=lead):
                turn(c.at, total, c.row, c.rows, out, lead)
        else:
            target = outs[out] if lead is None else outs[out].at[lead]
            held = lambda off, size, target=target, c=c: row_view(target, c.row + off, size)

            def finish(c):
                pass
        landings = [rest.pop(0) for _ in range(c.steps)]
        m = Mover(c, batch, source, base, held, landings, (send, recv), finish, early)
        m.settle_early = settle
        movers.append(m)
    starts, lag = [], specs["lag"]
    for i, m in enumerate(movers):
        starts.append(max(0, i // lag - len(m.early)))
    rounds = max(s + m.depth + 1 for s, m in zip(starts, movers))
    for r in range(rounds):
        if r == 1:
            vectors_on()
        if r == 2:
            end_b()
            turn(len(chunks), ride_fin, 0, ride_fin.shape[0], 1, 1)
        if r == 3:
            vectors_out()
            end_a()
        for s, m in zip(starts, movers):
            if 0 <= r - s <= m.depth:
                m.advance(r - s)
    for copy in late:
        copy.wait()


def tail_sum(arrays, ridden, sums, kinds, outputs, firsts, chunk_rows, hidden, ident):
    ns, nb = lax.axis_size("shard"), lax.axis_size("batch")
    low, full = jnp.bfloat16, jnp.float32
    chunks = []
    for i, a in enumerate(arrays):
        step = chunk_rows[i]
        columns = a.shape[1] // ns if kinds[i][0] == "gather" else a.shape[1]
        for row in range(0, a.shape[0], step):
            chunks.append(Chunk(len(chunks), i, row, step, columns, firsts[len(chunks) % len(firsts)], nb))
    depth = max(2 * c.steps for c in chunks)
    specs = dict(arrays=kinds, lag=2)
    width = sums[-1].shape[1]
    per = hidden // width
    small = -(-(28 + 2 * per) // 8) * 8
    dma = pltpu.SemaphoreType.DMA
    n = len(chunks)
    scratch = [
        dma((n, depth)), dma((n, depth)), dma((n + 1, ns)), dma((n + 1, ns)), dma((n, 3)), dma((n, 3)),
        dma((2,)), dma((2,)), dma((ns,)), dma((ns,)), dma((nb,)), dma((nb,)),
        pltpu.VMEM((ns, 24, width), full), pltpu.VMEM((ns, 24, width), full),
        pltpu.VMEM((small, width), full), pltpu.VMEM((nb, small, width), full),
        pltpu.VMEM((2 * ridden[1].shape[0], ridden[1].shape[1]), low),
    ]
    for c in chunks:
        if kinds[c.source][0] == "gather":
            scratch += [pltpu.VMEM((2, c.rows, c.columns), low), pltpu.VMEM((c.rows, c.columns), low)]
        if kinds[c.source][0] == "turn":
            scratch.append(pltpu.VMEM((c.rows, c.columns), low))
        scratch += [pltpu.VMEM(shape, low) for shape in c.landings]
    shape = jax.ShapeDtypeStruct
    shapes = [shape(s, low) for s in outputs]
    shapes += [shape((6, width), full), shape((16, width), full), shape((5, width), full), shape((2, hidden), full)]
    operands = list(arrays) + list(ridden) + list(sums)
    return pl.pallas_call(
        functools.partial(tail_body, specs, chunks, ns, nb, len(arrays), len(outputs)),
        out_shape=shapes,
        in_specs=[VMEM_SPEC] * len(operands),
        out_specs=[VMEM_SPEC] * len(shapes),
        scratch_shapes=scratch,
        compiler_params=pltpu.CompilerParams(
            collective_id=ident, has_side_effects=True, vmem_limit_bytes=62 << 20
        ),
        name="tail_sum",
    )(*operands)


class Links:
    def __init__(self, send, recv):
        self.send, self.recv, self.count = send, recv, 0
        s = lax.axis_index("shard")
        self.shard = s
        self.near = {"shard": flip_bits(s, 1)}
        self.far = {"shard": flip_bits(s, 2)}
        self.across = {"shard": flip_bits(s, 3)}

    def greet(self, devices):
        barrier = pltpu.get_barrier_semaphore()
        for device in devices:
            pl.semaphore_signal(barrier, inc=1, device_id=device, device_id_type=MESH)
        pl.semaphore_wait(barrier, len(devices))

    def go(self, src, dst, device):
        at = self.count
        self.count += 1
        copy = pltpu.make_async_remote_copy(
            src_ref=src, dst_ref=dst, send_sem=self.send.at[at], recv_sem=self.recv.at[at],
            device_id=device, device_id_type=MESH,
        )
        copy.start()
        return copy


def gather_work_scatter(links, x, work, part, send, land, cross, land_cross, tick=None):
    half = x.shape[1] // 2
    out = [
        links.go(x.at[0, pl.ds(h * half, half)], x.at[2 + h, pl.ds(0, half)], links.far)
        for h in range(2)
    ]
    near = links.go(x.at[0], x.at[1], links.near)

    def keep(cols, value):
        part[0, :, cols] = value

    work(0, keep)
    near.wait()

    def give(cols, value):
        send[0, :, cols] = b16(value[:half])
        send[1, :, cols] = b16(value[half:])

    work(1, give)
    last = [links.go(send.at[pl.ds(0, 2)], land.at[pl.ds(0, 2)], links.near)]
    if tick is not None:
        tick()
    for h in range(2):
        out[h].wait()
        on = links.go(x.at[2 + h, pl.ds(0, half)], x.at[2 + h, pl.ds(half, half)], links.near)
        on.wait()

        def split(cols, value, h=h):
            part[1, h * half : (h + 1) * half, cols] = value[:half]
            send[2 + h, :, cols] = b16(value[half:])

        work(2 + h, split)
        back = links.go(send.at[2 + h], land.at[2 + h], links.near)
        back.wait()
        cross[h] = b16(part[1, h * half : (h + 1) * half] + f32(land[2 + h]))
        last.append(links.go(cross.at[h], land_cross.at[h], links.far))

    def settle():
        for copy in last:
            copy.wait()

    def total(h):
        rows = slice(h * half, (h + 1) * half)
        return part[0, rows] + f32(land[h]) + f32(land_cross[h])

    return settle, total


def gws_scratch(rows, columns):
    half = rows // 2
    return [
        pltpu.VMEM((2, rows, columns), jnp.float32),
        pltpu.VMEM((4, half, columns), jnp.bfloat16),
        pltpu.VMEM((4, half, columns), jnp.bfloat16),
        pltpu.VMEM((2, half, columns), jnp.bfloat16),
        pltpu.VMEM((2, half, columns), jnp.bfloat16),
        pltpu.SemaphoreType.DMA((16,)),
        pltpu.SemaphoreType.DMA((16,)),
    ]


def tiles(total, size):
    def over(body):
        pl.loop(0, total // size)(
            lambda n: body(pl.ds(pl.multiple_of(n * size, size), size))
        )

    return over


def ffn_forward_body(
    which, at_rows, rows_ref, pack, b_ref, w_rows, ffn_in, out_ref, hid, act, slope,
    part, send, land, cross, land_cross, send_sem, recv_sem, w_in, local_sem,
):
    links = Links(send_sem, recv_sem)
    load = pltpu.make_async_copy(ffn_in.at[which], w_in, local_sem)
    load.start()
    links.greet([links.near, links.far])
    hid[0] = b16(
        norm_rows(rows_ref[...], vector_row(pack, at_rows[0]), vector_row(pack, at_rows[1]))
    )
    load.wait()
    columns = hid.shape[2]

    def work(block, emit):
        @tiles(w_in.shape[1], 512)
        def _(cols):
            pre = dot_rows(hid[block], w_in[:, cols]) + b_ref[which : which + 1, cols]
            gate = jax.nn.sigmoid(pre)
            act[block, :, cols] = b16(pre * gate)
            slope[block, :, cols] = b16(gate * (1.0 + pre * (1.0 - gate)))

        @tiles(columns, 512)
        def _(cols):
            emit(cols, dot_rows(act[block], w_rows[:, cols]))

    settle, total = gather_work_scatter(links, hid, work, part, send, land, cross, land_cross)
    settle()
    half = rows_ref.shape[0] // 2
    for h in range(2):
        rows = slice(h * half, (h + 1) * half)
        out_ref[rows] = rows_ref[rows] + 0.5 * (total(h) + vector_row(pack, at_rows[2]))


def ffn_forward(rows_in, pack, b_in, w_rows, ffn_in, which, at_rows, ident):
    rows, features = rows_in.shape
    hidden = ffn_in.shape[2]
    shape = lambda c: jax.ShapeDtypeStruct((4, rows, c), jnp.bfloat16)
    out, hid, act, slope = pl.pallas_call(
        functools.partial(ffn_forward_body, which, at_rows),
        out_shape=[
            jax.ShapeDtypeStruct((rows, features), jnp.float32),
            shape(features), shape(hidden), shape(hidden),
        ],
        in_specs=[VMEM_SPEC] * 4 + [pl.BlockSpec(memory_space=pl.ANY)],
        out_specs=[VMEM_SPEC] * 4,
        scratch_shapes=gws_scratch(rows, features)
        + [pltpu.VMEM((features, hidden), jnp.bfloat16), pltpu.SemaphoreType.DMA],
        compiler_params=pltpu.CompilerParams(
            collective_id=ident, has_side_effects=True, vmem_limit_bytes=40 << 20
        ),
        name="ffn_forward",
    )(rows_in, pack, b_in, w_rows, ffn_in)
    return out, (hid, act, slope)


def norm_parts(rows):
    row_mean = jnp.mean(rows, axis=-1, keepdims=True)
    centered = rows - row_mean
    inverse = lax.rsqrt(jnp.mean(centered * centered, axis=-1, keepdims=True) + epsilon)
    return centered * inverse, inverse


def norm_slope(grad, scaled, inverse, gain):
    inner = grad * gain
    return inverse * (
        inner
        - jnp.mean(inner, axis=-1, keepdims=True)
        - scaled * jnp.mean(inner * scaled, axis=-1, keepdims=True)
    )


def ffn_back_body(which, gain_at, nb, *refs):
    stages = []
    if which == 1:
        last_rows, cotangent, *refs = refs
        rows_ref, pack, hid, act, slope, w_rows, ffn_in, result, out_ref, gw_in, gw_out, sums_ref, *refs = refs
        stream_ref, *refs = refs
    else:
        stream_ref, ride_a, ride_b, *refs = refs
        rows_ref, pack, hid, act, slope, w_rows, ffn_in, out_ref, gw_in, gw_out, sums_ref, *refs = refs
        out_a, out_b, ride_send, ride_recv, *refs = refs
    grad, inner, part, send, land, cross, land_cross, send_sem, recv_sem, w_in, local_sem, *refs = refs
    links = Links(send_sem, recv_sem)
    load = pltpu.make_async_copy(ffn_in.at[which], w_in, local_sem)
    load.start()
    batch = lax.axis_index("batch")
    orders = ride_orders(nb)
    devices = [links.near, links.far]
    if which == 0:
        devices += [{"batch": flip_bits(batch, 1 << k)} for k in orders[0]]
    links.greet(devices)
    if which == 0:
        steps = len(orders[0]) - 1
        for at, (start, end) in enumerate(((ride_a, out_a), (ride_b, out_b))):
            rider = Rider(batch, ride_send, ride_recv, at * steps)
            between = refs[at * (steps - 1) : (at + 1) * (steps - 1)]
            stages.append(
                rider.chain([start, *between, end], orders[at][:0:-1], rider.double)
            )
    else:
        live = f32(pack[links.shard, 27:28, 0:1])
        mask = f32(f32(lax.broadcasted_iota(jnp.int32, (rows_ref.shape[0], 1), 0)) < live)
        scaled, inverse = norm_parts(last_rows[...])
        gain = vector_row(pack, 5)
        result[...] = (scaled * gain + vector_row(pack, 21)) * mask
        given = cotangent[...] * mask
        stream_ref[...] = norm_slope(given, scaled, inverse, gain)
        ends = (
            jnp.sum(given * scaled, axis=0, keepdims=True),
            jnp.sum(given, axis=0, keepdims=True),
        )

    def tick():
        for chain in stages:
            if chain:
                chain.pop(0)()

    tick()
    grad[0] = b16(0.5 * stream_ref[...])
    load.wait()
    columns = grad.shape[2]
    hidden = w_in.shape[1]

    def work(block, emit):
        @tiles(hidden, 512)
        def _(cols):
            wide = dot_back(grad[block], w_rows[cols, :])
            inner[block, :, cols] = b16(wide * f32(slope[block, :, cols]))

        @tiles(columns, 512)
        def _(cols):
            emit(cols, dot_back(inner[block], w_in[cols, :]))

    settle, total = gather_work_scatter(
        links, grad, work, part, send, land, cross, land_cross, None
    )
    tick()
    rows = stream_ref.shape[0]
    flat = lambda ref: ref[...].reshape(4 * rows, ref.shape[2])

    @tiles(hidden, 256)
    def _(cols):
        left = act[:, :, cols].reshape(4 * rows, 256)
        gw_out[cols, :] = b16(dot_over(left, flat(grad)))

    @tiles(hidden, 256)
    def _(cols):
        right = inner[:, :, cols].reshape(4 * rows, 256)
        gw_in[:, cols] = b16(dot_over(flat(hid), right))
        sums_ref[3:4, cols] = jnp.sum(f32(right), axis=0, keepdims=True)

    settle()
    for chain in stages:
        while chain:
            chain.pop(0)()
    gain = vector_row(pack, gain_at)
    sums_ref[0:3, :] = jnp.zeros((3, columns), jnp.float32)
    sums_ref[4:8, :] = jnp.zeros((4, columns), jnp.float32)
    if which == 1:
        sums_ref[4:5, :], sums_ref[5:6, :] = ends
    sums_ref[2:3, :] = jnp.sum(f32(grad[0]), axis=0, keepdims=True)
    half = rows // 2
    for h in range(2):
        at = slice(h * half, (h + 1) * half)
        scaled, inverse = norm_parts(rows_ref[at])
        given = total(h)
        out_ref[at] = stream_ref[at] + norm_slope(given, scaled, inverse, gain)
        sums_ref[0:1, :] += jnp.sum(given * scaled, axis=0, keepdims=True)
        sums_ref[1:2, :] += jnp.sum(given, axis=0, keepdims=True)


def ffn_back(given, rows_in, pack, saved, w_rows, ffn_in, which, gain_at, ident):
    rows, features = rows_in.shape
    hidden = ffn_in.shape[2]
    nb = lax.axis_size("batch")
    low, full = jnp.bfloat16, jnp.float32
    shape = jax.ShapeDtypeStruct
    shapes = [
        shape((rows, features), full), shape((features, hidden), low), shape((hidden, features), low),
        shape((8, features), full),
    ]
    scratch = []
    if which == 1:
        shapes = [shape((rows, features), full)] + shapes
        scratch = [pltpu.VMEM((rows, features), full)]
    else:
        first, steps = given[1].shape[0], nb.bit_length() - 2
        shapes += [shape((first << steps, r.shape[1]), low) for r in given[1:]]
        scratch = [pltpu.SemaphoreType.DMA((2 * steps,)), pltpu.SemaphoreType.DMA((2 * steps,))]
    extra = []
    if which == 0:
        for r in given[1:]:
            extra += [pltpu.VMEM((first << k, r.shape[1]), low) for k in range(1, steps)]
    return pl.pallas_call(
        functools.partial(ffn_back_body, which, gain_at, nb),
        out_shape=shapes,
        in_specs=[VMEM_SPEC] * (len(given) + 6) + [pl.BlockSpec(memory_space=pl.ANY)],
        out_specs=[VMEM_SPEC] * len(shapes),
        scratch_shapes=scratch
        + [
            pltpu.VMEM((4, rows, features), low),
            pltpu.VMEM((4, rows, hidden), low),
        ]
        + gws_scratch(rows, features)
        + [pltpu.VMEM((features, hidden), low), pltpu.SemaphoreType.DMA]
        + extra,
        compiler_params=pltpu.CompilerParams(
            collective_id=ident, has_side_effects=True, vmem_limit_bytes=48 << 20
        ),
        name="ffn_back_%d" % which,
    )(*given, rows_in, pack, *saved, w_rows, ffn_in)


class Fetch:
    def __init__(self, links, batch, local_sem):
        self.links, self.side = links, bit_of(batch, 0)
        self.beside = {"batch": flip_bits(batch, 1)}
        self.local_sem = local_sem
        self.open = []
        self.stages = []

    def run(self):
        if self.stages:
            self.stages.pop(0)()

    def drain(self):
        while self.stages:
            self.run()

    def go(self, src, dst, device):
        return self.links.go(src, dst, device)

    def columns(self, source, target, at):
        links, (rows, columns) = self.links, source.shape
        half = rows // 2
        block = lambda s: pl.ds(pl.multiple_of(s * columns, 128), columns)
        mine = pl.ds(pl.multiple_of(self.side * half, 16), half)
        far_index = flip_bits(links.shard, 2)
        held = {}

        def first():
            held["own"] = pltpu.make_async_copy(source, target.at[:, block(links.shard)], self.local_sem.at[at])
            held["own"].start()
            held["far"] = self.go(source.at[mine], target.at[mine, block(links.shard)], links.far)
            held["near"] = self.go(source, target.at[:, block(links.shard)], links.near)

        def second():
            held["far"].wait()
            held["x"] = self.go(target.at[mine, block(far_index)], target.at[mine, block(far_index)], self.beside)

        def third():
            held["x"].wait()
            held["on"] = self.go(target.at[:, block(far_index)], target.at[:, block(far_index)], links.near)

        def fourth():
            held["on"].wait()
            held["near"].wait()
            held["own"].wait()

        return [first, second, third, fourth]

    def rows(self, source, target, at, pieces):
        links, (rows, width) = self.links, target.shape
        columns = source.shape[1]
        half = rows // 2
        size = half // pieces
        block = lambda s: pl.ds(pl.multiple_of(s * columns, 128), columns)
        part = lambda base, p: pl.ds(pl.multiple_of(base + self.side * half + p * size, 16), size)
        held = {}
        far, across = flip_bits(links.shard, 2), flip_bits(links.shard, 3)
        near = flip_bits(links.shard, 1)
        whole = lambda t: pl.ds(pl.multiple_of(t * rows, 16), rows)

        def first():
            held["own"] = pltpu.make_async_copy(
                source.at[whole(links.shard)], target.at[:, block(links.shard)], self.local_sem.at[at]
            )
            held["own"].start()
            for p in range(pieces):
                for name, t, device in (("f", far, links.far), ("a", across, links.across)):
                    held[name, p] = self.go(
                        source.at[part(t * rows, p)], target.at[part(0, p), block(links.shard)], device
                    )
            held["near"] = self.go(source.at[whole(near)], target.at[:, block(links.shard)], links.near)

        def middle(p):
            def run():
                for name, t in (("f", far), ("a", across)):
                    held[name, p].wait()
                    at_p = target.at[part(0, p), block(t)]
                    held[name, p] = self.go(at_p, at_p, self.beside)

            return run

        def last():
            for p in range(pieces):
                held["f", p].wait()
                held["a", p].wait()
            held["near"].wait()
            held["own"].wait()

        return [first] + [middle(p) for p in range(pieces)] + [last]


def vector_row(pack, row):
    return f32(jnp.concatenate([pack[t, row : row + 1, :] for t in range(pack.shape[0])], 1))


def scatter_late(links, work, part, send, land, cross, land_cross):
    half = send.shape[1]
    backs = []
    for h in range(2):

        def split(cols, value, h=h):
            part[1, h * half : (h + 1) * half, cols] = value[:half]
            send[2 + h, :, cols] = b16(value[half:])

        work(2 + h, split)
        backs.append(links.go(send.at[2 + h], land.at[2 + h], links.near))
    last = []
    for h in range(2):
        backs[h].wait()
        cross[h] = b16(part[1, h * half : (h + 1) * half] + f32(land[2 + h]))
        last.append(links.go(cross.at[h], land_cross.at[h], links.far))

    def give(cols, value):
        send[0, :, cols] = b16(value[:half])
        send[1, :, cols] = b16(value[half:])

    work(1, give)
    last.append(links.go(send.at[pl.ds(0, 2)], land.at[pl.ds(0, 2)], links.near))

    def keep(cols, value):
        part[0, :, cols] = value

    work(0, keep)

    def settle():
        for copy in last:
            copy.wait()

    def total(h):
        rows = slice(h * half, (h + 1) * half)
        return part[0, rows] + f32(land[h]) + f32(land_cross[h])

    return settle, total


def opening_body(
    rows_ref, pack_in, b_ref, base_ref, pos_ref, ffn_in, ffn_out, out_proj,
    out_ref, hid, act, slope, pack, w_rows, table, proj, w_out,
    w_in, part, send, land, cross, land_cross, send_sem, recv_sem, local_sem,
):
    batch = lax.axis_index("batch")
    links = Links(send_sem, recv_sem)
    fetch = Fetch(links, batch, local_sem)
    load = pltpu.make_async_copy(ffn_in.at[0], w_in, local_sem.at[0])
    load.start()
    links.greet([links.near, links.far, links.across, fetch.beside])
    small = [
        links.go(pack_in, pack.at[links.shard], device)
        for device in (links.far, links.across, links.near)
    ]
    down = fetch.rows(ffn_out.at[0], w_rows, 1, 4)
    down.pop(0)()
    pack[links.shard] = pack_in[...]
    for copy in small:
        copy.wait()
    rows, features = rows_ref.shape
    hid[0] = b16(norm_rows(rows_ref[...], vector_row(pack, 0), vector_row(pack, 6)))
    half = rows // 2
    out = [
        links.go(hid.at[0, pl.ds(h * half, half)], hid.at[2 + h, pl.ds(0, half)], links.far)
        for h in range(2)
    ]
    near = links.go(hid.at[0], hid.at[1], links.near)
    load.wait()

    def up(block):
        @tiles(w_in.shape[1], 512)
        def _(cols):
            pre = dot_rows(hid[block], w_in[:, cols]) + b_ref[0:1, cols]
            gate = jax.nn.sigmoid(pre)
            act[block, :, cols] = b16(pre * gate)
            slope[block, :, cols] = b16(gate * (1.0 + pre * (1.0 - gate)))

    up(0)
    down.pop(0)()
    near.wait()
    up(1)
    lanes = features // 2

    @pl.loop(0, table.shape[0] // 16)
    def _(i):
        at = pl.ds(pl.multiple_of(i * 16, 16), 16)
        s_a, c_a = base_ref[pl.ds(16 + i, 1), 0:lanes], base_ref[pl.ds(16 + i, 1), lanes:]
        s_b, c_b = base_ref[0:16, 0:lanes], base_ref[0:16, lanes:]
        table[at, 0:lanes] = b16(s_a * c_b + c_a * s_b)
        table[at, lanes:] = b16(c_a * c_b - s_a * s_b)

    proj[...] = b16(dot_rows(table[...], pos_ref[...]))
    down.pop(0)()
    other = fetch.columns(out_proj, w_out, 2)
    for h in range(2):
        out[h].wait()
        on = links.go(hid.at[2 + h, pl.ds(0, half)], hid.at[2 + h, pl.ds(half, half)], links.near)
        on.wait()
        up(2 + h)
        down.pop(0)()
        if h == 0:
            other.pop(0)()
    while down:
        down.pop(0)()
    other.pop(0)()

    def work(block, emit):
        @tiles(features, 512)
        def _(cols):
            emit(cols, dot_rows(act[block], w_rows[:, cols]))

    settle, total = scatter_late(links, work, part, send, land, cross, land_cross)
    while other:
        other.pop(0)()
    settle()
    bias = vector_row(pack, 7)
    for h in range(2):
        at = slice(h * half, (h + 1) * half)
        out_ref[at] = rows_ref[at] + 0.5 * (total(h) + bias)


ANY_SPEC = pl.BlockSpec(memory_space=pl.ANY)


def link_scratch(count, local):
    return [
        pltpu.SemaphoreType.DMA((count,)),
        pltpu.SemaphoreType.DMA((count,)),
        pltpu.SemaphoreType.DMA((local,)),
    ]


def opening(rows_in, pack_in, b_in, base, pos_proj, ffn_in, ffn_out, out_proj, ident):
    ns = lax.axis_size("shard")
    rows, features = rows_in.shape
    hidden = ffn_in.shape[2]
    shape = jax.ShapeDtypeStruct
    low = jnp.bfloat16
    positions = 2 * rows
    return pl.pallas_call(
        opening_body,
        out_shape=[
            shape((rows, features), jnp.float32),
            shape((4, rows, features), low), shape((4, rows, hidden), low), shape((4, rows, hidden), low),
            shape((ns,) + pack_in.shape, low),
            shape((hidden, features), low),
            shape((positions, features), low),
            shape((positions, pos_proj.shape[1]), low),
            shape((features, features), low),
        ],
        in_specs=[VMEM_SPEC] * 5 + [ANY_SPEC] * 3,
        out_specs=[VMEM_SPEC] * 8 + [ANY_SPEC],
        scratch_shapes=[pltpu.VMEM((features, hidden), low)]
        + gws_scratch(rows, features)[:5]
        + link_scratch(48, 4),
        compiler_params=pltpu.CompilerParams(
            collective_id=ident, has_side_effects=True, vmem_limit_bytes=40 << 20
        ),
        name="opening",
    )(rows_in, pack_in, b_in, base, pos_proj, ffn_in, ffn_out, out_proj)


def mix_body(
    heads, size, rows_ref, pack, own_ref, w_qkv, proj, w_out, conv_in,
    out_ref, hid, with_u, with_v, key, value, soft_ref, mix, wc_in,
    turned, send_sem, recv_sem, local_sem,
):
    batch = lax.axis_index("batch")
    links = Links(send_sem, recv_sem)
    fetch = Fetch(links, batch, local_sem)
    scale = 1.0 / math.sqrt(size)
    rows, features = rows_ref.shape
    half = rows // 2
    links.greet([links.near, links.far, links.across, fetch.beside])
    hid[0] = b16(norm_rows(rows_ref[...], vector_row(pack, 1), vector_row(pack, 8)))
    out = [
        links.go(hid.at[0, pl.ds(h * half, half)], hid.at[2, pl.ds(h * half, half)], links.far)
        for h in range(2)
    ]
    near = links.go(hid.at[0], hid.at[1], links.near)
    own = f32(own_ref[...])
    keys = f32(lax.broadcasted_iota(jnp.int32, (rows, rows), 1))

    def attend(slot):
        hidden = hid[slot]
        query = dot_rows(hidden, w_qkv[0]) + own[3:4]
        with_u[slot] = b16(query + own[6:7])
        with_v[slot] = b16(query + own[7:8])
        key[slot] = b16(dot_rows(hidden, w_qkv[1]))
        value[slot] = b16(dot_rows(hidden, w_qkv[2]) + own[4:5])
        live = f32(pack[flip_bits(links.shard, slot), 27:28, 0:1])
        for h in range(heads):
            cols = slice(h * size, (h + 1) * size)
            wide = dot_back(with_v[slot, :, cols], proj[:, cols])
            moved = pltpu.roll(wide, rows + 1, 1, stride=1, stride_axis=0)[:, :rows]
            raw = dot_back(with_u[slot, :, cols], key[slot, :, cols]) + moved
            scores = jnp.where(keys < live, raw * scale, -1e30)
            grown = jnp.exp(scores - jnp.max(scores, axis=-1, keepdims=True))
            soft = grown / jnp.sum(grown, axis=-1, keepdims=True)
            soft_ref[slot, :, h * rows : (h + 1) * rows] = soft
            mix[slot, :, cols] = b16(dot_rows(b16(soft), value[slot, :, cols]))

    last = []
    attend(0)
    turned[links.shard] = mix[0]
    near.wait()
    attend(1)
    last.append(links.go(mix.at[1], turned.at[links.shard], links.near))
    on = []
    for h in range(2):
        out[h].wait()
        part = hid.at[2, pl.ds(h * half, half)]
        on.append(links.go(part, hid.at[3, pl.ds(h * half, half)], links.near))
    other = fetch.columns(conv_in, wc_in, 0)
    other.pop(0)()
    attend(2)
    last.append(links.go(mix.at[2], turned.at[links.shard], links.far))
    for copy in on:
        copy.wait()
    attend(3)
    last.append(links.go(mix.at[3], turned.at[links.shard], links.across))
    other.pop(0)()
    for copy in last:
        copy.wait()
    bias = vector_row(pack, 11)
    width = mix.shape[2]
    total = rows_ref[...] + bias
    for t in range(turned.shape[0]):
        total = total + dot_rows(turned[t], w_out[t * width : (t + 1) * width])
    out_ref[...] = total
    while other:
        other.pop(0)()


def mix_forward(rows_in, pack, own_biases, qkv_proj, proj, w_out, conv_in, heads, ident):
    ns = lax.axis_size("shard")
    rows, features = rows_in.shape
    width = features // ns
    shape = jax.ShapeDtypeStruct
    low = jnp.bfloat16
    narrow = shape((ns, rows, width), low)
    return pl.pallas_call(
        functools.partial(mix_body, heads, width // heads),
        out_shape=[
            shape((rows, features), jnp.float32), shape((ns, rows, features), low),
            narrow, narrow, narrow, narrow,
            shape((ns, rows, heads * rows), jnp.float32),
            narrow,
            shape((conv_in.shape[0], ns * conv_in.shape[1]), low),
        ],
        in_specs=[VMEM_SPEC] * 6 + [ANY_SPEC],
        out_specs=[VMEM_SPEC] * 8 + [ANY_SPEC],
        scratch_shapes=[pltpu.VMEM((ns, rows, width), low)] + link_scratch(16, 2),
        compiler_params=pltpu.CompilerParams(
            collective_id=ident, has_side_effects=True, vmem_limit_bytes=40 << 20
        ),
        name="mix_forward",
    )(rows_in, pack, own_biases, qkv_proj, proj, w_out, conv_in)


def pack_rows(ref, at, row):
    for i in range(row.shape[1] // 128):
        ref[at + i : at + i + 1, :] = row[:, i * 128 : (i + 1) * 128]


def unpack_rows(value, at, lanes):
    return jnp.concatenate([value[at + i : at + i + 1, :] for i in range(lanes)], 1)


def everywhere(links, nb, source, mid, land_s, land_b, result, small, sems):
    s, b = links.shard, lax.axis_index("batch")
    ns = land_s.shape[0]
    ss, rs, sb, rb = sems
    first = exchange("shard", s, ns, source, land_s, ss, rs)
    for copy in first:
        copy.start()
    land_s[s] = source[...]
    for copy in first:
        copy.wait()
    mid[...] = sum_slots(land_s, ns)
    second = exchange("batch", b, nb, mid, land_b, sb, rb)
    for copy in second:
        copy.start()
    land_b[b] = mid[...]
    small()
    for copy in second:
        copy.wait()
    return sum_slots(land_b, nb)


def conv_body(
    nb, rows_ref, pack, w_in, conv_out, ffn_out,
    out_ref, hid, open_ref, gate_ref, gated_ref, scaled_ref, act, slope, stats, w_out, w_rows,
    padded, source, mid, land_s, land_b, ss, rs, sb, rb, send_sem, recv_sem, local_sem,
):
    batch = lax.axis_index("batch")
    links = Links(send_sem, recv_sem)
    fetch = Fetch(links, batch, local_sem)
    rows, features = rows_ref.shape
    ns = land_s.shape[0]
    links.greet(
        [links.near, links.far, links.across]
        + [{"batch": lax.rem(batch + j, nb)} for j in range(1, nb)]
    )
    out_fetch = fetch.columns(conv_out, w_out, 0)
    out_fetch.pop(0)()
    live = f32(pack[links.shard, 27:28, 0:1])
    mask = f32(f32(lax.broadcasted_iota(jnp.int32, (rows, 1), 0)) < live)
    hid[...] = b16(norm_rows(rows_ref[...], vector_row(pack, 2), vector_row(pack, 14)))
    bias_v, bias_g = vector_row(pack, 15), vector_row(pack, 16)
    lead = 8
    tile = 512
    padded[0:lead, :] = jnp.zeros((lead, features), jnp.float32)
    padded[lead + rows :, :] = jnp.zeros((lead, features), jnp.float32)
    for n in range(features // tile):
        cols = slice(n * tile, (n + 1) * tile)
        left = dot_rows(hid[...], w_in[:, cols]) + bias_v[:, cols]
        right = dot_rows(hid[...], w_in[:, features + n * tile : features + (n + 1) * tile])
        gate = jax.nn.sigmoid(right + bias_g[:, cols])
        opened = gate * mask
        gated = left * opened
        open_ref[:, cols] = b16(opened)
        gate_ref[:, cols] = b16(gated * (1.0 - gate))
        gated_ref[:, cols] = b16(gated)
        padded[lead : lead + rows, cols] = gated
    out_fetch.pop(0)()
    down = fetch.rows(ffn_out.at[1], w_rows, 1, 1)
    down.pop(0)()
    taps = 5
    total = 0.0
    for k in range(taps):
        at = lead - (taps - 1) // 2 + k
        total = total + padded[at : at + rows, :] * vector_row(pack, 22 + k)
    live_total = total * mask
    lanes = features // 128
    pack_rows(source, 0, jnp.sum(live_total, axis=0, keepdims=True))
    pack_rows(source, lanes, jnp.sum(live_total * total, axis=0, keepdims=True))
    source[2 * lanes : 2 * lanes + 8, :] = jnp.broadcast_to(live, (8, 128))
    scaled_ref[...] = total

    sums = everywhere(links, nb, source, mid, land_s, land_b, None, out_fetch.pop(0), (ss, rs, sb, rb))
    frames = sums[2 * lanes : 2 * lanes + 1, 0:1]
    mean = unpack_rows(sums, 0, lanes) / frames
    inverse = lax.rsqrt(unpack_rows(sums, lanes, lanes) / frames - mean * mean + epsilon)
    stats[0:1, :] = inverse
    stats[1:2, :] = jnp.broadcast_to(frames, (1, features))
    stats[2:8, :] = jnp.zeros((6, features), jnp.float32)
    scaled = (scaled_ref[...] - mean) * inverse
    scaled_ref[...] = scaled
    normed = scaled * vector_row(pack, 3) + vector_row(pack, 17)
    gate = jax.nn.sigmoid(normed)
    act[...] = b16(normed * gate)
    slope[...] = b16(gate * (1.0 + normed * (1.0 - gate)))
    out_fetch.pop(0)()
    down.pop(0)()
    out_ref[...] = rows_ref[...] + (dot_rows(act[...], w_out[...]) + vector_row(pack, 18))
    down.pop(0)()


def conv_forward(rows_in, pack, w_in, conv_out, ffn_out, ident):
    ns, nb = lax.axis_size("shard"), lax.axis_size("batch")
    rows, features = rows_in.shape
    shape = jax.ShapeDtypeStruct
    low, full = jnp.bfloat16, jnp.float32
    plain = shape((rows, features), low)
    small = (24, 128)
    return pl.pallas_call(
        functools.partial(conv_body, nb),
        out_shape=[
            shape((rows, features), full), plain, plain, plain, plain,
            shape((rows, features), full), plain, plain, shape((8, features), full),
            shape((features, features), low),
            shape((ffn_out.shape[1] // ns, features), low),
        ],
        in_specs=[VMEM_SPEC] * 3 + [ANY_SPEC] * 2,
        out_specs=[VMEM_SPEC] * 10 + [ANY_SPEC],
        scratch_shapes=[
            pltpu.VMEM((rows + 16, features), full),
            pltpu.VMEM(small, full), pltpu.VMEM(small, full),
            pltpu.VMEM((ns,) + small, full), pltpu.VMEM((nb,) + small, full),
            pltpu.SemaphoreType.DMA((ns,)), pltpu.SemaphoreType.DMA((ns,)),
            pltpu.SemaphoreType.DMA((nb,)), pltpu.SemaphoreType.DMA((nb,)),
        ]
        + link_scratch(16, 3),
        compiler_params=pltpu.CompilerParams(
            collective_id=ident, has_side_effects=True, vmem_limit_bytes=40 << 20
        ),
        name="conv_forward",
    )(rows_in, pack, w_in, conv_out, ffn_out)


def conv_back_body(
    nb, stream_ref, rows_ref, pack, w_in, w_out, hid, open_ref, gate_ref, gated_ref, scaled_ref, act, slope, stats,
    ride_a, ride_b, out_ref, gw_out, gw_in, sums_ref, half_a, half_b,
    padded, normed, grad, inner, source, mid, land_s, land_b, ss, rs, sb, rb, send_sem, recv_sem,
):
    batch = lax.axis_index("batch")
    links = Links(send_sem, recv_sem)
    rows, features = rows_ref.shape
    links.greet(
        [links.near, links.far, links.across]
        + [{"batch": lax.rem(batch + j, nb)} for j in range(1, nb)]
    )
    orders = ride_orders(nb)
    ride = [
        Rider(batch, send_sem, recv_sem, at).halve(source_ref, landing, orders[at][0])
        for at, (source_ref, landing) in enumerate(((ride_a, half_a), (ride_b, half_b)))
    ]
    lanes = features // 128
    lead, tile, taps = 8, 512, 5
    grad[...] = b16(stream_ref[...])
    gain = vector_row(pack, 3)
    sums_ref[...] = jnp.zeros_like(sums_ref)
    for n in range(features // tile):
        cols = slice(n * tile, (n + 1) * tile)
        value = dot_back(grad[...], w_out[cols, :]) * f32(slope[:, cols])
        normed[:, cols] = value
        for at, total in (
            (0, jnp.sum(value, axis=0, keepdims=True)),
            (lanes, jnp.sum(value * scaled_ref[:, cols], axis=0, keepdims=True)),
        ):
            for i in range(tile // 128):
                row = at + n * (tile // 128) + i
                source[row : row + 1, :] = total[:, i * 128 : (i + 1) * 128]

    def meanwhile():
        @tiles(features, 256)
        def _(cols):
            gw_out[cols, :] = b16(dot_over(act[:, cols], grad[...]))

        sums_ref[4:5, :] = jnp.sum(f32(grad[...]), axis=0, keepdims=True)

    sums = everywhere(links, nb, source, mid, land_s, land_b, None, meanwhile, (ss, rs, sb, rb))
    beta, gamma = unpack_rows(sums, 0, lanes), unpack_rows(sums, lanes, lanes)
    sums_ref[5:6, :] = gamma
    sums_ref[6:7, :] = beta
    inverse, frames = stats[0:1, :], stats[1:2, 0:1]
    live = f32(pack[links.shard, 27:28, 0:1])
    mask = f32(f32(lax.broadcasted_iota(jnp.int32, (rows, 1), 0)) < live)
    padded[0:lead, :] = jnp.zeros((lead, features), jnp.float32)
    padded[lead + rows :, :] = jnp.zeros((lead, features), jnp.float32)
    padded[lead : lead + rows, :] = inverse * (
        normed[...] * gain - mask * (gain * beta + scaled_ref[...] * (gain * gamma)) / frames
    )
    given = 0.0
    gated = f32(gated_ref[...])
    for k in range(taps):
        at = lead + (taps - 1) // 2 - k
        moved = padded[at : at + rows, :]
        given = given + moved * vector_row(pack, 22 + k)
        sums_ref[8 + k : 9 + k, :] = jnp.sum(moved * gated, axis=0, keepdims=True)
    left = b16(given * f32(open_ref[...]))
    right = b16(given * f32(gate_ref[...]))
    inner[:, 0:features] = left
    inner[:, features:] = right
    sums_ref[2:3, :] = jnp.sum(f32(left), axis=0, keepdims=True)
    sums_ref[3:4, :] = jnp.sum(f32(right), axis=0, keepdims=True)
    total = dot_back(inner[...], w_in[...])
    scaled, inverse = norm_parts(rows_ref[...])
    out_ref[...] = stream_ref[...] + norm_slope(total, scaled, inverse, vector_row(pack, 2))
    sums_ref[0:1, :] = jnp.sum(total * scaled, axis=0, keepdims=True)
    sums_ref[1:2, :] = jnp.sum(total, axis=0, keepdims=True)

    @tiles(2 * features, 512)
    def _(cols):
        gw_in[:, cols] = b16(dot_over(hid[...], inner[:, cols]))

    for end in ride:
        end()


def conv_back(stream, rows_in, pack, w_in, w_out, saved, ridden, ident):
    ns, nb = lax.axis_size("shard"), lax.axis_size("batch")
    rows, features = rows_in.shape
    shape = jax.ShapeDtypeStruct
    low, full = jnp.bfloat16, jnp.float32
    small = (2 * features // 128, 128)
    return pl.pallas_call(
        functools.partial(conv_back_body, nb),
        out_shape=[
            shape((rows, features), full), shape((features, features), low),
            shape((features, 2 * features), low), shape((16, features), full),
        ]
        + [shape((r.shape[0] // 2, r.shape[1]), low) for r in ridden],
        in_specs=[VMEM_SPEC] * 15,
        out_specs=[VMEM_SPEC] * 6,
        scratch_shapes=[
            pltpu.VMEM((rows + 16, features), full), pltpu.VMEM((rows, features), full),
            pltpu.VMEM((rows, features), low), pltpu.VMEM((rows, 2 * features), low),
            pltpu.VMEM(small, full), pltpu.VMEM(small, full),
            pltpu.VMEM((ns,) + small, full), pltpu.VMEM((nb,) + small, full),
            pltpu.SemaphoreType.DMA((ns,)), pltpu.SemaphoreType.DMA((ns,)),
            pltpu.SemaphoreType.DMA((nb,)), pltpu.SemaphoreType.DMA((nb,)),
        ]
        + link_scratch(4, 1)[:2],
        compiler_params=pltpu.CompilerParams(
            collective_id=ident, has_side_effects=True, vmem_limit_bytes=48 << 20
        ),
        name="conv_back",
    )(stream, rows_in, pack, w_in, w_out, *saved, *ridden)


def mix_back_body(
    heads, size, nb, stream_ref, rows_ref, pack, hid, with_u, with_v, key, value, soft_ref, mix, table, proj,
    w_qkv, w_out, ride_a, ride_b, out_ref, gw_qkv, gw_pos, gw_out, sums_ref, own_sums, out_a, out_b,
    grad, dq, dk, dx, dp, part, send, land, cross, land_cross, send_sem, recv_sem, ride_send, ride_recv, *between,
):
    links = Links(send_sem, recv_sem)
    batch = lax.axis_index("batch")
    orders = ride_orders(nb)
    steps = len(orders[0]) - 1
    scale = 1.0 / math.sqrt(size)
    rows, features = rows_ref.shape
    half = rows // 2
    width = mix.shape[2]
    links.greet([links.near, links.far] + [{"batch": flip_bits(batch, 1 << k)} for k in orders[0]])
    stages = []
    for at, (start, end) in enumerate(((ride_a, out_a), (ride_b, out_b))):
        rider = Rider(batch, ride_send, ride_recv, at * steps)
        middle = between[at * (steps - 1) : (at + 1) * (steps - 1)]
        stages.append(rider.chain([start, *middle, end], orders[at][1:], rider.halve))

    def tick():
        for chain in stages:
            if chain:
                chain.pop(0)()

    tick()
    grad[0] = b16(stream_ref[...])
    out = [
        links.go(grad.at[0, pl.ds(h * half, half)], grad.at[2, pl.ds(h * half, half)], links.far)
        for h in range(2)
    ]
    near = links.go(grad.at[0], grad.at[1], links.near)
    at_row = lax.broadcasted_iota(jnp.int32, (rows, rows), 0)
    at_col = lax.broadcasted_iota(jnp.int32, (rows, rows), 1)
    flip = b16(f32(at_row + at_col == rows - 1))
    keys = f32(at_col)
    mine = pl.ds(pl.multiple_of(links.shard * width, 16), width)
    own_sums[...] = jnp.zeros_like(own_sums)

    def work(slot, emit):
        mixed = b16(dot_back(grad[slot], w_out[mine, :]))
        live = f32(pack[flip_bits(links.shard, slot), 27:28, 0:1])
        for h in range(heads):
            cols = slice(h * size, (h + 1) * size)
            soft = soft_ref[slot, :, h * rows : (h + 1) * rows]
            given = mixed[:, cols]
            grad_soft = dot_back(given, value[slot, :, cols])
            dx[slot, :, cols] = b16(dot_over(b16(soft), given))
            grad_scores = soft * (grad_soft - jnp.sum(grad_soft * soft, axis=-1, keepdims=True))
            raw = b16(jnp.where(keys < live, grad_scores, 0.0) * scale)
            grad_u = dot_rows(raw, key[slot, :, cols])
            dk[slot, :, cols] = b16(dot_over(raw, with_u[slot, :, cols]))
            turned = dot_rows(flip, raw)
            wide = jnp.concatenate([turned, jnp.zeros_like(turned)], 1)
            wide = b16(pltpu.roll(wide, 0, 1, stride=1, stride_axis=0))
            grad_v = dot_rows(wide, proj[:, cols])
            v_turned = b16(dot_rows(flip, with_v[slot, :, cols]))
            dp[slot, :, cols] = b16(dot_over(wide, v_turned))
            own_sums[2:3, cols] += jnp.sum(grad_u, axis=0, keepdims=True)
            own_sums[3:4, cols] += jnp.sum(grad_v, axis=0, keepdims=True)
            high = b16(grad_v)
            rest = b16(grad_v - f32(high))
            dq[slot, :, cols] = b16(grad_u + (dot_rows(flip, high) + dot_rows(flip, rest)))
        own_sums[0:1, :] += jnp.sum(f32(dq[slot]), axis=0, keepdims=True)
        own_sums[1:2, :] += jnp.sum(f32(dx[slot]), axis=0, keepdims=True)

        @tiles(features, 512)
        def _(cols):
            emit(
                cols,
                dot_back(dq[slot], w_qkv[0, cols, :])
                + dot_back(dk[slot], w_qkv[1, cols, :])
                + dot_back(dx[slot], w_qkv[2, cols, :]),
            )

    def keep(cols, value):
        part[0, :, cols] = value

    def keep_far(cols, value):
        part[1, :, cols] = value

    def give(cols, value):
        send[0, :, cols] = b16(value[:half])
        send[1, :, cols] = b16(value[half:])

    def give_far(cols, value):
        send[2, :, cols] = b16(value[:half])
        send[3, :, cols] = b16(value[half:])

    work(0, keep)
    near.wait()
    work(1, give)
    last = [links.go(send.at[pl.ds(0, 2)], land.at[pl.ds(0, 2)], links.near)]
    on = []
    for h in range(2):
        out[h].wait()
        there = pl.ds(h * half, half)
        on.append(links.go(grad.at[2, there], grad.at[3, there], links.near))
    for copy in on:
        copy.wait()
    tick()
    work(3, give_far)
    back = links.go(send.at[pl.ds(2, 2)], land.at[pl.ds(2, 2)], links.near)
    work(2, keep_far)
    back.wait()
    for h in range(2):
        cross[h] = b16(part[1, h * half : (h + 1) * half] + f32(land[2 + h]))
        last.append(links.go(cross.at[h], land_cross.at[h], links.far))
    flat = lambda ref: ref[...].reshape(4 * rows, ref.shape[2])
    for at, ref in enumerate((dq, dk, dx)):
        right = flat(ref)

        @tiles(features, 256)
        def _(cols, at=at, right=right):
            left = hid[:, :, cols].reshape(4 * rows, 256)
            gw_qkv[at, cols, :] = b16(dot_over(left, right))

    @tiles(features, 256)
    def _(cols):
        total = dot_over(table[:, cols], dp[0])
        for slot in range(1, 4):
            total = total + dot_over(table[:, cols], dp[slot])
        gw_pos[cols, :] = b16(total)

    gw_out[...] = b16(dot_over(flat(mix), flat(grad)))
    for copy in last:
        copy.wait()
    for chain in stages:
        while chain:
            chain.pop(0)()
    sums_ref[...] = jnp.zeros_like(sums_ref)
    sums_ref[2:3, :] = jnp.sum(f32(grad[0]), axis=0, keepdims=True)
    gain = vector_row(pack, 1)
    for h in range(2):
        at = slice(h * half, (h + 1) * half)
        given = part[0, at] + f32(land[h]) + f32(land_cross[h])
        scaled, inverse = norm_parts(rows_ref[at])
        out_ref[at] = stream_ref[at] + norm_slope(given, scaled, inverse, gain)
        sums_ref[0:1, :] += jnp.sum(given * scaled, axis=0, keepdims=True)
        sums_ref[1:2, :] += jnp.sum(given, axis=0, keepdims=True)


def mix_back(stream, rows_in, pack, saved, table, proj, w_qkv, w_out, ridden, heads, ident):
    rows, features = rows_in.shape
    hid, with_u, with_v, key, value, soft, mix = saved
    width = mix.shape[2]
    shape = jax.ShapeDtypeStruct
    low, full = jnp.bfloat16, jnp.float32
    narrow = pltpu.VMEM((4, rows, width), low)
    nb = lax.axis_size("batch")
    steps = nb.bit_length() - 2
    dma = pltpu.SemaphoreType.DMA((2 * steps,))
    between = []
    for r in ridden:
        between += [pltpu.VMEM((r.shape[0] >> k, r.shape[1]), low) for k in range(1, steps)]
    return pl.pallas_call(
        functools.partial(mix_back_body, heads, width // heads, nb),
        out_shape=[
            shape((rows, features), full), shape((3, features, width), low), shape((features, width), low),
            shape((width, features), low), shape((8, features), full), shape((8, width), full),
        ]
        + [shape((r.shape[0] >> steps, r.shape[1]), low) for r in ridden],
        in_specs=[VMEM_SPEC] * 16,
        out_specs=[VMEM_SPEC] * 8,
        scratch_shapes=[
            pltpu.VMEM((4, rows, features), low), narrow, narrow, narrow,
            pltpu.VMEM((4, 2 * rows, width), low),
        ]
        + gws_scratch(rows, features)
        + [dma, dma]
        + between,
        compiler_params=pltpu.CompilerParams(
            collective_id=ident, has_side_effects=True, vmem_limit_bytes=48 << 20
        ),
        name="mix_back",
    )(stream, rows_in, pack, *saved, table, proj, w_qkv, w_out, *ridden)


def body(
    tokens, cotangent, lengths, ffn_in, ffn_out, ffn_bias, qkv_proj, pos_proj, out_proj,
    conv_in, conv_out, depthwise, norm_gains, biases,
):
    _, length, features = tokens.shape
    ns, nb = lax.axis_size("shard"), lax.axis_size("batch")
    width = features // ns
    heads = HEADS // ns
    rows_in = tokens[0]

    own_length = jnp.broadcast_to(b16(f32(lengths))[:, None], (5, width))
    pack_in = jnp.concatenate([norm_gains, biases, depthwise, own_length], 0)
    b_in = f32(ffn_bias)

    rates = jnp.exp(
        jnp.arange(features // 2, dtype=jnp.float32) * (-2.0 * math.log(10000.0) / features)
    )
    turns = jnp.concatenate(
        [
            length - 1.0 - jnp.arange(16, dtype=jnp.float32),
            -16.0 * jnp.arange(2 * length // 16, dtype=jnp.float32),
        ]
    )
    angles = turns[:, None] * rates[None, :]
    base = jnp.concatenate([jnp.sin(angles), jnp.cos(angles)], 1)
    rows_one, *saved_one, pack, w_rows_one, table, proj, w_out = opening(
        rows_in, pack_in, b_in, base, pos_proj, ffn_in, ffn_out, out_proj, 5
    )
    rows_two, hid, with_u, with_v, key, value, soft, mix, wc_in = mix_forward(
        rows_one, pack, biases, qkv_proj, proj, w_out, conv_in, heads, 9
    )
    saved_mix = (hid, with_u, with_v, key, value, soft, mix)
    rows_three, *saved_conv, wc_out, w_rows_two = conv_forward(
        rows_two, pack, wc_in, conv_out, ffn_out, 10
    )
    rows_four, saved_two = ffn_forward(
        rows_three, pack, b_in, w_rows_two, ffn_in, 1, (4, 19, 20), 6
    )

    result, stream, two_in, two_out, two_sums = ffn_back(
        (rows_four, cotangent[0]), rows_three, pack, saved_two, w_rows_two, ffn_in, 1, 4, 7
    )
    stream, grad_conv_out, grad_conv_in, conv_sums, *ridden = conv_back(
        stream, rows_two, pack, wc_in, wc_out, saved_conv, (two_in, two_out), 11
    )
    stream, grad_qkv, grad_pos, grad_out, mix_sums, own_sums, *ridden = mix_back(
        stream, rows_one, pack, saved_mix, table, proj, qkv_proj, w_out, ridden, heads, 12
    )
    stream, one_in, one_out, one_sums, *ridden = ffn_back(
        (stream, *ridden), rows_in, pack, saved_one, w_rows_one, ffn_in, 0, 0, 8
    )
    tall, deep = one_in.shape
    piece = max(256, 8 * nb)
    *sums, out_gains, out_biases, out_taps, out_hidden = tail_sum(
        [grad_out, one_out, one_in] + [grad_qkv[at] for at in range(3)] + [grad_pos, grad_conv_in, grad_conv_out],
        ridden,
        [one_sums, mix_sums, two_sums, conv_sums, own_sums],
        [("turn", 4, None), ("turn", 1, 0), ("plain", 0, 0)]
        + [("plain", 2, at) for at in range(3)]
        + [("plain", 3, None), ("gather", 5, None), ("gather", 6, None)],
        [
            (2, tall, deep), (2, ns * deep, width), (3, tall, width), (tall, width), (tall, width),
            (tall, 2 * width), (tall, width),
        ],
        ["near", "line"],
        [width, piece, piece, tall, tall, tall, tall, 2 * piece, tall],
        deep,
        4,
    )
    return (
        result[None],
        stream[None],
        f32(sums[0]),
        f32(sums[1]),
        out_hidden,
        f32(sums[2]),
        f32(sums[3]),
        f32(sums[4]),
        f32(sums[5]),
        f32(sums[6]),
        out_taps,
        out_gains,
        out_biases,
    )


def solution(mesh):
    rows = P(("batch", "shard"), None, None)
    cube, flat = P(None, None, "shard"), P(None, "shard")
    return jax.shard_map(
        body,
        mesh=mesh,
        in_specs=(rows, rows, P(("batch", "shard")), cube, cube, flat, cube)
        + (flat,) * 7,
        out_specs=(rows, rows, cube, cube, flat, cube) + (flat,) * 7,
        check_vma=False,
    )
```

time: 804 us -> 654 us (0.81)
  Pallas kernels: 512 us -> 590 us
  blocking collectives: 69.1 us -> 0 us
  matrix products: 43 us -> 0 us
  local copies, waits for them, and re-layouts: 75.2 us -> 34.7 us
  other arithmetic: 43.8 us -> 19.4 us
  waiting for transfers between devices: 22.2 us -> 0 us
  between operations: 16.7 us -> 2.12 us
  starting transfers between devices: 11.2 us -> 0 us
    pallas_call x12 -> x9, Pallas kernels: 512 us -> 590 us  [the longest x1 248 us: tail_sum(): pl.pallas_call(functools.partial(tail_body, specs, chunks, ns, nb, len(ar...]
    all_gather x1 -> x0, blocking collectives: 69.1 us -> none  [body(): packed = f32(lax.all_gather(packed, 'shard', axis=1, tiled=True))]
    dot_general x32 -> x0, matrix products: 43 us -> none  [the longest x13 19.1 us: dot_over(): lax.dot_general(a, b, (((0,), (0,)), ((), ())), preferred_element_type=jn...]
    ppermute x18 -> x0, waiting for transfers between devices: 20.7 us -> none  [swap(): return lax.ppermute(x, axis, [(i, i ^ mask) for i in range(n)])]
    reduce_sum x21 -> x0, other arithmetic: 18.5 us -> none  [the longest x1 6 us: depth_conv(): summed = summed + padded[tap_index:tap_index + length] * kernel[tap_index]]
    convert_element_type x2 -> x8, other arithmetic: 0.01 us -> 18.1 us  [f32(): return a.astype(jnp.float32)]
    unnamed x207 -> x116, local copies, waits for them, and re-layouts: 47.8 us -> 33.5 us
    slice x23 -> x0, local copies, waits for them, and re-layouts: 12.9 us -> none  [the longest x1 2.49 us: body(): w_rows = [to_rows(ffn_out[0], shard), to_rows(ffn_out[1], shard)]]
  transfers between devices with their start and end apart: 24 -> 0, of which waited for: 5 -> 0; matrix products, arithmetic and copies ran while one was open for 13% -> 0% of each run, Pallas kernels for 17% -> 0%
where the time goes in v4:
time: 654 us; the launch traced here: 646 us
  Pallas kernels  590 us (90%)
  local copies, waits for them, and re-layouts  34.7 us (5%)
  other arithmetic  19.4 us (3%)
    pallas_call x1, Pallas kernels, tail_sum(): pl.pallas_call(functools.partial(tail_body, specs, chunks, ns, nb, len(ar...  248 us
    pallas_call x2, Pallas kernels, ffn_back(): pl.pallas_call(functools.partial(ffn_back_body, which, gain_at, nb), out_...  79.9 us
    pallas_call x1, Pallas kernels, opening(): pl.pallas_call(opening_body, out_shape=[shape((rows, features), jnp.float...  53.1 us
    pallas_call x1, Pallas kernels, conv_forward(): pl.pallas_call(functools.partial(conv_body, nb), out_shape=[shape((rows,...  48.5 us
    pallas_call x1, Pallas kernels, mix_back(): pl.pallas_call(functools.partial(mix_back_body, heads, width // heads, nb...  46.7 us
    pallas_call x1, Pallas kernels, conv_back(): pl.pallas_call(functools.partial(conv_back_body, nb), out_shape=[shape((r...  42.7 us
    pallas_call x1, Pallas kernels, mix_forward(): pl.pallas_call(functools.partial(mix_body, heads, width // heads), out_sh...  41.2 us
    unnamed x116, local copies, waits for them, and re-layouts  33.5 us

profile of v4, /device:TPU:0, one launch (start us, length us, event | category | flops | bytes accessed | tf_op | source)
XLA Modules:
  0.0 646.0 jit_solution(5543556585324239021)
XLA Ops:
  1.3 0.1 pad.7.clone
  1.4 0.1 pad_maximum_fusion.1
  1.5 0.7 convert_element_type.32.b_ref
  2.2 0.8 maximum_maximum_fusion.pack_in
  3.0 0.4 multiply_sine_fusion
  3.4 0.0 copy-start.4
  3.4 1.2 copy-done.4
  4.7 1.0 copy-done.28
  5.7 1.0 copy-done.29
  6.7 53.1 %opening.1 = (f32[256,1024]{1,0:T(8,128)S(1)}, bf16[4,256,1024]{2,1,0:T(8,128)(2,1)S(1)}, bf16[4,256,1024]{2,1,0:T(8,128)(2,1)S(1)}, bf16[4,256,1024]{2,1,0:T(8,...) custom-call(f32[256,1024]{1,0:T(8,128)S(1)} %bitcast.11, ...), custom_call_target="tpu_custom_call" | custom-call | tf_op jit(solution)/shard_map/opening/pallas_call | solution.py:1040
  59.9 1.3 copy-done.12
  61.2 1.4 copy-done.13
  62.6 1.3 copy-done.14
  63.9 1.3 copy-done.15
  65.2 1.0 copy-done.25
  66.2 0.0 copy-done.2
  66.2 2.0 copy-done.1
  68.2 41.2 %mix_forward.1 = (f32[256,1024]{1,0:T(8,128)S(1)}, bf16[4,256,1024]{2,1,0:T(8,128)(2,1)S(1)}, bf16[4,256,256]{2,1,0:T(8,128)(2,1)S(1)}, bf16[4,256,256]{2,1,0:T(...) custom-call(f32[256,1024]{1,0:T(8,128)S(1)} %get-tuple-element.82.ro, ...), custom_call_target="tpu_custom_call" | custom-call | tf_op jit(solution)/shard_map/mix_forward/pallas_call | solution.py:1142
  109.4 1.4 copy-done.7
  110.7 48.5 %conv_forward.1 = (f32[256,1024]{1,0:T(8,128)S(1)}, bf16[256,1024]{1,0:T(8,128)(2,1)S(1)}, bf16[256,1024]{1,0:T(8,128)(2,1)S(1)}, bf16[256,1024]{1,0:T(8,128)(2,...) custom-call(f32[256,1024]{1,0:T(8,128)S(1)} %get-tuple-element.86.ro, ...), custom_call_target="tpu_custom_call" | custom-call | tf_op jit(solution)/shard_map/conv_forward/pallas_call | solution.py:1267
  159.2 1.3 copy-done.16
  160.6 0.8 copy-done.33
  161.3 0.8 copy-done.35
  162.1 0.8 copy-done.37
  162.9 29.3 %ffn_forward.1 = (f32[256,1024]{1,0:T(8,128)S(1)}, bf16[4,256,1024]{2,1,0:T(8,128)(2,1)S(1)}, bf16[4,256,1024]{2,1,0:T(8,128)(2,1)S(1)}, bf16[4,256,1024]{2,1,0:T(8,128)(2,1)S(1)}) custom-call(f32[256,1024]{1,0:T(8,128)S(1)} %get-tuple-element.88.rows_ref.refs_2_, bf16[4,32,256]{2,1,0:T(8,128)(2,1)S(1)} %get-tuple-element.83.pack.refs_3_.refs_4_, ...), custom_call_target="tpu_custom_call" | custom-call | tf_op jit(solution)/shard_map/ffn_forward/pallas_call | solution.py:629
  192.3 0.0 copy-start.9
  192.3 1.3 copy-done.9
  193.6 1.3 copy-done.10
  194.9 1.3 copy-done.11
  196.3 34.9 %ffn_back_1.1 = (f32[256,1024]{1,0:T(8,128)S(1)}, f32[256,1024]{1,0:T(8,128)S(1)}, bf16[1024,1024]{1,0:T(8,128)(2,1)}, bf16[1024,1024]{1,0:T(8,128)(2,1)}, f32[8,1024]{1,0:T(8,128)S(1)}) custom-call(f32[256,1024]{1,0:T(8,128)S(1)} %get-tuple-element.90.refs_0_, f32[256,1024]{1,0:T(8,128)S(1)} %bitcast.15, ...), custom_call_target="tpu_custom_call" | custom-call | tf_op jit(solution)/shard_map/ffn_back_1/pallas_call | solution.py:785
  231.2 0.0 copy-start.20
  231.2 1.0 copy-done.20
  232.1 42.7 %conv_back.1 = (f32[256,1024]{1,0:T(8,128)S(1)}, bf16[1024,1024]{1,0:T(8,128)(2,1)}, bf16[1024,2048]{1,0:T(8,128)(2,1)}, f32[16,1024]{1,0:T(8,128)S(1)}, bf16[51...) custom-call(f32[256,1024]{1,0:T(8,128)} %copy-done.20, f32[256,1024]{1,0:T(8,128)} %copy-done.3, ...), custom_call_target="tpu_custom_call" | custom-call | tf_op jit(solution)/shard_map/conv_back/pallas_call | solution.py:1378
  274.9 0.0 copy-done.40
  274.9 0.0 copy-start.26
  274.9 1.0 copy-done.26
  275.9 1.0 copy-done.27
  276.9 46.7 %mix_back.1 = (f32[256,1024]{1,0:T(8,128)S(1)}, bf16[3,1024,256]{2,1,0:T(8,128)(2,1)}, bf16[1024,256]{1,0:T(8,128)(2,1)S(1)}, bf16[256,1024]{1,0:T(8,128)(2,1)S(...) custom-call(f32[256,1024]{1,0:T(8,128)} %copy-done.26, ...), custom_call_target="tpu_custom_call" | custom-call | tf_op jit(solution)/shard_map/mix_back/pallas_call | solution.py:1558
  323.6 0.0 copy-start.31
  323.6 0.0 copy-start.32
  323.6 0.0 copy-start.44
  323.7 45.0 %ffn_back_0.1 = (f32[256,1024]{1,0:T(8,128)S(1)}, bf16[1024,1024]{1,0:T(8,128)(2,1)}, bf16[1024,1024]{1,0:T(8,128)(2,1)}, f32[8,1024]{1,0:T(8,128)S(1)}, bf16[51...) custom-call(f32[256,1024]{1,0:T(8,128)S(1)} %get-tuple-element.118.refs_0_, ...), custom_call_target="tpu_custom_call" | custom-call | tf_op jit(solution)/shard_map/ffn_back_0/pallas_call | solution.py:785
  368.7 0.0 copy-start.17
  368.7 1.0 copy-done.17
  369.7 1.0 copy-done.18
  370.7 1.0 copy-done.21
  371.6 0.6 copy-done.42
  372.2 1.2 slice_bitcast_fusion
  373.4 248.3 %tail_sum.1 = (bf16[2,1024,1024]{2,1,0:T(8,128)(2,1)}, bf16[2,4096,256]{2,1,0:T(8,128)(2,1)}, bf16[3,1024,256]{2,1,0:T(8,128)(2,1)}, bf16[1024,256]{1,0:T(8,128)...) custom-call(bf16[256,1024]{1,0:T(8,128)(2,1)} %copy-done.32, ...), custom_call_target="tpu_custom_call" | custom-call | tf_op jit(solution)/shard_map/tail_sum/pallas_call | solution.py:482
  621.8 2.2 convert_element_type.36
  624.0 2.1 convert_element_type.37
  626.1 1.0 convert_element_type.39
  627.1 1.6 convert_element_type.38
  628.7 1.9 convert_element_type.35
  630.7 1.4 copy-done.46
  632.0 4.4 convert_element_type.33
  636.5 4.1 convert_element_type.34
  640.6 1.0 copy.34
  641.5 0.6 copy-done.22
  642.2 1.0 copy.35
  643.1 0.6 copy.36
  643.7 0.6 copy.37
  644.3 0.6 copy.38
  644.9 0.6 copy.39
  (79 shorter events, 0.2 us)
Async XLA Ops:
  3.4 1.2 copy-start.4
  4.7 1.0 copy-start.28
  5.7 1.0 copy-start.29
  6.7 59.5 %copy-start.2 = (bf16[3,1024,256]{2,1,0:T(8,128)(2,1)S(1)}, bf16[3,1024,256]{2,1,0:T(8,128)(2,1)}, u32[]{:S(2)}) copy-start(bf16[3,1024,256]{2,1,0:T(8,128)(2,1)} %w_qkv.3) | copy-start | bytes 4718596
  6.7 59.5 %copy-start.23 = (bf16[1024,512]{1,0:T(8,128)(2,1)S(1)}, bf16[1024,512]{1,0:T(8,128)(2,1)}, u32[]{:S(2)}) copy-start(bf16[1024,512]{1,0:T(8,128)(2,1)} %conv_in.1) | copy-start | bytes 3145732
  6.7 59.5 %copy-start.43 = (bf16[16,256]{1,0:T(8,128)(2,1)S(1)}, bf16[16,256]{1,0:T(8,128)(2,1)}, u32[]{:S(2)}) copy-start(bf16[16,256]{1,0:T(8,128)(2,1)} %own_ref.1) | copy-start | bytes 24580
  59.9 1.3 copy-start.12
  61.2 1.4 copy-start.13
  62.6 1.3 copy-start.14
  63.9 1.3 copy-start.15
  65.2 1.0 copy-start.25
  66.2 43.2 %copy-start.6 = (f32[256,1024]{1,0:T(8,128)}, f32[256,1024]{1,0:T(8,128)S(1)}, u32[]{:S(2)}) copy-start(f32[256,1024]{1,0:T(8,128)S(1)} %get-tuple-element.82.rows_ref) | copy-start | bytes 3145732
  66.2 2.0 copy-start.1
  68.2 42.6 %copy-start.30 = (bf16[1024,256]{1,0:T(8,128)(2,1)S(1)}, bf16[1024,256]{1,0:T(8,128)(2,1)}, u32[]{:S(2)}) copy-start(bf16[1024,256]{1,0:T(8,128)(2,1)} %conv_out.1) | copy-start | bytes 1572868
  109.4 1.4 copy-start.7
  110.7 48.5 %copy-start.3 = (f32[256,1024]{1,0:T(8,128)}, f32[256,1024]{1,0:T(8,128)S(1)}, u32[]{:S(2)}) copy-start(f32[256,1024]{1,0:T(8,128)S(1)} %get-tuple-element.86.rows_ref) | copy-start | bytes 3145732
  110.7 48.5 %copy-start.8 = (f32[4,256,512]{2,1,0:T(8,128)}, f32[4,256,512]{2,1,0:T(8,128)S(1)}, u32[]{:S(2)}) copy-start(f32[4,256,512]{2,1,0:T(8,128)S(1)} %get-tuple-element.113.soft_ref) | copy-start | bytes 6291460
  159.2 1.3 copy-start.16
  160.6 0.8 copy-start.33
  161.3 0.8 copy-start.35
  162.1 0.8 copy-start.37
  162.9 29.3 %copy-start = (bf16[1024,1024]{1,0:T(8,128)(2,1)}, bf16[1024,1024]{1,0:T(8,128)(2,1)S(1)}, u32[]{:S(2)}) copy-start(bf16[1024,1024]{1,0:T(8,128)(2,1)S(1)} %get-tuple-element.89.w_rows.refs_7_) | copy-start | bytes 6291460
  162.9 29.3 %copy-start.19 = (f32[256,1024]{1,0:T(8,128)}, f32[256,1024]{1,0:T(8,128)S(1)}, u32[]{:S(2)}) copy-start(f32[256,1024]{1,0:T(8,128)S(1)} %get-tuple-element.101.scaled_ref) | copy-start | bytes 3145732
  162.9 33.3 %copy-start.24 = (f32[1,256,1024]{2,1,0:T(8,128)S(1)}, f32[1,256,1024]{2,1,0:T(8,128)}, u32[]{:S(2)}) copy-start(f32[1,256,1024]{2,1,0:T(8,128)} %param.15) | copy-start | bytes 3145732
  192.3 1.3 copy-start.9
  193.6 1.3 copy-start.10
  194.9 1.3 copy-start.11
  196.2 35.9 %copy-start.34 = (bf16[256,1024]{1,0:T(8,128)(2,1)S(1)}, bf16[256,1024]{1,0:T(8,128)(2,1)}, u32[]{:S(2)}) copy-start(bf16[256,1024]{1,0:T(8,128)(2,1)} %copy-done.33) | copy-start | bytes 1572868
  196.3 35.9 %copy-start.36 = (bf16[256,1024]{1,0:T(8,128)(2,1)S(1)}, bf16[256,1024]{1,0:T(8,128)(2,1)}, u32[]{:S(2)}) copy-start(bf16[256,1024]{1,0:T(8,128)(2,1)} %copy-done.35) | copy-start | bytes 1572868
  196.3 35.9 %copy-start.38 = (bf16[256,1024]{1,0:T(8,128)(2,1)S(1)}, bf16[256,1024]{1,0:T(8,128)(2,1)}, u32[]{:S(2)}) copy-start(bf16[256,1024]{1,0:T(8,128)(2,1)} %copy-done.37) | copy-start | bytes 1572868
  231.2 1.0 copy-start.20
  232.1 42.8 %copy-start.40 = (f32[8,1024]{1,0:T(8,128)}, f32[8,1024]{1,0:T(8,128)S(1)}, u32[]{:S(2)}) copy-start(f32[8,1024]{1,0:T(8,128)S(1)} %get-tuple-element.137.refs_13_) | copy-start | bytes 98308
  274.9 1.0 copy-start.26
  275.9 1.0 copy-start.27
  276.9 46.7 %copy-start.39 = (f32[16,1024]{1,0:T(8,128)}, f32[16,1024]{1,0:T(8,128)S(1)}, u32[]{:S(2)}) copy-start(f32[16,1024]{1,0:T(8,128)S(1)} %get-tuple-element.138.refs_14_) | copy-start | bytes 196612
  276.9 46.8 %copy-start.5 = (f32[1,256,1024]{2,1,0:T(8,128)S(1)}, f32[1,256,1024]{2,1,0:T(8,128)}, u32[]{:S(2)}) copy-start(f32[1,256,1024]{2,1,0:T(8,128)} %param.14) | copy-start | bytes 3145732
  323.6 45.1 %copy-start.31 = (bf16[1024,256]{1,0:T(8,128)(2,1)}, bf16[1024,256]{1,0:T(8,128)(2,1)S(1)}, u32[]{:S(2)}) copy-start(bf16[1024,256]{1,0:T(8,128)(2,1)S(1)} %get-tuple-element.130.refs_6_) | copy-start | bytes 1572868
  323.6 45.1 %copy-start.32 = (bf16[256,1024]{1,0:T(8,128)(2,1)}, bf16[256,1024]{1,0:T(8,128)(2,1)S(1)}, u32[]{:S(2)}) copy-start(bf16[256,1024]{1,0:T(8,128)(2,1)S(1)} %get-tuple-element.126.refs_0_) | copy-start | bytes 1572868
  323.6 45.1 %copy-start.41 = (f32[8,1024]{1,0:T(8,128)}, f32[8,1024]{1,0:T(8,128)S(1)}, u32[]{:S(2)}) copy-start(f32[8,1024]{1,0:T(8,128)S(1)} %get-tuple-element.136.refs_12_) | copy-start | bytes 98308
  323.6 45.1 %copy-start.44 = (f32[8,256]{1,0:T(8,128)}, f32[8,256]{1,0:T(8,128)S(1)}, u32[]{:S(2)}) copy-start(f32[8,256]{1,0:T(8,128)S(1)} %get-tuple-element.139.refs_15_) | copy-start | bytes 24580
  323.6 48.6 %copy-start.47 = (bf16[3,1024,256]{2,1,0:T(8,128)(2,1)S(1)}, bf16[3,1024,256]{2,1,0:T(8,128)(2,1)}, u32[]{:S(2)}) copy-start(bf16[3,1024,256]{2,1,0:T(8,128)(2,1)} %get-tuple-element.129) | copy-start | bytes 4718596
  368.7 1.0 copy-start.17
  369.7 1.0 copy-start.18
  370.6 1.0 copy-start.21
  371.6 0.6 copy-start.42
  621.7 4.3 copy-start.50
  621.7 5.4 copy-start.49
  626.1 2.7 copy-start.48
  628.7 3.3 copy-start.46
  632.0 4.4 copy-start.45
  640.5 1.6 copy-start.22
  640.6 2.6 copy-start.54
  640.6 3.2 copy-start.53
  640.6 3.8 copy-start.52
  640.6 4.4 copy-start.51

commit v5 on v4

--- a/solution.py
+++ b/solution.py
@@ -11,6 +11,7 @@
 HEADS = 8
 MESH = pl.DeviceIdType.MESH
 VMEM_SPEC = pl.BlockSpec(memory_space=pltpu.VMEM)
+HBM_SPEC = pl.BlockSpec(memory_space=pltpu.HBM)
 epsilon = 1e-05
 
 
@@ -224,6 +225,27 @@
         self.at += 1
         copy.start()
         return copy
+
+    def halve_pieces(self, source, landing, bit, pieces):
+        half = landing.shape[0]
+        size = half // pieces
+        mine = bit_of(self.b, bit)
+        copies = []
+
+        def start(p):
+            copies.append(
+                self.go(
+                    row_view(source, (1 - mine) * half + p * size, size), row_view(landing, p * size, size), bit
+                )
+            )
+
+        def end():
+            for copy in copies:
+                copy.wait()
+            own = row_view(source, mine * half, half)
+            landing[...] = b16(f32(own[...]) + f32(landing[...]))
+
+        return start, end
 
     def halve(self, source, landing, bit):
         half = landing.shape[0]
@@ -589,9 +611,10 @@
 
 
 def ffn_forward_body(
-    which, at_rows, rows_ref, pack, b_ref, w_rows, ffn_in, out_ref, hid, act, slope,
-    part, send, land, cross, land_cross, send_sem, recv_sem, w_in, local_sem,
+    which, at_rows, rows_ref, pack, b_ref, w_rows, ffn_in, out_ref, hid_out, act_out, slope_out,
+    hid, act, slope, part, send, land, cross, land_cross, send_sem, recv_sem, w_in, local_sem, flush_sem,
 ):
+    flush = Flush(flush_sem)
     links = Links(send_sem, recv_sem)
     load = pltpu.make_async_copy(ffn_in.at[which], w_in, local_sem)
     load.start()
@@ -615,11 +638,14 @@
             emit(cols, dot_rows(act[block], w_rows[:, cols]))
 
     settle, total = gather_work_scatter(links, hid, work, part, send, land, cross, land_cross)
+    for pair in ((hid, hid_out), (act, act_out), (slope, slope_out)):
+        flush.go(*pair)
     settle()
     half = rows_ref.shape[0] // 2
     for h in range(2):
         rows = slice(h * half, (h + 1) * half)
         out_ref[rows] = rows_ref[rows] + 0.5 * (total(h) + vector_row(pack, at_rows[2]))
+    flush.settle()
 
 
 def ffn_forward(rows_in, pack, b_in, w_rows, ffn_in, which, at_rows, ident):
@@ -633,11 +659,14 @@
             shape(features), shape(hidden), shape(hidden),
         ],
         in_specs=[VMEM_SPEC] * 4 + [pl.BlockSpec(memory_space=pl.ANY)],
-        out_specs=[VMEM_SPEC] * 4,
-        scratch_shapes=gws_scratch(rows, features)
-        + [pltpu.VMEM((features, hidden), jnp.bfloat16), pltpu.SemaphoreType.DMA],
+        out_specs=[VMEM_SPEC] + [HBM_SPEC] * 3,
+        scratch_shapes=[pltpu.VMEM((4, rows, c), jnp.bfloat16) for c in (features, hidden, hidden)]
+        + gws_scratch(rows, features)
+        + [
+            pltpu.VMEM((features, hidden), jnp.bfloat16), pltpu.SemaphoreType.DMA, pltpu.SemaphoreType.DMA((3,)),
+        ],
         compiler_params=pltpu.CompilerParams(
-            collective_id=ident, has_side_effects=True, vmem_limit_bytes=40 << 20
+            collective_id=ident, has_side_effects=True, vmem_limit_bytes=60 << 20
         ),
         name="ffn_forward",
     )(rows_in, pack, b_in, w_rows, ffn_in)
@@ -725,7 +754,6 @@
     settle, total = gather_work_scatter(
         links, grad, work, part, send, land, cross, land_cross, None
     )
-    tick()
     rows = stream_ref.shape[0]
     flat = lambda ref: ref[...].reshape(4 * rows, ref.shape[2])
 
@@ -733,6 +761,8 @@
     def _(cols):
         left = act[:, :, cols].reshape(4 * rows, 256)
         gw_out[cols, :] = b16(dot_over(left, flat(grad)))
+
+    tick()
 
     @tiles(hidden, 256)
     def _(cols):
@@ -741,9 +771,6 @@
         sums_ref[3:4, cols] = jnp.sum(f32(right), axis=0, keepdims=True)
 
     settle()
-    for chain in stages:
-        while chain:
-            chain.pop(0)()
     gain = vector_row(pack, gain_at)
     sums_ref[0:3, :] = jnp.zeros((3, columns), jnp.float32)
     sums_ref[4:8, :] = jnp.zeros((4, columns), jnp.float32)
@@ -758,6 +785,9 @@
         out_ref[at] = stream_ref[at] + norm_slope(given, scaled, inverse, gain)
         sums_ref[0:1, :] += jnp.sum(given * scaled, axis=0, keepdims=True)
         sums_ref[1:2, :] += jnp.sum(given, axis=0, keepdims=True)
+    for chain in stages:
+        while chain:
+            chain.pop(0)()
 
 
 def ffn_back(given, rows_in, pack, saved, w_rows, ffn_in, which, gain_at, ident):
@@ -796,7 +826,7 @@
         + [pltpu.VMEM((features, hidden), low), pltpu.SemaphoreType.DMA]
         + extra,
         compiler_params=pltpu.CompilerParams(
-            collective_id=ident, has_side_effects=True, vmem_limit_bytes=48 << 20
+            collective_id=ident, has_side_effects=True, vmem_limit_bytes=60 << 20
         ),
         name="ffn_back_%d" % which,
     )(*given, rows_in, pack, *saved, w_rows, ffn_in)
@@ -804,93 +834,119 @@
 
 class Fetch:
     def __init__(self, links, batch, local_sem):
-        self.links, self.side = links, bit_of(batch, 0)
-        self.beside = {"batch": flip_bits(batch, 1)}
-        self.local_sem = local_sem
-        self.open = []
-        self.stages = []
-
-    def run(self):
-        if self.stages:
-            self.stages.pop(0)()
-
-    def drain(self):
-        while self.stages:
-            self.run()
-
-    def go(self, src, dst, device):
-        return self.links.go(src, dst, device)
+        self.links, self.local_sem = links, local_sem
+        self.quarter = bit_of(batch, 0) + 2 * bit_of(batch, 1)
+        self.peers = [{"batch": flip_bits(batch, 1)}, {"batch": flip_bits(batch, 2)}]
+
+    def flow(self, source_rows, target, blocks, rows):
+        links, size, held = self.links, rows // 8, {}
+        span = lambda q, p: pl.ds(pl.multiple_of(q * (2 * size) + p * size, 16), size)
+        mine = self.quarter
+        own = blocks[0]
+
+        def first():
+            for p in range(2):
+                for t, device, _ in blocks[1:]:
+                    held["y", p, t] = links.go(
+                        source_rows(t, mine * (2 * size) + p * size, size),
+                        target.at[span(mine, p), own],
+                        device,
+                    )
+
+        def pass_on(p, q, t, block, way):
+            there = target.at[span(q, p), block]
+            return links.go(there, there, self.peers[way])
+
+        def second(p):
+            def run():
+                for t, _, block in blocks[1:]:
+                    held["y", p, t].wait()
+                    held["a", p, t] = pass_on(p, mine, t, block, p)
+
+            return run
+
+        def third(p):
+            def run():
+                other = flip_bits(mine, 1 << p)
+                for t, _, block in blocks[1:]:
+                    held["a", p, t].wait()
+                    held["b", p, t] = pass_on(p, mine, t, block, 1 - p)
+                    held["c", p, t] = pass_on(p, other, t, block, 1 - p)
+
+            return run
+
+        def last():
+            for p in range(2):
+                for t, _, _ in blocks[1:]:
+                    held["b", p, t].wait()
+                    held["c", p, t].wait()
+
+        return [first, second(0), second(1), third(0), third(1), last]
 
     def columns(self, source, target, at):
         links, (rows, columns) = self.links, source.shape
-        half = rows // 2
-        block = lambda s: pl.ds(pl.multiple_of(s * columns, 128), columns)
-        mine = pl.ds(pl.multiple_of(self.side * half, 16), half)
-        far_index = flip_bits(links.shard, 2)
+        far = flip_bits(links.shard, 2)
+        own = column_block(links.shard, columns)
+        far_block = column_block(far, columns)
+        row = lambda t, start, size: source.at[pl.ds(pl.multiple_of(start, 16), size)]
+        stages = self.flow(row, target, [own, (2, links.far, far_block)], rows)
         held = {}
 
         def first():
-            held["own"] = pltpu.make_async_copy(source, target.at[:, block(links.shard)], self.local_sem.at[at])
+            stages[0]()
+            held["own"] = pltpu.make_async_copy(source, target.at[:, own], self.local_sem.at[at])
             held["own"].start()
-            held["far"] = self.go(source.at[mine], target.at[mine, block(links.shard)], links.far)
-            held["near"] = self.go(source, target.at[:, block(links.shard)], links.near)
-
-        def second():
-            held["far"].wait()
-            held["x"] = self.go(target.at[mine, block(far_index)], target.at[mine, block(far_index)], self.beside)
-
-        def third():
-            held["x"].wait()
-            held["on"] = self.go(target.at[:, block(far_index)], target.at[:, block(far_index)], links.near)
-
-        def fourth():
+            held["near"] = links.go(source, target.at[:, own], links.near)
+
+        def pass_near():
+            stages[-1]()
+            held["on"] = links.go(target.at[:, far_block], target.at[:, far_block], links.near)
+
+        def finish():
             held["on"].wait()
             held["near"].wait()
             held["own"].wait()
 
-        return [first, second, third, fourth]
-
-    def rows(self, source, target, at, pieces):
-        links, (rows, width) = self.links, target.shape
+        return [first] + stages[1:-1] + [pass_near, finish]
+
+    def rows(self, source, target, at):
+        links, rows = self.links, target.shape[0]
         columns = source.shape[1]
-        half = rows // 2
-        size = half // pieces
-        block = lambda s: pl.ds(pl.multiple_of(s * columns, 128), columns)
-        part = lambda base, p: pl.ds(pl.multiple_of(base + self.side * half + p * size, 16), size)
+        index = [flip_bits(links.shard, m) for m in range(4)]
+        own = column_block(links.shard, columns)
+        row = lambda m, start, size: source.at[pl.ds(pl.multiple_of(index[m] * rows + start, 16), size)]
+        blocks = [own] + [
+            (m, device, column_block(index[m], columns)) for m, device in ((2, links.far), (3, links.across))
+        ]
+        stages = self.flow(row, target, blocks, rows)
         held = {}
-        far, across = flip_bits(links.shard, 2), flip_bits(links.shard, 3)
-        near = flip_bits(links.shard, 1)
-        whole = lambda t: pl.ds(pl.multiple_of(t * rows, 16), rows)
 
         def first():
-            held["own"] = pltpu.make_async_copy(
-                source.at[whole(links.shard)], target.at[:, block(links.shard)], self.local_sem.at[at]
-            )
+            stages[0]()
+            held["own"] = pltpu.make_async_copy(row(0, 0, rows), target.at[:, own], self.local_sem.at[at])
             held["own"].start()
-            for p in range(pieces):
-                for name, t, device in (("f", far, links.far), ("a", across, links.across)):
-                    held[name, p] = self.go(
-                        source.at[part(t * rows, p)], target.at[part(0, p), block(links.shard)], device
-                    )
-            held["near"] = self.go(source.at[whole(near)], target.at[:, block(links.shard)], links.near)
-
-        def middle(p):
-            def run():
-                for name, t in (("f", far), ("a", across)):
-                    held[name, p].wait()
-                    at_p = target.at[part(0, p), block(t)]
-                    held[name, p] = self.go(at_p, at_p, self.beside)
-
-            return run
+            held["near"] = links.go(row(1, 0, rows), target.at[:, own], links.near)
 
         def last():
-            for p in range(pieces):
-                held["f", p].wait()
-                held["a", p].wait()
+            stages[-1]()
             held["near"].wait()
             held["own"].wait()
 
-        return [first] + [middle(p) for p in range(pieces)] + [last]
+        return [first] + stages[1:-1] + [last]
+
+
+class Flush:
+    def __init__(self, sem):
+        self.sem, self.open = sem, []
+
+    def go(self, src, dst):
+        copy = pltpu.make_async_copy(src, dst, self.sem.at[len(self.open)])
+        copy.start()
+        self.open.append(copy)
+
+    def settle(self):
+        for copy in self.open:
+            copy.wait()
 
 
 def vector_row(pack, row):
@@ -939,20 +995,21 @@
 
 def opening_body(
     rows_ref, pack_in, b_ref, base_ref, pos_ref, ffn_in, ffn_out, out_proj,
-    out_ref, hid, act, slope, pack, w_rows, table, proj, w_out,
-    w_in, part, send, land, cross, land_cross, send_sem, recv_sem, local_sem,
+    out_ref, pack, table, proj, w_out, hid_out, act_out, slope_out, w_rows_out,
+    hid, act, slope, w_rows, w_in, part, send, land, cross, land_cross, send_sem, recv_sem, local_sem, flush_sem,
 ):
+    flush = Flush(flush_sem)
     batch = lax.axis_index("batch")
     links = Links(send_sem, recv_sem)
     fetch = Fetch(links, batch, local_sem)
     load = pltpu.make_async_copy(ffn_in.at[0], w_in, local_sem.at[0])
     load.start()
-    links.greet([links.near, links.far, links.across, fetch.beside])
+    links.greet([links.near, links.far, links.across] + fetch.peers)
     small = [
         links.go(pack_in, pack.at[links.shard], device)
         for device in (links.far, links.across, links.near)
     ]
-    down = fetch.rows(ffn_out.at[0], w_rows, 1, 4)
+    down = fetch.rows(ffn_out.at[0], w_rows, 1)
     down.pop(0)()
     pack[links.shard] = pack_in[...]
     for copy in small:
@@ -976,9 +1033,10 @@
             slope[block, :, cols] = b16(gate * (1.0 + pre * (1.0 - gate)))
 
     up(0)
-    down.pop(0)()
     near.wait()
     up(1)
+    down.pop(0)()
+    down.pop(0)()
     lanes = features // 2
 
     @pl.loop(0, table.shape[0] // 16)
@@ -990,19 +1048,20 @@
         table[at, lanes:] = b16(c_a * c_b - s_a * s_b)
 
     proj[...] = b16(dot_rows(table[...], pos_ref[...]))
-    down.pop(0)()
     other = fetch.columns(out_proj, w_out, 2)
     for h in range(2):
         out[h].wait()
         on = links.go(hid.at[2 + h, pl.ds(0, half)], hid.at[2 + h, pl.ds(half, half)], links.near)
         on.wait()
+        if h == 1:
+            other.pop(0)()
         up(2 + h)
         down.pop(0)()
-        if h == 0:
-            other.pop(0)()
+    for pair in ((hid, hid_out), (act, act_out), (slope, slope_out)):
+        flush.go(*pair)
     while down:
         down.pop(0)()
-    other.pop(0)()
+    flush.go(w_rows, w_rows_out)
 
     def work(block, emit):
         @tiles(features, 512)
@@ -1017,6 +1076,7 @@
     for h in range(2):
         at = slice(h * half, (h + 1) * half)
         out_ref[at] = rows_ref[at] + 0.5 * (total(h) + bias)
+    flush.settle()
 
 
 ANY_SPEC = pl.BlockSpec(memory_space=pl.ANY)
@@ -1041,20 +1101,25 @@
         opening_body,
         out_shape=[
             shape((rows, features), jnp.float32),
-            shape((4, rows, features), low), shape((4, rows, hidden), low), shape((4, rows, hidden), low),
             shape((ns,) + pack_in.shape, low),
-            shape((hidden, features), low),
             shape((positions, features), low),
             shape((positions, pos_proj.shape[1]), low),
             shape((features, features), low),
+            shape((4, rows, features), low), shape((4, rows, hidden), low), shape((4, rows, hidden), low),
+            shape((hidden, features), low),
         ],
         in_specs=[VMEM_SPEC] * 5 + [ANY_SPEC] * 3,
-        out_specs=[VMEM_SPEC] * 8 + [ANY_SPEC],
-        scratch_shapes=[pltpu.VMEM((features, hidden), low)]
+        out_specs=[VMEM_SPEC] * 5 + [HBM_SPEC] * 4,
+        scratch_shapes=[
+            pltpu.VMEM((4, rows, features), low), pltpu.VMEM((4, rows, hidden), low),
+            pltpu.VMEM((4, rows, hidden), low), pltpu.VMEM((hidden, features), low),
+            pltpu.VMEM((features, hidden), low),
+        ]
         + gws_scratch(rows, features)[:5]
-        + link_scratch(48, 4),
+        + link_scratch(48, 4)
+        + [pltpu.SemaphoreType.DMA((4,))],
         compiler_params=pltpu.CompilerParams(
-            collective_id=ident, has_side_effects=True, vmem_limit_bytes=40 << 20
+            collective_id=ident, has_side_effects=True, vmem_limit_bytes=60 << 20
         ),
         name="opening",
     )(rows_in, pack_in, b_in, base, pos_proj, ffn_in, ffn_out, out_proj)
@@ -1062,16 +1127,17 @@
 
 def mix_body(
     heads, size, rows_ref, pack, own_ref, w_qkv, proj, w_out, conv_in,
-    out_ref, hid, with_u, with_v, key, value, soft_ref, mix, wc_in,
-    turned, send_sem, recv_sem, local_sem,
+    out_ref, with_u, with_v, key, value, mix, wc_in, hid_out, soft_out,
+    hid, soft_ref, turned, send_sem, recv_sem, local_sem, flush_sem,
 ):
+    flush = Flush(flush_sem)
     batch = lax.axis_index("batch")
     links = Links(send_sem, recv_sem)
     fetch = Fetch(links, batch, local_sem)
     scale = 1.0 / math.sqrt(size)
     rows, features = rows_ref.shape
     half = rows // 2
-    links.greet([links.near, links.far, links.across, fetch.beside])
+    links.greet([links.near, links.far, links.across] + fetch.peers)
     hid[0] = b16(norm_rows(rows_ref[...], vector_row(pack, 1), vector_row(pack, 8)))
     out = [
         links.go(hid.at[0, pl.ds(h * half, half)], hid.at[2, pl.ds(h * half, half)], links.far)
@@ -1115,10 +1181,15 @@
     other.pop(0)()
     attend(2)
     last.append(links.go(mix.at[2], turned.at[links.shard], links.far))
+    other.pop(0)()
+    other.pop(0)()
     for copy in on:
         copy.wait()
+    flush.go(hid, hid_out)
     attend(3)
     last.append(links.go(mix.at[3], turned.at[links.shard], links.across))
+    flush.go(soft_ref, soft_out)
+    other.pop(0)()
     other.pop(0)()
     for copy in last:
         copy.wait()
@@ -1130,6 +1201,7 @@
     out_ref[...] = total
     while other:
         other.pop(0)()
+    flush.settle()
 
 
 def mix_forward(rows_in, pack, own_biases, qkv_proj, proj, w_out, conv_in, heads, ident):
@@ -1142,17 +1214,23 @@
     return pl.pallas_call(
         functools.partial(mix_body, heads, width // heads),
         out_shape=[
-            shape((rows, features), jnp.float32), shape((ns, rows, features), low),
-            narrow, narrow, narrow, narrow,
+            shape((rows, features), jnp.float32),
+            narrow, narrow, narrow, narrow, narrow,
+            shape((conv_in.shape[0], ns * conv_in.shape[1]), low),
+            shape((ns, rows, features), low),
             shape((ns, rows, heads * rows), jnp.float32),
-            narrow,
-            shape((conv_in.shape[0], ns * conv_in.shape[1]), low),
         ],
         in_specs=[VMEM_SPEC] * 6 + [ANY_SPEC],
-        out_specs=[VMEM_SPEC] * 8 + [ANY_SPEC],
-        scratch_shapes=[pltpu.VMEM((ns, rows, width), low)] + link_scratch(16, 2),
+        out_specs=[VMEM_SPEC] * 7 + [HBM_SPEC] * 2,
+        scratch_shapes=[
+            pltpu.VMEM((ns, rows, features), low),
+            pltpu.VMEM((ns, rows, heads * rows), jnp.float32),
+            pltpu.VMEM((ns, rows, width), low),
+        ]
+        + link_scratch(24, 2)
+        + [pltpu.SemaphoreType.DMA((2,))],
         compiler_params=pltpu.CompilerParams(
-            collective_id=ident, has_side_effects=True, vmem_limit_bytes=40 << 20
+            collective_id=ident, has_side_effects=True, vmem_limit_bytes=60 << 20
         ),
         name="mix_forward",
     )(rows_in, pack, own_biases, qkv_proj, proj, w_out, conv_in)
@@ -1204,6 +1282,8 @@
     )
     out_fetch = fetch.columns(conv_out, w_out, 0)
     out_fetch.pop(0)()
+    down = fetch.rows(ffn_out.at[1], w_rows, 1)
+    down.pop(0)()
     live = f32(pack[links.shard, 27:28, 0:1])
     mask = f32(f32(lax.broadcasted_iota(jnp.int32, (rows, 1), 0)) < live)
     hid[...] = b16(norm_rows(rows_ref[...], vector_row(pack, 2), vector_row(pack, 14)))
@@ -1223,9 +1303,8 @@
         gate_ref[:, cols] = b16(gated * (1.0 - gate))
         gated_ref[:, cols] = b16(gated)
         padded[lead : lead + rows, cols] = gated
-    out_fetch.pop(0)()
-    down = fetch.rows(ffn_out.at[1], w_rows, 1, 1)
-    down.pop(0)()
+    for _ in range(4):
+        out_fetch.pop(0)()
     taps = 5
     total = 0.0
     for k in range(taps):
@@ -1239,6 +1318,8 @@
     scaled_ref[...] = total
 
     sums = everywhere(links, nb, source, mid, land_s, land_b, None, out_fetch.pop(0), (ss, rs, sb, rb))
+    down.pop(0)()
+    down.pop(0)()
     frames = sums[2 * lanes : 2 * lanes + 1, 0:1]
     mean = unpack_rows(sums, 0, lanes) / frames
     inverse = lax.rsqrt(unpack_rows(sums, lanes, lanes) / frames - mean * mean + epsilon)
@@ -1251,10 +1332,12 @@
     gate = jax.nn.sigmoid(normed)
     act[...] = b16(normed * gate)
     slope[...] = b16(gate * (1.0 + normed * (1.0 - gate)))
-    out_fetch.pop(0)()
+    while out_fetch:
+        out_fetch.pop(0)()
     down.pop(0)()
     out_ref[...] = rows_ref[...] + (dot_rows(act[...], w_out[...]) + vector_row(pack, 18))
-    down.pop(0)()
+    while down:
+        down.pop(0)()
 
 
 def conv_forward(rows_in, pack, w_in, conv_out, ffn_out, ident):
@@ -1273,7 +1356,7 @@
             shape((ffn_out.shape[1] // ns, features), low),
         ],
         in_specs=[VMEM_SPEC] * 3 + [ANY_SPEC] * 2,
-        out_specs=[VMEM_SPEC] * 10 + [ANY_SPEC],
+        out_specs=[VMEM_SPEC] * 11,
         scratch_shapes=[
             pltpu.VMEM((rows + 16, features), full),
             pltpu.VMEM(small, full), pltpu.VMEM(small, full),
@@ -1281,9 +1364,9 @@
             pltpu.SemaphoreType.DMA((ns,)), pltpu.SemaphoreType.DMA((ns,)),
             pltpu.SemaphoreType.DMA((nb,)), pltpu.SemaphoreType.DMA((nb,)),
         ]
-        + link_scratch(16, 3),
+        + link_scratch(32, 3),
         compiler_params=pltpu.CompilerParams(
-            collective_id=ident, has_side_effects=True, vmem_limit_bytes=40 << 20
+            collective_id=ident, has_side_effects=True, vmem_limit_bytes=60 << 20
         ),
         name="conv_forward",
     )(rows_in, pack, w_in, conv_out, ffn_out)
@@ -1302,10 +1385,13 @@
         + [{"batch": lax.rem(batch + j, nb)} for j in range(1, nb)]
     )
     orders = ride_orders(nb)
+    pieces = 4
     ride = [
-        Rider(batch, send_sem, recv_sem, at).halve(source_ref, landing, orders[at][0])
+        Rider(batch, send_sem, recv_sem, at * pieces).halve_pieces(source_ref, landing, orders[at][0], pieces)
         for at, (source_ref, landing) in enumerate(((ride_a, half_a), (ride_b, half_b)))
     ]
+    for start, _ in ride:
+        start(0)
     lanes = features // 128
     lead, tile, taps = 8, 512, 5
     grad[...] = b16(stream_ref[...])
@@ -1332,6 +1418,9 @@
 
     sums = everywhere(links, nb, source, mid, land_s, land_b, None, meanwhile, (ss, rs, sb, rb))
     beta, gamma = unpack_rows(sums, 0, lanes), unpack_rows(sums, lanes, lanes)
+    for p in range(1, pieces):
+        for start, _ in ride:
+            start(p)
     sums_ref[5:6, :] = gamma
     sums_ref[6:7, :] = beta
     inverse, frames = stats[0:1, :], stats[1:2, 0:1]
@@ -1365,7 +1454,7 @@
     def _(cols):
         gw_in[:, cols] = b16(dot_over(hid[...], inner[:, cols]))
 
-    for end in ride:
+    for _, end in ride:
         end()
 
 
@@ -1392,9 +1481,9 @@
             pltpu.SemaphoreType.DMA((ns,)), pltpu.SemaphoreType.DMA((ns,)),
             pltpu.SemaphoreType.DMA((nb,)), pltpu.SemaphoreType.DMA((nb,)),
         ]
-        + link_scratch(4, 1)[:2],
+        + link_scratch(8, 1)[:2],
         compiler_params=pltpu.CompilerParams(
-            collective_id=ident, has_side_effects=True, vmem_limit_bytes=48 << 20
+            collective_id=ident, has_side_effects=True, vmem_limit_bytes=60 << 20
         ),
         name="conv_back",
     )(stream, rows_in, pack, w_in, w_out, *saved, *ridden)
@@ -1493,6 +1582,7 @@
     near.wait()
     work(1, give)
     last = [links.go(send.at[pl.ds(0, 2)], land.at[pl.ds(0, 2)], links.near)]
+    tick()
     on = []
     for h in range(2):
         out[h].wait()
@@ -1500,7 +1590,6 @@
         on.append(links.go(grad.at[2, there], grad.at[3, there], links.near))
     for copy in on:
         copy.wait()
-    tick()
     work(3, give_far)
     back = links.go(send.at[pl.ds(2, 2)], land.at[pl.ds(2, 2)], links.near)
     work(2, keep_far)
@@ -1527,9 +1616,6 @@
     gw_out[...] = b16(dot_over(flat(mix), flat(grad)))
     for copy in last:
         copy.wait()
-    for chain in stages:
-        while chain:
-            chain.pop(0)()
     sums_ref[...] = jnp.zeros_like(sums_ref)
     sums_ref[2:3, :] = jnp.sum(f32(grad[0]), axis=0, keepdims=True)
     gain = vector_row(pack, 1)
@@ -1540,6 +1626,9 @@
         out_ref[at] = stream_ref[at] + norm_slope(given, scaled, inverse, gain)
         sums_ref[0:1, :] += jnp.sum(given * scaled, axis=0, keepdims=True)
         sums_ref[1:2, :] += jnp.sum(given, axis=0, keepdims=True)
+    for chain in stages:
+        while chain:
+            chain.pop(0)()
 
 
 def mix_back(stream, rows_in, pack, saved, table, proj, w_qkv, w_out, ridden, heads, ident):
@@ -1572,7 +1661,7 @@
         + [dma, dma]
         + between,
         compiler_params=pltpu.CompilerParams(
-            collective_id=ident, has_side_effects=True, vmem_limit_bytes=48 << 20
+            collective_id=ident, has_side_effects=True, vmem_limit_bytes=60 << 20
         ),
         name="mix_back",
     )(stream, rows_in, pack, *saved, table, proj, w_qkv, w_out, *ridden)
@@ -1603,10 +1692,10 @@
     )
     angles = turns[:, None] * rates[None, :]
     base = jnp.concatenate([jnp.sin(angles), jnp.cos(angles)], 1)
-    rows_one, *saved_one, pack, w_rows_one, table, proj, w_out = opening(
+    rows_one, pack, table, proj, w_out, *saved_one, w_rows_one = opening(
         rows_in, pack_in, b_in, base, pos_proj, ffn_in, ffn_out, out_proj, 5
     )
-    rows_two, hid, with_u, with_v, key, value, soft, mix, wc_in = mix_forward(
+    rows_two, with_u, with_v, key, value, mix, wc_in, hid, soft = mix_forward(
         rows_one, pack, biases, qkv_proj, proj, w_out, conv_in, heads, 9
     )
     saved_mix = (hid, with_u, with_v, key, value, soft, mix)
@@ -1630,7 +1719,7 @@
         (stream, *ridden), rows_in, pack, saved_one, w_rows_one, ffn_in, 0, 0, 8
     )
     tall, deep = one_in.shape
-    piece = max(256, 8 * nb)
+    piece = max(128, 8 * nb)
     *sums, out_gains, out_biases, out_taps, out_hidden = tail_sum(
         [grad_out, one_out, one_in] + [grad_qkv[at] for at in range(3)] + [grad_pos, grad_conv_in, grad_conv_out],
         ridden,
@@ -1643,7 +1732,7 @@
             (tall, 2 * width), (tall, width),
         ],
         ["near", "line"],
-        [width, piece, piece, tall, tall, tall, tall, 2 * piece, tall],
+        [width, piece, piece] + [min(tall, 4 * piece)] * 4 + [2 * piece, min(tall, 4 * piece)],
         deep,
         4,
     )

time: 654 us -> 589 us (0.901)
  Pallas kernels: 590 us -> 555 us
  local copies, waits for them, and re-layouts: 34.7 us -> 7.63 us
    unnamed x116 -> x30, local copies, waits for them, and re-layouts: 33.5 us -> 6.37 us
    pallas_call x1, Pallas kernels: 248 us -> 222 us  [tail_sum(): pl.pallas_call(functools.partial(tail_body, specs, chunks, ns, nb, len(ar...]
    pallas_call x1, Pallas kernels: 48.5 us -> 39.4 us  [conv_forward(): pl.pallas_call(functools.partial(conv_body, nb), out_shape=[shape((rows,...]
where the time goes in v5:
time: 589 us; the launch traced here: 585 us
  Pallas kernels  555 us (94%)
  other arithmetic  21.3 us (4%)
  local copies, waits for them, and re-layouts  7.63 us (1%)
    pallas_call x1, Pallas kernels, tail_sum(): pl.pallas_call(functools.partial(tail_body, specs, chunks, ns, nb, len(ar...  222 us
    pallas_call x2, Pallas kernels, ffn_back(): pl.pallas_call(functools.partial(ffn_back_body, which, gain_at, nb), out_...  81.7 us
    pallas_call x1, Pallas kernels, opening(): pl.pallas_call(opening_body, out_shape=[shape((rows, features), jnp.float...  53.5 us
    pallas_call x1, Pallas kernels, mix_back(): pl.pallas_call(functools.partial(mix_back_body, heads, width // heads, nb...  45.9 us
    pallas_call x1, Pallas kernels, mix_forward(): pl.pallas_call(functools.partial(mix_body, heads, width // heads), out_sh...  41.5 us
    pallas_call x1, Pallas kernels, conv_forward(): pl.pallas_call(functools.partial(conv_body, nb), out_shape=[shape((rows,...  39.4 us
    pallas_call x1, Pallas kernels, conv_back(): pl.pallas_call(functools.partial(conv_back_body, nb), out_shape=[shape((r...  39.3 us
    pallas_call x1, Pallas kernels, ffn_forward(): pl.pallas_call(functools.partial(ffn_forward_body, which, at_rows), out_s...  31.6 us

profile of v5, /device:TPU:0, one launch (start us, length us, event | category | flops | bytes accessed | tf_op | source)
XLA Modules:
  0.0 585.4 jit_solution(8148649684518427629)
XLA Ops:
  1.3 0.1 pad.7.clone
  1.4 0.1 pad_maximum_fusion.1
  1.5 1.3 convert_element_type.32.b_ref
  2.8 1.4 maximum_maximum_fusion.pack_in
  4.2 0.4 multiply_sine_fusion
  4.6 0.7 pad_maximum_fusion.base_ref
  5.3 53.5 %opening.1 = (f32[256,1024]{1,0:T(8,128)}, bf16[4,32,256]{2,1,0:T(8,128)(2,1)}, bf16[512,1024]{1,0:T(8,128)(2,1)}, bf16[512,256]{1,0:T(8,128)(2,1)}, bf16[1024,1...) custom-call(f32[256,1024]{1,0:T(8,128)} %bitcast.11, ...), custom_call_target="tpu_custom_call" | custom-call | tf_op jit(solution)/shard_map/opening/pallas_call | solution.py:1100
  58.8 41.5 %mix_forward.1 = (f32[256,1024]{1,0:T(8,128)}, bf16[4,256,256]{2,1,0:T(8,128)(2,1)}, bf16[4,256,256]{2,1,0:T(8,128)(2,1)}, bf16[4,256,256]{2,1,0:T(8,128)(2,1)},...) custom-call(f32[256,1024]{1,0:T(8,128)} %get-tuple-element.82.rows_r, ...), custom_call_target="tpu_custom_call" | custom-call | tf_op jit(solution)/shard_map/mix_forward/pallas_call | solution.py:1214
  100.3 39.4 %conv_forward.1 = (f32[256,1024]{1,0:T(8,128)}, bf16[256,1024]{1,0:T(8,128)(2,1)}, bf16[256,1024]{1,0:T(8,128)(2,1)}, bf16[256,1024]{1,0:T(8,128)(2,1)}, bf16[25...) custom-call(f32[256,1024]{1,0:T(8,128)} %get-tuple-element.86.rows_r, ...), custom_call_target="tpu_custom_call" | custom-call | tf_op jit(solution)/shard_map/conv_forward/pallas_call | solution.py:1350
  139.7 31.6 %ffn_forward.1 = (f32[256,1024]{1,0:T(8,128)}, bf16[4,256,1024]{2,1,0:T(8,128)(2,1)}, bf16[4,256,1024]{2,1,0:T(8,128)(2,1)}, bf16[4,256,1024]{2,1,0:T(8,128)(2,1)}) custom-call(f32[256,1024]{1,0:T(8,128)} %get-tuple-element.88.rows_ref.refs_2_, bf16[4,32,256]{2,1,0:T(8,128)(2,1)} %get-tuple-element.83.pack.refs_3_.refs_4_, ...), custom_call_target="tpu_custom_call" | custom-call | tf_op jit(solution)/shard_map/ffn_forward/pallas_call | solution.py:655
  171.2 35.6 %ffn_back_1.1 = (f32[256,1024]{1,0:T(8,128)}, f32[256,1024]{1,0:T(8,128)}, bf16[1024,1024]{1,0:T(8,128)(2,1)}, bf16[1024,1024]{1,0:T(8,128)(2,1)}, f32[8,1024]{1,0:T(8,128)}) custom-call(f32[256,1024]{1,0:T(8,128)} %get-tuple-element.90.refs_0_, f32[256,1024]{1,0:T(8,128)} %bitcast.15, f32[256,1024]{1,0:T(8,128)} %get-tuple-element.88.rows_ref.refs_2_, ...), custom_call_target="tpu_custom_call" | custom-call | tf_op jit(solution)/shard_map/ffn_back_1/pallas_call | solution.py:815
  206.8 39.3 %conv_back.1 = (f32[256,1024]{1,0:T(8,128)}, bf16[1024,1024]{1,0:T(8,128)(2,1)}, bf16[1024,2048]{1,0:T(8,128)(2,1)}, f32[16,1024]{1,0:T(8,128)}, bf16[512,1024]{1,0:T(8,128)(2,1)}, /*index=5*/bf16[512,1024]{1,0:T(8,128)(2,1)}) custom-call(f32[256,1024]{1,0:T(8,128)} %get-tuple-element.95.stream_ref, f32[256,1024]{1,0:T(8,128)} %get-tuple-element.86.rows_ref, ...), custom_call_target="tpu_custom_call" | custom-call | tf_op jit(solution)/shard_map/conv_back/pallas_call | solution.py:1467
  246.1 45.9 %mix_back.1 = (f32[256,1024]{1,0:T(8,128)}, bf16[3,1024,256]{2,1,0:T(8,128)(2,1)}, bf16[1024,256]{1,0:T(8,128)(2,1)}, bf16[256,1024]{1,0:T(8,128)(2,1)}, f32[8,1...) custom-call(f32[256,1024]{1,0:T(8,128)} %get-tuple-element.107.stream_ref, ...), custom_call_target="tpu_custom_call" | custom-call | tf_op jit(solution)/shard_map/mix_back/pallas_call | solution.py:1647
  292.0 0.0 copy-start.2
  292.0 46.1 %ffn_back_0.1 = (f32[256,1024]{1,0:T(8,128)}, bf16[1024,1024]{1,0:T(8,128)(2,1)}, bf16[1024,1024]{1,0:T(8,128)(2,1)}, f32[8,1024]{1,0:T(8,128)}, bf16[512,1024]{1,0:T(8,128)(2,1)}, /*index=5*/bf16[512,1024]{1,0:T(8,128)(2,1)}) custom-call(f32[256,1024]{1,0:T(8,128)} %get-tuple-element.118.refs_0_, bf16[128,1024]{1,0:T(8,128)(2,1)} %get-tuple-element.119.refs_1_, ...), custom_call_target="tpu_custom_call" | custom-call | tf_op jit(solution)/shard_map/ffn_back_0/pallas_call | solution.py:815
  338.2 0.0 copy-done.2
  338.2 1.2 slice_bitcast_fusion
  339.3 221.8 %tail_sum.1 = (bf16[2,1024,1024]{2,1,0:T(8,128)(2,1)}, bf16[2,4096,256]{2,1,0:T(8,128)(2,1)}, bf16[3,1024,256]{2,1,0:T(8,128)(2,1)}, bf16[1024,256]{1,0:T(8,128)...) custom-call(bf16[256,1024]{1,0:T(8,128)(2,1)} %get-tuple-element.126, ...), custom_call_target="tpu_custom_call" | custom-call | tf_op jit(solution)/shard_map/tail_sum/pallas_call | solution.py:504
  561.2 0.0 copy-start.7
  561.2 0.0 copy-start.4
  561.2 2.2 convert_element_type.36
  563.4 2.1 convert_element_type.37
  565.5 0.0 copy-done.7
  565.5 0.0 copy-start.3
  565.5 1.0 convert_element_type.39
  566.5 0.0 copy-done.4
  566.5 1.6 convert_element_type.38
  568.2 0.0 copy-done.3
  568.2 0.0 copy-start.1
  568.2 1.9 convert_element_type.35
  570.1 1.4 copy-done.1
  571.5 0.0 copy-start
  571.5 4.4 convert_element_type.33
  575.9 0.0 copy-done
  575.9 0.0 copy-start.5
  575.9 4.1 convert_element_type.34
  580.0 0.0 copy-done.5
  580.0 0.0 copy-start.6
  580.0 0.0 copy-start.11
  580.0 0.0 copy-start.10
  580.0 0.0 copy-start.9
  580.0 0.0 copy-start.8
  580.0 1.0 copy.34
  581.0 0.6 copy-done.6
  581.6 1.0 copy.35
  582.6 0.0 copy-done.11
  582.6 0.6 copy.36
  583.2 0.0 copy-done.10
  583.2 0.6 copy.37
  583.8 0.0 copy-done.9
  583.8 0.6 copy.38
  584.4 0.0 copy-done.8
  584.4 0.6 copy.39
  (4 shorter events, 0.0 us)
Async XLA Ops:
  292.0 46.2 %copy-start.2 = (bf16[3,1024,256]{2,1,0:T(8,128)(2,1)S(1)}, bf16[3,1024,256]{2,1,0:T(8,128)(2,1)}, u32[]{:S(2)}) copy-start(bf16[3,1024,256]{2,1,0:T(8,128)(2,1)} %get-tuple-element.129) | copy-start | bytes 4718596
  561.2 4.3 copy-start.7
  561.2 5.4 copy-start.4
  565.5 2.7 copy-start.3
  568.2 3.3 copy-start.1
  571.5 4.4 copy-start
  575.9 4.1 copy-start.5
  580.0 1.6 copy-start.6
  580.0 2.6 copy-start.11
  580.0 3.2 copy-start.10
  580.0 3.8 copy-start.9
  580.0 4.4 copy-start.8

commit v6 on v5

--- a/solution.py
+++ b/solution.py
@@ -226,8 +226,7 @@
         copy.start()
         return copy
 
-    def halve_pieces(self, source, landing, bit, pieces):
-        half = landing.shape[0]
+    def halve_pieces(self, source, landing, bit, pieces, half):
         size = half // pieces
         mine = bit_of(self.b, bit)
         copies = []
@@ -239,13 +238,11 @@
                 )
             )
 
-        def end():
+        def settle():
             for copy in copies:
                 copy.wait()
-            own = row_view(source, mine * half, half)
-            landing[...] = b16(f32(own[...]) + f32(landing[...]))
-
-        return start, end
+
+        return start, settle, row_view(source, mine * half, half)
 
     def halve(self, source, landing, bit):
         half = landing.shape[0]
@@ -540,55 +537,7 @@
         return copy
 
 
-def gather_work_scatter(links, x, work, part, send, land, cross, land_cross, tick=None):
-    half = x.shape[1] // 2
-    out = [
-        links.go(x.at[0, pl.ds(h * half, half)], x.at[2 + h, pl.ds(0, half)], links.far)
-        for h in range(2)
-    ]
-    near = links.go(x.at[0], x.at[1], links.near)
-
-    def keep(cols, value):
-        part[0, :, cols] = value
-
-    work(0, keep)
-    near.wait()
-
-    def give(cols, value):
-        send[0, :, cols] = b16(value[:half])
-        send[1, :, cols] = b16(value[half:])
-
-    work(1, give)
-    last = [links.go(send.at[pl.ds(0, 2)], land.at[pl.ds(0, 2)], links.near)]
-    if tick is not None:
-        tick()
-    for h in range(2):
-        out[h].wait()
-        on = links.go(x.at[2 + h, pl.ds(0, half)], x.at[2 + h, pl.ds(half, half)], links.near)
-        on.wait()
-
-        def split(cols, value, h=h):
-            part[1, h * half : (h + 1) * half, cols] = value[:half]
-            send[2 + h, :, cols] = b16(value[half:])
-
-        work(2 + h, split)
-        back = links.go(send.at[2 + h], land.at[2 + h], links.near)
-        back.wait()
-        cross[h] = b16(part[1, h * half : (h + 1) * half] + f32(land[2 + h]))
-        last.append(links.go(cross.at[h], land_cross.at[h], links.far))
-
-    def settle():
-        for copy in last:
-            copy.wait()
-
-    def total(h):
-        rows = slice(h * half, (h + 1) * half)
-        return part[0, rows] + f32(land[h]) + f32(land_cross[h])
-
-    return settle, total
-
-
-def gws_scratch(rows, columns):
+def sums_scratch(rows, columns):
     half = rows // 2
     return [
         pltpu.VMEM((2, rows, columns), jnp.float32),
@@ -596,9 +545,80 @@
         pltpu.VMEM((4, half, columns), jnp.bfloat16),
         pltpu.VMEM((2, half, columns), jnp.bfloat16),
         pltpu.VMEM((2, half, columns), jnp.bfloat16),
-        pltpu.SemaphoreType.DMA((16,)),
-        pltpu.SemaphoreType.DMA((16,)),
     ]
+
+
+class Sums:
+    def __init__(self, links, refs):
+        self.links = links
+        self.part, self.send, self.land, self.cross, self.land_cross = refs
+        self.half = self.send.shape[1]
+        self.near, self.crossing, self.backs = None, [], []
+
+    def rows(self, h):
+        return slice(h * self.half, (h + 1) * self.half)
+
+    def keep(self, cols, value):
+        self.part[0, :, cols] = value
+
+    def keep_far(self, cols, value):
+        self.part[1, :, cols] = value
+
+    def give(self, cols, value):
+        self.send[0, :, cols] = b16(value[: self.half])
+        self.send[1, :, cols] = b16(value[self.half :])
+
+    def give_far(self, cols, value):
+        self.send[2, :, cols] = b16(value[: self.half])
+        self.send[3, :, cols] = b16(value[self.half :])
+
+    def split(self, h):
+        def emit(cols, value):
+            self.part[1, self.rows(h), cols] = value[: self.half]
+            self.send[2 + h, :, cols] = b16(value[self.half :])
+
+        return emit
+
+    def send_near(self):
+        both = pl.ds(0, 2)
+        self.near = self.links.go(self.send.at[both], self.land.at[both], self.links.near)
+
+    def send_back(self, h):
+        self.backs.append(self.links.go(self.send.at[2 + h], self.land.at[2 + h], self.links.near))
+
+    def send_cross(self, h):
+        self.backs[h].wait()
+        self.cross[h] = b16(self.part[1, self.rows(h)] + f32(self.land[2 + h]))
+        self.crossing.append(self.links.go(self.cross.at[h], self.land_cross.at[h], self.links.far))
+
+    def arrive(self, h):
+        if self.near is not None:
+            self.near.wait()
+            self.near = None
+        self.crossing[h].wait()
+        return self.part[0, self.rows(h)] + f32(self.land[h]) + f32(self.land_cross[h])
+
+
+def gather_work_scatter(links, x, fill, work, refs):
+    sums = Sums(links, refs)
+    half = x.shape[1] // 2
+    out = []
+    for h in range(2):
+        fill(h)
+        out.append(links.go(x.at[0, pl.ds(h * half, half)], x.at[2 + h, pl.ds(0, half)], links.far))
+    near = links.go(x.at[0], x.at[1], links.near)
+    work(0, sums.keep)
+    near.wait()
+    work(1, sums.give)
+    sums.send_near()
+    for h in range(2):
+        out[h].wait()
+        on = links.go(x.at[2 + h, pl.ds(0, half)], x.at[2 + h, pl.ds(half, half)], links.near)
+        on.wait()
+        work(2 + h, sums.split(h))
+        sums.send_back(h)
+        sums.send_cross(h)
+    return sums
 
 
 def tiles(total, size):
@@ -608,69 +628,6 @@
         )
 
     return over
-
-
-def ffn_forward_body(
-    which, at_rows, rows_ref, pack, b_ref, w_rows, ffn_in, out_ref, hid_out, act_out, slope_out,
-    hid, act, slope, part, send, land, cross, land_cross, send_sem, recv_sem, w_in, local_sem, flush_sem,
-):
-    flush = Flush(flush_sem)
-    links = Links(send_sem, recv_sem)
-    load = pltpu.make_async_copy(ffn_in.at[which], w_in, local_sem)
-    load.start()
-    links.greet([links.near, links.far])
-    hid[0] = b16(
-        norm_rows(rows_ref[...], vector_row(pack, at_rows[0]), vector_row(pack, at_rows[1]))
-    )
-    load.wait()
-    columns = hid.shape[2]
-
-    def work(block, emit):
-        @tiles(w_in.shape[1], 512)
-        def _(cols):
-            pre = dot_rows(hid[block], w_in[:, cols]) + b_ref[which : which + 1, cols]
-            gate = jax.nn.sigmoid(pre)
-            act[block, :, cols] = b16(pre * gate)
-            slope[block, :, cols] = b16(gate * (1.0 + pre * (1.0 - gate)))
-
-        @tiles(columns, 512)
-        def _(cols):
-            emit(cols, dot_rows(act[block], w_rows[:, cols]))
-
-    settle, total = gather_work_scatter(links, hid, work, part, send, land, cross, land_cross)
-    for pair in ((hid, hid_out), (act, act_out), (slope, slope_out)):
-        flush.go(*pair)
-    settle()
-    half = rows_ref.shape[0] // 2
-    for h in range(2):
-        rows = slice(h * half, (h + 1) * half)
-        out_ref[rows] = rows_ref[rows] + 0.5 * (total(h) + vector_row(pack, at_rows[2]))
-    flush.settle()
-
-
-def ffn_forward(rows_in, pack, b_in, w_rows, ffn_in, which, at_rows, ident):
-    rows, features = rows_in.shape
-    hidden = ffn_in.shape[2]
-    shape = lambda c: jax.ShapeDtypeStruct((4, rows, c), jnp.bfloat16)
-    out, hid, act, slope = pl.pallas_call(
-        functools.partial(ffn_forward_body, which, at_rows),
-        out_shape=[
-            jax.ShapeDtypeStruct((rows, features), jnp.float32),
-            shape(features), shape(hidden), shape(hidden),
-        ],
-        in_specs=[VMEM_SPEC] * 4 + [pl.BlockSpec(memory_space=pl.ANY)],
-        out_specs=[VMEM_SPEC] + [HBM_SPEC] * 3,
-        scratch_shapes=[pltpu.VMEM((4, rows, c), jnp.bfloat16) for c in (features, hidden, hidden)]
-        + gws_scratch(rows, features)
-        + [
-            pltpu.VMEM((features, hidden), jnp.bfloat16), pltpu.SemaphoreType.DMA, pltpu.SemaphoreType.DMA((3,)),
-        ],
-        compiler_params=pltpu.CompilerParams(
-            collective_id=ident, has_side_effects=True, vmem_limit_bytes=60 << 20
-        ),
-        name="ffn_forward",
-    )(rows_in, pack, b_in, w_rows, ffn_in)
-    return out, (hid, act, slope)
 
 
 def norm_parts(rows):
@@ -689,147 +646,65 @@
     )
 
 
-def ffn_back_body(which, gain_at, nb, *refs):
-    stages = []
-    if which == 1:
-        last_rows, cotangent, *refs = refs
-        rows_ref, pack, hid, act, slope, w_rows, ffn_in, result, out_ref, gw_in, gw_out, sums_ref, *refs = refs
-        stream_ref, *refs = refs
-    else:
-        stream_ref, ride_a, ride_b, *refs = refs
-        rows_ref, pack, hid, act, slope, w_rows, ffn_in, out_ref, gw_in, gw_out, sums_ref, *refs = refs
-        out_a, out_b, ride_send, ride_recv, *refs = refs
-    grad, inner, part, send, land, cross, land_cross, send_sem, recv_sem, w_in, local_sem, *refs = refs
-    links = Links(send_sem, recv_sem)
-    load = pltpu.make_async_copy(ffn_in.at[which], w_in, local_sem)
-    load.start()
-    batch = lax.axis_index("batch")
-    orders = ride_orders(nb)
-    devices = [links.near, links.far]
-    if which == 0:
-        devices += [{"batch": flip_bits(batch, 1 << k)} for k in orders[0]]
-    links.greet(devices)
-    if which == 0:
-        steps = len(orders[0]) - 1
-        for at, (start, end) in enumerate(((ride_a, out_a), (ride_b, out_b))):
-            rider = Rider(batch, ride_send, ride_recv, at * steps)
-            between = refs[at * (steps - 1) : (at + 1) * (steps - 1)]
-            stages.append(
-                rider.chain([start, *between, end], orders[at][:0:-1], rider.double)
-            )
-    else:
-        live = f32(pack[links.shard, 27:28, 0:1])
-        mask = f32(f32(lax.broadcasted_iota(jnp.int32, (rows_ref.shape[0], 1), 0)) < live)
-        scaled, inverse = norm_parts(last_rows[...])
-        gain = vector_row(pack, 5)
-        result[...] = (scaled * gain + vector_row(pack, 21)) * mask
-        given = cotangent[...] * mask
-        stream_ref[...] = norm_slope(given, scaled, inverse, gain)
-        ends = (
-            jnp.sum(given * scaled, axis=0, keepdims=True),
-            jnp.sum(given, axis=0, keepdims=True),
-        )
-
-    def tick():
-        for chain in stages:
-            if chain:
-                chain.pop(0)()
-
-    tick()
-    grad[0] = b16(0.5 * stream_ref[...])
-    load.wait()
-    columns = grad.shape[2]
-    hidden = w_in.shape[1]
-
-    def work(block, emit):
-        @tiles(hidden, 512)
+def column_sum(value):
+    return jnp.sum(value, axis=0, keepdims=True)
+
+
+def ffn_up(hid, act, slope, w_in, b_ref, which):
+    def run(block):
+        @tiles(w_in.shape[1], 512)
+        def _(cols):
+            pre = dot_rows(hid[block], w_in[:, cols]) + b_ref[which : which + 1, cols]
+            gate = jax.nn.sigmoid(pre)
+            act[block, :, cols] = b16(pre * gate)
+            slope[block, :, cols] = b16(gate * (1.0 + pre * (1.0 - gate)))
+
+    return run
+
+
+def ffn_down(act, w_rows):
+    def run(block, emit):
+        @tiles(w_rows.shape[1], 512)
+        def _(cols):
+            emit(cols, dot_rows(act[block], w_rows[:, cols]))
+
+    return run
+
+
+def ffn_inward(grad, inner, slope, w_in, w_rows):
+    def run(block, emit):
+        @tiles(w_in.shape[1], 512)
         def _(cols):
             wide = dot_back(grad[block], w_rows[cols, :])
             inner[block, :, cols] = b16(wide * f32(slope[block, :, cols]))
 
-        @tiles(columns, 512)
+        @tiles(w_in.shape[0], 512)
         def _(cols):
             emit(cols, dot_back(inner[block], w_in[cols, :]))
 
-    settle, total = gather_work_scatter(
-        links, grad, work, part, send, land, cross, land_cross, None
-    )
-    rows = stream_ref.shape[0]
-    flat = lambda ref: ref[...].reshape(4 * rows, ref.shape[2])
-
-    @tiles(hidden, 256)
+    return run
+
+
+def flat(ref):
+    return ref[...].reshape(ref.shape[0] * ref.shape[1], ref.shape[2])
+
+
+def flat_columns(ref, cols, size):
+    return ref[:, :, cols].reshape(ref.shape[0] * ref.shape[1], size)
+
+
+def weight_out(act, grad, gw_out):
+    @tiles(act.shape[2], 256)
     def _(cols):
-        left = act[:, :, cols].reshape(4 * rows, 256)
-        gw_out[cols, :] = b16(dot_over(left, flat(grad)))
-
-    tick()
-
-    @tiles(hidden, 256)
+        gw_out[cols, :] = b16(dot_over(flat_columns(act, cols, 256), flat(grad)))
+
+
+def weight_in(hid, inner, gw_in, sums_ref):
+    @tiles(inner.shape[2], 256)
     def _(cols):
-        right = inner[:, :, cols].reshape(4 * rows, 256)
+        right = flat_columns(inner, cols, 256)
         gw_in[:, cols] = b16(dot_over(flat(hid), right))
-        sums_ref[3:4, cols] = jnp.sum(f32(right), axis=0, keepdims=True)
-
-    settle()
-    gain = vector_row(pack, gain_at)
-    sums_ref[0:3, :] = jnp.zeros((3, columns), jnp.float32)
-    sums_ref[4:8, :] = jnp.zeros((4, columns), jnp.float32)
-    if which == 1:
-        sums_ref[4:5, :], sums_ref[5:6, :] = ends
-    sums_ref[2:3, :] = jnp.sum(f32(grad[0]), axis=0, keepdims=True)
-    half = rows // 2
-    for h in range(2):
-        at = slice(h * half, (h + 1) * half)
-        scaled, inverse = norm_parts(rows_ref[at])
-        given = total(h)
-        out_ref[at] = stream_ref[at] + norm_slope(given, scaled, inverse, gain)
-        sums_ref[0:1, :] += jnp.sum(given * scaled, axis=0, keepdims=True)
-        sums_ref[1:2, :] += jnp.sum(given, axis=0, keepdims=True)
-    for chain in stages:
-        while chain:
-            chain.pop(0)()
-
-
-def ffn_back(given, rows_in, pack, saved, w_rows, ffn_in, which, gain_at, ident):
-    rows, features = rows_in.shape
-    hidden = ffn_in.shape[2]
-    nb = lax.axis_size("batch")
-    low, full = jnp.bfloat16, jnp.float32
-    shape = jax.ShapeDtypeStruct
-    shapes = [
-        shape((rows, features), full), shape((features, hidden), low), shape((hidden, features), low),
-        shape((8, features), full),
-    ]
-    scratch = []
-    if which == 1:
-        shapes = [shape((rows, features), full)] + shapes
-        scratch = [pltpu.VMEM((rows, features), full)]
-    else:
-        first, steps = given[1].shape[0], nb.bit_length() - 2
-        shapes += [shape((first << steps, r.shape[1]), low) for r in given[1:]]
-        scratch = [pltpu.SemaphoreType.DMA((2 * steps,)), pltpu.SemaphoreType.DMA((2 * steps,))]
-    extra = []
-    if which == 0:
-        for r in given[1:]:
-            extra += [pltpu.VMEM((first << k, r.shape[1]), low) for k in range(1, steps)]
-    return pl.pallas_call(
-        functools.partial(ffn_back_body, which, gain_at, nb),
-        out_shape=shapes,
-        in_specs=[VMEM_SPEC] * (len(given) + 6) + [pl.BlockSpec(memory_space=pl.ANY)],
-        out_specs=[VMEM_SPEC] * len(shapes),
-        scratch_shapes=scratch
-        + [
-            pltpu.VMEM((4, rows, features), low),
-            pltpu.VMEM((4, rows, hidden), low),
-        ]
-        + gws_scratch(rows, features)
-        + [pltpu.VMEM((features, hidden), low), pltpu.SemaphoreType.DMA]
-        + extra,
-        compiler_params=pltpu.CompilerParams(
-            collective_id=ident, has_side_effects=True, vmem_limit_bytes=60 << 20
-        ),
-        name="ffn_back_%d" % which,
-    )(*given, rows_in, pack, *saved, w_rows, ffn_in)
+        sums_ref[3:4, cols] = column_sum(f32(right))
 
 
 class Fetch:
@@ -952,64 +827,48 @@
 def vector_row(pack, row):
     return f32(jnp.concatenate([pack[t, row : row + 1, :] for t in range(pack.shape[0])], 1))
 
-
-def scatter_late(links, work, part, send, land, cross, land_cross):
-    half = send.shape[1]
-    backs = []
-    for h in range(2):
-
-        def split(cols, value, h=h):
-            part[1, h * half : (h + 1) * half, cols] = value[:half]
-            send[2 + h, :, cols] = b16(value[half:])
-
-        work(2 + h, split)
-        backs.append(links.go(send.at[2 + h], land.at[2 + h], links.near))
-    last = []
-    for h in range(2):
-        backs[h].wait()
-        cross[h] = b16(part[1, h * half : (h + 1) * half] + f32(land[2 + h]))
-        last.append(links.go(cross.at[h], land_cross.at[h], links.far))
-
-    def give(cols, value):
-        send[0, :, cols] = b16(value[:half])
-        send[1, :, cols] = b16(value[half:])
-
-    work(1, give)
-    last.append(links.go(send.at[pl.ds(0, 2)], land.at[pl.ds(0, 2)], links.near))
-
-    def keep(cols, value):
-        part[0, :, cols] = value
-
-    work(0, keep)
-
-    def settle():
-        for copy in last:
-            copy.wait()
-
-    def total(h):
-        rows = slice(h * half, (h + 1) * half)
-        return part[0, rows] + f32(land[h]) + f32(land_cross[h])
-
-    return settle, total
-
-
-def opening_body(
-    rows_ref, pack_in, b_ref, base_ref, pos_ref, ffn_in, ffn_out, out_proj,
-    out_ref, pack, table, proj, w_out, hid_out, act_out, slope_out, w_rows_out,
-    hid, act, slope, w_rows, w_in, part, send, land, cross, land_cross, send_sem, recv_sem, local_sem, flush_sem,
+def link_scratch(count, local):
+    return [
+        pltpu.SemaphoreType.DMA((count,)),
+        pltpu.SemaphoreType.DMA((count,)),
+        pltpu.SemaphoreType.DMA((local,)),
+    ]
+
+
+class Loads:
+    def __init__(self, sem, pairs):
+        self.open = []
+        for at, (src, dst) in enumerate(pairs):
+            copy = pltpu.make_async_copy(src, dst, sem.at[at])
+            copy.start()
+            self.open.append(copy)
+
+    def need(self, *which):
+        for at in which:
+            if self.open[at] is not None:
+                self.open[at].wait()
+                self.open[at] = None
+
+
+def front_body(
+    heads, size,
+    rows_ref, pack_in, b_ref, base_ref, own_ref, pos_hbm, qkv_hbm, ffn_in, ffn_out, out_proj, conv_in,
+    one_ref, two_ref, pack, table, proj, with_u, with_v, key, value, mix, wc_in, w_mine,
+    hid_out, act_out, slope_out, w_rows_out, hidden_out, soft_out,
+    hid, act, slope, w_rows, w_in, w_out, pos_ref, w_qkv, hid_b, soft_ref, turned,
+    part, send, land, cross, land_cross, send_sem, recv_sem, local_sem, load_sem, flush_sem,
 ):
-    flush = Flush(flush_sem)
     batch = lax.axis_index("batch")
     links = Links(send_sem, recv_sem)
     fetch = Fetch(links, batch, local_sem)
-    load = pltpu.make_async_copy(ffn_in.at[0], w_in, local_sem.at[0])
-    load.start()
+    flush = Flush(flush_sem)
+    loads = Loads(load_sem, [(ffn_in.at[0], w_in), (pos_hbm, pos_ref), (qkv_hbm, w_qkv)])
     links.greet([links.near, links.far, links.across] + fetch.peers)
     small = [
         links.go(pack_in, pack.at[links.shard], device)
         for device in (links.far, links.across, links.near)
     ]
-    down = fetch.rows(ffn_out.at[0], w_rows, 1)
+    down = fetch.rows(ffn_out.at[0], w_rows, 0)
     down.pop(0)()
     pack[links.shard] = pack_in[...]
     for copy in small:
@@ -1022,16 +881,8 @@
         for h in range(2)
     ]
     near = links.go(hid.at[0], hid.at[1], links.near)
-    load.wait()
-
-    def up(block):
-        @tiles(w_in.shape[1], 512)
-        def _(cols):
-            pre = dot_rows(hid[block], w_in[:, cols]) + b_ref[0:1, cols]
-            gate = jax.nn.sigmoid(pre)
-            act[block, :, cols] = b16(pre * gate)
-            slope[block, :, cols] = b16(gate * (1.0 + pre * (1.0 - gate)))
-
+    up = ffn_up(hid, act, slope, w_in, b_ref, 0)
+    loads.need(0)
     up(0)
     near.wait()
     up(1)
@@ -1047,8 +898,9 @@
         table[at, 0:lanes] = b16(s_a * c_b + c_a * s_b)
         table[at, lanes:] = b16(c_a * c_b - s_a * s_b)
 
+    loads.need(1)
     proj[...] = b16(dot_rows(table[...], pos_ref[...]))
-    other = fetch.columns(out_proj, w_out, 2)
+    other = fetch.columns(out_proj, w_out, 1)
     for h in range(2):
         out[h].wait()
         on = links.go(hid.at[2 + h, pl.ds(0, half)], hid.at[2 + h, pl.ds(half, half)], links.near)
@@ -1062,93 +914,39 @@
     while down:
         down.pop(0)()
     flush.go(w_rows, w_rows_out)
-
-    def work(block, emit):
-        @tiles(features, 512)
-        def _(cols):
-            emit(cols, dot_rows(act[block], w_rows[:, cols]))
-
-    settle, total = scatter_late(links, work, part, send, land, cross, land_cross)
+    sums = Sums(links, (part, send, land, cross, land_cross))
+    work = ffn_down(act, w_rows)
+    for h in range(2):
+        work(2 + h, sums.split(h))
+        sums.send_back(h)
+    for h in range(2):
+        sums.send_cross(h)
+    work(1, sums.give)
+    sums.send_near()
+    work(0, sums.keep)
+    for _ in range(4):
+        other.pop(0)()
+
+    out_bias, gain, shift = vector_row(pack, 7), vector_row(pack, 1), vector_row(pack, 8)
+    out = []
+    for h in range(2):
+        at = slice(h * half, (h + 1) * half)
+        one = rows_ref[at] + 0.5 * (sums.arrive(h) + out_bias)
+        one_ref[at] = one
+        hid_b[0, at] = b16(norm_rows(one, gain, shift))
+        there = pl.ds(h * half, half)
+        out.append(links.go(hid_b.at[0, there], hid_b.at[2, there], links.far))
+    near = links.go(hid_b.at[0], hid_b.at[1], links.near)
     while other:
         other.pop(0)()
-    settle()
-    bias = vector_row(pack, 7)
-    for h in range(2):
-        at = slice(h * half, (h + 1) * half)
-        out_ref[at] = rows_ref[at] + 0.5 * (total(h) + bias)
-    flush.settle()
-
-
-ANY_SPEC = pl.BlockSpec(memory_space=pl.ANY)
-
-
-def link_scratch(count, local):
-    return [
-        pltpu.SemaphoreType.DMA((count,)),
-        pltpu.SemaphoreType.DMA((count,)),
-        pltpu.SemaphoreType.DMA((local,)),
-    ]
-
-
-def opening(rows_in, pack_in, b_in, base, pos_proj, ffn_in, ffn_out, out_proj, ident):
-    ns = lax.axis_size("shard")
-    rows, features = rows_in.shape
-    hidden = ffn_in.shape[2]
-    shape = jax.ShapeDtypeStruct
-    low = jnp.bfloat16
-    positions = 2 * rows
-    return pl.pallas_call(
-        opening_body,
-        out_shape=[
-            shape((rows, features), jnp.float32),
-            shape((ns,) + pack_in.shape, low),
-            shape((positions, features), low),
-            shape((positions, pos_proj.shape[1]), low),
-            shape((features, features), low),
-            shape((4, rows, features), low), shape((4, rows, hidden), low), shape((4, rows, hidden), low),
-            shape((hidden, features), low),
-        ],
-        in_specs=[VMEM_SPEC] * 5 + [ANY_SPEC] * 3,
-        out_specs=[VMEM_SPEC] * 5 + [HBM_SPEC] * 4,
-        scratch_shapes=[
-            pltpu.VMEM((4, rows, features), low), pltpu.VMEM((4, rows, hidden), low),
-            pltpu.VMEM((4, rows, hidden), low), pltpu.VMEM((hidden, features), low),
-            pltpu.VMEM((features, hidden), low),
-        ]
-        + gws_scratch(rows, features)[:5]
-        + link_scratch(48, 4)
-        + [pltpu.SemaphoreType.DMA((4,))],
-        compiler_params=pltpu.CompilerParams(
-            collective_id=ident, has_side_effects=True, vmem_limit_bytes=60 << 20
-        ),
-        name="opening",
-    )(rows_in, pack_in, b_in, base, pos_proj, ffn_in, ffn_out, out_proj)
-
-
-def mix_body(
-    heads, size, rows_ref, pack, own_ref, w_qkv, proj, w_out, conv_in,
-    out_ref, with_u, with_v, key, value, mix, wc_in, hid_out, soft_out,
-    hid, soft_ref, turned, send_sem, recv_sem, local_sem, flush_sem,
-):
-    flush = Flush(flush_sem)
-    batch = lax.axis_index("batch")
-    links = Links(send_sem, recv_sem)
-    fetch = Fetch(links, batch, local_sem)
-    scale = 1.0 / math.sqrt(size)
-    rows, features = rows_ref.shape
-    half = rows // 2
-    links.greet([links.near, links.far, links.across] + fetch.peers)
-    hid[0] = b16(norm_rows(rows_ref[...], vector_row(pack, 1), vector_row(pack, 8)))
-    out = [
-        links.go(hid.at[0, pl.ds(h * half, half)], hid.at[2, pl.ds(h * half, half)], links.far)
-        for h in range(2)
-    ]
-    near = links.go(hid.at[0], hid.at[1], links.near)
+    entering = fetch.columns(conv_in, wc_in, 2)
     own = f32(own_ref[...])
     keys = f32(lax.broadcasted_iota(jnp.int32, (rows, rows), 1))
+    scale = 1.0 / math.sqrt(size)
+    loads.need(2)
 
     def attend(slot):
-        hidden = hid[slot]
+        hidden = hid_b[slot]
         query = dot_rows(hidden, w_qkv[0]) + own[3:4]
         with_u[slot] = b16(query + own[6:7])
         with_v[slot] = b16(query + own[7:8])
@@ -1175,65 +973,185 @@
     on = []
     for h in range(2):
         out[h].wait()
-        part = hid.at[2, pl.ds(h * half, half)]
-        on.append(links.go(part, hid.at[3, pl.ds(h * half, half)], links.near))
-    other = fetch.columns(conv_in, wc_in, 0)
-    other.pop(0)()
+        there = pl.ds(h * half, half)
+        on.append(links.go(hid_b.at[2, there], hid_b.at[3, there], links.near))
+        if h == 0:
+            entering.pop(0)()
     attend(2)
     last.append(links.go(mix.at[2], turned.at[links.shard], links.far))
-    other.pop(0)()
-    other.pop(0)()
+    entering.pop(0)()
+    entering.pop(0)()
     for copy in on:
         copy.wait()
-    flush.go(hid, hid_out)
+    flush.go(hid_b, hidden_out)
     attend(3)
     last.append(links.go(mix.at[3], turned.at[links.shard], links.across))
     flush.go(soft_ref, soft_out)
-    other.pop(0)()
-    other.pop(0)()
+    entering.pop(0)()
+    entering.pop(0)()
     for copy in last:
         copy.wait()
-    bias = vector_row(pack, 11)
     width = mix.shape[2]
-    total = rows_ref[...] + bias
+    total = one_ref[...] + vector_row(pack, 11)
     for t in range(turned.shape[0]):
         total = total + dot_rows(turned[t], w_out[t * width : (t + 1) * width])
-    out_ref[...] = total
-    while other:
-        other.pop(0)()
+    two_ref[...] = total
+    w_mine[...] = w_out[pl.ds(pl.multiple_of(links.shard * width, 16), width), :]
+    while entering:
+        entering.pop(0)()
     flush.settle()
 
 
-def mix_forward(rows_in, pack, own_biases, qkv_proj, proj, w_out, conv_in, heads, ident):
+def front(rows_in, pack_in, b_in, base, own_biases, pos_proj, qkv_proj, ffn_in, ffn_out, out_proj, conv_in, heads, ident):
     ns = lax.axis_size("shard")
     rows, features = rows_in.shape
+    hidden = ffn_in.shape[2]
     width = features // ns
-    shape = jax.ShapeDtypeStruct
-    low = jnp.bfloat16
+    low, full = jnp.bfloat16, jnp.float32
+    shape, vmem = jax.ShapeDtypeStruct, pltpu.VMEM
     narrow = shape((ns, rows, width), low)
+    dma = pltpu.SemaphoreType.DMA
     return pl.pallas_call(
-        functools.partial(mix_body, heads, width // heads),
+        functools.partial(front_body, heads, width // heads),
         out_shape=[
-            shape((rows, features), jnp.float32),
+            shape((rows, features), full), shape((rows, features), full),
+            shape((ns,) + pack_in.shape, low),
+            shape((2 * rows, features), low), shape((2 * rows, width), low),
             narrow, narrow, narrow, narrow, narrow,
             shape((conv_in.shape[0], ns * conv_in.shape[1]), low),
+            shape((width, features), low),
+            shape((4, rows, features), low), shape((4, rows, hidden), low), shape((4, rows, hidden), low),
+            shape((hidden, features), low),
             shape((ns, rows, features), low),
-            shape((ns, rows, heads * rows), jnp.float32),
+            shape((ns, rows, heads * rows), full),
         ],
-        in_specs=[VMEM_SPEC] * 6 + [ANY_SPEC],
-        out_specs=[VMEM_SPEC] * 7 + [HBM_SPEC] * 2,
+        in_specs=[VMEM_SPEC] * 5 + [HBM_SPEC] * 6,
+        out_specs=[VMEM_SPEC] * 12 + [HBM_SPEC] * 6,
         scratch_shapes=[
-            pltpu.VMEM((ns, rows, features), low),
-            pltpu.VMEM((ns, rows, heads * rows), jnp.float32),
-            pltpu.VMEM((ns, rows, width), low),
+            vmem((4, rows, features), low), vmem((4, rows, hidden), low), vmem((4, rows, hidden), low),
+            vmem((hidden, features), low), vmem((features, hidden), low), vmem((features, features), low),
+            vmem(pos_proj.shape, low), vmem(qkv_proj.shape, low),
+            vmem((ns, rows, features), low), vmem((ns, rows, heads * rows), full), vmem((ns, rows, width), low),
         ]
-        + link_scratch(24, 2)
-        + [pltpu.SemaphoreType.DMA((2,))],
+        + sums_scratch(rows, features)
+        + link_scratch(72, 3)
+        + [dma((3,)), dma((6,))],
         compiler_params=pltpu.CompilerParams(
             collective_id=ident, has_side_effects=True, vmem_limit_bytes=60 << 20
         ),
-        name="mix_forward",
-    )(rows_in, pack, own_biases, qkv_proj, proj, w_out, conv_in)
+        name="front",
+    )(rows_in, pack_in, b_in, base, own_biases, pos_proj, qkv_proj, ffn_in, ffn_out, out_proj, conv_in)
+
+
+def middle_body(
+    nb, early, rows_ref, pack, b_ref, w_rows, cotangent_hbm, ffn_in,
+    result, out_ref, gw_in, gw_out, sums_ref, early_a, early_b,
+    hid, act, slope, grad, inner, w_in, cotangent, stream, *refs,
+):
+    first, second, refs = refs[:5], refs[5:10], refs[10:]
+    send_sem, recv_sem, ride_send, ride_recv, load_sem = refs
+    batch = lax.axis_index("batch")
+    links = Links(send_sem, recv_sem)
+    loads = Loads(load_sem, [(ffn_in.at[1], w_in), (cotangent_hbm, cotangent)])
+    orders = ride_orders(nb)
+    links.greet([links.near, links.far] + [{"batch": flip_bits(batch, 1 << k)} for k in range(2)])
+    rows, features = rows_ref.shape
+    half = rows // 2
+    gain, shift = vector_row(pack, 4), vector_row(pack, 19)
+
+    def fill(h):
+        at = slice(h * half, (h + 1) * half)
+        hid[0, at] = b16(norm_rows(rows_ref[at], gain, shift))
+
+    up, down = ffn_up(hid, act, slope, w_in, b_ref, 1), ffn_down(act, w_rows)
+
+    def work(block, emit):
+        loads.need(0)
+        up(block)
+        down(block, emit)
+
+    sums = gather_work_scatter(links, hid, fill, work, first)
+    last_gain, last_shift, out_bias = vector_row(pack, 5), vector_row(pack, 21), vector_row(pack, 20)
+    live = f32(pack[links.shard, 27:28, 0:1])
+    mask = f32(f32(lax.broadcasted_iota(jnp.int32, (rows, 1), 0)) < live)
+    loads.need(1)
+    ends = []
+
+    def turn_back(h):
+        at = slice(h * half, (h + 1) * half)
+        scaled, inverse = norm_parts(rows_ref[at] + 0.5 * (sums.arrive(h) + out_bias))
+        result[at] = (scaled * last_gain + last_shift) * mask[at]
+        given = cotangent[at] * mask[at]
+        slide = norm_slope(given, scaled, inverse, last_gain)
+        stream[at] = slide
+        grad[0, at] = b16(0.5 * slide)
+        ends.append((column_sum(given * scaled), column_sum(given)))
+
+    back = gather_work_scatter(
+        links, grad, turn_back, ffn_inward(grad, inner, slope, w_in, w_rows), second
+    )
+    pieces = 4
+    riders = [
+        Rider(batch, ride_send, ride_recv, at * early).halve_pieces(
+            (gw_in, gw_out)[at], (early_a, early_b)[at], orders[at][0], pieces, gw_in.shape[0] // 2
+        )
+        for at in range(2)
+    ]
+    weight_out(act, grad, gw_out)
+    for p in range(early):
+        riders[1][0](p)
+    weight_in(hid, inner, gw_in, sums_ref)
+    for p in range(early):
+        riders[0][0](p)
+    sums_ref[0:3, :] = jnp.zeros((3, features), jnp.float32)
+    sums_ref[2:3, :] = column_sum(f32(grad[0]))
+    sums_ref[4:5, :] = ends[0][0] + ends[1][0]
+    sums_ref[5:6, :] = ends[0][1] + ends[1][1]
+    sums_ref[6:8, :] = jnp.zeros((2, features), jnp.float32)
+    for h in range(2):
+        at = slice(h * half, (h + 1) * half)
+        scaled, inverse = norm_parts(rows_ref[at])
+        given = back.arrive(h)
+        out_ref[at] = stream[at] + norm_slope(given, scaled, inverse, gain)
+        sums_ref[0:1, :] += column_sum(given * scaled)
+        sums_ref[1:2, :] += column_sum(given)
+    for _, settle, _ in riders:
+        settle()
+
+
+EARLY = 1
+
+
+def middle(rows_in, pack, b_in, w_rows, cotangent, ffn_in, ident):
+    rows, features = rows_in.shape
+    hidden = ffn_in.shape[2]
+    nb = lax.axis_size("batch")
+    low, full = jnp.bfloat16, jnp.float32
+    shape, vmem = jax.ShapeDtypeStruct, pltpu.VMEM
+    dma = pltpu.SemaphoreType.DMA
+    piece = features // 8
+    return pl.pallas_call(
+        functools.partial(middle_body, nb, EARLY),
+        out_shape=[
+            shape((rows, features), full), shape((rows, features), full),
+            shape((features, hidden), low), shape((hidden, features), low), shape((8, features), full),
+            shape((EARLY * piece, hidden), low), shape((EARLY * piece, features), low),
+        ],
+        in_specs=[VMEM_SPEC] * 4 + [HBM_SPEC] * 2,
+        out_specs=[VMEM_SPEC] * 7,
+        scratch_shapes=[
+            vmem((4, rows, features), low), vmem((4, rows, hidden), low), vmem((4, rows, hidden), low),
+            vmem((4, rows, features), low), vmem((4, rows, hidden), low), vmem((features, hidden), low),
+            vmem((rows, features), full), vmem((rows, features), full),
+        ]
+        + sums_scratch(rows, features)
+        + sums_scratch(rows, features)
+        + [dma((20,)), dma((20,)), dma((2 * EARLY,)), dma((2 * EARLY,)), dma((2,))],
+        compiler_params=pltpu.CompilerParams(
+            collective_id=ident, has_side_effects=True, vmem_limit_bytes=60 << 20
+        ),
+        name="middle",
+    )(rows_in, pack, b_in, w_rows, cotangent, ffn_in)
 
 
 def pack_rows(ref, at, row):
@@ -1355,7 +1273,7 @@
             shape((features, features), low),
             shape((ffn_out.shape[1] // ns, features), low),
         ],
-        in_specs=[VMEM_SPEC] * 3 + [ANY_SPEC] * 2,
+        in_specs=[VMEM_SPEC] * 3 + [HBM_SPEC] * 2,
         out_specs=[VMEM_SPEC] * 11,
         scratch_shapes=[
             pltpu.VMEM((rows + 16, features), full),
@@ -1374,7 +1292,7 @@
 
 def conv_back_body(
     nb, stream_ref, rows_ref, pack, w_in, w_out, hid, open_ref, gate_ref, gated_ref, scaled_ref, act, slope, stats,
-    ride_a, ride_b, out_ref, gw_out, gw_in, sums_ref, half_a, half_b,
+    ride_a, ride_b, early_a, early_b, out_ref, gw_out, gw_in, sums_ref, half_a, half_b,
     padded, normed, grad, inner, source, mid, land_s, land_b, ss, rs, sb, rb, send_sem, recv_sem,
 ):
     batch = lax.axis_index("batch")
@@ -1387,11 +1305,13 @@
     orders = ride_orders(nb)
     pieces = 4
     ride = [
-        Rider(batch, send_sem, recv_sem, at * pieces).halve_pieces(source_ref, landing, orders[at][0], pieces)
+        Rider(batch, send_sem, recv_sem, at * pieces).halve_pieces(
+            source_ref, landing, orders[at][0], pieces, landing.shape[0]
+        )
         for at, (source_ref, landing) in enumerate(((ride_a, half_a), (ride_b, half_b)))
     ]
-    for start, _ in ride:
-        start(0)
+    for start, _, _ in ride:
+        start(EARLY)
     lanes = features // 128
     lead, tile, taps = 8, 512, 5
     grad[...] = b16(stream_ref[...])
@@ -1418,8 +1338,8 @@
 
     sums = everywhere(links, nb, source, mid, land_s, land_b, None, meanwhile, (ss, rs, sb, rb))
     beta, gamma = unpack_rows(sums, 0, lanes), unpack_rows(sums, lanes, lanes)
-    for p in range(1, pieces):
-        for start, _ in ride:
+    for p in range(EARLY + 1, pieces):
+        for start, _, _ in ride:
             start(p)
     sums_ref[5:6, :] = gamma
     sums_ref[6:7, :] = beta
@@ -1454,11 +1374,14 @@
     def _(cols):
         gw_in[:, cols] = b16(dot_over(hid[...], inner[:, cols]))
 
-    for _, end in ride:
-        end()
-
-
-def conv_back(stream, rows_in, pack, w_in, w_out, saved, ridden, ident):
+    for (_, settle, own), landing, early in zip(ride, (half_a, half_b), (early_a, early_b)):
+        settle()
+        done = early.shape[0]
+        landing[0:done] = b16(f32(own[0:done]) + f32(early[...]))
+        landing[done:] = b16(f32(own[done:]) + f32(landing[done:]))
+
+
+def conv_back(stream, rows_in, pack, w_in, w_out, saved, ridden, early, ident):
     ns, nb = lax.axis_size("shard"), lax.axis_size("batch")
     rows, features = rows_in.shape
     shape = jax.ShapeDtypeStruct
@@ -1471,7 +1394,7 @@
             shape((features, 2 * features), low), shape((16, features), full),
         ]
         + [shape((r.shape[0] // 2, r.shape[1]), low) for r in ridden],
-        in_specs=[VMEM_SPEC] * 15,
+        in_specs=[VMEM_SPEC] * 17,
         out_specs=[VMEM_SPEC] * 6,
         scratch_shapes=[
             pltpu.VMEM((rows + 16, features), full), pltpu.VMEM((rows, features), full),
@@ -1486,35 +1409,49 @@
             collective_id=ident, has_side_effects=True, vmem_limit_bytes=60 << 20
         ),
         name="conv_back",
-    )(stream, rows_in, pack, w_in, w_out, *saved, *ridden)
-
-
-def mix_back_body(
-    heads, size, nb, stream_ref, rows_ref, pack, hid, with_u, with_v, key, value, soft_ref, mix, table, proj,
-    w_qkv, w_out, ride_a, ride_b, out_ref, gw_qkv, gw_pos, gw_out, sums_ref, own_sums, out_a, out_b,
-    grad, dq, dk, dx, dp, part, send, land, cross, land_cross, send_sem, recv_sem, ride_send, ride_recv, *between,
+    )(stream, rows_in, pack, w_in, w_out, *saved, *ridden, *early)
+
+
+def rear_body(
+    heads, size, nb, stream_ref, rows_ref, pack, hid_b, with_u, with_v, key, value, soft_ref, mix, table, proj,
+    w_qkv, w_mine, ride_a, ride_b, start_hbm, hid_hbm, act_hbm, slope_hbm, w_rows_hbm, ffn_in,
+    out_ref, gw_qkv, gw_pos, gw_mix, mix_sums, own_sums, gw_in, gw_out, sums_ref, out_a, out_b,
+    grad, dq, dk, dx, dp, stream, grad_b, inner, start, hid, act, slope, w_rows, w_in, *refs,
 ):
+    first, second, refs = refs[:5], refs[5:10], refs[10:]
+    send_sem, recv_sem, ride_send, ride_recv, load_sem, *between = refs
     links = Links(send_sem, recv_sem)
     batch = lax.axis_index("batch")
+    loads = Loads(
+        load_sem,
+        [
+            (slope_hbm, slope), (w_rows_hbm, w_rows), (ffn_in.at[0], w_in), (act_hbm, act), (hid_hbm, hid),
+            (start_hbm, start),
+        ],
+    )
     orders = ride_orders(nb)
     steps = len(orders[0]) - 1
     scale = 1.0 / math.sqrt(size)
     rows, features = rows_ref.shape
     half = rows // 2
-    width = mix.shape[2]
     links.greet([links.near, links.far] + [{"batch": flip_bits(batch, 1 << k)} for k in orders[0]])
-    stages = []
-    for at, (start, end) in enumerate(((ride_a, out_a), (ride_b, out_b))):
-        rider = Rider(batch, ride_send, ride_recv, at * steps)
-        middle = between[at * (steps - 1) : (at + 1) * (steps - 1)]
-        stages.append(rider.chain([start, *middle, end], orders[at][1:], rider.halve))
-
-    def tick():
-        for chain in stages:
+    inward, outward = [], []
+    count = 2 * steps - 1
+    for at, (begin, end) in enumerate(((ride_a, out_a), (ride_b, out_b))):
+        middle_refs = between[at * count : (at + 1) * count]
+        down_refs = [begin, *middle_refs[:steps]]
+        up_refs = [*middle_refs[steps - 1 :], end]
+        rider = Rider(batch, ride_send, ride_recv, at * 2 * steps)
+        inward.append(rider.chain(down_refs, orders[at][1:], rider.halve))
+        rider = Rider(batch, ride_send, ride_recv, at * 2 * steps + steps)
+        outward.append(rider.chain(up_refs, orders[at][:0:-1], rider.double))
+
+    def tick(chains):
+        for chain in chains:
             if chain:
                 chain.pop(0)()
 
-    tick()
+    tick(inward)
     grad[0] = b16(stream_ref[...])
     out = [
         links.go(grad.at[0, pl.ds(h * half, half)], grad.at[2, pl.ds(h * half, half)], links.far)
@@ -1525,11 +1462,10 @@
     at_col = lax.broadcasted_iota(jnp.int32, (rows, rows), 1)
     flip = b16(f32(at_row + at_col == rows - 1))
     keys = f32(at_col)
-    mine = pl.ds(pl.multiple_of(links.shard * width, 16), width)
     own_sums[...] = jnp.zeros_like(own_sums)
 
     def work(slot, emit):
-        mixed = b16(dot_back(grad[slot], w_out[mine, :]))
+        mixed = b16(dot_back(grad[slot], w_mine[...]))
         live = f32(pack[flip_bits(links.shard, slot), 27:28, 0:1])
         for h in range(heads):
             cols = slice(h * size, (h + 1) * size)
@@ -1547,13 +1483,13 @@
             grad_v = dot_rows(wide, proj[:, cols])
             v_turned = b16(dot_rows(flip, with_v[slot, :, cols]))
             dp[slot, :, cols] = b16(dot_over(wide, v_turned))
-            own_sums[2:3, cols] += jnp.sum(grad_u, axis=0, keepdims=True)
-            own_sums[3:4, cols] += jnp.sum(grad_v, axis=0, keepdims=True)
+            own_sums[2:3, cols] += column_sum(grad_u)
+            own_sums[3:4, cols] += column_sum(grad_v)
             high = b16(grad_v)
             rest = b16(grad_v - f32(high))
             dq[slot, :, cols] = b16(grad_u + (dot_rows(flip, high) + dot_rows(flip, rest)))
-        own_sums[0:1, :] += jnp.sum(f32(dq[slot]), axis=0, keepdims=True)
-        own_sums[1:2, :] += jnp.sum(f32(dx[slot]), axis=0, keepdims=True)
+        own_sums[0:1, :] += column_sum(f32(dq[slot]))
+        own_sums[1:2, :] += column_sum(f32(dx[slot]))
 
         @tiles(features, 512)
         def _(cols):
@@ -1564,25 +1500,12 @@
                 + dot_back(dx[slot], w_qkv[2, cols, :]),
             )
 
-    def keep(cols, value):
-        part[0, :, cols] = value
-
-    def keep_far(cols, value):
-        part[1, :, cols] = value
-
-    def give(cols, value):
-        send[0, :, cols] = b16(value[:half])
-        send[1, :, cols] = b16(value[half:])
-
-    def give_far(cols, value):
-        send[2, :, cols] = b16(value[:half])
-        send[3, :, cols] = b16(value[half:])
-
-    work(0, keep)
+    sums = Sums(links, first)
+    work(0, sums.keep)
     near.wait()
-    work(1, give)
-    last = [links.go(send.at[pl.ds(0, 2)], land.at[pl.ds(0, 2)], links.near)]
-    tick()
+    work(1, sums.give)
+    sums.send_near()
+    tick(inward)
     on = []
     for h in range(2):
         out[h].wait()
@@ -1590,21 +1513,18 @@
         on.append(links.go(grad.at[2, there], grad.at[3, there], links.near))
     for copy in on:
         copy.wait()
-    work(3, give_far)
-    back = links.go(send.at[pl.ds(2, 2)], land.at[pl.ds(2, 2)], links.near)
-    work(2, keep_far)
-    back.wait()
+    work(3, sums.give_far)
     for h in range(2):
-        cross[h] = b16(part[1, h * half : (h + 1) * half] + f32(land[2 + h]))
-        last.append(links.go(cross.at[h], land_cross.at[h], links.far))
-    flat = lambda ref: ref[...].reshape(4 * rows, ref.shape[2])
+        sums.send_back(h)
+    work(2, sums.keep_far)
+    for h in range(2):
+        sums.send_cross(h)
     for at, ref in enumerate((dq, dk, dx)):
         right = flat(ref)
 
         @tiles(features, 256)
         def _(cols, at=at, right=right):
-            left = hid[:, :, cols].reshape(4 * rows, 256)
-            gw_qkv[at, cols, :] = b16(dot_over(left, right))
+            gw_qkv[at, cols, :] = b16(dot_over(flat_columns(hid_b, cols, 256), right))
 
     @tiles(features, 256)
     def _(cols):
@@ -1613,58 +1533,92 @@
             total = total + dot_over(table[:, cols], dp[slot])
         gw_pos[cols, :] = b16(total)
 
-    gw_out[...] = b16(dot_over(flat(mix), flat(grad)))
-    for copy in last:
-        copy.wait()
-    sums_ref[...] = jnp.zeros_like(sums_ref)
-    sums_ref[2:3, :] = jnp.sum(f32(grad[0]), axis=0, keepdims=True)
+    gw_mix[...] = b16(dot_over(flat(mix), flat(grad)))
+    mix_sums[...] = jnp.zeros_like(mix_sums)
+    mix_sums[2:3, :] = column_sum(f32(grad[0]))
     gain = vector_row(pack, 1)
+
+    def fill(h):
+        at = slice(h * half, (h + 1) * half)
+        given = sums.arrive(h)
+        scaled, inverse = norm_parts(rows_ref[at])
+        slide = stream_ref[at] + norm_slope(given, scaled, inverse, gain)
+        stream[at] = slide
+        grad_b[0, at] = b16(0.5 * slide)
+        mix_sums[0:1, :] += column_sum(given * scaled)
+        mix_sums[1:2, :] += column_sum(given)
+
+    step = ffn_inward(grad_b, inner, slope, w_in, w_rows)
+
+    def back_work(block, emit):
+        loads.need(0, 1, 2)
+        if block == 1:
+            for chain in inward:
+                while chain:
+                    chain.pop(0)()
+            tick(outward)
+        step(block, emit)
+
+    back = gather_work_scatter(links, grad_b, fill, back_work, second)
+    loads.need(3, 4, 5)
+    weight_out(act, grad_b, gw_out)
+    tick(outward)
+    weight_in(hid, inner, gw_in, sums_ref)
+    sums_ref[0:3, :] = jnp.zeros((3, features), jnp.float32)
+    sums_ref[2:3, :] = column_sum(f32(grad_b[0]))
+    sums_ref[4:8, :] = jnp.zeros((4, features), jnp.float32)
+    gain = vector_row(pack, 0)
     for h in range(2):
         at = slice(h * half, (h + 1) * half)
-        given = part[0, at] + f32(land[h]) + f32(land_cross[h])
-        scaled, inverse = norm_parts(rows_ref[at])
-        out_ref[at] = stream_ref[at] + norm_slope(given, scaled, inverse, gain)
-        sums_ref[0:1, :] += jnp.sum(given * scaled, axis=0, keepdims=True)
-        sums_ref[1:2, :] += jnp.sum(given, axis=0, keepdims=True)
-    for chain in stages:
+        scaled, inverse = norm_parts(start[at])
+        given = back.arrive(h)
+        out_ref[at] = stream[at] + norm_slope(given, scaled, inverse, gain)
+        sums_ref[0:1, :] += column_sum(given * scaled)
+        sums_ref[1:2, :] += column_sum(given)
+    for chain in outward:
         while chain:
             chain.pop(0)()
 
 
-def mix_back(stream, rows_in, pack, saved, table, proj, w_qkv, w_out, ridden, heads, ident):
-    rows, features = rows_in.shape
-    hid, with_u, with_v, key, value, soft, mix = saved
-    width = mix.shape[2]
-    shape = jax.ShapeDtypeStruct
-    low, full = jnp.bfloat16, jnp.float32
-    narrow = pltpu.VMEM((4, rows, width), low)
+def rear(stream, rows_one, pack, saved_mix, table, proj, w_qkv, w_mine, ridden, rows_in, saved, w_rows, ffn_in, heads, ident):
+    rows, features = rows_one.shape
+    hidden = ffn_in.shape[2]
+    width = proj.shape[1]
     nb = lax.axis_size("batch")
     steps = nb.bit_length() - 2
-    dma = pltpu.SemaphoreType.DMA((2 * steps,))
+    low, full = jnp.bfloat16, jnp.float32
+    shape, vmem = jax.ShapeDtypeStruct, pltpu.VMEM
+    dma = pltpu.SemaphoreType.DMA
+    narrow = vmem((4, rows, width), low)
     between = []
     for r in ridden:
-        between += [pltpu.VMEM((r.shape[0] >> k, r.shape[1]), low) for k in range(1, steps)]
+        sizes = [r.shape[0] >> k for k in range(1, steps + 1)]
+        between += [vmem((size, r.shape[1]), low) for size in sizes + sizes[-2::-1]]
     return pl.pallas_call(
-        functools.partial(mix_back_body, heads, width // heads, nb),
+        functools.partial(rear_body, heads, width // heads, nb),
         out_shape=[
             shape((rows, features), full), shape((3, features, width), low), shape((features, width), low),
             shape((width, features), low), shape((8, features), full), shape((8, width), full),
+            shape((features, hidden), low), shape((hidden, features), low), shape((8, features), full),
         ]
-        + [shape((r.shape[0] >> steps, r.shape[1]), low) for r in ridden],
-        in_specs=[VMEM_SPEC] * 16,
-        out_specs=[VMEM_SPEC] * 8,
+        + [shape(r.shape, low) for r in ridden],
+        in_specs=[VMEM_SPEC] * 16 + [HBM_SPEC] * 6,
+        out_specs=[VMEM_SPEC] * 11,
         scratch_shapes=[
-            pltpu.VMEM((4, rows, features), low), narrow, narrow, narrow,
-            pltpu.VMEM((4, 2 * rows, width), low),
+            vmem((4, rows, features), low), narrow, narrow, narrow, vmem((4, 2 * rows, width), low),
+            vmem((rows, features), full), vmem((4, rows, features), low), vmem((4, rows, hidden), low),
+            vmem((rows, features), full), vmem((4, rows, features), low), vmem((4, rows, hidden), low),
+            vmem((4, rows, hidden), low), vmem((hidden, features), low), vmem((features, hidden), low),
         ]
-        + gws_scratch(rows, features)
-        + [dma, dma]
+        + sums_scratch(rows, features)
+        + sums_scratch(rows, features)
+        + [dma((24,)), dma((24,)), dma((4 * steps,)), dma((4 * steps,)), dma((6,))]
         + between,
         compiler_params=pltpu.CompilerParams(
-            collective_id=ident, has_side_effects=True, vmem_limit_bytes=60 << 20
+            collective_id=ident, has_side_effects=True, vmem_limit_bytes=62 << 20
         ),
-        name="mix_back",
-    )(stream, rows_in, pack, *saved, table, proj, w_qkv, w_out, *ridden)
+        name="rear",
+    )(stream, rows_one, pack, *saved_mix, table, proj, w_qkv, w_mine, *ridden, rows_in, *saved, w_rows, ffn_in)
 
 
 def body(
@@ -1692,31 +1646,26 @@
     )
     angles = turns[:, None] * rates[None, :]
     base = jnp.concatenate([jnp.sin(angles), jnp.cos(angles)], 1)
-    rows_one, pack, table, proj, w_out, *saved_one, w_rows_one = opening(
-        rows_in, pack_in, b_in, base, pos_proj, ffn_in, ffn_out, out_proj, 5
+    (
+        rows_one, rows_two, pack, table, proj, with_u, with_v, key, value, mix, wc_in, w_mine,
+        *saved_one, w_rows_one, hidden_mix, soft,
+    ) = front(
+        rows_in, pack_in, b_in, base, biases, pos_proj, qkv_proj, ffn_in, ffn_out, out_proj, conv_in, heads, 5
     )
-    rows_two, with_u, with_v, key, value, mix, wc_in, hid, soft = mix_forward(
-        rows_one, pack, biases, qkv_proj, proj, w_out, conv_in, heads, 9
-    )
-    saved_mix = (hid, with_u, with_v, key, value, soft, mix)
+    saved_mix = (hidden_mix, with_u, with_v, key, value, soft, mix)
     rows_three, *saved_conv, wc_out, w_rows_two = conv_forward(
         rows_two, pack, wc_in, conv_out, ffn_out, 10
     )
-    rows_four, saved_two = ffn_forward(
-        rows_three, pack, b_in, w_rows_two, ffn_in, 1, (4, 19, 20), 6
+    result, stream, two_in, two_out, two_sums, *early = middle(
+        rows_three, pack, b_in, w_rows_two, cotangent[0], ffn_in, 6
     )
 
-    result, stream, two_in, two_out, two_sums = ffn_back(
-        (rows_four, cotangent[0]), rows_three, pack, saved_two, w_rows_two, ffn_in, 1, 4, 7
+    stream, grad_conv_out, grad_conv_in, conv_sums, *ridden = conv_back(
+        stream, rows_two, pack, wc_in, wc_out, saved_conv, (two_in, two_out), early, 11
     )
-    stream, grad_conv_out, grad_conv_in, conv_sums, *ridden = conv_back(
-        stream, rows_two, pack, wc_in, wc_out, saved_conv, (two_in, two_out), 11
-    )
-    stream, grad_qkv, grad_pos, grad_out, mix_sums, own_sums, *ridden = mix_back(
-        stream, rows_one, pack, saved_mix, table, proj, qkv_proj, w_out, ridden, heads, 12
-    )
-    stream, one_in, one_out, one_sums, *ridden = ffn_back(
-        (stream, *ridden), rows_in, pack, saved_one, w_rows_one, ffn_in, 0, 0, 8
+    stream, grad_qkv, grad_pos, grad_out, mix_sums, own_sums, one_in, one_out, one_sums, *ridden = rear(
+        stream, rows_one, pack, saved_mix, table, proj, qkv_proj, w_mine, ridden, rows_in, saved_one, w_rows_one,
+        ffn_in, heads, 12
     )
     tall, deep = one_in.shape
     piece = max(128, 8 * nb)

time: 589 us -> 565 us (0.959)
  Pallas kernels: 555 us -> 529 us
    pallas_call x6 -> x3, Pallas kernels: 254 us -> 236 us  [the longest x1 85.9 us: rear(): pl.pallas_call(functools.partial(rear_body, heads, width // heads, nb), o...]
    pallas_call x1, Pallas kernels: 39.3 us -> 33.4 us  [conv_back(): pl.pallas_call(functools.partial(conv_back_body, nb), out_shape=[shape((r...]
where the time goes in v6:
time: 565 us; the launch traced here: 561 us
  Pallas kernels  529 us (94%)
  other arithmetic  21.3 us (4%)
  local copies, waits for them, and re-layouts  8.98 us (2%)
    pallas_call x1, Pallas kernels, tail_sum(): pl.pallas_call(functools.partial(tail_body, specs, chunks, ns, nb, len(ar...  222 us
    pallas_call x1, Pallas kernels, rear(): pl.pallas_call(functools.partial(rear_body, heads, width // heads, nb), o...  85.9 us
    pallas_call x1, Pallas kernels, front(): pl.pallas_call(functools.partial(front_body, heads, width // heads), out_...  85.8 us
    pallas_call x1, Pallas kernels, middle(): pl.pallas_call(functools.partial(middle_body, nb, EARLY), out_shape=[shap...  64.1 us
    pallas_call x1, Pallas kernels, conv_forward(): pl.pallas_call(functools.partial(conv_body, nb), out_shape=[shape((rows,...  38.1 us
    pallas_call x1, Pallas kernels, conv_back(): pl.pallas_call(functools.partial(conv_back_body, nb), out_shape=[shape((r...  33.4 us
    convert_element_type x8, other arithmetic, f32(): return a.astype(jnp.float32)  18.7 us

profile of v6, /device:TPU:0, one launch (start us, length us, event | category | flops | bytes accessed | tf_op | source)
XLA Modules:
  0.0 561.5 jit_solution(1976930801440451519)
XLA Ops:
  1.3 0.1 pad.7.clone
  1.4 0.1 pad_maximum_fusion.1
  1.5 1.3 convert_element_type.32.b_ref
  2.8 1.4 maximum_maximum_fusion.pack_in
  4.2 0.4 multiply_sine_fusion
  4.6 0.7 pad_maximum_fusion.base_ref
  5.3 85.8 %front.1 = (f32[256,1024]{1,0:T(8,128)}, f32[256,1024]{1,0:T(8,128)}, bf16[4,32,256]{2,1,0:T(8,128)(2,1)}, bf16[512,1024]{1,0:T(8,128)(2,1)}, bf16[512,256]{1,0:...) custom-call(f32[256,1024]{1,0:T(8,128)} %bitcast.11, ...), custom_call_target="tpu_custom_call" | custom-call | tf_op jit(solution)/shard_map/front/pallas_call | solution.py:1014
  91.1 38.1 %conv_forward.1 = (f32[256,1024]{1,0:T(8,128)}, bf16[256,1024]{1,0:T(8,128)(2,1)}, bf16[256,1024]{1,0:T(8,128)(2,1)}, bf16[256,1024]{1,0:T(8,128)(2,1)}, bf16[25...) custom-call(f32[256,1024]{1,0:T(8,128)} %get-tuple-element.77.rows_r, ...), custom_call_target="tpu_custom_call" | custom-call | tf_op jit(solution)/shard_map/conv_forward/pallas_call | solution.py:1268
  129.2 64.1 %middle.1 = (f32[256,1024]{1,0:T(8,128)}, f32[256,1024]{1,0:T(8,128)}, bf16[1024,1024]{1,0:T(8,128)(2,1)}, bf16[1024,1024]{1,0:T(8,128)(2,1)}, f32[8,1024]{1,0:T...) custom-call(f32[256,1024]{1,0:T(8,128)} %get-tuple-element.80.rows_ref, ...), custom_call_target="tpu_custom_call" | custom-call | tf_op jit(solution)/shard_map/middle/pallas_call | solution.py:1133
  193.3 33.4 %conv_back.1 = (f32[256,1024]{1,0:T(8,128)}, bf16[1024,1024]{1,0:T(8,128)(2,1)}, bf16[1024,2048]{1,0:T(8,128)(2,1)}, f32[16,1024]{1,0:T(8,128)}, bf16[512,1024]{1,0:T(8,128)(2,1)}, /*index=5*/bf16[512,1024]{1,0:T(8,128)(2,1)}) custom-call(f32[256,1024]{1,0:T(8,128)} %get-tuple-element.83.stream_ref, f32[256,1024]{1,0:T(8,128)} %get-tuple-element.77.rows_ref, ...), custom_call_target="tpu_custom_call" | custom-call | tf_op jit(solution)/shard_map/conv_back/pallas_call | solution.py:1390
  226.7 85.9 %rear.1 = (f32[256,1024]{1,0:T(8,128)}, bf16[3,1024,256]{2,1,0:T(8,128)(2,1)}, bf16[1024,256]{1,0:T(8,128)(2,1)}, bf16[256,1024]{1,0:T(8,128)(2,1)}, f32[8,1024]...) custom-call(f32[256,1024]{1,0:T(8,128)} %get-tuple-element.97.stream, ...), custom_call_target="tpu_custom_call" | custom-call | tf_op jit(solution)/shard_map/rear/pallas_call | solution.py:1597
  312.6 2.5 slice_bitcast_fusion
  315.1 222.1 %tail_sum.1 = (bf16[2,1024,1024]{2,1,0:T(8,128)(2,1)}, bf16[2,4096,256]{2,1,0:T(8,128)(2,1)}, bf16[3,1024,256]{2,1,0:T(8,128)(2,1)}, bf16[1024,256]{1,0:T(8,128)...) custom-call(bf16[256,1024]{1,0:T(8,128)(2,1)} %get-tuple-element.116, ...), custom_call_target="tpu_custom_call" | custom-call | tf_op jit(solution)/shard_map/tail_sum/pallas_call | solution.py:501
  537.3 0.0 copy-start.6
  537.3 0.0 copy-start.3
  537.3 2.2 convert_element_type.36
  539.5 2.1 convert_element_type.37
  541.6 0.0 copy-done.6
  541.6 0.0 copy-start.2
  541.6 1.0 convert_element_type.39
  542.6 0.0 copy-done.3
  542.6 1.6 convert_element_type.38
  544.2 0.0 copy-done.2
  544.2 0.0 copy-start.1
  544.2 1.9 convert_element_type.35
  546.2 1.4 copy-done.1
  547.6 0.0 copy-start
  547.6 4.4 convert_element_type.33
  552.0 0.0 copy-done
  552.0 0.0 copy-start.4
  552.0 4.1 convert_element_type.34
  556.1 0.0 copy-done.4
  556.1 0.0 copy-start.5
  556.1 0.0 copy-start.10
  556.1 0.0 copy-start.9
  556.1 0.0 copy-start.8
  556.1 0.0 copy-start.7
  556.1 1.0 copy.34
  557.1 0.6 copy-done.5
  557.7 1.0 copy.35
  558.6 0.0 copy-done.10
  558.6 0.6 copy.36
  559.2 0.0 copy-done.9
  559.2 0.6 copy.37
  559.8 0.0 copy-done.8
  559.8 0.6 copy.38
  560.4 0.0 copy-done.7
  560.4 0.6 copy.39
  (4 shorter events, 0.0 us)
Async XLA Ops:
  537.3 4.3 copy-start.6
  537.3 5.4 copy-start.3
  541.6 2.7 copy-start.2
  544.2 3.3 copy-start.1
  547.6 4.4 copy-start
  552.0 4.1 copy-start.4
  556.1 1.6 copy-start.5
  556.1 2.6 copy-start.10
  556.1 3.2 copy-start.9
  556.1 3.8 copy-start.8
  556.1 4.4 copy-start.7

commit v7 on v6

--- a/solution.py
+++ b/solution.py
@@ -64,6 +64,35 @@
     for j in range(1, count):
         total = total + ref[j]
     return total
+
+
+class Loads:
+    def __init__(self, sem, pairs):
+        self.open = []
+        for at, (src, dst) in enumerate(pairs):
+            copy = pltpu.make_async_copy(src, dst, sem.at[at])
+            copy.start()
+            self.open.append(copy)
+
+    def need(self, *which):
+        for at in which:
+            if self.open[at] is not None:
+                self.open[at].wait()
+                self.open[at] = None
+
+
+class Flush:
+    def __init__(self, sem):
+        self.sem, self.open = sem, []
+
+    def go(self, src, dst):
+        copy = pltpu.make_async_copy(src, dst, self.sem.at[len(self.open)])
+        copy.start()
+        self.open.append(copy)
+
+    def settle(self):
+        for copy in self.open:
+            copy.wait()
 
 
 class Chunk:
@@ -283,14 +312,33 @@
 
 
 def tail_body(specs, chunks, ns, nb, n_in, n_out, *refs):
-    ins, refs = refs[:n_in], refs[n_in:]
-    ridden, refs = refs[:2], refs[2:]
     (one_sums, mix_sums, two_sums, conv_sums, own_sums), refs = refs[:5], refs[5:]
-    outs, refs = refs[:n_out], refs[n_out:]
+    given, refs = refs[: n_in + 2], refs[n_in + 2 :]
+    outs_hbm, refs = refs[:n_out], refs[n_out:]
     (o_gains, o_biases, o_taps, o_hidden), refs = refs[:4], refs[4:]
     send, recv, turn_send, turn_recv, pre_send, pre_recv, ride_send, ride_recv = refs[:8]
-    ss, rs, sb, rb, wide, land_s, mid, land_b, ride_fin = refs[8:17]
-    rest = list(refs[17:])
+    ss, rs, sb, rb, wide, land_s, mid, land_b, ride_fin, load_sem = refs[8:18]
+    shard, batch = lax.axis_index("shard"), lax.axis_index("batch")
+    flush = Flush(refs[18])
+    outs = refs[19 : 19 + n_out]
+    rest = list(refs[19 + n_out :])
+    pairs, ins, blocks = [], [], {}
+    for i, ref in enumerate(given):
+        if i < n_in and specs["arrays"][i][0] == "gather":
+            pair = []
+            for index in (shard, flip_bits(shard, 2)):
+                held_block = rest.pop(0)
+                pairs.append((ref.at[:, column_block(index, held_block.shape[1])], held_block))
+                pair.append(held_block)
+            blocks[i] = (pair, (len(pairs) - 2, len(pairs) - 1))
+            ins.append(ref)
+        else:
+            held_ref = rest.pop(0)
+            pairs.append((ref, held_ref))
+            blocks[i] = (None, (len(pairs) - 1,))
+            ins.append(held_ref)
+    loads = Loads(load_sem, pairs)
+    ins, ridden = ins[:n_in], ins[n_in:]
     shard, batch = lax.axis_index("shard"), lax.axis_index("batch")
     barrier = pltpu.get_barrier_semaphore()
     greeted = [{"batch": lax.rem(batch + j, nb)} for j in range(1, nb)]
@@ -356,6 +404,12 @@
                 o_hidden[k : k + 1, t * width : (t + 1) * width] = row(at)
 
     late = []
+
+    def leave(out, lead, start, rows):
+        src, dst = outs[out], outs_hbm[out]
+        if lead is not None:
+            src, dst = src.at[lead], dst.at[lead]
+        flush.go(src.at[pl.ds(start, rows)], dst.at[pl.ds(start, rows)])
 
     def turn(c_at, total, row, rows, out, lead):
         target = outs[out] if lead is None else outs[out].at[lead]
@@ -376,13 +430,21 @@
             copy.start()
             copies.append(copy)
         there[...] = total[:, column_block(shard, columns)]
-        late.extend(copies)
+
+        def after():
+            for copy in copies:
+                copy.wait()
+            for t in range(ns):
+                leave(out, lead, t * height + row, rows)
+
+        late.append(after)
 
     rides = []
     orders = ride_orders(nb)
     plain_target = outs[0].at[1]
     rider_a = Rider(batch, ride_send, ride_recv, 0)
     rider_b = Rider(batch, ride_send, ride_recv, 1)
+    loads.need(*blocks[n_in][1], *blocks[n_in + 1][1])
     end_a = rider_a.double(ridden[0], plain_target, orders[0][0])
     end_b = rider_b.double(ridden[1], ride_fin, orders[1][0])
 
@@ -393,7 +455,7 @@
         if kind == "gather":
             near_land, far_land = rest.pop(0), rest.pop(0)
             whole, columns, rows = ins[c.source], c.columns, pl.ds(c.row, c.rows)
-            far = flip_bits(shard, 2)
+            own_block, far_block = blocks[c.source][0]
             state = {}
 
             def pre(at, src, dst, mask, c=c):
@@ -411,20 +473,19 @@
                 ]
 
             def second(
-                near_land=near_land, far_land=far_land, whole=whole, columns=columns, rows=rows, state=state,
-                pre=pre, far=far,
+                near_land=near_land, far_land=far_land, far_block=far_block, rows=rows, state=state, pre=pre,
             ):
                 for copy in state["n"]:
                     copy.wait()
-                near_land[1] = b16(f32(near_land[1]) + f32(whole[rows, column_block(far, columns)]))
+                near_land[1] = b16(f32(near_land[1]) + f32(far_block[rows]))
                 state["f"] = pre(2, near_land.at[1], far_land, 2)
 
             def settle(
-                near_land=near_land, far_land=far_land, whole=whole, columns=columns, rows=rows, state=state,
+                near_land=near_land, far_land=far_land, own_block=own_block, rows=rows, state=state,
             ):
                 state["f"].wait()
                 far_land[...] = b16(
-                    f32(far_land[...]) + f32(near_land[0]) + f32(whole[rows, column_block(shard, columns)])
+                    f32(far_land[...]) + f32(near_land[0]) + f32(own_block[rows])
                 )
 
             early = [first, second]
@@ -439,8 +500,8 @@
             target = outs[out] if lead is None else outs[out].at[lead]
             held = lambda off, size, target=target, c=c: row_view(target, c.row + off, size)
 
-            def finish(c):
-                pass
+            def finish(c, out=out, lead=lead):
+                leave(out, lead, c.row, c.rows)
         landings = [rest.pop(0) for _ in range(c.steps)]
         m = Mover(c, batch, source, base, held, landings, (send, recv), finish, early)
         m.settle_early = settle
@@ -450,6 +511,7 @@
         starts.append(max(0, i // lag - len(m.early)))
     rounds = max(s + m.depth + 1 for s, m in zip(starts, movers))
     for r in range(rounds):
+        ready, late[:] = late[:], []
         if r == 1:
             vectors_on()
         if r == 2:
@@ -458,11 +520,16 @@
         if r == 3:
             vectors_out()
             end_a()
+            leave(0, 1, 0, outs[0].shape[1])
         for s, m in zip(starts, movers):
             if 0 <= r - s <= m.depth:
+                loads.need(*blocks[m.c.source][1])
                 m.advance(r - s)
-    for copy in late:
-        copy.wait()
+        for after in ready:
+            after()
+    for after in late:
+        after()
+    flush.settle()
 
 
 def tail_sum(arrays, ridden, sums, kinds, outputs, firsts, chunk_rows, hidden, ident):
@@ -487,7 +554,15 @@
         pltpu.VMEM((ns, 24, width), full), pltpu.VMEM((ns, 24, width), full),
         pltpu.VMEM((small, width), full), pltpu.VMEM((nb, small, width), full),
         pltpu.VMEM((2 * ridden[1].shape[0], ridden[1].shape[1]), low),
+        dma((2 * len(arrays) + 2,)),
+        dma(((ns + 1) * (n + 1) + 1,)),
     ]
+    scratch += [pltpu.VMEM(o, low) for o in outputs]
+    for i, a in enumerate(list(arrays) + list(ridden)):
+        if i < len(arrays) and kinds[i][0] == "gather":
+            scratch += [pltpu.VMEM((a.shape[0], a.shape[1] // ns), low)] * 2
+        else:
+            scratch.append(pltpu.VMEM(a.shape, low))
     for c in chunks:
         if kinds[c.source][0] == "gather":
             scratch += [pltpu.VMEM((2, c.rows, c.columns), low), pltpu.VMEM((c.rows, c.columns), low)]
@@ -497,18 +572,86 @@
     shape = jax.ShapeDtypeStruct
     shapes = [shape(s, low) for s in outputs]
     shapes += [shape((6, width), full), shape((16, width), full), shape((5, width), full), shape((2, hidden), full)]
-    operands = list(arrays) + list(ridden) + list(sums)
+    operands = list(sums) + list(arrays) + list(ridden)
     return pl.pallas_call(
         functools.partial(tail_body, specs, chunks, ns, nb, len(arrays), len(outputs)),
         out_shape=shapes,
-        in_specs=[VMEM_SPEC] * len(operands),
-        out_specs=[VMEM_SPEC] * len(shapes),
+        in_specs=[VMEM_SPEC] * len(sums) + [HBM_SPEC] * (len(arrays) + 2),
+        out_specs=[HBM_SPEC] * len(outputs) + [VMEM_SPEC] * 4,
         scratch_shapes=scratch,
         compiler_params=pltpu.CompilerParams(
-            collective_id=ident, has_side_effects=True, vmem_limit_bytes=62 << 20
+            collective_id=ident, has_side_effects=True, vmem_limit_bytes=60 << 20
         ),
         name="tail_sum",
     )(*operands)
+
+
+def widen_body(count, others, slots, *refs):
+    n = count + others
+    ins, outs = refs[:n], refs[n : 2 * n]
+    stages, in_sem, out_sem, pass_sem = refs[2 * n : -3], refs[-3], refs[-2], refs[-1]
+    passed = []
+    for at in range(others):
+        passed.append(pltpu.make_async_copy(ins[count + at], outs[count + at], pass_sem.at[at]))
+        passed[-1].start()
+    half = len(stages) // 2
+    items, used = [], {}
+    for src, dst in zip(ins[:count], outs[:count]):
+        for lead in range(src.shape[0]) if len(src.shape) == 3 else [None]:
+            source = src if lead is None else src.at[lead]
+            target = dst if lead is None else dst.at[lead]
+            rows, columns = source.shape
+            kind = [k.shape[2] for k in stages[:half]].index(columns)
+            size = stages[kind].shape[1]
+            for row in range(0, rows, size):
+                slot = used.get(kind, 0) % slots
+                used[kind] = used.get(kind, 0) + 1
+                items.append((source.at[pl.ds(row, size)], target.at[pl.ds(row, size)], kind, slot))
+    items.sort(key=lambda item: item[2])
+    loads, stores = {}, {}
+
+    def load(i):
+        if i < len(items):
+            source, _, kind, slot = items[i]
+            loads[i] = pltpu.make_async_copy(source, stages[kind].at[slot], in_sem.at[kind, slot])
+            loads[i].start()
+
+    ahead = slots - 1
+    for i in range(ahead):
+        load(i)
+    for i, (_, target, kind, slot) in enumerate(items):
+        loads[i].wait()
+        if (kind, slot) in stores:
+            stores.pop((kind, slot)).wait()
+        narrow, wide = stages[kind].at[slot], stages[half + kind].at[slot]
+
+        @pl.loop(0, narrow.shape[0] // 64)
+        def _(k, narrow=narrow, wide=wide):
+            part = pl.ds(pl.multiple_of(k * 64, 64), 64)
+            wide[part] = f32(narrow[part])
+
+        stores[kind, slot] = pltpu.make_async_copy(wide, target, out_sem.at[kind, slot])
+        stores[kind, slot].start()
+        load(i + ahead)
+    for copy in list(stores.values()) + passed:
+        copy.wait()
+
+
+def widen(arrays, others):
+    columns = sorted({a.shape[-1] for a in arrays})
+    slots = 6
+    least = lambda c: min([a.shape[-2] for a in arrays if a.shape[-1] == c] + [(256 * 1024) // c])
+    stages = [pltpu.VMEM((slots, least(c), c), d) for d in (jnp.bfloat16, jnp.float32) for c in columns]
+    dma = pltpu.SemaphoreType.DMA
+    return pl.pallas_call(
+        functools.partial(widen_body, len(arrays), len(others), slots),
+        out_shape=[jax.ShapeDtypeStruct(a.shape, jnp.float32) for a in (*arrays, *others)],
+        in_specs=[HBM_SPEC] * len(arrays) + [VMEM_SPEC] * len(others),
+        out_specs=[HBM_SPEC] * (len(arrays) + len(others)),
+        scratch_shapes=stages + [dma((len(columns), slots)), dma((len(columns), slots)), dma((len(others),))],
+        compiler_params=pltpu.CompilerParams(vmem_limit_bytes=60 << 20),
+        name="widen",
+    )(*arrays, *others)
 
 
 class Links:
@@ -654,7 +797,7 @@
     def run(block):
         @tiles(w_in.shape[1], 512)
         def _(cols):
-            pre = dot_rows(hid[block], w_in[:, cols]) + b_ref[which : which + 1, cols]
+            pre = dot_rows(hid[block], w_in[:, cols]) + f32(b_ref[which : which + 1, cols])
             gate = jax.nn.sigmoid(pre)
             act[block, :, cols] = b16(pre * gate)
             slope[block, :, cols] = b16(gate * (1.0 + pre * (1.0 - gate)))
@@ -810,20 +953,6 @@
         return [first] + stages[1:-1] + [last]
 
 
-class Flush:
-    def __init__(self, sem):
-        self.sem, self.open = sem, []
-
-    def go(self, src, dst):
-        copy = pltpu.make_async_copy(src, dst, self.sem.at[len(self.open)])
-        copy.start()
-        self.open.append(copy)
-
-    def settle(self):
-        for copy in self.open:
-            copy.wait()
-
-
 def vector_row(pack, row):
     return f32(jnp.concatenate([pack[t, row : row + 1, :] for t in range(pack.shape[0])], 1))
 
@@ -835,33 +964,23 @@
     ]
 
 
-class Loads:
-    def __init__(self, sem, pairs):
-        self.open = []
-        for at, (src, dst) in enumerate(pairs):
-            copy = pltpu.make_async_copy(src, dst, sem.at[at])
-            copy.start()
-            self.open.append(copy)
-
-    def need(self, *which):
-        for at in which:
-            if self.open[at] is not None:
-                self.open[at].wait()
-                self.open[at] = None
-
-
 def front_body(
     heads, size,
-    rows_ref, pack_in, b_ref, base_ref, own_ref, pos_hbm, qkv_hbm, ffn_in, ffn_out, out_proj, conv_in,
-    one_ref, two_ref, pack, table, proj, with_u, with_v, key, value, mix, wc_in, w_mine,
+    rows_ref, gains_ref, own_ref, taps_ref, b_ref, base_ref, length_ref,
+    pos_hbm, qkv_hbm, ffn_in, ffn_out, out_proj, conv_in, conv_out,
+    one_ref, two_ref, pack, table, proj, with_u, with_v, key, value, mix, wc_in, w_mine, wc_out,
     hid_out, act_out, slope_out, w_rows_out, hidden_out, soft_out,
     hid, act, slope, w_rows, w_in, w_out, pos_ref, w_qkv, hid_b, soft_ref, turned,
-    part, send, land, cross, land_cross, send_sem, recv_sem, local_sem, load_sem, flush_sem,
+    part, send, land, cross, land_cross, send_sem, recv_sem, local_sem, load_sem, flush_sem, pack_in,
 ):
     batch = lax.axis_index("batch")
     links = Links(send_sem, recv_sem)
     fetch = Fetch(links, batch, local_sem)
     flush = Flush(flush_sem)
+    pack_in[0:6, :] = gains_ref[...]
+    pack_in[6:22, :] = own_ref[...]
+    pack_in[22:27, :] = taps_ref[...]
+    pack_in[27:32, :] = b16(jnp.full((5, pack_in.shape[1]), length_ref[0], jnp.int32).astype(jnp.float32))
     loads = Loads(load_sem, [(ffn_in.at[0], w_in), (pos_hbm, pos_ref), (qkv_hbm, w_qkv)])
     links.greet([links.near, links.far, links.across] + fetch.peers)
     small = [
@@ -901,12 +1020,14 @@
     loads.need(1)
     proj[...] = b16(dot_rows(table[...], pos_ref[...]))
     other = fetch.columns(out_proj, w_out, 1)
+    leaving = fetch.columns(conv_out, wc_out, 3)
     for h in range(2):
         out[h].wait()
         on = links.go(hid.at[2 + h, pl.ds(0, half)], hid.at[2 + h, pl.ds(half, half)], links.near)
         on.wait()
         if h == 1:
             other.pop(0)()
+            leaving.pop(0)()
         up(2 + h)
         down.pop(0)()
     for pair in ((hid, hid_out), (act, act_out), (slope, slope_out)):
@@ -926,6 +1047,7 @@
     work(0, sums.keep)
     for _ in range(4):
         other.pop(0)()
+        leaving.pop(0)()
 
     out_bias, gain, shift = vector_row(pack, 7), vector_row(pack, 1), vector_row(pack, 8)
     out = []
@@ -939,6 +1061,7 @@
     near = links.go(hid_b.at[0], hid_b.at[1], links.near)
     while other:
         other.pop(0)()
+        leaving.pop(0)()
     entering = fetch.columns(conv_in, wc_in, 2)
     own = f32(own_ref[...])
     keys = f32(lax.broadcasted_iota(jnp.int32, (rows, rows), 1))
@@ -1002,7 +1125,10 @@
     flush.settle()
 
 
-def front(rows_in, pack_in, b_in, base, own_biases, pos_proj, qkv_proj, ffn_in, ffn_out, out_proj, conv_in, heads, ident):
+def front(
+    rows_in, gains, own_biases, taps, lengths, b_in, base, pos_proj, qkv_proj, ffn_in, ffn_out, out_proj, conv_in,
+    conv_out, heads, ident,
+):
     ns = lax.axis_size("shard")
     rows, features = rows_in.shape
     hidden = ffn_in.shape[2]
@@ -1015,18 +1141,19 @@
         functools.partial(front_body, heads, width // heads),
         out_shape=[
             shape((rows, features), full), shape((rows, features), full),
-            shape((ns,) + pack_in.shape, low),
+            shape((ns, 32, width), low),
             shape((2 * rows, features), low), shape((2 * rows, width), low),
             narrow, narrow, narrow, narrow, narrow,
             shape((conv_in.shape[0], ns * conv_in.shape[1]), low),
             shape((width, features), low),
+            shape((features, features), low),
             shape((4, rows, features), low), shape((4, rows, hidden), low), shape((4, rows, hidden), low),
             shape((hidden, features), low),
             shape((ns, rows, features), low),
             shape((ns, rows, heads * rows), full),
         ],
-        in_specs=[VMEM_SPEC] * 5 + [HBM_SPEC] * 6,
-        out_specs=[VMEM_SPEC] * 12 + [HBM_SPEC] * 6,
+        in_specs=[VMEM_SPEC] * 6 + [pl.BlockSpec(memory_space=pltpu.SMEM)] + [HBM_SPEC] * 7,
+        out_specs=[VMEM_SPEC] * 13 + [HBM_SPEC] * 6,
         scratch_shapes=[
             vmem((4, rows, features), low), vmem((4, rows, hidden), low), vmem((4, rows, hidden), low),
             vmem((hidden, features), low), vmem((features, hidden), low), vmem((features, features), low),
@@ -1034,25 +1161,28 @@
             vmem((ns, rows, features), low), vmem((ns, rows, heads * rows), full), vmem((ns, rows, width), low),
         ]
         + sums_scratch(rows, features)
-        + link_scratch(72, 3)
-        + [dma((3,)), dma((6,))],
+        + link_scratch(80, 4)
+        + [dma((3,)), dma((6,)), vmem((32, width), low)],
         compiler_params=pltpu.CompilerParams(
             collective_id=ident, has_side_effects=True, vmem_limit_bytes=60 << 20
         ),
         name="front",
-    )(rows_in, pack_in, b_in, base, own_biases, pos_proj, qkv_proj, ffn_in, ffn_out, out_proj, conv_in)
+    )(
+        rows_in, gains, own_biases, taps, b_in, base, lengths, pos_proj, qkv_proj, ffn_in, ffn_out, out_proj,
+        conv_in, conv_out,
+    )
 
 
 def middle_body(
-    nb, early, rows_ref, pack, b_ref, w_rows, cotangent_hbm, ffn_in,
+    nb, early, rows_ref, pack, b_ref, w_rows_hbm, cotangent_hbm, ffn_in,
     result, out_ref, gw_in, gw_out, sums_ref, early_a, early_b,
-    hid, act, slope, grad, inner, w_in, cotangent, stream, *refs,
+    hid, act, slope, grad, inner, w_in, cotangent, stream, w_rows, *refs,
 ):
     first, second, refs = refs[:5], refs[5:10], refs[10:]
     send_sem, recv_sem, ride_send, ride_recv, load_sem = refs
     batch = lax.axis_index("batch")
     links = Links(send_sem, recv_sem)
-    loads = Loads(load_sem, [(ffn_in.at[1], w_in), (cotangent_hbm, cotangent)])
+    loads = Loads(load_sem, [(ffn_in.at[1], w_in), (cotangent_hbm, cotangent), (w_rows_hbm, w_rows)])
     orders = ride_orders(nb)
     links.greet([links.near, links.far] + [{"batch": flip_bits(batch, 1 << k)} for k in range(2)])
     rows, features = rows_ref.shape
@@ -1068,6 +1198,7 @@
     def work(block, emit):
         loads.need(0)
         up(block)
+        loads.need(2)
         down(block, emit)
 
     sums = gather_work_scatter(links, hid, fill, work, first)
@@ -1137,16 +1268,16 @@
             shape((features, hidden), low), shape((hidden, features), low), shape((8, features), full),
             shape((EARLY * piece, hidden), low), shape((EARLY * piece, features), low),
         ],
-        in_specs=[VMEM_SPEC] * 4 + [HBM_SPEC] * 2,
+        in_specs=[VMEM_SPEC] * 3 + [HBM_SPEC] * 3,
         out_specs=[VMEM_SPEC] * 7,
         scratch_shapes=[
             vmem((4, rows, features), low), vmem((4, rows, hidden), low), vmem((4, rows, hidden), low),
             vmem((4, rows, features), low), vmem((4, rows, hidden), low), vmem((features, hidden), low),
-            vmem((rows, features), full), vmem((rows, features), full),
+            vmem((rows, features), full), vmem((rows, features), full), vmem((hidden, features), low),
         ]
         + sums_scratch(rows, features)
         + sums_scratch(rows, features)
-        + [dma((20,)), dma((20,)), dma((2 * EARLY,)), dma((2 * EARLY,)), dma((2,))],
+        + [dma((20,)), dma((20,)), dma((2 * EARLY,)), dma((2 * EARLY,)), dma((3,))],
         compiler_params=pltpu.CompilerParams(
             collective_id=ident, has_side_effects=True, vmem_limit_bytes=60 << 20
         ),
@@ -1185,8 +1316,8 @@
 
 
 def conv_body(
-    nb, rows_ref, pack, w_in, conv_out, ffn_out,
-    out_ref, hid, open_ref, gate_ref, gated_ref, scaled_ref, act, slope, stats, w_out, w_rows,
+    nb, rows_ref, pack, w_in, w_out, ffn_out,
+    out_ref, hid, open_ref, gate_ref, gated_ref, scaled_ref, act, slope, stats, w_rows,
     padded, source, mid, land_s, land_b, ss, rs, sb, rb, send_sem, recv_sem, local_sem,
 ):
     batch = lax.axis_index("batch")
@@ -1198,8 +1329,6 @@
         [links.near, links.far, links.across]
         + [{"batch": lax.rem(batch + j, nb)} for j in range(1, nb)]
     )
-    out_fetch = fetch.columns(conv_out, w_out, 0)
-    out_fetch.pop(0)()
     down = fetch.rows(ffn_out.at[1], w_rows, 1)
     down.pop(0)()
     live = f32(pack[links.shard, 27:28, 0:1])
@@ -1221,8 +1350,6 @@
         gate_ref[:, cols] = b16(gated * (1.0 - gate))
         gated_ref[:, cols] = b16(gated)
         padded[lead : lead + rows, cols] = gated
-    for _ in range(4):
-        out_fetch.pop(0)()
     taps = 5
     total = 0.0
     for k in range(taps):
@@ -1234,8 +1361,9 @@
     pack_rows(source, lanes, jnp.sum(live_total * total, axis=0, keepdims=True))
     source[2 * lanes : 2 * lanes + 8, :] = jnp.broadcast_to(live, (8, 128))
     scaled_ref[...] = total
-
-    sums = everywhere(links, nb, source, mid, land_s, land_b, None, out_fetch.pop(0), (ss, rs, sb, rb))
+    down.pop(0)()
+    down.pop(0)()
+    sums = everywhere(links, nb, source, mid, land_s, land_b, None, lambda: None, (ss, rs, sb, rb))
     down.pop(0)()
     down.pop(0)()
     frames = sums[2 * lanes : 2 * lanes + 1, 0:1]
@@ -1250,15 +1378,12 @@
     gate = jax.nn.sigmoid(normed)
     act[...] = b16(normed * gate)
     slope[...] = b16(gate * (1.0 + normed * (1.0 - gate)))
-    while out_fetch:
-        out_fetch.pop(0)()
-    down.pop(0)()
     out_ref[...] = rows_ref[...] + (dot_rows(act[...], w_out[...]) + vector_row(pack, 18))
     while down:
         down.pop(0)()
 
 
-def conv_forward(rows_in, pack, w_in, conv_out, ffn_out, ident):
+def conv_forward(rows_in, pack, w_in, w_out, ffn_out, ident):
     ns, nb = lax.axis_size("shard"), lax.axis_size("batch")
     rows, features = rows_in.shape
     shape = jax.ShapeDtypeStruct
@@ -1270,11 +1395,10 @@
         out_shape=[
             shape((rows, features), full), plain, plain, plain, plain,
             shape((rows, features), full), plain, plain, shape((8, features), full),
-            shape((features, features), low),
             shape((ffn_out.shape[1] // ns, features), low),
         ],
-        in_specs=[VMEM_SPEC] * 3 + [HBM_SPEC] * 2,
-        out_specs=[VMEM_SPEC] * 11,
+        in_specs=[VMEM_SPEC] * 4 + [HBM_SPEC],
+        out_specs=[VMEM_SPEC] * 10,
         scratch_shapes=[
             pltpu.VMEM((rows + 16, features), full),
             pltpu.VMEM(small, full), pltpu.VMEM(small, full),
@@ -1287,16 +1411,22 @@
             collective_id=ident, has_side_effects=True, vmem_limit_bytes=60 << 20
         ),
         name="conv_forward",
-    )(rows_in, pack, w_in, conv_out, ffn_out)
+    )(rows_in, pack, w_in, w_out, ffn_out)
 
 
 def conv_back_body(
-    nb, stream_ref, rows_ref, pack, w_in, w_out, hid, open_ref, gate_ref, gated_ref, scaled_ref, act, slope, stats,
-    ride_a, ride_b, early_a, early_b, out_ref, gw_out, gw_in, sums_ref, half_a, half_b,
+    nb, stream_ref, rows_ref, pack, w_out, hid, open_ref, gate_ref, gated_ref, scaled_ref, act, slope, stats,
+    early_a, early_b, w_in_hbm, ride_a, ride_b, out_ref, gw_out, gw_in, sums_ref, half_a, half_b,
     padded, normed, grad, inner, source, mid, land_s, land_b, ss, rs, sb, rb, send_sem, recv_sem,
+    w_in, kept_a, kept_b, load_sem,
 ):
     batch = lax.axis_index("batch")
     links = Links(send_sem, recv_sem)
+    kept = [
+        row_view(ref, bit_of(batch, order[0]) * out.shape[0], out.shape[0])
+        for ref, out, order in zip((ride_a, ride_b), (kept_a, kept_b), ride_orders(nb))
+    ]
+    loads = Loads(load_sem, [(w_in_hbm, w_in), (kept[0], kept_a), (kept[1], kept_b)])
     rows, features = rows_ref.shape
     links.greet(
         [links.near, links.far, links.across]
@@ -1364,6 +1494,7 @@
     inner[:, features:] = right
     sums_ref[2:3, :] = jnp.sum(f32(left), axis=0, keepdims=True)
     sums_ref[3:4, :] = jnp.sum(f32(right), axis=0, keepdims=True)
+    loads.need(0)
     total = dot_back(inner[...], w_in[...])
     scaled, inverse = norm_parts(rows_ref[...])
     out_ref[...] = stream_ref[...] + norm_slope(total, scaled, inverse, vector_row(pack, 2))
@@ -1374,7 +1505,8 @@
     def _(cols):
         gw_in[:, cols] = b16(dot_over(hid[...], inner[:, cols]))
 
-    for (_, settle, own), landing, early in zip(ride, (half_a, half_b), (early_a, early_b)):
+    loads.need(1, 2)
+    for (_, settle, _), own, landing, early in zip(ride, (kept_a, kept_b), (half_a, half_b), (early_a, early_b)):
         settle()
         done = early.shape[0]
         landing[0:done] = b16(f32(own[0:done]) + f32(early[...]))
@@ -1394,7 +1526,7 @@
             shape((features, 2 * features), low), shape((16, features), full),
         ]
         + [shape((r.shape[0] // 2, r.shape[1]), low) for r in ridden],
-        in_specs=[VMEM_SPEC] * 17,
+        in_specs=[VMEM_SPEC] * 14 + [HBM_SPEC] * 3,
         out_specs=[VMEM_SPEC] * 6,
         scratch_shapes=[
             pltpu.VMEM((rows + 16, features), full), pltpu.VMEM((rows, features), full),
@@ -1404,19 +1536,24 @@
             pltpu.SemaphoreType.DMA((ns,)), pltpu.SemaphoreType.DMA((ns,)),
             pltpu.SemaphoreType.DMA((nb,)), pltpu.SemaphoreType.DMA((nb,)),
         ]
-        + link_scratch(8, 1)[:2],
+        + link_scratch(8, 1)[:2]
+        + [pltpu.VMEM(w_in.shape, low)]
+        + [pltpu.VMEM((r.shape[0] // 2, r.shape[1]), low) for r in ridden]
+        + [pltpu.SemaphoreType.DMA((3,))],
         compiler_params=pltpu.CompilerParams(
             collective_id=ident, has_side_effects=True, vmem_limit_bytes=60 << 20
         ),
         name="conv_back",
-    )(stream, rows_in, pack, w_in, w_out, *saved, *ridden, *early)
+    )(stream, rows_in, pack, w_out, *saved, *early, w_in, *ridden)
 
 
 def rear_body(
-    heads, size, nb, stream_ref, rows_ref, pack, hid_b, with_u, with_v, key, value, soft_ref, mix, table, proj,
-    w_qkv, w_mine, ride_a, ride_b, start_hbm, hid_hbm, act_hbm, slope_hbm, w_rows_hbm, ffn_in,
-    out_ref, gw_qkv, gw_pos, gw_mix, mix_sums, own_sums, gw_in, gw_out, sums_ref, out_a, out_b,
-    grad, dq, dk, dx, dp, stream, grad_b, inner, start, hid, act, slope, w_rows, w_in, *refs,
+    heads, size, nb, stream_ref, rows_ref, pack, w_mine, ride_a, ride_b,
+    hid_b_hbm, with_u_hbm, with_v_hbm, key_hbm, value_hbm, soft_hbm, mix_hbm, table_hbm, proj_hbm, w_qkv_hbm,
+    start_hbm, hid_hbm, act_hbm, slope_hbm, w_rows_hbm, ffn_in,
+    out_ref, gw_q, gw_k, gw_x, gw_pos, gw_mix, mix_sums, own_sums, gw_in, gw_out, sums_ref, out_a, out_b,
+    grad, dq, dk, dx, dp, stream, grad_b, inner, start, hid, act, slope, w_rows, w_in,
+    hid_b, with_u, with_v, key, value, soft_ref, mix, table, proj, w_qkv, *refs,
 ):
     first, second, refs = refs[:5], refs[5:10], refs[10:]
     send_sem, recv_sem, ride_send, ride_recv, load_sem, *between = refs
@@ -1425,6 +1562,8 @@
     loads = Loads(
         load_sem,
         [
+            (soft_hbm, soft_ref), (value_hbm, value), (key_hbm, key), (with_u_hbm, with_u), (with_v_hbm, with_v),
+            (proj_hbm, proj), (w_qkv_hbm, w_qkv), (hid_b_hbm, hid_b), (mix_hbm, mix), (table_hbm, table),
             (slope_hbm, slope), (w_rows_hbm, w_rows), (ffn_in.at[0], w_in), (act_hbm, act), (hid_hbm, hid),
             (start_hbm, start),
         ],
@@ -1501,6 +1640,7 @@
             )
 
     sums = Sums(links, first)
+    loads.need(*range(7))
     work(0, sums.keep)
     near.wait()
     work(1, sums.give)
@@ -1519,12 +1659,13 @@
     work(2, sums.keep_far)
     for h in range(2):
         sums.send_cross(h)
-    for at, ref in enumerate((dq, dk, dx)):
+    loads.need(7, 8, 9)
+    for ref, target in ((dq, gw_q), (dk, gw_k), (dx, gw_x)):
         right = flat(ref)
 
         @tiles(features, 256)
-        def _(cols, at=at, right=right):
-            gw_qkv[at, cols, :] = b16(dot_over(flat_columns(hid_b, cols, 256), right))
+        def _(cols, target=target, right=right):
+            target[cols, :] = b16(dot_over(flat_columns(hid_b, cols, 256), right))
 
     @tiles(features, 256)
     def _(cols):
@@ -1551,7 +1692,7 @@
     step = ffn_inward(grad_b, inner, slope, w_in, w_rows)
 
     def back_work(block, emit):
-        loads.need(0, 1, 2)
+        loads.need(10, 11, 12)
         if block == 1:
             for chain in inward:
                 while chain:
@@ -1560,7 +1701,7 @@
         step(block, emit)
 
     back = gather_work_scatter(links, grad_b, fill, back_work, second)
-    loads.need(3, 4, 5)
+    loads.need(13, 14, 15)
     weight_out(act, grad_b, gw_out)
     tick(outward)
     weight_in(hid, inner, gw_in, sums_ref)
@@ -1597,28 +1738,33 @@
     return pl.pallas_call(
         functools.partial(rear_body, heads, width // heads, nb),
         out_shape=[
-            shape((rows, features), full), shape((3, features, width), low), shape((features, width), low),
+            shape((rows, features), full),
+            shape((features, width), low), shape((features, width), low), shape((features, width), low),
+            shape((features, width), low),
             shape((width, features), low), shape((8, features), full), shape((8, width), full),
             shape((features, hidden), low), shape((hidden, features), low), shape((8, features), full),
         ]
         + [shape(r.shape, low) for r in ridden],
-        in_specs=[VMEM_SPEC] * 16 + [HBM_SPEC] * 6,
-        out_specs=[VMEM_SPEC] * 11,
+        in_specs=[VMEM_SPEC] * 6 + [HBM_SPEC] * 16,
+        out_specs=[VMEM_SPEC] * 13,
         scratch_shapes=[
             vmem((4, rows, features), low), narrow, narrow, narrow, vmem((4, 2 * rows, width), low),
             vmem((rows, features), full), vmem((4, rows, features), low), vmem((4, rows, hidden), low),
             vmem((rows, features), full), vmem((4, rows, features), low), vmem((4, rows, hidden), low),
             vmem((4, rows, hidden), low), vmem((hidden, features), low), vmem((features, hidden), low),
         ]
+        + [vmem(a.shape, a.dtype) for a in (*saved_mix, table, proj, w_qkv)]
         + sums_scratch(rows, features)
         + sums_scratch(rows, features)
-        + [dma((24,)), dma((24,)), dma((4 * steps,)), dma((4 * steps,)), dma((6,))]
+        + [dma((24,)), dma((24,)), dma((4 * steps,)), dma((4 * steps,)), dma((16,))]
         + between,
         compiler_params=pltpu.CompilerParams(
             collective_id=ident, has_side_effects=True, vmem_limit_bytes=62 << 20
         ),
         name="rear",
-    )(stream, rows_one, pack, *saved_mix, table, proj, w_qkv, w_mine, *ridden, rows_in, *saved, w_rows, ffn_in)
+    )(
+        stream, rows_one, pack, w_mine, *ridden, *saved_mix, table, proj, w_qkv, rows_in, *saved, w_rows, ffn_in
+    )
 
 
 def body(
@@ -1630,10 +1776,6 @@
     width = features // ns
     heads = HEADS // ns
     rows_in = tokens[0]
-
-    own_length = jnp.broadcast_to(b16(f32(lengths))[:, None], (5, width))
-    pack_in = jnp.concatenate([norm_gains, biases, depthwise, own_length], 0)
-    b_in = f32(ffn_bias)
 
     rates = jnp.exp(
         jnp.arange(features // 2, dtype=jnp.float32) * (-2.0 * math.log(10000.0) / features)
@@ -1647,30 +1789,31 @@
     angles = turns[:, None] * rates[None, :]
     base = jnp.concatenate([jnp.sin(angles), jnp.cos(angles)], 1)
     (
-        rows_one, rows_two, pack, table, proj, with_u, with_v, key, value, mix, wc_in, w_mine,
+        rows_one, rows_two, pack, table, proj, with_u, with_v, key, value, mix, wc_in, w_mine, wc_out,
         *saved_one, w_rows_one, hidden_mix, soft,
     ) = front(
-        rows_in, pack_in, b_in, base, biases, pos_proj, qkv_proj, ffn_in, ffn_out, out_proj, conv_in, heads, 5
+        rows_in, norm_gains, biases, depthwise, lengths, ffn_bias, base, pos_proj, qkv_proj, ffn_in, ffn_out, out_proj, conv_in, conv_out,
+        heads, 5,
     )
     saved_mix = (hidden_mix, with_u, with_v, key, value, soft, mix)
-    rows_three, *saved_conv, wc_out, w_rows_two = conv_forward(
-        rows_two, pack, wc_in, conv_out, ffn_out, 10
+    rows_three, *saved_conv, w_rows_two = conv_forward(
+        rows_two, pack, wc_in, wc_out, ffn_out, 10
     )
     result, stream, two_in, two_out, two_sums, *early = middle(
-        rows_three, pack, b_in, w_rows_two, cotangent[0], ffn_in, 6
+        rows_three, pack, ffn_bias, w_rows_two, cotangent[0], ffn_in, 6
     )
 
     stream, grad_conv_out, grad_conv_in, conv_sums, *ridden = conv_back(
         stream, rows_two, pack, wc_in, wc_out, saved_conv, (two_in, two_out), early, 11
     )
-    stream, grad_qkv, grad_pos, grad_out, mix_sums, own_sums, one_in, one_out, one_sums, *ridden = rear(
+    stream, grad_q, grad_k, grad_x, grad_pos, grad_out, mix_sums, own_sums, one_in, one_out, one_sums, *ridden = rear(
         stream, rows_one, pack, saved_mix, table, proj, qkv_proj, w_mine, ridden, rows_in, saved_one, w_rows_one,
         ffn_in, heads, 12
     )
     tall, deep = one_in.shape
     piece = max(128, 8 * nb)
     *sums, out_gains, out_biases, out_taps, out_hidden = tail_sum(
-        [grad_out, one_out, one_in] + [grad_qkv[at] for at in range(3)] + [grad_pos, grad_conv_in, grad_conv_out],
+        [grad_out, one_out, one_in, grad_q, grad_k, grad_x, grad_pos, grad_conv_in, grad_conv_out],
         ridden,
         [one_sums, mix_sums, two_sums, conv_sums, own_sums],
         [("turn", 4, None), ("turn", 1, 0), ("plain", 0, 0)]
@@ -1685,17 +1828,20 @@
         deep,
         4,
     )
+    *sums, result, stream, out_gains, out_biases, out_taps, out_hidden = widen(
+        sums, [result, stream, out_gains, out_biases, out_taps, out_hidden]
+    )
     return (
         result[None],
         stream[None],
-        f32(sums[0]),
-        f32(sums[1]),
+        sums[0],
+        sums[1],
         out_hidden,
-        f32(sums[2]),
-        f32(sums[3]),
-        f32(sums[4]),
-        f32(sums[5]),
-        f32(sums[6]),
+        sums[2],
+        sums[3],
+        sums[4],
+        sums[5],
+        sums[6],
         out_taps,
         out_gains,
         out_biases,

time: 565 us -> 535 us (0.947)
  other arithmetic: 21.3 us -> 1.22 us
  local copies, waits for them, and re-layouts: 8.98 us -> 0 us
    convert_element_type x8 -> x0, other arithmetic: 18.7 us -> none  [f32(): return a.astype(jnp.float32)]
    pallas_call x0 -> x1, Pallas kernels: none -> 15.6 us  [widen(): pl.pallas_call(functools.partial(widen_body, len(arrays), len(others), sl...]
    pallas_call x1, Pallas kernels: 38.1 us -> 31.5 us  [conv_forward(): pl.pallas_call(functools.partial(conv_body, nb), out_shape=[shape((rows,...]
    unnamed x28 -> x0, local copies, waits for them, and re-layouts: 6.37 us -> none
where the time goes in v7:
time: 535 us; the launch traced here: 531 us
  Pallas kernels  528 us (99%)
    pallas_call x1, Pallas kernels, tail_sum(): pl.pallas_call(functools.partial(tail_body, specs, chunks, ns, nb, len(ar...  218 us
    pallas_call x1, Pallas kernels, front(): pl.pallas_call(functools.partial(front_body, heads, width // heads), out_...  86.6 us
    pallas_call x1, Pallas kernels, rear(): pl.pallas_call(functools.partial(rear_body, heads, width // heads, nb), o...  83.3 us
    pallas_call x1, Pallas kernels, middle(): pl.pallas_call(functools.partial(middle_body, nb, EARLY), out_shape=[shap...  61.7 us
    pallas_call x1, Pallas kernels, conv_forward(): pl.pallas_call(functools.partial(conv_body, nb), out_shape=[shape((rows,...  31.5 us
    pallas_call x1, Pallas kernels, conv_back(): pl.pallas_call(functools.partial(conv_back_body, nb), out_shape=[shape((r...  31.5 us
    pallas_call x1, Pallas kernels, widen(): pl.pallas_call(functools.partial(widen_body, len(arrays), len(others), sl...  15.6 us

profile of v7, /device:TPU:0, one launch (start us, length us, event | category | flops | bytes accessed | tf_op | source)
XLA Modules:
  0.0 531.2 jit_solution(3350700894147476399)
XLA Ops:
  1.3 0.1 pad_maximum_fusion.1
  1.4 0.4 multiply_sine_fusion
  1.8 0.7 pad_maximum_fusion.base_ref
  2.5 86.6 %front.1 = (f32[256,1024]{1,0:T(8,128)}, f32[256,1024]{1,0:T(8,128)}, bf16[4,32,256]{2,1,0:T(8,128)(2,1)}, bf16[512,1024]{1,0:T(8,128)(2,1)}, bf16[512,256]{1,0:...) custom-call(f32[256,1024]{1,0:T(8,128)} %bitcast.4, ...), custom_call_target="tpu_custom_call" | custom-call | tf_op jit(solution)/shard_map/front/pallas_call | solution.py:1140
  89.2 31.5 %conv_forward.1 = (f32[256,1024]{1,0:T(8,128)}, bf16[256,1024]{1,0:T(8,128)(2,1)}, bf16[256,1024]{1,0:T(8,128)(2,1)}, bf16[256,1024]{1,0:T(8,128)(2,1)}, bf16[25...) custom-call(f32[256,1024]{1,0:T(8,128)} %get-tuple-element.92.rows_r, ...), custom_call_target="tpu_custom_call" | custom-call | tf_op jit(solution)/shard_map/conv_forward/pallas_call | solution.py:1393
  120.7 61.7 %middle.1 = (f32[256,1024]{1,0:T(8,128)}, f32[256,1024]{1,0:T(8,128)}, bf16[1024,1024]{1,0:T(8,128)(2,1)}, bf16[1024,1024]{1,0:T(8,128)(2,1)}, f32[8,1024]{1,0:T...) custom-call(f32[256,1024]{1,0:T(8,128)} %get-tuple-element.96.rows_ref, ...), custom_call_target="tpu_custom_call" | custom-call | tf_op jit(solution)/shard_map/middle/pallas_call | solution.py:1264
  182.4 31.5 %conv_back.1 = (f32[256,1024]{1,0:T(8,128)}, bf16[1024,1024]{1,0:T(8,128)(2,1)}, bf16[1024,2048]{1,0:T(8,128)(2,1)}, f32[16,1024]{1,0:T(8,128)}, bf16[512,1024]{1,0:T(8,128)(2,1)}, /*index=5*/bf16[512,1024]{1,0:T(8,128)(2,1)}) custom-call(f32[256,1024]{1,0:T(8,128)} %get-tuple-element.98.stream_ref, f32[256,1024]{1,0:T(8,128)} %get-tuple-element.92.rows_ref, ...), custom_call_target="tpu_custom_call" | custom-call | tf_op jit(solution)/shard_map/conv_back/pallas_call | solution.py:1522
  213.9 83.3 %rear.1 = (f32[256,1024]{1,0:T(8,128)}, bf16[1024,256]{1,0:T(8,128)(2,1)}, bf16[1024,256]{1,0:T(8,128)(2,1)}, bf16[1024,256]{1,0:T(8,128)(2,1)}, bf16[1024,256]{...) custom-call(f32[256,1024]{1,0:T(8,128)} %get-tuple-element.111.strea, ...), custom_call_target="tpu_custom_call" | custom-call | tf_op jit(solution)/shard_map/rear/pallas_call | solution.py:1738
  297.2 217.9 %tail_sum.1 = (bf16[2,1024,1024]{2,1,0:T(8,128)(2,1)}, bf16[2,4096,256]{2,1,0:T(8,128)(2,1)}, bf16[3,1024,256]{2,1,0:T(8,128)(2,1)}, bf16[1024,256]{1,0:T(8,128)...) custom-call(f32[8,1024]{1,0:T(8,128)} %get-tuple-element.129.refs_0_, ...), custom_call_target="tpu_custom_call" | custom-call | tf_op jit(solution)/shard_map/tail_sum/pallas_call | solution.py:576
  515.1 15.6 %widen.1 = (f32[2,1024,1024]{2,1,0:T(8,128)}, f32[2,4096,256]{2,1,0:T(8,128)}, f32[3,1024,256]{2,1,0:T(8,128)}, f32[1024,256]{1,0:T(8,128)}, f32[1024,256]{1,0:T...) custom-call(bf16[2,1024,1024]{2,1,0:T(8,128)(2,1)} %get-tuple-elemen, ...), custom_call_target="tpu_custom_call" | custom-call | tf_op jit(solution)/shard_map/widen/pallas_call | solution.py:646
  (3 shorter events, 0.0 us)

commit v8 on v7

--- a/solution.py
+++ b/solution.py
@@ -968,7 +968,7 @@
     heads, size,
     rows_ref, gains_ref, own_ref, taps_ref, b_ref, base_ref, length_ref,
     pos_hbm, qkv_hbm, ffn_in, ffn_out, out_proj, conv_in, conv_out,
-    one_ref, two_ref, pack, table, proj, with_u, with_v, key, value, mix, wc_in, w_mine, wc_out,
+    one_ref, two_ref, pack, table, proj, with_u, with_v, key, value, mix, wc_in, w_mine, wc_out, w_rows_two,
     hid_out, act_out, slope_out, w_rows_out, hidden_out, soft_out,
     hid, act, slope, w_rows, w_in, w_out, pos_ref, w_qkv, hid_b, soft_ref, turned,
     part, send, land, cross, land_cross, send_sem, recv_sem, local_sem, load_sem, flush_sem, pack_in,
@@ -1003,10 +1003,10 @@
     up = ffn_up(hid, act, slope, w_in, b_ref, 0)
     loads.need(0)
     up(0)
+    down.pop(0)()
+    down.pop(0)()
     near.wait()
     up(1)
-    down.pop(0)()
-    down.pop(0)()
     lanes = features // 2
 
     @pl.loop(0, table.shape[0] // 16)
@@ -1019,17 +1019,19 @@
 
     loads.need(1)
     proj[...] = b16(dot_rows(table[...], pos_ref[...]))
+    down.pop(0)()
+    down.pop(0)()
     other = fetch.columns(out_proj, w_out, 1)
-    leaving = fetch.columns(conv_out, wc_out, 3)
+    leaving = fetch.columns(conv_in, wc_in, 3)
+    second = fetch.rows(ffn_out.at[1], w_rows_two, 4)
     for h in range(2):
         out[h].wait()
         on = links.go(hid.at[2 + h, pl.ds(0, half)], hid.at[2 + h, pl.ds(half, half)], links.near)
         on.wait()
         if h == 1:
             other.pop(0)()
-            leaving.pop(0)()
         up(2 + h)
-        down.pop(0)()
+    leaving.pop(0)()
     for pair in ((hid, hid_out), (act, act_out), (slope, slope_out)):
         flush.go(*pair)
     while down:
@@ -1042,6 +1044,7 @@
         sums.send_back(h)
     for h in range(2):
         sums.send_cross(h)
+    second.pop(0)()
     work(1, sums.give)
     sums.send_near()
     work(0, sums.keep)
@@ -1062,7 +1065,7 @@
     while other:
         other.pop(0)()
         leaving.pop(0)()
-    entering = fetch.columns(conv_in, wc_in, 2)
+    entering = fetch.columns(conv_out, wc_out, 2)
     own = f32(own_ref[...])
     keys = f32(lax.broadcasted_iota(jnp.int32, (rows, rows), 1))
     scale = 1.0 / math.sqrt(size)
@@ -1091,7 +1094,11 @@
     attend(0)
     turned[links.shard] = mix[0]
     near.wait()
+    second.pop(0)()
+    second.pop(0)()
     attend(1)
+    second.pop(0)()
+    second.pop(0)()
     last.append(links.go(mix.at[1], turned.at[links.shard], links.near))
     on = []
     for h in range(2):
@@ -1122,6 +1129,8 @@
     w_mine[...] = w_out[pl.ds(pl.multiple_of(links.shard * width, 16), width), :]
     while entering:
         entering.pop(0)()
+    while second:
+        second.pop(0)()
     flush.settle()
 
 
@@ -1147,13 +1156,14 @@
             shape((conv_in.shape[0], ns * conv_in.shape[1]), low),
             shape((width, features), low),
             shape((features, features), low),
+            shape((hidden, features), low),
             shape((4, rows, features), low), shape((4, rows, hidden), low), shape((4, rows, hidden), low),
             shape((hidden, features), low),
             shape((ns, rows, features), low),
             shape((ns, rows, heads * rows), full),
         ],
         in_specs=[VMEM_SPEC] * 6 + [pl.BlockSpec(memory_space=pltpu.SMEM)] + [HBM_SPEC] * 7,
-        out_specs=[VMEM_SPEC] * 13 + [HBM_SPEC] * 6,
+        out_specs=[VMEM_SPEC] * 14 + [HBM_SPEC] * 6,
         scratch_shapes=[
             vmem((4, rows, features), low), vmem((4, rows, hidden), low), vmem((4, rows, hidden), low),
             vmem((hidden, features), low), vmem((features, hidden), low), vmem((features, features), low),
@@ -1161,7 +1171,7 @@
             vmem((ns, rows, features), low), vmem((ns, rows, heads * rows), full), vmem((ns, rows, width), low),
         ]
         + sums_scratch(rows, features)
-        + link_scratch(80, 4)
+        + link_scratch(100, 5)
         + [dma((3,)), dma((6,)), vmem((32, width), low)],
         compiler_params=pltpu.CompilerParams(
             collective_id=ident, has_side_effects=True, vmem_limit_bytes=60 << 20
@@ -1316,25 +1326,24 @@
 
 
 def conv_body(
-    nb, rows_ref, pack, w_in, w_out, ffn_out,
-    out_ref, hid, open_ref, gate_ref, gated_ref, scaled_ref, act, slope, stats, w_rows,
-    padded, source, mid, land_s, land_b, ss, rs, sb, rb, send_sem, recv_sem, local_sem,
+    nb, rows_ref, pack, w_in_hbm, w_out_hbm,
+    out_ref, hid, open_ref, gate_ref, gated_ref, scaled_ref, act, slope, stats,
+    padded, source, mid, land_s, land_b, ss, rs, sb, rb, send_sem, recv_sem, local_sem, w_in, w_out, load_sem,
 ):
     batch = lax.axis_index("batch")
     links = Links(send_sem, recv_sem)
-    fetch = Fetch(links, batch, local_sem)
+    loads = Loads(load_sem, [(w_in_hbm, w_in), (w_out_hbm, w_out)])
     rows, features = rows_ref.shape
     ns = land_s.shape[0]
     links.greet(
         [links.near, links.far, links.across]
         + [{"batch": lax.rem(batch + j, nb)} for j in range(1, nb)]
     )
-    down = fetch.rows(ffn_out.at[1], w_rows, 1)
-    down.pop(0)()
     live = f32(pack[links.shard, 27:28, 0:1])
     mask = f32(f32(lax.broadcasted_iota(jnp.int32, (rows, 1), 0)) < live)
     hid[...] = b16(norm_rows(rows_ref[...], vector_row(pack, 2), vector_row(pack, 14)))
     bias_v, bias_g = vector_row(pack, 15), vector_row(pack, 16)
+    loads.need(0)
     lead = 8
     tile = 512
     padded[0:lead, :] = jnp.zeros((lead, features), jnp.float32)
@@ -1361,11 +1370,7 @@
     pack_rows(source, lanes, jnp.sum(live_total * total, axis=0, keepdims=True))
     source[2 * lanes : 2 * lanes + 8, :] = jnp.broadcast_to(live, (8, 128))
     scaled_ref[...] = total
-    down.pop(0)()
-    down.pop(0)()
     sums = everywhere(links, nb, source, mid, land_s, land_b, None, lambda: None, (ss, rs, sb, rb))
-    down.pop(0)()
-    down.pop(0)()
     frames = sums[2 * lanes : 2 * lanes + 1, 0:1]
     mean = unpack_rows(sums, 0, lanes) / frames
     inverse = lax.rsqrt(unpack_rows(sums, lanes, lanes) / frames - mean * mean + epsilon)
@@ -1378,12 +1383,11 @@
     gate = jax.nn.sigmoid(normed)
     act[...] = b16(normed * gate)
     slope[...] = b16(gate * (1.0 + normed * (1.0 - gate)))
+    loads.need(1)
     out_ref[...] = rows_ref[...] + (dot_rows(act[...], w_out[...]) + vector_row(pack, 18))
-    while down:
-        down.pop(0)()
-
-
-def conv_forward(rows_in, pack, w_in, w_out, ffn_out, ident):
+
+
+def conv_forward(rows_in, pack, w_in, w_out, ident):
     ns, nb = lax.axis_size("shard"), lax.axis_size("batch")
     rows, features = rows_in.shape
     shape = jax.ShapeDtypeStruct
@@ -1395,10 +1399,9 @@
         out_shape=[
             shape((rows, features), full), plain, plain, plain, plain,
             shape((rows, features), full), plain, plain, shape((8, features), full),
-            shape((ffn_out.shape[1] // ns, features), low),
         ],
-        in_specs=[VMEM_SPEC] * 4 + [HBM_SPEC],
-        out_specs=[VMEM_SPEC] * 10,
+        in_specs=[VMEM_SPEC] * 2 + [HBM_SPEC] * 2,
+        out_specs=[VMEM_SPEC] * 9,
         scratch_shapes=[
             pltpu.VMEM((rows + 16, features), full),
             pltpu.VMEM(small, full), pltpu.VMEM(small, full),
@@ -1406,12 +1409,13 @@
             pltpu.SemaphoreType.DMA((ns,)), pltpu.SemaphoreType.DMA((ns,)),
             pltpu.SemaphoreType.DMA((nb,)), pltpu.SemaphoreType.DMA((nb,)),
         ]
-        + link_scratch(32, 3),
+        + link_scratch(2, 1)
+        + [pltpu.VMEM(w_in.shape, low), pltpu.VMEM(w_out.shape, low), pltpu.SemaphoreType.DMA((2,))],
         compiler_params=pltpu.CompilerParams(
             collective_id=ident, has_side_effects=True, vmem_limit_bytes=60 << 20
         ),
         name="conv_forward",
-    )(rows_in, pack, w_in, w_out, ffn_out)
+    )(rows_in, pack, w_in, w_out)
 
 
 def conv_back_body(
@@ -1790,14 +1794,14 @@
     base = jnp.concatenate([jnp.sin(angles), jnp.cos(angles)], 1)
     (
         rows_one, rows_two, pack, table, proj, with_u, with_v, key, value, mix, wc_in, w_mine, wc_out,
-        *saved_one, w_rows_one, hidden_mix, soft,
+        w_rows_two, *saved_one, w_rows_one, hidden_mix, soft,
     ) = front(
         rows_in, norm_gains, biases, depthwise, lengths, ffn_bias, base, pos_proj, qkv_proj, ffn_in, ffn_out, out_proj, conv_in, conv_out,
         heads, 5,
     )
     saved_mix = (hidden_mix, with_u, with_v, key, value, soft, mix)
-    rows_three, *saved_conv, w_rows_two = conv_forward(
-        rows_two, pack, wc_in, wc_out, ffn_out, 10
+    rows_three, *saved_conv = conv_forward(
+        rows_two, pack, wc_in, wc_out, 10
     )
     result, stream, two_in, two_out, two_sums, *early = middle(
         rows_three, pack, ffn_bias, w_rows_two, cotangent[0], ffn_in, 6

time: 535 us -> 517 us (0.966)
  Pallas kernels: 528 us -> 510 us
    pallas_call x1, Pallas kernels: 31.5 us -> 17.2 us  [conv_forward(): pl.pallas_call(functools.partial(conv_body, nb), out_shape=[shape((rows,...]
where the time goes in v8:
time: 517 us; the launch traced here: 513 us
  Pallas kernels  510 us (99%)
    pallas_call x1, Pallas kernels, tail_sum(): pl.pallas_call(functools.partial(tail_body, specs, chunks, ns, nb, len(ar...  217 us
    pallas_call x1, Pallas kernels, front(): pl.pallas_call(functools.partial(front_body, heads, width // heads), out_...  84 us
    pallas_call x1, Pallas kernels, rear(): pl.pallas_call(functools.partial(rear_body, heads, width // heads, nb), o...  83.3 us
    pallas_call x1, Pallas kernels, middle(): pl.pallas_call(functools.partial(middle_body, nb, EARLY), out_shape=[shap...  62.4 us
    pallas_call x1, Pallas kernels, conv_back(): pl.pallas_call(functools.partial(conv_back_body, nb), out_shape=[shape((r...  30.9 us
    pallas_call x1, Pallas kernels, conv_forward(): pl.pallas_call(functools.partial(conv_body, nb), out_shape=[shape((rows,...  17.2 us
    pallas_call x1, Pallas kernels, widen(): pl.pallas_call(functools.partial(widen_body, len(arrays), len(others), sl...  15.6 us

profile of v8, /device:TPU:0, one launch (start us, length us, event | category | flops | bytes accessed | tf_op | source)
XLA Modules:
  0.0 513.5 jit_solution(16175957939619217546)
XLA Ops:
  1.3 0.1 pad_maximum_fusion.1
  1.4 0.4 multiply_sine_fusion
  1.8 0.7 pad_maximum_fusion.base_ref
  2.5 84.0 %front.1 = (f32[256,1024]{1,0:T(8,128)}, f32[256,1024]{1,0:T(8,128)}, bf16[4,32,256]{2,1,0:T(8,128)(2,1)}, bf16[512,1024]{1,0:T(8,128)(2,1)}, bf16[512,256]{1,0:...) custom-call(f32[256,1024]{1,0:T(8,128)} %bitcast.4, ...), custom_call_target="tpu_custom_call" | custom-call | tf_op jit(solution)/shard_map/front/pallas_call | solution.py:1149
  86.6 17.2 %conv_forward.1 = (f32[256,1024]{1,0:T(8,128)}, bf16[256,1024]{1,0:T(8,128)(2,1)}, bf16[256,1024]{1,0:T(8,128)(2,1)}, bf16[256,1024]{1,0:T(8,128)(2,1)}, bf16[25...) custom-call(f32[256,1024]{1,0:T(8,128)} %get-tuple-element.92.rows_r, ...), custom_call_target="tpu_custom_call" | custom-call | tf_op jit(solution)/shard_map/conv_forward/pallas_call | solution.py:1397
  103.8 62.4 %middle.1 = (f32[256,1024]{1,0:T(8,128)}, f32[256,1024]{1,0:T(8,128)}, bf16[1024,1024]{1,0:T(8,128)(2,1)}, bf16[1024,1024]{1,0:T(8,128)(2,1)}, f32[8,1024]{1,0:T...) custom-call(f32[256,1024]{1,0:T(8,128)} %get-tuple-element.96.rows_ref, ...), custom_call_target="tpu_custom_call" | custom-call | tf_op jit(solution)/shard_map/middle/pallas_call | solution.py:1274
  166.2 30.9 %conv_back.1 = (f32[256,1024]{1,0:T(8,128)}, bf16[1024,1024]{1,0:T(8,128)(2,1)}, bf16[1024,2048]{1,0:T(8,128)(2,1)}, f32[16,1024]{1,0:T(8,128)}, bf16[512,1024]{1,0:T(8,128)(2,1)}, /*index=5*/bf16[512,1024]{1,0:T(8,128)(2,1)}) custom-call(f32[256,1024]{1,0:T(8,128)} %get-tuple-element.98.stream_ref, f32[256,1024]{1,0:T(8,128)} %get-tuple-element.92.rows_ref, ...), custom_call_target="tpu_custom_call" | custom-call | tf_op jit(solution)/shard_map/conv_back/pallas_call | solution.py:1526
  197.2 83.3 %rear.1 = (f32[256,1024]{1,0:T(8,128)}, bf16[1024,256]{1,0:T(8,128)(2,1)}, bf16[1024,256]{1,0:T(8,128)(2,1)}, bf16[1024,256]{1,0:T(8,128)(2,1)}, bf16[1024,256]{...) custom-call(f32[256,1024]{1,0:T(8,128)} %get-tuple-element.111.strea, ...), custom_call_target="tpu_custom_call" | custom-call | tf_op jit(solution)/shard_map/rear/pallas_call | solution.py:1742
  280.5 216.9 %tail_sum.1 = (bf16[2,1024,1024]{2,1,0:T(8,128)(2,1)}, bf16[2,4096,256]{2,1,0:T(8,128)(2,1)}, bf16[3,1024,256]{2,1,0:T(8,128)(2,1)}, bf16[1024,256]{1,0:T(8,128)...) custom-call(f32[8,1024]{1,0:T(8,128)} %get-tuple-element.129.refs_0_, ...), custom_call_target="tpu_custom_call" | custom-call | tf_op jit(solution)/shard_map/tail_sum/pallas_call | solution.py:576
  497.4 15.6 %widen.1 = (f32[2,1024,1024]{2,1,0:T(8,128)}, f32[2,4096,256]{2,1,0:T(8,128)}, f32[3,1024,256]{2,1,0:T(8,128)}, f32[1024,256]{1,0:T(8,128)}, f32[1024,256]{1,0:T...) custom-call(bf16[2,1024,1024]{2,1,0:T(8,128)(2,1)} %get-tuple-elemen, ...), custom_call_target="tpu_custom_call" | custom-call | tf_op jit(solution)/shard_map/widen/pallas_call | solution.py:646
  (3 shorter events, 0.0 us)

commit v9 on v8

--- a/solution.py
+++ b/solution.py
@@ -100,8 +100,11 @@
         self.at, self.source, self.row, self.rows, self.columns = at, source, row, rows, columns
         extra = [(1 << k, k) for k in range(3, count.bit_length() - 1)]
         line = (6, 1)
+        self.halved = first == "half"
         if first == "near":
             self.pre, self.post = [(1, 0)], [line] + extra
+        elif self.halved:
+            self.pre, self.post = [], [line] + extra
         else:
             self.pre, self.post = [], [line, (1, 0)] + extra
         size, self.landings = rows, []
@@ -156,6 +159,8 @@
         here, base = self.source, self.base
         off, size, step = 0, c.rows, 0
         plan, trail = [], []
+        if c.halved:
+            trail.append(("all", 1, off, size))
         sequence = [("all",) + p for p in c.pre] + [("fold", 2, None)]
         sequence += [("inner",) + p for p in c.post]
         for kind, mask, sel in sequence:
@@ -502,6 +507,15 @@
 
             def finish(c, out=out, lead=lead):
                 leave(out, lead, c.row, c.rows)
+
+            if c.halved:
+                apart = outs[out].shape[-2] // 2
+                mine = bit_of(batch, 0) * apart
+                held = lambda off, size, target=target, c=c, mine=mine: row_view(target, mine + c.row + off, size)
+
+                def finish(c, out=out, lead=lead, apart=apart):
+                    leave(out, lead, c.row, c.rows)
+                    leave(out, lead, apart + c.row, c.rows)
         landings = [rest.pop(0) for _ in range(c.steps)]
         m = Mover(c, batch, source, base, held, landings, (send, recv), finish, early)
         m.settle_early = settle
@@ -540,8 +554,9 @@
         step = chunk_rows[i]
         columns = a.shape[1] // ns if kinds[i][0] == "gather" else a.shape[1]
         for row in range(0, a.shape[0], step):
-            chunks.append(Chunk(len(chunks), i, row, step, columns, firsts[len(chunks) % len(firsts)], nb))
-    depth = max(2 * c.steps for c in chunks)
+            first = "half" if kinds[i][0] == "half" else firsts[len(chunks) % len(firsts)]
+            chunks.append(Chunk(len(chunks), i, row, step, columns, first, nb))
+    depth = max(2 * c.steps + c.halved for c in chunks)
     specs = dict(arrays=kinds, lag=2)
     width = sums[-1].shape[1]
     per = hidden // width
@@ -1183,118 +1198,6 @@
     )
 
 
-def middle_body(
-    nb, early, rows_ref, pack, b_ref, w_rows_hbm, cotangent_hbm, ffn_in,
-    result, out_ref, gw_in, gw_out, sums_ref, early_a, early_b,
-    hid, act, slope, grad, inner, w_in, cotangent, stream, w_rows, *refs,
-):
-    first, second, refs = refs[:5], refs[5:10], refs[10:]
-    send_sem, recv_sem, ride_send, ride_recv, load_sem = refs
-    batch = lax.axis_index("batch")
-    links = Links(send_sem, recv_sem)
-    loads = Loads(load_sem, [(ffn_in.at[1], w_in), (cotangent_hbm, cotangent), (w_rows_hbm, w_rows)])
-    orders = ride_orders(nb)
-    links.greet([links.near, links.far] + [{"batch": flip_bits(batch, 1 << k)} for k in range(2)])
-    rows, features = rows_ref.shape
-    half = rows // 2
-    gain, shift = vector_row(pack, 4), vector_row(pack, 19)
-
-    def fill(h):
-        at = slice(h * half, (h + 1) * half)
-        hid[0, at] = b16(norm_rows(rows_ref[at], gain, shift))
-
-    up, down = ffn_up(hid, act, slope, w_in, b_ref, 1), ffn_down(act, w_rows)
-
-    def work(block, emit):
-        loads.need(0)
-        up(block)
-        loads.need(2)
-        down(block, emit)
-
-    sums = gather_work_scatter(links, hid, fill, work, first)
-    last_gain, last_shift, out_bias = vector_row(pack, 5), vector_row(pack, 21), vector_row(pack, 20)
-    live = f32(pack[links.shard, 27:28, 0:1])
-    mask = f32(f32(lax.broadcasted_iota(jnp.int32, (rows, 1), 0)) < live)
-    loads.need(1)
-    ends = []
-
-    def turn_back(h):
-        at = slice(h * half, (h + 1) * half)
-        scaled, inverse = norm_parts(rows_ref[at] + 0.5 * (sums.arrive(h) + out_bias))
-        result[at] = (scaled * last_gain + last_shift) * mask[at]
-        given = cotangent[at] * mask[at]
-        slide = norm_slope(given, scaled, inverse, last_gain)
-        stream[at] = slide
-        grad[0, at] = b16(0.5 * slide)
-        ends.append((column_sum(given * scaled), column_sum(given)))
-
-    back = gather_work_scatter(
-        links, grad, turn_back, ffn_inward(grad, inner, slope, w_in, w_rows), second
-    )
-    pieces = 4
-    riders = [
-        Rider(batch, ride_send, ride_recv, at * early).halve_pieces(
-            (gw_in, gw_out)[at], (early_a, early_b)[at], orders[at][0], pieces, gw_in.shape[0] // 2
-        )
-        for at in range(2)
-    ]
-    weight_out(act, grad, gw_out)
-    for p in range(early):
-        riders[1][0](p)
-    weight_in(hid, inner, gw_in, sums_ref)
-    for p in range(early):
-        riders[0][0](p)
-    sums_ref[0:3, :] = jnp.zeros((3, features), jnp.float32)
-    sums_ref[2:3, :] = column_sum(f32(grad[0]))
-    sums_ref[4:5, :] = ends[0][0] + ends[1][0]
-    sums_ref[5:6, :] = ends[0][1] + ends[1][1]
-    sums_ref[6:8, :] = jnp.zeros((2, features), jnp.float32)
-    for h in range(2):
-        at = slice(h * half, (h + 1) * half)
-        scaled, inverse = norm_parts(rows_ref[at])
-        given = back.arrive(h)
-        out_ref[at] = stream[at] + norm_slope(given, scaled, inverse, gain)
-        sums_ref[0:1, :] += column_sum(given * scaled)
-        sums_ref[1:2, :] += column_sum(given)
-    for _, settle, _ in riders:
-        settle()
-
-
-EARLY = 1
-
-
-def middle(rows_in, pack, b_in, w_rows, cotangent, ffn_in, ident):
-    rows, features = rows_in.shape
-    hidden = ffn_in.shape[2]
-    nb = lax.axis_size("batch")
-    low, full = jnp.bfloat16, jnp.float32
-    shape, vmem = jax.ShapeDtypeStruct, pltpu.VMEM
-    dma = pltpu.SemaphoreType.DMA
-    piece = features // 8
-    return pl.pallas_call(
-        functools.partial(middle_body, nb, EARLY),
-        out_shape=[
-            shape((rows, features), full), shape((rows, features), full),
-            shape((features, hidden), low), shape((hidden, features), low), shape((8, features), full),
-            shape((EARLY * piece, hidden), low), shape((EARLY * piece, features), low),
-        ],
-        in_specs=[VMEM_SPEC] * 3 + [HBM_SPEC] * 3,
-        out_specs=[VMEM_SPEC] * 7,
-        scratch_shapes=[
-            vmem((4, rows, features), low), vmem((4, rows, hidden), low), vmem((4, rows, hidden), low),
-            vmem((4, rows, features), low), vmem((4, rows, hidden), low), vmem((features, hidden), low),
-            vmem((rows, features), full), vmem((rows, features), full), vmem((hidden, features), low),
-        ]
-        + sums_scratch(rows, features)
-        + sums_scratch(rows, features)
-        + [dma((20,)), dma((20,)), dma((2 * EARLY,)), dma((2 * EARLY,)), dma((3,))],
-        compiler_params=pltpu.CompilerParams(
-            collective_id=ident, has_side_effects=True, vmem_limit_bytes=60 << 20
-        ),
-        name="middle",
-    )(rows_in, pack, b_in, w_rows, cotangent, ffn_in)
-
-
 def pack_rows(ref, at, row):
     for i in range(row.shape[1] // 128):
         ref[at + i : at + i + 1, :] = row[:, i * 128 : (i + 1) * 128]
@@ -1325,20 +1228,12 @@
     return sum_slots(land_b, nb)
 
 
-def conv_body(
-    nb, rows_ref, pack, w_in_hbm, w_out_hbm,
+def conv_part(
+    links, nb, loads, rows_ref, pack, w_in, w_out,
     out_ref, hid, open_ref, gate_ref, gated_ref, scaled_ref, act, slope, stats,
-    padded, source, mid, land_s, land_b, ss, rs, sb, rb, send_sem, recv_sem, local_sem, w_in, w_out, load_sem,
+    padded, source, mid, land_s, land_b, sems,
 ):
-    batch = lax.axis_index("batch")
-    links = Links(send_sem, recv_sem)
-    loads = Loads(load_sem, [(w_in_hbm, w_in), (w_out_hbm, w_out)])
     rows, features = rows_ref.shape
-    ns = land_s.shape[0]
-    links.greet(
-        [links.near, links.far, links.across]
-        + [{"batch": lax.rem(batch + j, nb)} for j in range(1, nb)]
-    )
     live = f32(pack[links.shard, 27:28, 0:1])
     mask = f32(f32(lax.broadcasted_iota(jnp.int32, (rows, 1), 0)) < live)
     hid[...] = b16(norm_rows(rows_ref[...], vector_row(pack, 2), vector_row(pack, 14)))
@@ -1370,7 +1265,7 @@
     pack_rows(source, lanes, jnp.sum(live_total * total, axis=0, keepdims=True))
     source[2 * lanes : 2 * lanes + 8, :] = jnp.broadcast_to(live, (8, 128))
     scaled_ref[...] = total
-    sums = everywhere(links, nb, source, mid, land_s, land_b, None, lambda: None, (ss, rs, sb, rb))
+    sums = everywhere(links, nb, source, mid, land_s, land_b, None, lambda: None, sems)
     frames = sums[2 * lanes : 2 * lanes + 1, 0:1]
     mean = unpack_rows(sums, 0, lanes) / frames
     inverse = lax.rsqrt(unpack_rows(sums, lanes, lanes) / frames - mean * mean + epsilon)
@@ -1387,65 +1282,73 @@
     out_ref[...] = rows_ref[...] + (dot_rows(act[...], w_out[...]) + vector_row(pack, 18))
 
 
-def conv_forward(rows_in, pack, w_in, w_out, ident):
-    ns, nb = lax.axis_size("shard"), lax.axis_size("batch")
-    rows, features = rows_in.shape
-    shape = jax.ShapeDtypeStruct
-    low, full = jnp.bfloat16, jnp.float32
-    plain = shape((rows, features), low)
-    small = (24, 128)
-    return pl.pallas_call(
-        functools.partial(conv_body, nb),
-        out_shape=[
-            shape((rows, features), full), plain, plain, plain, plain,
-            shape((rows, features), full), plain, plain, shape((8, features), full),
-        ],
-        in_specs=[VMEM_SPEC] * 2 + [HBM_SPEC] * 2,
-        out_specs=[VMEM_SPEC] * 9,
-        scratch_shapes=[
-            pltpu.VMEM((rows + 16, features), full),
-            pltpu.VMEM(small, full), pltpu.VMEM(small, full),
-            pltpu.VMEM((ns,) + small, full), pltpu.VMEM((nb,) + small, full),
-            pltpu.SemaphoreType.DMA((ns,)), pltpu.SemaphoreType.DMA((ns,)),
-            pltpu.SemaphoreType.DMA((nb,)), pltpu.SemaphoreType.DMA((nb,)),
-        ]
-        + link_scratch(2, 1)
-        + [pltpu.VMEM(w_in.shape, low), pltpu.VMEM(w_out.shape, low), pltpu.SemaphoreType.DMA((2,))],
-        compiler_params=pltpu.CompilerParams(
-            collective_id=ident, has_side_effects=True, vmem_limit_bytes=60 << 20
-        ),
-        name="conv_forward",
-    )(rows_in, pack, w_in, w_out)
-
-
-def conv_back_body(
-    nb, stream_ref, rows_ref, pack, w_out, hid, open_ref, gate_ref, gated_ref, scaled_ref, act, slope, stats,
-    early_a, early_b, w_in_hbm, ride_a, ride_b, out_ref, gw_out, gw_in, sums_ref, half_a, half_b,
-    padded, normed, grad, inner, source, mid, land_s, land_b, ss, rs, sb, rb, send_sem, recv_sem,
-    w_in, kept_a, kept_b, load_sem,
+def middle_part(
+    links, loads, riders, rows_ref, pack, b_ref, result, out_ref, gw_in, gw_out, sums_ref,
+    hid, act, slope, grad, inner, w_in, w_rows, cotangent, stream, first, second,
 ):
-    batch = lax.axis_index("batch")
-    links = Links(send_sem, recv_sem)
-    kept = [
-        row_view(ref, bit_of(batch, order[0]) * out.shape[0], out.shape[0])
-        for ref, out, order in zip((ride_a, ride_b), (kept_a, kept_b), ride_orders(nb))
-    ]
-    loads = Loads(load_sem, [(w_in_hbm, w_in), (kept[0], kept_a), (kept[1], kept_b)])
     rows, features = rows_ref.shape
-    links.greet(
-        [links.near, links.far, links.across]
-        + [{"batch": lax.rem(batch + j, nb)} for j in range(1, nb)]
+    half = rows // 2
+    gain, shift = vector_row(pack, 4), vector_row(pack, 19)
+
+    def fill(h):
+        at = slice(h * half, (h + 1) * half)
+        hid[0, at] = b16(norm_rows(rows_ref[at], gain, shift))
+
+    up, down = ffn_up(hid, act, slope, w_in, b_ref, 1), ffn_down(act, w_rows)
+
+    def work(block, emit):
+        loads.need(2)
+        up(block)
+        loads.need(3)
+        down(block, emit)
+
+    sums = gather_work_scatter(links, hid, fill, work, first)
+    last_gain, last_shift, out_bias = vector_row(pack, 5), vector_row(pack, 21), vector_row(pack, 20)
+    live = f32(pack[links.shard, 27:28, 0:1])
+    mask = f32(f32(lax.broadcasted_iota(jnp.int32, (rows, 1), 0)) < live)
+    loads.need(4)
+    ends = []
+
+    def turn_back(h):
+        at = slice(h * half, (h + 1) * half)
+        scaled, inverse = norm_parts(rows_ref[at] + 0.5 * (sums.arrive(h) + out_bias))
+        result[at] = (scaled * last_gain + last_shift) * mask[at]
+        given = cotangent[at] * mask[at]
+        slide = norm_slope(given, scaled, inverse, last_gain)
+        stream[at] = slide
+        grad[0, at] = b16(0.5 * slide)
+        ends.append((column_sum(given * scaled), column_sum(given)))
+
+    back = gather_work_scatter(
+        links, grad, turn_back, ffn_inward(grad, inner, slope, w_in, w_rows), second
     )
-    orders = ride_orders(nb)
-    pieces = 4
-    ride = [
-        Rider(batch, send_sem, recv_sem, at * pieces).halve_pieces(
-            source_ref, landing, orders[at][0], pieces, landing.shape[0]
-        )
-        for at, (source_ref, landing) in enumerate(((ride_a, half_a), (ride_b, half_b)))
-    ]
-    for start, _, _ in ride:
-        start(EARLY)
+    weight_out(act, grad, gw_out)
+    for p in range(EARLY):
+        riders[1][0](p)
+    weight_in(hid, inner, gw_in, sums_ref)
+    for p in range(EARLY):
+        riders[0][0](p)
+    sums_ref[0:3, :] = jnp.zeros((3, features), jnp.float32)
+    sums_ref[2:3, :] = column_sum(f32(grad[0]))
+    sums_ref[4:5, :] = ends[0][0] + ends[1][0]
+    sums_ref[5:6, :] = ends[0][1] + ends[1][1]
+    sums_ref[6:8, :] = jnp.zeros((2, features), jnp.float32)
+    for h in range(2):
+        at = slice(h * half, (h + 1) * half)
+        scaled, inverse = norm_parts(rows_ref[at])
+        given = back.arrive(h)
+        out_ref[at] = stream[at] + norm_slope(given, scaled, inverse, gain)
+        sums_ref[0:1, :] += column_sum(given * scaled)
+        sums_ref[1:2, :] += column_sum(given)
+
+
+def conv_back_part(
+    links, nb, ride_on, stream_ref, rows_ref, pack, w_in, w_out,
+    hid, open_ref, gate_ref, gated_ref, scaled_ref, act, slope, stats,
+    out_ref, gw_out, gw_in, sums_ref,
+    padded, normed, grad, inner, source, mid, land_s, land_b, sems,
+):
+    rows, features = rows_ref.shape
     lanes = features // 128
     lead, tile, taps = 8, 512, 5
     grad[...] = b16(stream_ref[...])
@@ -1470,11 +1373,9 @@
 
         sums_ref[4:5, :] = jnp.sum(f32(grad[...]), axis=0, keepdims=True)
 
-    sums = everywhere(links, nb, source, mid, land_s, land_b, None, meanwhile, (ss, rs, sb, rb))
+    sums = everywhere(links, nb, source, mid, land_s, land_b, None, meanwhile, sems)
     beta, gamma = unpack_rows(sums, 0, lanes), unpack_rows(sums, lanes, lanes)
-    for p in range(EARLY + 1, pieces):
-        for start, _, _ in ride:
-            start(p)
+    ride_on()
     sums_ref[5:6, :] = gamma
     sums_ref[6:7, :] = beta
     inverse, frames = stats[0:1, :], stats[1:2, 0:1]
@@ -1498,7 +1399,6 @@
     inner[:, features:] = right
     sums_ref[2:3, :] = jnp.sum(f32(left), axis=0, keepdims=True)
     sums_ref[3:4, :] = jnp.sum(f32(right), axis=0, keepdims=True)
-    loads.need(0)
     total = dot_back(inner[...], w_in[...])
     scaled, inverse = norm_parts(rows_ref[...])
     out_ref[...] = stream_ref[...] + norm_slope(total, scaled, inverse, vector_row(pack, 2))
@@ -1509,58 +1409,120 @@
     def _(cols):
         gw_in[:, cols] = b16(dot_over(hid[...], inner[:, cols]))
 
-    loads.need(1, 2)
-    for (_, settle, _), own, landing, early in zip(ride, (kept_a, kept_b), (half_a, half_b), (early_a, early_b)):
+
+def centre_body(nb, *refs):
+    rows_ref, pack, b_ref, cw_in_hbm, cw_out_hbm, w_rows_hbm, cotangent_hbm, ffn_in, *refs = refs
+    result, out_ref, gwc_out, gwc_in, two_sums, conv_sums, half_a, half_b, *refs = refs
+    cw_in, cw_out, w_in, w_rows, cotangent, *refs = refs
+    three, hid_c, open_ref, gate_ref, gated_ref, scaled_ref, act_c, slope_c, stats, padded, *refs = refs
+    hid, act, slope, grad, inner, gw_in, gw_out, stream, between, normed, grad_c, inner_c, *refs = refs
+    sums_a, sums_b, (first, second) = refs[:5], refs[5:10], (refs[10:18], refs[18:26])
+    send_sem, recv_sem, ride_send, ride_recv, load_sem = refs[26:]
+    batch = lax.axis_index("batch")
+    links = Links(send_sem, recv_sem)
+    loads = Loads(
+        load_sem,
+        [
+            (cw_in_hbm, cw_in), (cw_out_hbm, cw_out), (ffn_in.at[1], w_in), (w_rows_hbm, w_rows),
+            (cotangent_hbm, cotangent),
+        ],
+    )
+    links.greet(
+        [links.near, links.far, links.across]
+        + [{"batch": lax.rem(batch + j, nb)} for j in range(1, nb)]
+    )
+    saved = (hid_c, open_ref, gate_ref, gated_ref, scaled_ref, act_c, slope_c, stats)
+    conv_part(links, nb, loads, rows_ref, pack, cw_in, cw_out, three, *saved, padded, *first[:4], first[4:])
+    orders = ride_orders(nb)
+    pieces = 4
+    riders = [
+        Rider(batch, ride_send, ride_recv, at * pieces).halve_pieces(
+            source, landing, orders[at][0], pieces, landing.shape[0]
+        )
+        for at, (source, landing) in enumerate(((gw_in, half_a), (gw_out, half_b)))
+    ]
+    middle_part(
+        links, loads, riders, three, pack, b_ref, result, between, gw_in, gw_out, two_sums,
+        hid, act, slope, grad, inner, w_in, w_rows, cotangent, stream, sums_a, sums_b,
+    )
+    for start, _, _ in riders:
+        start(EARLY)
+
+    def ride_on():
+        for p in range(EARLY + 1, pieces):
+            for start, _, _ in riders:
+                start(p)
+
+    conv_back_part(
+        links, nb, ride_on, between, rows_ref, pack, cw_in, cw_out, *saved, out_ref, gwc_out, gwc_in, conv_sums,
+        padded, normed, grad_c, inner_c, *second[:4], second[4:],
+    )
+    for (_, settle, own), landing in zip(riders, (half_a, half_b)):
         settle()
-        done = early.shape[0]
-        landing[0:done] = b16(f32(own[0:done]) + f32(early[...]))
-        landing[done:] = b16(f32(own[done:]) + f32(landing[done:]))
-
-
-def conv_back(stream, rows_in, pack, w_in, w_out, saved, ridden, early, ident):
+        landing[...] = b16(f32(own[...]) + f32(landing[...]))
+
+
+EARLY = 1
+
+
+def centre(rows_in, pack, b_in, wc_in, wc_out, w_rows, cotangent, ffn_in, ident):
     ns, nb = lax.axis_size("shard"), lax.axis_size("batch")
     rows, features = rows_in.shape
-    shape = jax.ShapeDtypeStruct
+    hidden = ffn_in.shape[2]
     low, full = jnp.bfloat16, jnp.float32
-    small = (2 * features // 128, 128)
+    shape, vmem, dma = jax.ShapeDtypeStruct, pltpu.VMEM, pltpu.SemaphoreType.DMA
+    wide, plain = vmem((4, rows, features), low), vmem((rows, features), low)
+    tall = vmem((4, rows, hidden), low)
+    whole = vmem((rows, features), full)
+    lanes = features // 128
+
+    def exchange_scratch(count):
+        small = (count, 128)
+        return [
+            vmem(small, full), vmem(small, full), vmem((ns,) + small, full), vmem((nb,) + small, full),
+            dma((ns,)), dma((ns,)), dma((nb,)), dma((nb,)),
+        ]
+
     return pl.pallas_call(
-        functools.partial(conv_back_body, nb),
+        functools.partial(centre_body, nb),
         out_shape=[
-            shape((rows, features), full), shape((features, features), low),
-            shape((features, 2 * features), low), shape((16, features), full),
+            shape((rows, features), full), shape((rows, features), full),
+            shape((features, features), low), shape((features, 2 * features), low),
+            shape((8, features), full), shape((16, features), full),
+            shape((features // 2, hidden), low), shape((hidden // 2, features), low),
+        ],
+        in_specs=[VMEM_SPEC] * 3 + [HBM_SPEC] * 5,
+        out_specs=[VMEM_SPEC] * 8,
+        scratch_shapes=[
+            vmem(wc_in.shape, low), vmem(wc_out.shape, low), vmem((features, hidden), low),
+            vmem((hidden, features), low), whole,
+            whole, plain, plain, plain, plain, whole, plain, plain, vmem((8, features), full),
+            vmem((rows + 16, features), full),
+            wide, tall, tall, wide, tall, vmem((features, hidden), low), vmem((hidden, features), low),
+            whole, whole, whole, plain, vmem((rows, 2 * features), low),
         ]
-        + [shape((r.shape[0] // 2, r.shape[1]), low) for r in ridden],
-        in_specs=[VMEM_SPEC] * 14 + [HBM_SPEC] * 3,
-        out_specs=[VMEM_SPEC] * 6,
-        scratch_shapes=[
-            pltpu.VMEM((rows + 16, features), full), pltpu.VMEM((rows, features), full),
-            pltpu.VMEM((rows, features), low), pltpu.VMEM((rows, 2 * features), low),
-            pltpu.VMEM(small, full), pltpu.VMEM(small, full),
-            pltpu.VMEM((ns,) + small, full), pltpu.VMEM((nb,) + small, full),
-            pltpu.SemaphoreType.DMA((ns,)), pltpu.SemaphoreType.DMA((ns,)),
-            pltpu.SemaphoreType.DMA((nb,)), pltpu.SemaphoreType.DMA((nb,)),
-        ]
-        + link_scratch(8, 1)[:2]
-        + [pltpu.VMEM(w_in.shape, low)]
-        + [pltpu.VMEM((r.shape[0] // 2, r.shape[1]), low) for r in ridden]
-        + [pltpu.SemaphoreType.DMA((3,))],
+        + sums_scratch(rows, features)
+        + sums_scratch(rows, features)
+        + exchange_scratch(2 * lanes + 8)
+        + exchange_scratch(2 * lanes)
+        + [dma((20,)), dma((20,)), dma((8,)), dma((8,)), dma((5,))],
         compiler_params=pltpu.CompilerParams(
-            collective_id=ident, has_side_effects=True, vmem_limit_bytes=60 << 20
+            collective_id=ident, has_side_effects=True, vmem_limit_bytes=62 << 20
         ),
-        name="conv_back",
-    )(stream, rows_in, pack, w_out, *saved, *early, w_in, *ridden)
+        name="centre",
+    )(rows_in, pack, b_in, wc_in, wc_out, w_rows, cotangent, ffn_in)
 
 
 def rear_body(
     heads, size, nb, stream_ref, rows_ref, pack, w_mine, ride_a, ride_b,
     hid_b_hbm, with_u_hbm, with_v_hbm, key_hbm, value_hbm, soft_hbm, mix_hbm, table_hbm, proj_hbm, w_qkv_hbm,
     start_hbm, hid_hbm, act_hbm, slope_hbm, w_rows_hbm, ffn_in,
-    out_ref, gw_q, gw_k, gw_x, gw_pos, gw_mix, mix_sums, own_sums, gw_in, gw_out, sums_ref, out_a, out_b,
+    out_ref, half_q, half_k, half_x, half_pos, gw_mix, mix_sums, own_sums, gw_in, gw_out, sums_ref, out_a, out_b,
     grad, dq, dk, dx, dp, stream, grad_b, inner, start, hid, act, slope, w_rows, w_in,
     hid_b, with_u, with_v, key, value, soft_ref, mix, table, proj, w_qkv, *refs,
 ):
     first, second, refs = refs[:5], refs[5:10], refs[10:]
-    send_sem, recv_sem, ride_send, ride_recv, load_sem, *between = refs
+    send_sem, recv_sem, ride_send, ride_recv, load_sem, gw_q, gw_k, gw_x, gw_pos, halve_send, halve_recv, *between = refs
     links = Links(send_sem, recv_sem)
     batch = lax.axis_index("batch")
     loads = Loads(
@@ -1678,6 +1640,11 @@
             total = total + dot_over(table[:, cols], dp[slot])
         gw_pos[cols, :] = b16(total)
 
+    halver = Rider(batch, halve_send, halve_recv, 0)
+    halvings = [
+        halver.halve(source, landing, 0)
+        for source, landing in ((gw_q, half_q), (gw_k, half_k), (gw_x, half_x), (gw_pos, half_pos))
+    ]
     gw_mix[...] = b16(dot_over(flat(mix), flat(grad)))
     mix_sums[...] = jnp.zeros_like(mix_sums)
     mix_sums[2:3, :] = column_sum(f32(grad[0]))
@@ -1720,6 +1687,8 @@
         out_ref[at] = stream[at] + norm_slope(given, scaled, inverse, gain)
         sums_ref[0:1, :] += column_sum(given * scaled)
         sums_ref[1:2, :] += column_sum(given)
+    for end in halvings:
+        end()
     for chain in outward:
         while chain:
             chain.pop(0)()
@@ -1743,8 +1712,8 @@
         functools.partial(rear_body, heads, width // heads, nb),
         out_shape=[
             shape((rows, features), full),
-            shape((features, width), low), shape((features, width), low), shape((features, width), low),
-            shape((features, width), low),
+            shape((features // 2, width), low), shape((features // 2, width), low),
+            shape((features // 2, width), low), shape((features // 2, width), low),
             shape((width, features), low), shape((8, features), full), shape((8, width), full),
             shape((features, hidden), low), shape((hidden, features), low), shape((8, features), full),
         ]
@@ -1761,6 +1730,8 @@
         + sums_scratch(rows, features)
         + sums_scratch(rows, features)
         + [dma((24,)), dma((24,)), dma((4 * steps,)), dma((4 * steps,)), dma((16,))]
+        + [vmem((features, width), low)] * 4
+        + [dma((4,)), dma((4,))]
         + between,
         compiler_params=pltpu.CompilerParams(
             collective_id=ident, has_side_effects=True, vmem_limit_bytes=62 << 20
@@ -1800,15 +1771,8 @@
         heads, 5,
     )
     saved_mix = (hidden_mix, with_u, with_v, key, value, soft, mix)
-    rows_three, *saved_conv = conv_forward(
-        rows_two, pack, wc_in, wc_out, 10
-    )
-    result, stream, two_in, two_out, two_sums, *early = middle(
-        rows_three, pack, ffn_bias, w_rows_two, cotangent[0], ffn_in, 6
-    )
-
-    stream, grad_conv_out, grad_conv_in, conv_sums, *ridden = conv_back(
-        stream, rows_two, pack, wc_in, wc_out, saved_conv, (two_in, two_out), early, 11
+    result, stream, grad_conv_out, grad_conv_in, two_sums, conv_sums, *ridden = centre(
+        rows_two, pack, ffn_bias, wc_in, wc_out, w_rows_two, cotangent[0], ffn_in, 6
     )
     stream, grad_q, grad_k, grad_x, grad_pos, grad_out, mix_sums, own_sums, one_in, one_out, one_sums, *ridden = rear(
         stream, rows_one, pack, saved_mix, table, proj, qkv_proj, w_mine, ridden, rows_in, saved_one, w_rows_one,
@@ -1821,14 +1785,14 @@
         ridden,
         [one_sums, mix_sums, two_sums, conv_sums, own_sums],
         [("turn", 4, None), ("turn", 1, 0), ("plain", 0, 0)]
-        + [("plain", 2, at) for at in range(3)]
-        + [("plain", 3, None), ("gather", 5, None), ("gather", 6, None)],
+        + [("half", 2, at) for at in range(3)]
+        + [("half", 3, None), ("gather", 5, None), ("gather", 6, None)],
         [
             (2, tall, deep), (2, ns * deep, width), (3, tall, width), (tall, width), (tall, width),
             (tall, 2 * width), (tall, width),
         ],
         ["near", "line"],
-        [width, piece, piece] + [min(tall, 4 * piece)] * 4 + [2 * piece, min(tall, 4 * piece)],
+        [width, piece, piece] + [tall // 4] * 4 + [2 * piece, min(tall, 4 * piece)],
         deep,
         4,
     )

time: 517 us -> 500 us (0.967)
  Pallas kernels: 510 us -> 493 us
    pallas_call x3 -> x1, Pallas kernels: 111 us -> 95.7 us  [centre(): pl.pallas_call(functools.partial(centre_body, nb), out_shape=[shape((rows...]
where the time goes in v9:
time: 500 us; the launch traced here: 496 us
  Pallas kernels  493 us (99%)
    pallas_call x1, Pallas kernels, tail_sum(): pl.pallas_call(functools.partial(tail_body, specs, chunks, ns, nb, len(ar...  214 us
    pallas_call x1, Pallas kernels, centre(): pl.pallas_call(functools.partial(centre_body, nb), out_shape=[shape((rows...  95.7 us
    pallas_call x1, Pallas kernels, front(): pl.pallas_call(functools.partial(front_body, heads, width // heads), out_...  84 us
    pallas_call x1, Pallas kernels, rear(): pl.pallas_call(functools.partial(rear_body, heads, width // heads, nb), o...  83.6 us
    pallas_call x1, Pallas kernels, widen(): pl.pallas_call(functools.partial(widen_body, len(arrays), len(others), sl...  15.6 us

profile of v9, /device:TPU:0, one launch (start us, length us, event | category | flops | bytes accessed | tf_op | source)
XLA Modules:
  0.0 495.9 jit_solution(7332453613553647489)
XLA Ops:
  1.3 0.1 pad_maximum_fusion.1
  1.4 0.4 multiply_sine_fusion
  1.8 0.7 pad_maximum_fusion.base_ref
  2.5 84.0 %front.1 = (f32[256,1024]{1,0:T(8,128)}, f32[256,1024]{1,0:T(8,128)}, bf16[4,32,256]{2,1,0:T(8,128)(2,1)}, bf16[512,1024]{1,0:T(8,128)(2,1)}, bf16[512,256]{1,0:...) custom-call(f32[256,1024]{1,0:T(8,128)} %bitcast.4, ...), custom_call_target="tpu_custom_call" | custom-call | tf_op jit(solution)/shard_map/front/pallas_call | solution.py:1164
  86.5 95.7 %centre.1 = (f32[256,1024]{1,0:T(8,128)}, f32[256,1024]{1,0:T(8,128)}, bf16[1024,1024]{1,0:T(8,128)(2,1)}, bf16[1024,2048]{1,0:T(8,128)(2,1)}, f32[8,1024]{1,0:T...) custom-call(f32[256,1024]{1,0:T(8,128)} %get-tuple-element.78.refs_0_, ...), custom_call_target="tpu_custom_call" | custom-call | tf_op jit(solution)/shard_map/centre/pallas_call | solution.py:1486
  182.2 83.6 %rear.1 = (f32[256,1024]{1,0:T(8,128)}, bf16[512,256]{1,0:T(8,128)(2,1)}, bf16[512,256]{1,0:T(8,128)(2,1)}, bf16[512,256]{1,0:T(8,128)(2,1)}, bf16[512,256]{1,0:...) custom-call(f32[256,1024]{1,0:T(8,128)} %get-tuple-element.83.stream, ...), custom_call_target="tpu_custom_call" | custom-call | tf_op jit(solution)/shard_map/rear/pallas_call | solution.py:1711
  265.8 214.2 %tail_sum.1 = (bf16[2,1024,1024]{2,1,0:T(8,128)(2,1)}, bf16[2,4096,256]{2,1,0:T(8,128)(2,1)}, bf16[3,1024,256]{2,1,0:T(8,128)(2,1)}, bf16[1024,256]{1,0:T(8,128)...) custom-call(f32[8,1024]{1,0:T(8,128)} %get-tuple-element.101.refs_0_, ...), custom_call_target="tpu_custom_call" | custom-call | tf_op jit(solution)/shard_map/tail_sum/pallas_call | solution.py:591
  480.0 15.6 %widen.1 = (f32[2,1024,1024]{2,1,0:T(8,128)}, f32[2,4096,256]{2,1,0:T(8,128)}, f32[3,1024,256]{2,1,0:T(8,128)}, f32[1024,256]{1,0:T(8,128)}, f32[1024,256]{1,0:T...) custom-call(bf16[2,1024,1024]{2,1,0:T(8,128)(2,1)} %get-tuple-elemen, ...), custom_call_target="tpu_custom_call" | custom-call | tf_op jit(solution)/shard_map/widen/pallas_call | solution.py:661
  (3 shorter events, 0.0 us)

commit v10 on v9

--- a/solution.py
+++ b/solution.py
@@ -528,11 +528,12 @@
         ready, late[:] = late[:], []
         if r == 1:
             vectors_on()
-        if r == 2:
+        if r == 1:
             end_b()
             turn(len(chunks), ride_fin, 0, ride_fin.shape[0], 1, 1)
         if r == 3:
             vectors_out()
+        if r == 1:
             end_a()
             leave(0, 1, 0, outs[0].shape[1])
         for s, m in zip(starts, movers):
@@ -1611,12 +1612,12 @@
     near.wait()
     work(1, sums.give)
     sums.send_near()
-    tick(inward)
     on = []
     for h in range(2):
         out[h].wait()
         there = pl.ds(h * half, half)
         on.append(links.go(grad.at[2, there], grad.at[3, there], links.near))
+    tick(inward)
     for copy in on:
         copy.wait()
     work(3, sums.give_far)

time: 500 us -> 498 us (level)
  no operation moved by 1% of the time
where the time goes in v10:
time: 498 us; the launch traced here: 495 us
  Pallas kernels  492 us (99%)
    pallas_call x1, Pallas kernels, tail_sum(): pl.pallas_call(functools.partial(tail_body, specs, chunks, ns, nb, len(ar...  214 us
    pallas_call x1, Pallas kernels, centre(): pl.pallas_call(functools.partial(centre_body, nb), out_shape=[shape((rows...  95.7 us
    pallas_call x1, Pallas kernels, front(): pl.pallas_call(functools.partial(front_body, heads, width // heads), out_...  84 us
    pallas_call x1, Pallas kernels, rear(): pl.pallas_call(functools.partial(rear_body, heads, width // heads, nb), o...  82.9 us
    pallas_call x1, Pallas kernels, widen(): pl.pallas_call(functools.partial(widen_body, len(arrays), len(others), sl...  15.6 us

profile of v10, /device:TPU:0, one launch (start us, length us, event | category | flops | bytes accessed | tf_op | source)
XLA Modules:
  0.0 494.5 jit_solution(11377853846627382102)
XLA Ops:
  1.3 0.1 pad_maximum_fusion.1
  1.4 0.4 multiply_sine_fusion
  1.8 0.7 pad_maximum_fusion.base_ref
  2.5 84.0 %front.1 = (f32[256,1024]{1,0:T(8,128)}, f32[256,1024]{1,0:T(8,128)}, bf16[4,32,256]{2,1,0:T(8,128)(2,1)}, bf16[512,1024]{1,0:T(8,128)(2,1)}, bf16[512,256]{1,0:...) custom-call(f32[256,1024]{1,0:T(8,128)} %bitcast.4, ...), custom_call_target="tpu_custom_call" | custom-call | tf_op jit(solution)/shard_map/front/pallas_call | solution.py:1165
  86.5 95.7 %centre.1 = (f32[256,1024]{1,0:T(8,128)}, f32[256,1024]{1,0:T(8,128)}, bf16[1024,1024]{1,0:T(8,128)(2,1)}, bf16[1024,2048]{1,0:T(8,128)(2,1)}, f32[8,1024]{1,0:T...) custom-call(f32[256,1024]{1,0:T(8,128)} %get-tuple-element.78.refs_0_, ...), custom_call_target="tpu_custom_call" | custom-call | tf_op jit(solution)/shard_map/centre/pallas_call | solution.py:1487
  182.2 82.9 %rear.1 = (f32[256,1024]{1,0:T(8,128)}, bf16[512,256]{1,0:T(8,128)(2,1)}, bf16[512,256]{1,0:T(8,128)(2,1)}, bf16[512,256]{1,0:T(8,128)(2,1)}, bf16[512,256]{1,0:...) custom-call(f32[256,1024]{1,0:T(8,128)} %get-tuple-element.83.stream, ...), custom_call_target="tpu_custom_call" | custom-call | tf_op jit(solution)/shard_map/rear/pallas_call | solution.py:1712
  265.1 213.6 %tail_sum.1 = (bf16[2,1024,1024]{2,1,0:T(8,128)(2,1)}, bf16[2,4096,256]{2,1,0:T(8,128)(2,1)}, bf16[3,1024,256]{2,1,0:T(8,128)(2,1)}, bf16[1024,256]{1,0:T(8,128)...) custom-call(f32[8,1024]{1,0:T(8,128)} %get-tuple-element.101.refs_0_, ...), custom_call_target="tpu_custom_call" | custom-call | tf_op jit(solution)/shard_map/tail_sum/pallas_call | solution.py:592
  478.7 15.6 %widen.1 = (f32[2,1024,1024]{2,1,0:T(8,128)}, f32[2,4096,256]{2,1,0:T(8,128)}, f32[3,1024,256]{2,1,0:T(8,128)}, f32[1024,256]{1,0:T(8,128)}, f32[1024,256]{1,0:T...) custom-call(bf16[2,1024,1024]{2,1,0:T(8,128)(2,1)} %get-tuple-elemen, ...), custom_call_target="tpu_custom_call" | custom-call | tf_op jit(solution)/shard_map/widen/pallas_call | solution.py:662
  (3 shorter events, 0.0 us)
